TPU v7x, 32 devices: a whole 2x2x4 slice. The times are simulated.
32 devices in a mesh: groups: 1, context: 8 (over y, x, core), span: 4 (over z).
Axes of the slice: x: 2, y: 2, z: 4, core: 2. Of those that a mesh axis runs over, the one named last changes fastest.
Arguments:
- raw_tokens: bfloat16 [1536, 2048], P(('groups', 'context'), 'span'), may hold values from -6 to 6
- keep: int32 [8, 32], P(('groups', 'context')), may hold values from -1 to 191, as said below
- attn_gain: float32 [2048], replicated, may hold values from 0.25 to 1.75
- query_weight: bfloat16 [2048, 4608], P(None, 'span'), may hold values from -5 to 5
- latent_weight: bfloat16 [2048, 576], P(None, 'span'), may hold values from -0.5 to 0.5
- kv_gain: float32 [512], replicated, may hold values from 0.25 to 1.75
- out_weight: bfloat16 [4096, 2048], P('span', 'context'), may hold values from -0.25 to 0.25
- moe_gain: float32 [2048], replicated, may hold values from 0.25 to 1.75
- expert_ids: int32 [256, 6], P(('groups', 'context', 'span')), may hold values from 0 to 15, all different within a row; in each aligned block of 8 rows (0 to 7, 8 to 15, ...) at most 6 rows name the same one
- gate_values: float32 [256, 6], P(('groups', 'context', 'span')), may hold values from 0.05 to 0.5
- expert_slot: int32 [16], replicated, may hold values from 0 to 15, each once
- expert_in: bfloat16 [32, 2, 2048, 704], P(('context', 'span')), may hold values from -0.125 to 0.125
- expert_out: bfloat16 [32, 704, 2048], P(('context', 'span')), may hold values from -0.15625 to 0.15625
Outputs:
- layer_out: bfloat16 [256, 2048], P(('groups', 'context', 'span'))
- latent_cache: bfloat16 [256, 576], P(('groups', 'context'))
Inputs may be any that keep to these rules, and one draw needn't show every extreme that they name: `keep`: row c lists the kept positions among the 192 raw tokens of span c in increasing order, then -1 in the empty entries; every span keeps 32 // 2 or more, and in every draw some span keeps 32. `expert_ids`: in each aligned block of 8 rows (the rows of one device) no expert is named more than 6 times, a bound that some block reaches. `expert_slot`: each stored slot holds exactly one routed expert.
All inputs are finite; a program needn't handle non-finite values.
Results may differ from a plain program's by a relative error of at most 0.013.
Values may be sent and summed in bfloat16 or wider, within the bound.
No kernel may reach another device: no remote copies, remote signals or barrier semaphores. Data moves between devices by JAX's collectives and lax.ppermute only.
A program may use at most 64 MiB of HBM per device.

v0:
```python
import functools
import math

import jax
import jax.numpy as jnp
from jax import lax
from jax.experimental import pallas as pl
from jax.experimental.pallas import tpu as pltpu
from jax.sharding import PartitionSpec as P


EPS = 1e-06
THETA = 50000.0
SCALE = 192.0 ** (-0.5)
NEGATIVE = -1e30
LANES = 128
F32 = jnp.float32
BF16 = jnp.bfloat16
MIB = 1 << 20


VM = pl.BlockSpec(memory_space=pltpu.VMEM)
ANY = pl.BlockSpec(memory_space=pl.ANY)
HBM = pl.BlockSpec(memory_space=pltpu.HBM)


def up(count, unit=LANES):
    return -(-count // unit) * unit


def shape(dims, dtype):
    return jax.ShapeDtypeStruct(tuple(dims), dtype)


def call(kernel, outs, in_specs, args, scratch=(), flops=0, moved=0, limit=16):
    single = not isinstance(outs, (list, tuple))
    args = [
        pltpu.with_memory_space_constraint(value, pltpu.HBM) if spec is HBM else value
        for spec, value in zip(in_specs, args)
    ]
    return pl.pallas_call(
        kernel,
        out_shape=outs,
        in_specs=in_specs,
        out_specs=VM if single else [VM] * len(outs),
        scratch_shapes=list(scratch),
        compiler_params=pltpu.CompilerParams(vmem_limit_bytes=limit * MIB),
        cost_estimate=pl.CostEstimate(flops=flops, bytes_accessed=moved, transcendentals=0),
    )(*args)


def nt(left, right):
    return lax.dot_general(left, right, (((1,), (1,)), ((), ())), preferred_element_type=F32)


def nn(left, right):
    return jnp.dot(left, right, preferred_element_type=F32)


def here():
    return lax.axis_index("context"), lax.axis_index("span")


def partner(values, axis, mask):
    count = lax.axis_size(axis)
    return lax.ppermute(values, axis, [(i, i ^ mask) for i in range(count)])


def gathered(values, axis, masks):
    parts = [values]
    for mask in masks:
        parts.append(partner(values, axis, mask))
    return parts


def natural(parts, index):
    bit = 1
    while bit < len(parts):
        swap = (index & bit) != 0
        parts = [jnp.where(swap, parts[k ^ bit], parts[k]) for k in range(len(parts))]
        bit *= 2
    return parts


def pick_kernel(
    keep_hbm,
    raw_hbm,
    weight_hbm,
    gain_hbm,
    ids_hbm,
    gates_hbm,
    slot_hbm,
    out_ref,
    weight_ref,
    gain_ref,
    dense_ref,
    keep_ref,
    raw_ref,
    ids_ref,
    gates_ref,
    slot_ref,
    sem,
):
    pairs = [
        (keep_hbm, keep_ref),
        (raw_hbm, raw_ref),
        (ids_hbm, ids_ref),
        (gates_hbm, gates_ref),
        (slot_hbm, slot_ref),
        (gain_hbm, gain_ref),
        (weight_hbm, weight_ref),
    ]
    copies = [pltpu.make_async_copy(a, b, sem.at[n]) for n, (a, b) in enumerate(pairs)]
    for copy in copies:
        copy.start()
    copies[0].wait()
    copies[1].wait()
    rows = lax.broadcasted_iota(jnp.int32, (raw_ref.shape[0], keep_ref.shape[1]), 0)
    hits = jnp.where(rows == keep_ref[...], 1.0, 0.0).astype(BF16)
    out_ref[...] = lax.dot_general(
        hits, raw_ref[...], (((0,), (0,)), ((), ())), preferred_element_type=F32
    ).astype(BF16)
    for copy in copies[2:]:
        copy.wait()
    ids = ids_ref[...]
    slots = jnp.zeros_like(ids)
    for e in range(slot_ref.shape[0]):
        slots = jnp.where(ids == e, slot_ref[e], slots)
    lane = lax.broadcasted_iota(jnp.int32, dense_ref.shape, 1)
    gates = jnp.zeros(dense_ref.shape, F32)
    for t in range(ids.shape[1]):
        gates = gates + jnp.where(lane == slots[:, t : t + 1], gates_ref[:, t : t + 1], 0.0)
    dense_ref[...] = gates


def latent_kernel(spans, *refs):
    parts = refs[:spans]
    gain_ref, weight_ref, dense_ref, compact_ref, normed_ref, sent_ref = refs[spans:]
    index = here()[1]
    rows, block = parts[0].shape
    values = [p[...].astype(F32) for p in parts]
    square = sum(jnp.sum(v * v, axis=1, keepdims=True) for v in values)
    factor = lax.rsqrt(square / (spans * block) + EPS)
    for k in range(spans):
        at = pl.ds(pl.multiple_of((index ^ k) * block, block), block)
        compact_ref[:, at] = parts[k][...]
        normed_ref[:, at] = (values[k] * factor * gain_ref[:, at]).astype(BF16)
    sent_ref[0:rows, :] = jnp.zeros((rows, sent_ref.shape[1]), F32)
    sent_ref[0:rows, 0 : weight_ref.shape[0]] = nt(normed_ref[...], weight_ref[...])
    sent_ref[rows:, :] = dense_ref[...]


def rotated(values, cosine, sine):
    half = values.shape[1] // 2
    swapped = jnp.concatenate([values[:, half:], values[:, :half]], axis=1)
    return values * cosine + swapped * sine


def query_kernel(
    heads,
    raw_rows,
    normed_ref,
    weight_ref,
    keep_hbm,
    kv_hbm,
    moe_hbm,
    out_ref,
    cos_ref,
    sin_ref,
    live_ref,
    kv_ref,
    moe_ref,
    buf,
    keep_ref,
    sem,
):
    rows = normed_ref.shape[0]
    latent = weight_ref.shape[1] // heads
    steps = buf.shape[0]
    deep = buf.shape[1]
    small = [(keep_hbm, keep_ref), (kv_hbm, kv_ref), (moe_hbm, moe_ref)]
    small = [pltpu.make_async_copy(a, b, sem.at[steps + n]) for n, (a, b) in enumerate(small)]
    copies = [
        pltpu.make_async_copy(weight_ref.at[pl.ds(n * deep, deep), :], buf.at[n], sem.at[n])
        for n in range(steps)
    ]
    for copy in small + copies:
        copy.start()
    small[0].wait()
    diagonal = lax.broadcasted_iota(jnp.int32, (rows, rows), 0) == lax.broadcasted_iota(
        jnp.int32, (rows, rows), 1
    )
    listing = jnp.sum(
        jnp.where(diagonal, keep_ref[...].astype(F32), 0.0), axis=1, keepdims=True
    )
    live_ref[...] = jnp.where(listing >= 0, 1.0, 0.0)
    positions = (here()[0] * raw_rows).astype(F32) + jnp.maximum(listing, 0.0)
    rope = cos_ref.shape[1]
    half = rope // 2
    lane = lax.broadcasted_iota(jnp.int32, (rows, rope), 1)
    first = lane < half
    place = jnp.where(first, lane, lane - half).astype(F32)
    angles = positions * jnp.exp(place * (-2.0 / rope * math.log(THETA)))
    cos_ref[...] = jnp.cos(angles)
    sine = jnp.sin(angles)
    sin_ref[...] = jnp.where(first, -sine, sine)
    total = jnp.zeros((rows, weight_ref.shape[1]), F32)
    for n in range(steps):
        copies[n].wait()
        total = total + nn(normed_ref[:, n * deep : (n + 1) * deep], buf[n])
    kv_rank = latent - rope
    out_ref[...] = jnp.zeros(out_ref.shape, BF16)
    for h in range(heads):
        one = total[:, h * latent : (h + 1) * latent]
        out_ref[h * rows : (h + 1) * rows, 0:kv_rank] = one[:, :kv_rank].astype(BF16)
        out_ref[h * rows : (h + 1) * rows, kv_rank:latent] = rotated(
            one[:, kv_rank:], cos_ref[...], sin_ref[...]
        ).astype(BF16)
    for copy in small[1:]:
        copy.wait()


def cache_kernel(spans, width, experts, *refs):
    parts = refs[:spans]
    live_ref, gain_ref, cos_ref, sin_ref, cached_ref, sent_ref = refs[spans:]
    rows = live_ref.shape[0]
    kv_rank = gain_ref.shape[1]
    values = natural([p[...] for p in parts], here()[1])
    latent = jnp.concatenate([v[:rows, :width] for v in values], axis=1)
    gates = jnp.concatenate([v[rows:, :experts] for v in values], axis=0)
    nope = latent[:, :kv_rank]
    factor = lax.rsqrt(jnp.mean(nope * nope, axis=1, keepdims=True) + EPS)
    nope = nope * factor * gain_ref[...]
    rope = rotated(latent[:, kv_rank:], cos_ref[...], sin_ref[...])
    cached_ref[:, :kv_rank] = nope.astype(BF16)
    cached_ref[:, kv_rank:] = rope.astype(BF16)
    high = gates.astype(BF16).astype(F32)
    used = rope.shape[1] + 2 * experts + 1
    tail = [rope, high, gates - high, live_ref[...]]
    rest = sent_ref.shape[1] - kv_rank - used
    if rest:
        tail.append(jnp.zeros((rows, rest), F32))
    sent_ref[:, :kv_rank] = nope.astype(BF16)
    sent_ref[:, kv_rank:] = jnp.concatenate(tail, axis=1).astype(BF16)


def attend_kernel(heads, kv_rank, flag_lane, blocks, query_ref, mine_ref, theirs_ref, *refs):
    weights = refs[:blocks]
    out_ref, buf, sem = refs[blocks:]
    copies = [pltpu.make_async_copy(weights[n], buf.at[n], sem.at[n]) for n in range(blocks)]
    for copy in copies:
        copy.start()
    count = query_ref.shape[0] // heads
    index = here()[0]
    keys = jnp.concatenate([mine_ref[...], theirs_ref[...]], axis=0)
    total = keys.shape[0]
    width = keys.shape[1]
    lane = lax.broadcasted_iota(jnp.int32, (8, width), 1)
    flags = nt(jnp.where(lane == flag_lane, 1.0, 0.0).astype(BF16), keys)[0:1, :]
    row = lax.broadcasted_iota(jnp.int32, (count, total), 0)
    col = lax.broadcasted_iota(jnp.int32, (count, total), 1)
    half = blocks // 2
    at = col // count
    which = jnp.where(at < half, 2 * at, 2 * (at - half) + 1)
    key_ids = (which ^ index) * count + col % count
    allowed = (key_ids <= index * count + row) & (flags > 0)
    mixed = []
    for h in range(heads):
        scores = nt(query_ref[h * count : (h + 1) * count, :], keys) * SCALE
        scores = jnp.where(allowed, scores, NEGATIVE)
        highest = jnp.max(scores, axis=1, keepdims=True)
        weight = jnp.where(allowed, jnp.exp(scores - highest), 0.0)
        denominator = jnp.sum(weight, axis=1, keepdims=True)
        summed = nn(weight.astype(BF16), keys[:, :kv_rank])
        mixed.append((summed / denominator).astype(BF16))
    mixed = jnp.concatenate(mixed, axis=1)
    block = buf.shape[2]
    for n in range(blocks):
        i = 2 * n if n < half else 2 * (n - half) + 1
        copies[n].wait()
        place = pl.ds(pl.multiple_of((index ^ i) * block, block), block)
        out_ref[:, place] = nn(mixed, buf[n]).astype(BF16)


def resid_kernel(spans, *refs):
    parts = refs[:spans]
    compact_ref, gain_ref, own_ref, out_ref, buf = refs[spans:]
    resid = compact_ref[...].astype(F32) + sum(p[...].astype(F32) for p in parts)
    factor = lax.rsqrt(jnp.mean(resid * resid, axis=1, keepdims=True) + EPS)
    out_ref[...] = (resid * factor * gain_ref[...]).astype(BF16)
    buf[...] = resid
    count = own_ref.shape[0]
    own_ref[...] = buf[pl.ds(pl.multiple_of(here()[1] * count, count), count), :]


def expert_kernel(
    first_lane,
    tail_at,
    experts,
    cuts,
    columns,
    mine_ref,
    theirs_ref,
    mine_tail_ref,
    theirs_tail_ref,
    in_ref,
    out_weight_ref,
    near_ref,
    far_ref,
    act_ref,
):
    rows = jnp.concatenate([mine_ref[...], theirs_ref[...]], axis=0)
    tail = jnp.concatenate([mine_tail_ref[:, tail_at:], theirs_tail_ref[:, tail_at:]], axis=0)
    tail = tail.astype(F32)
    lane = lax.broadcasted_iota(jnp.int32, tail.shape, 1) - first_lane
    index = here()
    slot = lax.div(index[0] * lax.axis_size("span") + index[1], 2)
    scale = jnp.sum(
        jnp.where((lane == slot) | (lane == slot + experts), tail, 0.0), axis=1, keepdims=True
    )
    for start, size in cuts:
        gate = nt(rows, in_ref[0, start : start + size, :])
        upper = nt(rows, in_ref[1, start : start + size, :])
        act_ref[:, start : start + size] = (gate / (1.0 + jnp.exp(-gate)) * upper).astype(BF16)
    half = mine_ref.shape[0]
    width = out_weight_ref.shape[1] // columns
    for n in range(columns):
        span = slice(n * width, (n + 1) * width)
        done = nn(act_ref[...], out_weight_ref[:, span])
        done = jnp.where(scale > 0, done * scale, 0.0).astype(BF16)
        near_ref[:, span] = done[:half]
        far_ref[:, span] = done[half:]


def level_kernel(near_ref, back_ref, *outs):
    rows = outs[0].shape[0]
    for n, out in enumerate(outs):
        at = slice(n * rows, (n + 1) * rows)
        out[...] = (near_ref[at, :].astype(F32) + back_ref[at, :].astype(F32)).astype(out.dtype)


def rows_kernel(spans, *refs):
    parts, outs, buf = refs[: -spans - 1], refs[-spans - 1 : -1], refs[-1]
    index = here()[1]
    total = parts[0][...]
    for p in parts[1:]:
        total = total + p[...].astype(F32)
    buf[...] = total
    count = outs[0].shape[0]
    for k, out in enumerate(outs):
        at = pl.ds(pl.multiple_of((index ^ k) * count, count), count)
        out[...] = buf[at, :].astype(out.dtype)


def last_kernel(spans, *refs):
    parts = refs[:spans]
    own_ref, live_ref, out_ref = refs[spans:]
    count = out_ref.shape[0]
    routed = sum(p[...].astype(F32) for p in parts)
    at = pl.ds(pl.multiple_of(here()[1] * count, count), count)
    total = own_ref[...] + routed
    out_ref[...] = jnp.where(live_ref[at, :] > 0, total, 0.0).astype(BF16)


def per_device(
    raw_tokens,
    keep,
    attn_gain,
    query_weight,
    latent_weight,
    kv_gain,
    out_weight,
    moe_gain,
    expert_ids,
    gate_values,
    expert_slot,
    expert_in,
    expert_out,
):
    kv_rank = kv_gain.shape[0]
    spans = lax.axis_size("span")
    contexts = lax.axis_size("context")
    part_width = latent_weight.shape[1]
    latent_width = part_width * spans
    rope = latent_width - kv_rank
    model = attn_gain.shape[0]
    kept = keep.shape[1]
    raw_rows = raw_tokens.shape[0]
    heads = query_weight.shape[1] // latent_width
    rows_dev = expert_ids.shape[0]
    experts = expert_slot.shape[0]
    hidden = expert_in.shape[3]
    evens = list(range(0, contexts, 2))

    sent_width = up(max(part_width, experts))
    picked, near_weight, gain, dense = call(
        pick_kernel,
        [
            shape((kept, raw_tokens.shape[1]), BF16),
            shape((part_width, model), BF16),
            shape((1, model), F32),
            shape((rows_dev, sent_width), F32),
        ],
        [HBM] * 7,
        (keep, raw_tokens, latent_weight.T, attn_gain[None], expert_ids, gate_values, expert_slot),
        scratch=[
            pltpu.VMEM(keep.shape, jnp.int32),
            pltpu.VMEM(raw_tokens.shape, BF16),
            pltpu.VMEM(expert_ids.shape, jnp.int32),
            pltpu.VMEM(gate_values.shape, F32),
            pltpu.SMEM(expert_slot.shape, jnp.int32),
            pltpu.SemaphoreType.DMA((7,)),
        ],
        limit=4,
    )
    parts = gathered(picked, "span", range(1, spans))
    weights_even = gathered(out_weight, "context", evens[1:])
    weights_odd = [partner(w, "context", 1) for w in weights_even]

    compact, normed, sent = call(
        functools.partial(latent_kernel, spans),
        [
            shape((kept, model), BF16),
            shape((kept, model), BF16),
            shape((kept + rows_dev, sent_width), F32),
        ],
        [VM] * (spans + 3),
        (*parts, gain, near_weight, dense),
        flops=2 * kept * latent_weight.size,
        moved=2 * latent_weight.size,
        limit=4,
    )
    parts = gathered(sent, "span", range(1, spans))
    steps = 8
    row_width = up(latent_width + 2 * experts + 1)
    query, cosine, sine, live, near_kv, near_moe = call(
        functools.partial(query_kernel, heads, raw_rows),
        [
            shape((heads * kept, row_width), BF16),
            shape((kept, rope), F32),
            shape((kept, rope), F32),
            shape((kept, 1), F32),
            shape((1, kv_rank), F32),
            shape((1, model), F32),
        ],
        [VM] + [HBM] * 4,
        (normed, query_weight, keep, kv_gain[None], moe_gain[None]),
        scratch=[
            pltpu.VMEM((steps, model // steps, query_weight.shape[1]), BF16),
            pltpu.VMEM(keep.shape, jnp.int32),
            pltpu.SemaphoreType.DMA((steps + 3,)),
        ],
        flops=2 * kept * query_weight.size,
        moved=2 * query_weight.size,
        limit=10,
    )
    cached, sent = call(
        functools.partial(cache_kernel, spans, part_width, experts),
        [shape((kept, latent_width), BF16), shape((kept, row_width), BF16)],
        [VM] * (spans + 4),
        (*parts, live, near_kv, cosine, sine),
        limit=4,
    )

    mine_keys = jnp.concatenate(gathered(sent, "context", evens[1:]), axis=0)
    their_keys = partner(mine_keys, "context", 1)
    partial = call(
        functools.partial(
            attend_kernel, heads, kv_rank, latent_width + 2 * experts, contexts
        ),
        shape((kept, model), BF16),
        [VM, VM, VM, HBM] + [ANY] * (contexts - 1),
        (query, mine_keys, their_keys, *weights_even, *weights_odd),
        scratch=[
            pltpu.VMEM((contexts, *out_weight.shape), BF16),
            pltpu.SemaphoreType.DMA((contexts,)),
        ],
        flops=2 * kept * contexts * out_weight.size,
        moved=2 * contexts * out_weight.size,
        limit=12,
    )

    got = gathered(partial, "span", range(1, spans))
    own, moe_in = call(
        functools.partial(resid_kernel, spans),
        [shape((rows_dev, model), F32), shape((kept, model), BF16)],
        [VM] * (spans + 2),
        (*got, compact, near_moe),
        scratch=[pltpu.VMEM((kept, model), F32)],
        limit=6,
    )

    mine = jnp.concatenate(gathered(moe_in, "context", evens[1:]), axis=0)
    theirs = partner(mine, "context", 1)
    half = mine.shape[0]
    cuts, start = [], 0
    while start < hidden:
        size = min(2 * LANES, hidden - start)
        cuts.append((start, size))
        start += size
    near, far = call(
        functools.partial(expert_kernel, latent_width - kv_rank, kv_rank, experts, cuts, 4),
        [shape((half, model), BF16), shape((half, model), BF16)],
        [VM] * 6,
        (mine, theirs, mine_keys, their_keys, jnp.swapaxes(expert_in[0], 1, 2), expert_out[0]),
        scratch=[pltpu.VMEM((2 * half, hidden), BF16)],
        flops=6 * 2 * half * hidden * model,
        moved=6 * hidden * model,
        limit=24,
    )

    levels = call(
        level_kernel,
        [shape((kept, model), F32)] + [shape((kept, model), BF16)] * (len(evens) - 1),
        [VM, VM],
        (near, partner(far, "context", 1)),
        limit=6,
    )
    got = [partner(level, "context", i) for level, i in zip(levels[1:], evens[1:])]
    rows = call(
        functools.partial(rows_kernel, spans),
        [shape((rows_dev, model), F32)] + [shape((rows_dev, model), BF16)] * (spans - 1),
        [VM] * len(levels),
        (levels[0], *got),
        scratch=[pltpu.VMEM((kept, model), F32)],
        limit=6,
    )
    got = []
    for k in range(1, spans):
        got.append(partner(rows[k], "span", k))
    layer_out = call(
        functools.partial(last_kernel, spans),
        shape((rows_dev, model), BF16),
        [VM] * (spans + 2),
        (rows[0], *got, own, live),
        limit=4,
    )
    return (layer_out, cached)


def solution(mesh):
    placed = (
        P(("groups", "context"), "span"),
        P(("groups", "context"), None),
        P(),
        P(None, "span"),
        P(None, "span"),
        P(),
        P("span", "context"),
        P(),
        P(("groups", "context", "span"), None),
        P(("groups", "context", "span"), None),
        P(),
        P(("context", "span"), None, None, None),
        P(("context", "span"), None, None),
    )
    return jax.shard_map(
        per_device,
        mesh=mesh,
        in_specs=placed,
        out_specs=(P(("groups", "context", "span"), None), P(("groups", "context"), None)),
        check_vma=False,
    )
```

profile of v0, /device:TPU:0, one launch (start us, length us, event | category | flops | bytes accessed | tf_op | source)
XLA Modules:
  0.0 95.2 jit_solution(17495921374173817198)
XLA Ops:
  0.6 3.0 %collective-permute-start.10 = (bf16[1024,256]{1,0:T(8,128)(2,1)}, bf16[1024,256]{1,0:T(8,128)(2,1)S(1)}, u32[]{:S(2)}, u32[]{:S(2)}) collective-permute-start(bf16[1024,256]{1,0:T(8,128)(2,1)} %refs_0_.1), channel_id=1, source_target_pairs={{0,8},{4,12},{8,0},{12,4},{16,24},{20,28},{24,16},{28,20},{1,9},{5... | collective-permute-start | bytes 1572872 | tf_op jit(solution)/shard_map/ppermute | solution.py:66
  3.7 1.5 %collective-permute-start.11 = (bf16[1024,256]{1,0:T(8,128)(2,1)}, bf16[1024,256]{1,0:T(8,128)(2,1)S(1)}, u32[]{:S(2)}, u32[]{:S(2)}) collective-permute-start(bf16[1024,256]{1,0:T(8,128)(2,1)} %refs_0_.1), channel_id=1, source_target_pairs={{0,16},{4,20},{8,24},{12,28},{16,0},{20,4},{24,8},{28,12},{1,17},{... | collective-permute-start | bytes 1572872 | tf_op jit(solution)/shard_map/ppermute | solution.py:66
  6.6 2.1 %collective-permute-start = (bf16[32,512]{1,0:T(8,128)(2,1)S(1)}, bf16[32,512]{1,0:T(8,128)(2,1)S(1)}, u32[]{:S(2)}, u32[]{:S(2)}) collective-permute-start(bf16[32,512]{1,0:T(8,128)(2,1)S(1)} %get-tuple-element.29.refs_0_), channel_id=1, source_target_pairs={{0,1},{1,0},{2,3},{3,2},{4,5},{5,4},{6,7},{7,6},{8,9},{9,8},{10,11... | collective-permute-start | bytes 98312 | tf_op jit(solution)/shard_map/ppermute | solution.py:66
  8.7 2.6 %collective-permute-start.1 = (bf16[32,512]{1,0:T(8,128)(2,1)S(1)}, bf16[32,512]{1,0:T(8,128)(2,1)S(1)}, u32[]{:S(2)}, u32[]{:S(2)}) collective-permute-start(bf16[32,512]{1,0:T(8,128)(2,1)S(1)} %get-tuple-element.29.refs_0_), channel_id=1, source_target_pairs={{0,2},{1,3},{2,0},{3,1},{4,6},{5,7},{6,4},{7,5},{8,10},{9,11},{10,... | collective-permute-start | bytes 98312 | tf_op jit(solution)/shard_map/ppermute | solution.py:66
  11.3 3.3 %collective-permute-start.2 = (bf16[32,512]{1,0:T(8,128)(2,1)S(1)}, bf16[32,512]{1,0:T(8,128)(2,1)S(1)}, u32[]{:S(2)}, u32[]{:S(2)}) collective-permute-start(bf16[32,512]{1,0:T(8,128)(2,1)S(1)} %get-tuple-element.29.refs_0_), channel_id=1, source_target_pairs={{0,3},{1,2},{2,1},{3,0},{4,7},{5,6},{6,5},{7,4},{8,11},{9,10},{10,... | collective-permute-start | bytes 98312 | tf_op jit(solution)/shard_map/ppermute | solution.py:66
  14.6 2.4 %collective-permute-done.2.refs_3_ = bf16[32,512]{1,0:T(8,128)(2,1)S(1)} collective-permute-done((bf16[32,512]{1,0:T(8,128)(2,1)S(1)}, bf16[32,512]{1,0:T(8,128)(2,1)S(1)}, u32[]{:S(2)}, u32[]{:S(2)}) %collective-permute-start.2) | collective-permute-done | bytes 32800 | tf_op jit(solution)/shard_map/ppermute | solution.py:66
  17.5 3.9 %collective-permute-start.4 = (f32[40,256]{1,0:T(8,128)S(1)}, f32[40,256]{1,0:T(8,128)S(1)}, u32[]{:S(2)}, u32[]{:S(2)}) collective-permute-start(f32[40,256]{1,0:T(8,128)S(1)} %get-tuple-element.35.refs_0_), channel_id=1, source_target_pairs={{0,2},{1,3},{2,0},{3,1},{4,6},{5,7},{6,4},{7,5},{8,10},{9,11},{10,... | collective-permute-start | bytes 122888 | tf_op jit(solution)/shard_map/ppermute | solution.py:66
  21.5 3.3 %collective-permute-start.5 = (f32[40,256]{1,0:T(8,128)S(1)}, f32[40,256]{1,0:T(8,128)S(1)}, u32[]{:S(2)}, u32[]{:S(2)}) collective-permute-start(f32[40,256]{1,0:T(8,128)S(1)} %get-tuple-element.35.refs_0_), channel_id=1, source_target_pairs={{0,3},{1,2},{2,1},{3,0},{4,7},{5,6},{6,5},{7,4},{8,11},{9,10},{10,... | collective-permute-start | bytes 122888 | tf_op jit(solution)/shard_map/ppermute | solution.py:66
  24.8 3.3 %shard_map.142 = (bf16[64,640]{1,0:T(8,128)(2,1)S(1)}, f32[32,64]{1,0:T(8,128)S(1)}, f32[32,64]{1,0:T(8,128)S(1)}, f32[32,1]{1,0:T(8,128)S(1)}, f32[1,512]{1,0:T(1,128)S(1)}, /*index=5*/f32[1,2048]{1,0:T(1,128)S(1)}) custom-call(bf16[32,2048]{1,0:T(8,128)(2,1)S(1)} %get-tuple-element.33.normed_ref, bf16[2048,1152]{1,0:T(8,128)(2,1)} %weight_ref.1, ...), custom_call_target="tpu_custom_call" | custom-call | flops 150994944 | bytes 4718592 | tf_op jit(solution)/shard_map/pallas_call | solution.py:41
  29.1 1.5 %collective-permute-start.6 = (bf16[32,640]{1,0:T(8,128)(2,1)S(1)}, bf16[32,640]{1,0:T(8,128)(2,1)S(1)}, u32[]{:S(2)}, u32[]{:S(2)}) collective-permute-start(bf16[32,640]{1,0:T(8,128)(2,1)S(1)} %get-tuple-element.40), channel_id=1, source_target_pairs={{0,8},{4,12},{8,0},{12,4},{16,24},{20,28},{24,16},{28,20},{1,9},{5... | collective-permute-start | bytes 122888 | tf_op jit(solution)/shard_map/ppermute | solution.py:66
  31.3 1.8 %collective-permute-done.6 = bf16[32,640]{1,0:T(8,128)(2,1)S(1)} collective-permute-done((bf16[32,640]{1,0:T(8,128)(2,1)S(1)}, bf16[32,640]{1,0:T(8,128)(2,1)S(1)}, u32[]{:S(2)}, u32[]{:S(2)}) %collective-permute-start.6) | collective-permute-done | bytes 40992 | tf_op jit(solution)/shard_map/ppermute | solution.py:66
  33.1 1.5 %collective-permute-start.7 = (bf16[32,640]{1,0:T(8,128)(2,1)S(1)}, bf16[32,640]{1,0:T(8,128)(2,1)S(1)}, u32[]{:S(2)}, u32[]{:S(2)}) collective-permute-start(bf16[32,640]{1,0:T(8,128)(2,1)S(1)} %get-tuple-element.40), channel_id=1, source_target_pairs={{0,16},{4,20},{8,24},{12,28},{16,0},{20,4},{24,8},{28,12},{1,17},{... | collective-permute-start | bytes 122888 | tf_op jit(solution)/shard_map/ppermute | solution.py:66
  34.6 2.5 %collective-permute-done.7 = bf16[32,640]{1,0:T(8,128)(2,1)S(1)} collective-permute-done((bf16[32,640]{1,0:T(8,128)(2,1)S(1)}, bf16[32,640]{1,0:T(8,128)(2,1)S(1)}, u32[]{:S(2)}, u32[]{:S(2)}) %collective-permute-start.7) | collective-permute-done | bytes 40992 | tf_op jit(solution)/shard_map/ppermute | solution.py:66
  37.1 2.4 %collective-permute-start.8 = (bf16[32,640]{1,0:T(8,128)(2,1)S(1)}, bf16[32,640]{1,0:T(8,128)(2,1)S(1)}, u32[]{:S(2)}, u32[]{:S(2)}) collective-permute-start(bf16[32,640]{1,0:T(8,128)(2,1)S(1)} %get-tuple-element.40), channel_id=1, source_target_pairs={{0,24},{4,28},{8,16},{12,20},{16,8},{20,12},{24,0},{28,4},{1,25},{... | collective-permute-start | bytes 122888 | tf_op jit(solution)/shard_map/ppermute | solution.py:66
  39.5 2.4 %collective-permute-done.8 = bf16[32,640]{1,0:T(8,128)(2,1)S(1)} collective-permute-done((bf16[32,640]{1,0:T(8,128)(2,1)S(1)}, bf16[32,640]{1,0:T(8,128)(2,1)S(1)}, u32[]{:S(2)}, u32[]{:S(2)}) %collective-permute-start.8) | collective-permute-done | bytes 40992 | tf_op jit(solution)/shard_map/ppermute | solution.py:66
  43.4 3.4 %shard_map.144.refs_0_ = bf16[32,2048]{1,0:T(8,128)(2,1)S(1)} custom-call(bf16[64,640]{1,0:T(8,128)(2,1)S(1)} %get-tuple-element.34.query_ref, bf16[128,640]{1,0:T(8,128)(2,1)S(1)} %constant_dynamic-update-slice_fusion.mine_ref.mine_tail_ref, bf16[128,640]{1,0:T(8,128)(2,1)S(1)} %collective-permute-done.9.theirs_ref.theirs_tail_ref, ...), custom_call_target="tpu_custom_call" | custom-call | flops 134217728 | bytes 4194304 | tf_op jit(solution)/shard_map/pallas_call | solution.py:41
  46.9 2.9 %collective-permute-start.18 = (bf16[32,2048]{1,0:T(8,128)(2,1)S(1)}, bf16[32,2048]{1,0:T(8,128)(2,1)S(1)}, u32[]{:S(2)}, u32[]{:S(2)}) collective-permute-start(bf16[32,2048]{1,0:T(8,128)(2,1)S(1)} %shard_map.144.refs_0_), channel_id=1, source_target_pairs={{0,2},{1,3},{2,0},{3,1},{4,6},{5,7},{6,4},{7,5},{8,10},{9,11},{10,... | collective-permute-start | bytes 393224 | tf_op jit(solution)/shard_map/ppermute | solution.py:66
  49.8 1.5 %collective-permute-start.19 = (bf16[32,2048]{1,0:T(8,128)(2,1)S(1)}, bf16[32,2048]{1,0:T(8,128)(2,1)S(1)}, u32[]{:S(2)}, u32[]{:S(2)}) collective-permute-start(bf16[32,2048]{1,0:T(8,128)(2,1)S(1)} %shard_map.144.refs_0_), channel_id=1, source_target_pairs={{0,3},{1,2},{2,1},{3,0},{4,7},{5,6},{6,5},{7,4},{8,11},{9,10},{10,... | collective-permute-start | bytes 393224 | tf_op jit(solution)/shard_map/ppermute | solution.py:66
  51.2 3.4 %collective-permute-done.17.refs_1_ = bf16[32,2048]{1,0:T(8,128)(2,1)S(1)} collective-permute-done((bf16[32,2048]{1,0:T(8,128)(2,1)S(1)}, bf16[32,2048]{1,0:T(8,128)(2,1)S(1)}, u32[]{:S(2)}, u32[]{:S(2)}) %collective-permute-start.17) | collective-permute-done | bytes 131104 | tf_op jit(solution)/shard_map/ppermute | solution.py:66
  54.6 5.2 %collective-permute-done.18.refs_2_ = bf16[32,2048]{1,0:T(8,128)(2,1)S(1)} collective-permute-done((bf16[32,2048]{1,0:T(8,128)(2,1)S(1)}, bf16[32,2048]{1,0:T(8,128)(2,1)S(1)}, u32[]{:S(2)}, u32[]{:S(2)}) %collective-permute-start.18) | collective-permute-done | bytes 131104 | tf_op jit(solution)/shard_map/ppermute | solution.py:66
  60.1 1.6 %collective-permute-start.20 = (bf16[32,2048]{1,0:T(8,128)(2,1)S(1)}, bf16[32,2048]{1,0:T(8,128)(2,1)S(1)}, u32[]{:S(2)}, u32[]{:S(2)}) collective-permute-start(bf16[32,2048]{1,0:T(8,128)(2,1)S(1)} %get-tuple-element.43), channel_id=1, source_target_pairs={{0,8},{4,12},{8,0},{12,4},{16,24},{20,28},{24,16},{28,20},{1,9},{5... | collective-permute-start | bytes 393224 | tf_op jit(solution)/shard_map/ppermute | solution.py:66
  61.6 1.5 %collective-permute-start.21 = (bf16[32,2048]{1,0:T(8,128)(2,1)S(1)}, bf16[32,2048]{1,0:T(8,128)(2,1)S(1)}, u32[]{:S(2)}, u32[]{:S(2)}) collective-permute-start(bf16[32,2048]{1,0:T(8,128)(2,1)S(1)} %get-tuple-element.43), channel_id=1, source_target_pairs={{0,16},{4,20},{8,24},{12,28},{16,0},{20,4},{24,8},{28,12},{1,17},{... | collective-permute-start | bytes 393224 | tf_op jit(solution)/shard_map/ppermute | solution.py:66
  63.6 2.7 %collective-permute-done.20 = bf16[32,2048]{1,0:T(8,128)(2,1)S(1)} collective-permute-done((bf16[32,2048]{1,0:T(8,128)(2,1)S(1)}, bf16[32,2048]{1,0:T(8,128)(2,1)S(1)}, u32[]{:S(2)}, u32[]{:S(2)}) %collective-permute-start.20) | collective-permute-done | bytes 131104 | tf_op jit(solution)/shard_map/ppermute | solution.py:66
  67.5 1.5 %collective-permute-done.22 = bf16[32,2048]{1,0:T(8,128)(2,1)S(1)} collective-permute-done((bf16[32,2048]{1,0:T(8,128)(2,1)S(1)}, bf16[32,2048]{1,0:T(8,128)(2,1)S(1)}, u32[]{:S(2)}, u32[]{:S(2)}) %collective-permute-start.22) | collective-permute-done | bytes 131104 | tf_op jit(solution)/shard_map/ppermute | solution.py:66
  69.1 1.9 %collective-permute-done.23.theirs_ref = bf16[128,2048]{1,0:T(8,128)(2,1)S(1)} collective-permute-done((bf16[128,2048]{1,0:T(8,128)(2,1)S(1)}, bf16[128,2048]{1,0:T(8,128)(2,1)S(1)}, u32[]{:S(2)}, u32[]{:S(2)}) %collective-permute-start.23) | collective-permute-done | bytes 524320 | tf_op jit(solution)/shard_map/ppermute | solution.py:66
  71.0 2.7 %shard_map.146 = (bf16[128,2048]{1,0:T(8,128)(2,1)S(1)}, bf16[128,2048]{1,0:T(8,128)(2,1)S(1)}) custom-call(bf16[128,2048]{1,0:T(8,128)(2,1)S(1)} %constant_dynamic-update-slice_fusion.4.mine_ref, bf16[128,2048]{1,0:T(8,128)(2,1)S(1)} %collective-permute-done.23.theirs_ref, bf16[128,640]{1,0:T(8,128)(2,1)S(1)} %constant_dynamic-update-slice_fusion.mine_ref.mine_tail_ref, ...), custom_call_target="tpu_custom_call" | custom-call | flops 2214592512 | bytes 8650752 | tf_op jit(solution)/shard_map/pallas_call | solution.py:41
  73.9 1.8 %collective-permute-done.24.back_ref = bf16[128,2048]{1,0:T(8,128)(2,1)S(1)} collective-permute-done((bf16[128,2048]{1,0:T(8,128)(2,1)S(1)}, bf16[128,2048]{1,0:T(8,128)(2,1)S(1)}, u32[]{:S(2)}, u32[]{:S(2)}) %collective-permute-start.24) | collective-permute-done | bytes 524320 | tf_op jit(solution)/shard_map/ppermute | solution.py:66
  76.9 2.4 %collective-permute-start.27 = (bf16[32,2048]{1,0:T(8,128)(2,1)S(1)}, bf16[32,2048]{1,0:T(8,128)(2,1)S(1)}, u32[]{:S(2)}, u32[]{:S(2)}) collective-permute-start(bf16[32,2048]{1,0:T(8,128)(2,1)S(1)} %get-tuple-element.49), channel_id=1, source_target_pairs={{0,24},{4,28},{8,16},{12,20},{16,8},{20,12},{24,0},{28,4},{1,25},{... | collective-permute-start | bytes 393224 | tf_op jit(solution)/shard_map/ppermute | solution.py:66
  79.3 2.9 %collective-permute-done.25.refs_1_ = bf16[32,2048]{1,0:T(8,128)(2,1)S(1)} collective-permute-done((bf16[32,2048]{1,0:T(8,128)(2,1)S(1)}, bf16[32,2048]{1,0:T(8,128)(2,1)S(1)}, u32[]{:S(2)}, u32[]{:S(2)}) %collective-permute-start.25) | collective-permute-done | bytes 131104 | tf_op jit(solution)/shard_map/ppermute | solution.py:66
  82.3 2.3 %collective-permute-done.27.refs_3_ = bf16[32,2048]{1,0:T(8,128)(2,1)S(1)} collective-permute-done((bf16[32,2048]{1,0:T(8,128)(2,1)S(1)}, bf16[32,2048]{1,0:T(8,128)(2,1)S(1)}, u32[]{:S(2)}, u32[]{:S(2)}) %collective-permute-start.27) | collective-permute-done | bytes 131104 | tf_op jit(solution)/shard_map/ppermute | solution.py:66
  84.7 3.2 %collective-permute-start.28 = (bf16[8,2048]{1,0:T(8,128)(2,1)S(1)}, bf16[8,2048]{1,0:T(8,128)(2,1)S(1)}, u32[]{:S(2)}, u32[]{:S(2)}) collective-permute-start(bf16[8,2048]{1,0:T(8,128)(2,1)S(1)} %get-tuple-element.51), channel_id=1, source_target_pairs={{0,1},{1,0},{2,3},{3,2},{4,5},{5,4},{6,7},{7,6},{8,9},{9,8},{10,11... | collective-permute-start | bytes 98312 | tf_op jit(solution)/shard_map/ppermute | solution.py:66
  90.3 2.9 %collective-permute-done.29.refs_2_ = bf16[8,2048]{1,0:T(8,128)(2,1)S(1)} collective-permute-done((bf16[8,2048]{1,0:T(8,128)(2,1)S(1)}, bf16[8,2048]{1,0:T(8,128)(2,1)S(1)}, u32[]{:S(2)}, u32[]{:S(2)}) %collective-permute-start.29) | collective-permute-done | bytes 32800 | tf_op jit(solution)/shard_map/ppermute | solution.py:66
  (54 shorter events, 13.2 us)
Async XLA Ops:
  0.6 29.9 %collective-permute-start.10 = (bf16[1024,256]{1,0:T(8,128)(2,1)}, bf16[1024,256]{1,0:T(8,128)(2,1)S(1)}, u32[]{:S(2)}, u32[]{:S(2)}) collective-permute-start(bf16[1024,256]{1,0:T(8,128)(2,1)} %refs_0_.1), channel_id=1, source_target_pairs={{0,8},{4,12},{8,0},{12,4},{16,24},{20,28},{24,16},{28,20},{1,9},{5... | collective-permute-start | bytes 1572872 | tf_op jit(solution)/shard_map/ppermute | solution.py:66
  3.7 27.1 %collective-permute-start.11 = (bf16[1024,256]{1,0:T(8,128)(2,1)}, bf16[1024,256]{1,0:T(8,128)(2,1)S(1)}, u32[]{:S(2)}, u32[]{:S(2)}) collective-permute-start(bf16[1024,256]{1,0:T(8,128)(2,1)} %refs_0_.1), channel_id=1, source_target_pairs={{0,16},{4,20},{8,24},{12,28},{16,0},{20,4},{24,8},{28,12},{1,17},{... | collective-permute-start | bytes 1572872 | tf_op jit(solution)/shard_map/ppermute | solution.py:66
  5.2 25.9 %collective-permute-start.12 = (bf16[1024,256]{1,0:T(8,128)(2,1)}, bf16[1024,256]{1,0:T(8,128)(2,1)S(1)}, u32[]{:S(2)}, u32[]{:S(2)}) collective-permute-start(bf16[1024,256]{1,0:T(8,128)(2,1)} %refs_0_.1), channel_id=1, source_target_pairs={{0,24},{4,28},{8,16},{12,20},{16,8},{20,12},{24,0},{28,4},{1,25},{... | collective-permute-start | bytes 1572872 | tf_op jit(solution)/shard_map/ppermute | solution.py:66
  6.6 4.7 %collective-permute-start = (bf16[32,512]{1,0:T(8,128)(2,1)S(1)}, bf16[32,512]{1,0:T(8,128)(2,1)S(1)}, u32[]{:S(2)}, u32[]{:S(2)}) collective-permute-start(bf16[32,512]{1,0:T(8,128)(2,1)S(1)} %get-tuple-element.29.refs_0_), channel_id=1, source_target_pairs={{0,1},{1,0},{2,3},{3,2},{4,5},{5,4},{6,7},{7,6},{8,9},{9,8},{10,11... | collective-permute-start | bytes 98312 | tf_op jit(solution)/shard_map/ppermute | solution.py:66
  8.7 5.9 %collective-permute-start.1 = (bf16[32,512]{1,0:T(8,128)(2,1)S(1)}, bf16[32,512]{1,0:T(8,128)(2,1)S(1)}, u32[]{:S(2)}, u32[]{:S(2)}) collective-permute-start(bf16[32,512]{1,0:T(8,128)(2,1)S(1)} %get-tuple-element.29.refs_0_), channel_id=1, source_target_pairs={{0,2},{1,3},{2,0},{3,1},{4,6},{5,7},{6,4},{7,5},{8,10},{9,11},{10,... | collective-permute-start | bytes 98312 | tf_op jit(solution)/shard_map/ppermute | solution.py:66
  11.3 5.7 %collective-permute-start.2 = (bf16[32,512]{1,0:T(8,128)(2,1)S(1)}, bf16[32,512]{1,0:T(8,128)(2,1)S(1)}, u32[]{:S(2)}, u32[]{:S(2)}) collective-permute-start(bf16[32,512]{1,0:T(8,128)(2,1)S(1)} %get-tuple-element.29.refs_0_), channel_id=1, source_target_pairs={{0,3},{1,2},{2,1},{3,0},{4,7},{5,6},{6,5},{7,4},{8,11},{9,10},{10,... | collective-permute-start | bytes 98312 | tf_op jit(solution)/shard_map/ppermute | solution.py:66
  17.4 4.1 %collective-permute-start.3 = (f32[40,256]{1,0:T(8,128)S(1)}, f32[40,256]{1,0:T(8,128)S(1)}, u32[]{:S(2)}, u32[]{:S(2)}) collective-permute-start(f32[40,256]{1,0:T(8,128)S(1)} %get-tuple-element.35.refs_0_), channel_id=1, source_target_pairs={{0,1},{1,0},{2,3},{3,2},{4,5},{5,4},{6,7},{7,6},{8,9},{9,8},{10,11... | collective-permute-start | bytes 122888 | tf_op jit(solution)/shard_map/ppermute | solution.py:66
  17.5 10.7 %collective-permute-start.4 = (f32[40,256]{1,0:T(8,128)S(1)}, f32[40,256]{1,0:T(8,128)S(1)}, u32[]{:S(2)}, u32[]{:S(2)}) collective-permute-start(f32[40,256]{1,0:T(8,128)S(1)} %get-tuple-element.35.refs_0_), channel_id=1, source_target_pairs={{0,2},{1,3},{2,0},{3,1},{4,6},{5,7},{6,4},{7,5},{8,10},{9,11},{10,... | collective-permute-start | bytes 122888 | tf_op jit(solution)/shard_map/ppermute | solution.py:66
  21.5 6.8 %collective-permute-start.5 = (f32[40,256]{1,0:T(8,128)S(1)}, f32[40,256]{1,0:T(8,128)S(1)}, u32[]{:S(2)}, u32[]{:S(2)}) collective-permute-start(f32[40,256]{1,0:T(8,128)S(1)} %get-tuple-element.35.refs_0_), channel_id=1, source_target_pairs={{0,3},{1,2},{2,1},{3,0},{4,7},{5,6},{6,5},{7,4},{8,11},{9,10},{10,... | collective-permute-start | bytes 122888 | tf_op jit(solution)/shard_map/ppermute | solution.py:66
  24.8 46.2 %copy-start.1 = (bf16[1,704,2048]{2,1,0:T(8,128)(2,1)S(1)}, bf16[1,704,2048]{2,1,0:T(8,128)(2,1)}, u32[]{:S(2)}) copy-start(bf16[1,704,2048]{2,1,0:T(8,128)(2,1)} %param.25) | copy-start | bytes 8650756
  28.2 15.2 %collective-permute-start.13 = (bf16[1024,256]{1,0:T(8,128)(2,1)S(1)}, bf16[1024,256]{1,0:T(8,128)(2,1)S(1)}, u32[]{:S(2)}, u32[]{:S(2)}) collective-permute-start(bf16[1024,256]{1,0:T(8,128)(2,1)S(1)} %copy-done.2), channel_id=1, source_target_pairs={{0,4},{4,0},{8,12},{12,8},{16,20},{20,16},{24,28},{28,24},{1,5},{5... | collective-permute-start | bytes 1572872 | tf_op jit(solution)/shard_map/ppermute | solution.py:66
  29.1 4.0 %collective-permute-start.6 = (bf16[32,640]{1,0:T(8,128)(2,1)S(1)}, bf16[32,640]{1,0:T(8,128)(2,1)S(1)}, u32[]{:S(2)}, u32[]{:S(2)}) collective-permute-start(bf16[32,640]{1,0:T(8,128)(2,1)S(1)} %get-tuple-element.40), channel_id=1, source_target_pairs={{0,8},{4,12},{8,0},{12,4},{16,24},{20,28},{24,16},{28,20},{1,9},{5... | collective-permute-start | bytes 122888 | tf_op jit(solution)/shard_map/ppermute | solution.py:66
  30.6 12.8 %collective-permute-start.14 = (bf16[1024,256]{1,0:T(8,128)(2,1)S(1)}, bf16[1024,256]{1,0:T(8,128)(2,1)S(1)}, u32[]{:S(2)}, u32[]{:S(2)}) collective-permute-start(bf16[1024,256]{1,0:T(8,128)(2,1)S(1)} %collective-permute-done.10.refs_1_), channel_id=1, source_target_pairs={{0,4},{4,0},{8,12},{12,8},{16,20},{20,16},{24,28},{28,24},{1,5},{5... | collective-permute-start | bytes 1572872 | tf_op jit(solution)/shard_map/ppermute | solution.py:66
  30.8 12.6 %collective-permute-start.15 = (bf16[1024,256]{1,0:T(8,128)(2,1)S(1)}, bf16[1024,256]{1,0:T(8,128)(2,1)S(1)}, u32[]{:S(2)}, u32[]{:S(2)}) collective-permute-start(bf16[1024,256]{1,0:T(8,128)(2,1)S(1)} %collective-permute-done.11.refs_2_), channel_id=1, source_target_pairs={{0,4},{4,0},{8,12},{12,8},{16,20},{20,16},{24,28},{28,24},{1,5},{5... | collective-permute-start | bytes 1572872 | tf_op jit(solution)/shard_map/ppermute | solution.py:66
  31.1 12.3 %collective-permute-start.16 = (bf16[1024,256]{1,0:T(8,128)(2,1)S(1)}, bf16[1024,256]{1,0:T(8,128)(2,1)S(1)}, u32[]{:S(2)}, u32[]{:S(2)}) collective-permute-start(bf16[1024,256]{1,0:T(8,128)(2,1)S(1)} %collective-permute-done.12.refs_3_), channel_id=1, source_target_pairs={{0,4},{4,0},{8,12},{12,8},{16,20},{20,16},{24,28},{28,24},{1,5},{5... | collective-permute-start | bytes 1572872 | tf_op jit(solution)/shard_map/ppermute | solution.py:66
  33.1 4.0 %collective-permute-start.7 = (bf16[32,640]{1,0:T(8,128)(2,1)S(1)}, bf16[32,640]{1,0:T(8,128)(2,1)S(1)}, u32[]{:S(2)}, u32[]{:S(2)}) collective-permute-start(bf16[32,640]{1,0:T(8,128)(2,1)S(1)} %get-tuple-element.40), channel_id=1, source_target_pairs={{0,16},{4,20},{8,24},{12,28},{16,0},{20,4},{24,8},{28,12},{1,17},{... | collective-permute-start | bytes 122888 | tf_op jit(solution)/shard_map/ppermute | solution.py:66
  37.1 4.9 %collective-permute-start.8 = (bf16[32,640]{1,0:T(8,128)(2,1)S(1)}, bf16[32,640]{1,0:T(8,128)(2,1)S(1)}, u32[]{:S(2)}, u32[]{:S(2)}) collective-permute-start(bf16[32,640]{1,0:T(8,128)(2,1)S(1)} %get-tuple-element.40), channel_id=1, source_target_pairs={{0,24},{4,28},{8,16},{12,20},{16,8},{20,12},{24,0},{28,4},{1,25},{... | collective-permute-start | bytes 122888 | tf_op jit(solution)/shard_map/ppermute | solution.py:66
  42.0 1.4 %collective-permute-start.9 = (bf16[128,640]{1,0:T(8,128)(2,1)S(1)}, bf16[128,640]{1,0:T(8,128)(2,1)S(1)}, u32[]{:S(2)}, u32[]{:S(2)}) collective-permute-start(bf16[128,640]{1,0:T(8,128)(2,1)S(1)} %constant_dynamic-update-slice_fusion.mine_ref.mine_tail_ref), channel_id=1, source_target_pairs={{0,4},{4,0},{8,12},{12,8},{16,20},{20,16},{24,28},{28,24},{1,5},{5... | collective-permute-start | bytes 491528 | tf_op jit(solution)/shard_map/ppermute | solution.py:66
  46.8 7.8 %collective-permute-start.17 = (bf16[32,2048]{1,0:T(8,128)(2,1)S(1)}, bf16[32,2048]{1,0:T(8,128)(2,1)S(1)}, u32[]{:S(2)}, u32[]{:S(2)}) collective-permute-start(bf16[32,2048]{1,0:T(8,128)(2,1)S(1)} %shard_map.144.refs_0_), channel_id=1, source_target_pairs={{0,1},{1,0},{2,3},{3,2},{4,5},{5,4},{6,7},{7,6},{8,9},{9,8},{10,11... | collective-permute-start | bytes 393224 | tf_op jit(solution)/shard_map/ppermute | solution.py:66
  46.9 13.0 %collective-permute-start.18 = (bf16[32,2048]{1,0:T(8,128)(2,1)S(1)}, bf16[32,2048]{1,0:T(8,128)(2,1)S(1)}, u32[]{:S(2)}, u32[]{:S(2)}) collective-permute-start(bf16[32,2048]{1,0:T(8,128)(2,1)S(1)} %shard_map.144.refs_0_), channel_id=1, source_target_pairs={{0,2},{1,3},{2,0},{3,1},{4,6},{5,7},{6,4},{7,5},{8,10},{9,11},{10,... | collective-permute-start | bytes 393224 | tf_op jit(solution)/shard_map/ppermute | solution.py:66
  49.8 10.1 %collective-permute-start.19 = (bf16[32,2048]{1,0:T(8,128)(2,1)S(1)}, bf16[32,2048]{1,0:T(8,128)(2,1)S(1)}, u32[]{:S(2)}, u32[]{:S(2)}) collective-permute-start(bf16[32,2048]{1,0:T(8,128)(2,1)S(1)} %shard_map.144.refs_0_), channel_id=1, source_target_pairs={{0,3},{1,2},{2,1},{3,0},{4,7},{5,6},{6,5},{7,4},{8,11},{9,10},{10,... | collective-permute-start | bytes 393224 | tf_op jit(solution)/shard_map/ppermute | solution.py:66
  60.1 6.2 %collective-permute-start.20 = (bf16[32,2048]{1,0:T(8,128)(2,1)S(1)}, bf16[32,2048]{1,0:T(8,128)(2,1)S(1)}, u32[]{:S(2)}, u32[]{:S(2)}) collective-permute-start(bf16[32,2048]{1,0:T(8,128)(2,1)S(1)} %get-tuple-element.43), channel_id=1, source_target_pairs={{0,8},{4,12},{8,0},{12,4},{16,24},{20,28},{24,16},{28,20},{1,9},{5... | collective-permute-start | bytes 393224 | tf_op jit(solution)/shard_map/ppermute | solution.py:66
  61.6 5.9 %collective-permute-start.21 = (bf16[32,2048]{1,0:T(8,128)(2,1)S(1)}, bf16[32,2048]{1,0:T(8,128)(2,1)S(1)}, u32[]{:S(2)}, u32[]{:S(2)}) collective-permute-start(bf16[32,2048]{1,0:T(8,128)(2,1)S(1)} %get-tuple-element.43), channel_id=1, source_target_pairs={{0,16},{4,20},{8,24},{12,28},{16,0},{20,4},{24,8},{28,12},{1,17},{... | collective-permute-start | bytes 393224 | tf_op jit(solution)/shard_map/ppermute | solution.py:66
  63.1 5.9 %collective-permute-start.22 = (bf16[32,2048]{1,0:T(8,128)(2,1)S(1)}, bf16[32,2048]{1,0:T(8,128)(2,1)S(1)}, u32[]{:S(2)}, u32[]{:S(2)}) collective-permute-start(bf16[32,2048]{1,0:T(8,128)(2,1)S(1)} %get-tuple-element.43), channel_id=1, source_target_pairs={{0,24},{4,28},{8,16},{12,20},{16,8},{20,12},{24,0},{28,4},{1,25},{... | collective-permute-start | bytes 393224 | tf_op jit(solution)/shard_map/ppermute | solution.py:66
  69.0 2.0 %collective-permute-start.23 = (bf16[128,2048]{1,0:T(8,128)(2,1)S(1)}, bf16[128,2048]{1,0:T(8,128)(2,1)S(1)}, u32[]{:S(2)}, u32[]{:S(2)}) collective-permute-start(bf16[128,2048]{1,0:T(8,128)(2,1)S(1)} %constant_dynamic-update-slice_fusion.4.mine_ref), channel_id=1, source_target_pairs={{0,4},{4,0},{8,12},{12,8},{16,20},{20,16},{24,28},{28,24},{1,5},{5... | collective-permute-start | bytes 1572872 | tf_op jit(solution)/shard_map/ppermute | solution.py:66
  73.7 2.0 %collective-permute-start.24 = (bf16[128,2048]{1,0:T(8,128)(2,1)S(1)}, bf16[128,2048]{1,0:T(8,128)(2,1)S(1)}, u32[]{:S(2)}, u32[]{:S(2)}) collective-permute-start(bf16[128,2048]{1,0:T(8,128)(2,1)S(1)} %get-tuple-element.45), channel_id=1, source_target_pairs={{0,4},{4,0},{8,12},{12,8},{16,20},{20,16},{24,28},{28,24},{1,5},{5... | collective-permute-start | bytes 1572872 | tf_op jit(solution)/shard_map/ppermute | solution.py:66
  75.8 6.4 %collective-permute-start.25 = (bf16[32,2048]{1,0:T(8,128)(2,1)S(1)}, bf16[32,2048]{1,0:T(8,128)(2,1)S(1)}, u32[]{:S(2)}, u32[]{:S(2)}) collective-permute-start(bf16[32,2048]{1,0:T(8,128)(2,1)S(1)} %get-tuple-element.47), channel_id=1, source_target_pairs={{0,8},{4,12},{8,0},{12,4},{16,24},{20,28},{24,16},{28,20},{1,9},{5... | collective-permute-start | bytes 393224 | tf_op jit(solution)/shard_map/ppermute | solution.py:66
  76.4 5.9 %collective-permute-start.26 = (bf16[32,2048]{1,0:T(8,128)(2,1)S(1)}, bf16[32,2048]{1,0:T(8,128)(2,1)S(1)}, u32[]{:S(2)}, u32[]{:S(2)}) collective-permute-start(bf16[32,2048]{1,0:T(8,128)(2,1)S(1)} %get-tuple-element.48), channel_id=1, source_target_pairs={{0,16},{4,20},{8,24},{12,28},{16,0},{20,4},{24,8},{28,12},{1,17},{... | collective-permute-start | bytes 393224 | tf_op jit(solution)/shard_map/ppermute | solution.py:66
  76.9 7.7 %collective-permute-start.27 = (bf16[32,2048]{1,0:T(8,128)(2,1)S(1)}, bf16[32,2048]{1,0:T(8,128)(2,1)S(1)}, u32[]{:S(2)}, u32[]{:S(2)}) collective-permute-start(bf16[32,2048]{1,0:T(8,128)(2,1)S(1)} %get-tuple-element.49), channel_id=1, source_target_pairs={{0,24},{4,28},{8,16},{12,20},{16,8},{20,12},{24,0},{28,4},{1,25},{... | collective-permute-start | bytes 393224 | tf_op jit(solution)/shard_map/ppermute | solution.py:66
  84.7 5.6 %collective-permute-start.28 = (bf16[8,2048]{1,0:T(8,128)(2,1)S(1)}, bf16[8,2048]{1,0:T(8,128)(2,1)S(1)}, u32[]{:S(2)}, u32[]{:S(2)}) collective-permute-start(bf16[8,2048]{1,0:T(8,128)(2,1)S(1)} %get-tuple-element.51), channel_id=1, source_target_pairs={{0,1},{1,0},{2,3},{3,2},{4,5},{5,4},{6,7},{7,6},{8,9},{9,8},{10,11... | collective-permute-start | bytes 98312 | tf_op jit(solution)/shard_map/ppermute | solution.py:66
  87.8 5.3 %collective-permute-start.29 = (bf16[8,2048]{1,0:T(8,128)(2,1)S(1)}, bf16[8,2048]{1,0:T(8,128)(2,1)S(1)}, u32[]{:S(2)}, u32[]{:S(2)}) collective-permute-start(bf16[8,2048]{1,0:T(8,128)(2,1)S(1)} %get-tuple-element.52), channel_id=1, source_target_pairs={{0,2},{1,3},{2,0},{3,1},{4,6},{5,7},{6,4},{7,5},{8,10},{9,11},{10,... | collective-permute-start | bytes 98312 | tf_op jit(solution)/shard_map/ppermute | solution.py:66
  88.8 5.7 %collective-permute-start.30 = (bf16[8,2048]{1,0:T(8,128)(2,1)S(1)}, bf16[8,2048]{1,0:T(8,128)(2,1)S(1)}, u32[]{:S(2)}, u32[]{:S(2)}) collective-permute-start(bf16[8,2048]{1,0:T(8,128)(2,1)S(1)} %get-tuple-element.53), channel_id=1, source_target_pairs={{0,3},{1,2},{2,1},{3,0},{4,7},{5,6},{6,5},{7,4},{8,11},{9,10},{10,... | collective-permute-start | bytes 98312 | tf_op jit(solution)/shard_map/ppermute | solution.py:66
  (2 other events, 70.4 us)
where the time goes:
time: 95.4 us; the launch traced here: 95.2 us
  starting transfers between devices  43.6 us (46%)
  waiting for transfers between devices  37.7 us (40%)
  Pallas kernels  13 us (14%)
    ppermute x31, starting transfers between devices, partner(): return lax.ppermute(values, axis, [(i, i ^ mask) for i in range(count)])  43.6 us
    ppermute x31, waiting for transfers between devices, partner(): return lax.ppermute(values, axis, [(i, i ^ mask) for i in range(count)])  37.7 us
    pallas_call x10, Pallas kernels, call(): pl.pallas_call(kernel, out_shape=outs, in_specs=in_specs, out_specs=VM if...  13 us
  transfers between devices with their start and end apart: 31, of which 18 were waited for; matrix products, arithmetic and copies ran while one was open for 0% of the time, Pallas kernels for 6%

commit v1 on v0

--- a/solution.py
+++ b/solution.py
@@ -20,7 +20,6 @@
 
 
 VM = pl.BlockSpec(memory_space=pltpu.VMEM)
-ANY = pl.BlockSpec(memory_space=pl.ANY)
 HBM = pl.BlockSpec(memory_space=pltpu.HBM)
 
 
@@ -222,7 +221,7 @@
 
 def cache_kernel(spans, width, experts, *refs):
     parts = refs[:spans]
-    live_ref, gain_ref, cos_ref, sin_ref, cached_ref, sent_ref = refs[spans:]
+    live_ref, gain_ref, cos_ref, sin_ref, query_ref, cached_ref, sent_ref = refs[spans:]
     rows = live_ref.shape[0]
     kv_rank = gain_ref.shape[1]
     values = natural([p[...] for p in parts], here()[1])
@@ -240,57 +239,85 @@
     rest = sent_ref.shape[1] - kv_rank - used
     if rest:
         tail.append(jnp.zeros((rows, rest), F32))
-    sent_ref[:, :kv_rank] = nope.astype(BF16)
-    sent_ref[:, kv_rank:] = jnp.concatenate(tail, axis=1).astype(BF16)
-
-
-def attend_kernel(heads, kv_rank, flag_lane, blocks, query_ref, mine_ref, theirs_ref, *refs):
-    weights = refs[:blocks]
-    out_ref, buf, sem = refs[blocks:]
-    copies = [pltpu.make_async_copy(weights[n], buf.at[n], sem.at[n]) for n in range(blocks)]
-    for copy in copies:
-        copy.start()
-    count = query_ref.shape[0] // heads
+    sent_ref[:rows, :kv_rank] = nope.astype(BF16)
+    sent_ref[:rows, kv_rank:] = jnp.concatenate(tail, axis=1).astype(BF16)
+    sent_ref[rows:, :] = query_ref[...]
+
+
+def places(blocks):
+    return list(range(0, blocks, 2)) + list(range(1, blocks, 2))
+
+
+def attend_kernel(
+    heads, kv_rank, flag_lane, blocks, mine_ref, theirs_ref, weight_hbm, out_ref, weight_ref, sem
+):
+    copy = pltpu.make_async_copy(weight_hbm, weight_ref, sem)
+    copy.start()
+    count = mine_ref.shape[1] // (1 + heads)
     index = here()[0]
-    keys = jnp.concatenate([mine_ref[...], theirs_ref[...]], axis=0)
-    total = keys.shape[0]
-    width = keys.shape[1]
+    half = blocks // 2
+    pieces = [(mine_ref, n) for n in range(half)] + [(theirs_ref, n) for n in range(half)]
+
+    def gather(n):
+        return jnp.concatenate(
+            [ref[p, n * count : (n + 1) * count, :] for ref, p in pieces], axis=0
+        )
+
+    keys = gather(0)
+    total, width = keys.shape
     lane = lax.broadcasted_iota(jnp.int32, (8, width), 1)
     flags = nt(jnp.where(lane == flag_lane, 1.0, 0.0).astype(BF16), keys)[0:1, :]
-    row = lax.broadcasted_iota(jnp.int32, (count, total), 0)
-    col = lax.broadcasted_iota(jnp.int32, (count, total), 1)
-    half = blocks // 2
-    at = col // count
-    which = jnp.where(at < half, 2 * at, 2 * (at - half) + 1)
-    key_ids = (which ^ index) * count + col % count
-    allowed = (key_ids <= index * count + row) & (flags > 0)
-    mixed = []
+
+    def slot(dims, axis):
+        line = lax.broadcasted_iota(jnp.int32, dims, axis)
+        at = line // count
+        which = jnp.where(at < half, 2 * at, 2 * (at - half) + 1)
+        return (which ^ index) * count + line % count
+
+    allowed = (slot((1, total), 1) <= slot((total, 1), 0)) & (flags > 0)
+    result = jnp.zeros(out_ref.shape, F32)
     for h in range(heads):
-        scores = nt(query_ref[h * count : (h + 1) * count, :], keys) * SCALE
+        scores = nt(gather(1 + h), keys) * SCALE
         scores = jnp.where(allowed, scores, NEGATIVE)
         highest = jnp.max(scores, axis=1, keepdims=True)
         weight = jnp.where(allowed, jnp.exp(scores - highest), 0.0)
         denominator = jnp.sum(weight, axis=1, keepdims=True)
         summed = nn(weight.astype(BF16), keys[:, :kv_rank])
-        mixed.append((summed / denominator).astype(BF16))
-    mixed = jnp.concatenate(mixed, axis=1)
-    block = buf.shape[2]
+        mixed = (summed / denominator).astype(BF16)
+        if h == 0:
+            copy.wait()
+        result = result + nn(mixed, weight_ref[h * kv_rank : (h + 1) * kv_rank, :])
+    out_ref[...] = result.astype(BF16)
+
+
+def sum_kernel(*refs):
+    refs[-1][...] = sum(ref[...].astype(F32) for ref in refs[:-1]).astype(BF16)
+
+
+def resid_kernel(blocks, *refs):
+    mine_ref, theirs_ref, mine_rows, their_rows, gain_ref, own_ref, out_ref, buf = refs
+    order = places(blocks)
+    half = blocks // 2
+    index = here()
+    count, width = mine_rows.shape[1], mine_ref.shape[2]
+    for n, i in enumerate(order):
+        ref, p = (mine_ref, n) if n < half else (theirs_ref, n - half)
+        lanes = pl.ds(pl.multiple_of((index[0] ^ i) * width, width), width)
+        for at, j in enumerate(order):
+            to = order.index(i ^ j)
+            buf[to * count : (to + 1) * count, lanes] = ref[
+                p, at * count : (at + 1) * count, :
+            ].astype(F32)
     for n in range(blocks):
-        i = 2 * n if n < half else 2 * (n - half) + 1
-        copies[n].wait()
-        place = pl.ds(pl.multiple_of((index ^ i) * block, block), block)
-        out_ref[:, place] = nn(mixed, buf[n]).astype(BF16)
-
-
-def resid_kernel(spans, *refs):
-    parts = refs[:spans]
-    compact_ref, gain_ref, own_ref, out_ref, buf = refs[spans:]
-    resid = compact_ref[...].astype(F32) + sum(p[...].astype(F32) for p in parts)
-    factor = lax.rsqrt(jnp.mean(resid * resid, axis=1, keepdims=True) + EPS)
-    out_ref[...] = (resid * factor * gain_ref[...]).astype(BF16)
-    buf[...] = resid
-    count = own_ref.shape[0]
-    own_ref[...] = buf[pl.ds(pl.multiple_of(here()[1] * count, count), count), :]
+        rows, p = (mine_rows, n) if n < half else (their_rows, n - half)
+        at = slice(n * count, (n + 1) * count)
+        resid = rows[p].astype(F32) + buf[at, :]
+        factor = lax.rsqrt(jnp.mean(resid * resid, axis=1, keepdims=True) + EPS)
+        out_ref[at, :] = (resid * factor * gain_ref[...]).astype(BF16)
+        if n == 0:
+            buf[at, :] = resid
+    size = own_ref.shape[0]
+    own_ref[...] = buf[pl.ds(pl.multiple_of(index[1] * size, size), size), :]
 
 
 def expert_kernel(
@@ -299,8 +326,7 @@
     experts,
     cuts,
     columns,
-    mine_ref,
-    theirs_ref,
+    rows_ref,
     mine_tail_ref,
     theirs_tail_ref,
     in_ref,
@@ -309,8 +335,13 @@
     far_ref,
     act_ref,
 ):
-    rows = jnp.concatenate([mine_ref[...], theirs_ref[...]], axis=0)
-    tail = jnp.concatenate([mine_tail_ref[:, tail_at:], theirs_tail_ref[:, tail_at:]], axis=0)
+    rows = rows_ref[...]
+    pieces = mine_tail_ref.shape[0]
+    count = rows.shape[0] // (2 * pieces)
+    tail = jnp.concatenate(
+        [ref[p, :count, tail_at:] for ref in (mine_tail_ref, theirs_tail_ref) for p in range(pieces)],
+        axis=0,
+    )
     tail = tail.astype(F32)
     lane = lax.broadcasted_iota(jnp.int32, tail.shape, 1) - first_lane
     index = here()
@@ -322,7 +353,7 @@
         gate = nt(rows, in_ref[0, start : start + size, :])
         upper = nt(rows, in_ref[1, start : start + size, :])
         act_ref[:, start : start + size] = (gate / (1.0 + jnp.exp(-gate)) * upper).astype(BF16)
-    half = mine_ref.shape[0]
+    half = near_ref.shape[0]
     width = out_weight_ref.shape[1] // columns
     for n in range(columns):
         span = slice(n * width, (n + 1) * width)
@@ -414,9 +445,6 @@
         limit=4,
     )
     parts = gathered(picked, "span", range(1, spans))
-    weights_even = gathered(out_weight, "context", evens[1:])
-    weights_odd = [partner(w, "context", 1) for w in weights_even]
-
     compact, normed, sent = call(
         functools.partial(latent_kernel, spans),
         [
@@ -456,43 +484,46 @@
     )
     cached, sent = call(
         functools.partial(cache_kernel, spans, part_width, experts),
-        [shape((kept, latent_width), BF16), shape((kept, row_width), BF16)],
-        [VM] * (spans + 4),
-        (*parts, live, near_kv, cosine, sine),
+        [shape((kept, latent_width), BF16), shape(((1 + heads) * kept, row_width), BF16)],
+        [VM] * (spans + 5),
+        (*parts, live, near_kv, cosine, sine, query),
         limit=4,
     )
 
-    mine_keys = jnp.concatenate(gathered(sent, "context", evens[1:]), axis=0)
+    mine_keys = jnp.stack(gathered(sent, "context", evens[1:]))
     their_keys = partner(mine_keys, "context", 1)
     partial = call(
-        functools.partial(
-            attend_kernel, heads, kv_rank, latent_width + 2 * experts, contexts
-        ),
-        shape((kept, model), BF16),
-        [VM, VM, VM, HBM] + [ANY] * (contexts - 1),
-        (query, mine_keys, their_keys, *weights_even, *weights_odd),
-        scratch=[
-            pltpu.VMEM((contexts, *out_weight.shape), BF16),
-            pltpu.SemaphoreType.DMA((contexts,)),
-        ],
+        functools.partial(attend_kernel, heads, kv_rank, latent_width + 2 * experts, contexts),
+        shape((contexts * kept, out_weight.shape[1]), BF16),
+        [VM, VM, HBM],
+        (mine_keys, their_keys, out_weight),
+        scratch=[pltpu.VMEM(out_weight.shape, BF16), pltpu.SemaphoreType.DMA],
         flops=2 * kept * contexts * out_weight.size,
-        moved=2 * contexts * out_weight.size,
+        moved=2 * out_weight.size,
         limit=12,
     )
 
-    got = gathered(partial, "span", range(1, spans))
+    column = call(
+        sum_kernel,
+        shape(partial.shape, BF16),
+        [VM] * spans,
+        gathered(partial, "span", range(1, spans)),
+        limit=4,
+    )
+    mine_rows = jnp.stack(gathered(compact, "context", evens[1:]))
+    their_rows = partner(mine_rows, "context", 1)
+
+    mine = jnp.stack(gathered(column, "context", evens[1:]))
+    theirs = partner(mine, "context", 1)
+    half = mine.shape[0] * kept
     own, moe_in = call(
-        functools.partial(resid_kernel, spans),
-        [shape((rows_dev, model), F32), shape((kept, model), BF16)],
-        [VM] * (spans + 2),
-        (*got, compact, near_moe),
-        scratch=[pltpu.VMEM((kept, model), F32)],
-        limit=6,
-    )
-
-    mine = jnp.concatenate(gathered(moe_in, "context", evens[1:]), axis=0)
-    theirs = partner(mine, "context", 1)
-    half = mine.shape[0]
+        functools.partial(resid_kernel, contexts),
+        [shape((rows_dev, model), F32), shape((2 * half, model), BF16)],
+        [VM] * 5,
+        (mine, theirs, mine_rows, their_rows, near_moe),
+        scratch=[pltpu.VMEM((2 * half, model), F32)],
+        limit=16,
+    )
     cuts, start = [], 0
     while start < hidden:
         size = min(2 * LANES, hidden - start)
@@ -501,8 +532,8 @@
     near, far = call(
         functools.partial(expert_kernel, latent_width - kv_rank, kv_rank, experts, cuts, 4),
         [shape((half, model), BF16), shape((half, model), BF16)],
-        [VM] * 6,
-        (mine, theirs, mine_keys, their_keys, jnp.swapaxes(expert_in[0], 1, 2), expert_out[0]),
+        [VM] * 5,
+        (moe_in, mine_keys, their_keys, jnp.swapaxes(expert_in[0], 1, 2), expert_out[0]),
         scratch=[pltpu.VMEM((2 * half, hidden), BF16)],
         flops=6 * 2 * half * hidden * model,
         moved=6 * hidden * model,

time: 95.4 us -> 81.3 us (0.85)
  starting transfers between devices: 43.6 us -> 33.3 us
  waiting for transfers between devices: 37.7 us -> 34.5 us
    ppermute x31 -> x28, starting transfers between devices: 43.6 us -> 33.3 us  [partner(): return lax.ppermute(values, axis, [(i, i ^ mask) for i in range(count)])]
    ppermute x31 -> x28, waiting for transfers between devices: 37.7 us -> 34.5 us  [partner(): return lax.ppermute(values, axis, [(i, i ^ mask) for i in range(count)])]
    pallas_call x10 -> x11, Pallas kernels: 13 us -> 12.3 us  [call(): pl.pallas_call(kernel, out_shape=outs, in_specs=in_specs, out_specs=VM if...]
  transfers between devices with their start and end apart: 31 -> 28, of which waited for: 18 -> 18; matrix products, arithmetic and copies ran while one was open for 0% -> 0% of each run, Pallas kernels for 6% -> 4%
where the time goes in v1:
time: 81.3 us; the launch traced here: 81.1 us
  waiting for transfers between devices  34.5 us (42%)
  starting transfers between devices  33.3 us (41%)
  Pallas kernels  12.3 us (15%)
    ppermute x28, waiting for transfers between devices, partner(): return lax.ppermute(values, axis, [(i, i ^ mask) for i in range(count)])  34.5 us
    ppermute x28, starting transfers between devices, partner(): return lax.ppermute(values, axis, [(i, i ^ mask) for i in range(count)])  33.3 us
    pallas_call x11, Pallas kernels, call(): pl.pallas_call(kernel, out_shape=outs, in_specs=in_specs, out_specs=VM if...  12.3 us
  transfers between devices with their start and end apart: 28, of which 18 were waited for; matrix products, arithmetic and copies ran while one was open for 0% of the time, Pallas kernels for 4%

profile of v1, /device:TPU:0, one launch (start us, length us, event | category | flops | bytes accessed | tf_op | source)
XLA Modules:
  0.0 81.1 jit_solution(15245336721867754645)
XLA Ops:
  0.6 1.4 %shard_map.140 = (bf16[32,512]{1,0:T(8,128)(2,1)S(1)}, bf16[144,2048]{1,0:T(8,128)(2,1)S(1)}, f32[1,2048]{1,0:T(1,128)S(1)}, f32[8,256]{1,0:T(8,128)S(1)}) custom-call(s32[1,32]{1,0:T(1,128)} %keep_hbm.3, bf16[192,512]{1,0:T(8,128)(2,1)} %raw_hbm.1, bf16[144,2048]{1,0:T(8,128)(2,1)} %bitcast.25, f32[1,2048]{1,0:T(1,128)} %bitcast.35, s32[8,6]{1,0:T(8,128)} %ids_hbm.1, ...), custom_call_target="tpu_custom_call" | custom-call | tf_op jit(solution)/shard_map/pallas_call | solution.py:40
  2.0 5.1 %collective-permute-start.2 = (bf16[32,512]{1,0:T(8,128)(2,1)S(1)}, bf16[32,512]{1,0:T(8,128)(2,1)S(1)}, u32[]{:S(2)}, u32[]{:S(2)}) collective-permute-start(bf16[32,512]{1,0:T(8,128)(2,1)S(1)} %get-tuple-element.29.refs_0_), channel_id=1, source_target_pairs={{0,3},{1,2},{2,1},{3,0},{4,7},{5,6},{6,5},{7,4},{8,11},{9,10},{10,... | collective-permute-start | bytes 98312 | tf_op jit(solution)/shard_map/ppermute | solution.py:65
  7.8 1.3 %collective-permute-done.2.refs_3_ = bf16[32,512]{1,0:T(8,128)(2,1)S(1)} collective-permute-done((bf16[32,512]{1,0:T(8,128)(2,1)S(1)}, bf16[32,512]{1,0:T(8,128)(2,1)S(1)}, u32[]{:S(2)}, u32[]{:S(2)}) %collective-permute-start.2) | collective-permute-done | bytes 32800 | tf_op jit(solution)/shard_map/ppermute | solution.py:65
  9.1 2.9 %collective-permute-done.1.refs_2_ = bf16[32,512]{1,0:T(8,128)(2,1)S(1)} collective-permute-done((bf16[32,512]{1,0:T(8,128)(2,1)S(1)}, bf16[32,512]{1,0:T(8,128)(2,1)S(1)}, u32[]{:S(2)}, u32[]{:S(2)}) %collective-permute-start.1) | collective-permute-done | bytes 32800 | tf_op jit(solution)/shard_map/ppermute | solution.py:65
  12.4 1.5 %collective-permute-start.5 = (f32[40,256]{1,0:T(8,128)S(1)}, f32[40,256]{1,0:T(8,128)S(1)}, u32[]{:S(2)}, u32[]{:S(2)}) collective-permute-start(f32[40,256]{1,0:T(8,128)S(1)} %get-tuple-element.33.refs_0_), channel_id=1, source_target_pairs={{0,3},{1,2},{2,1},{3,0},{4,7},{5,6},{6,5},{7,4},{8,11},{9,10},{10,... | collective-permute-start | bytes 122888 | tf_op jit(solution)/shard_map/ppermute | solution.py:65
  14.5 2.3 %collective-permute-start.3 = (f32[40,256]{1,0:T(8,128)S(1)}, f32[40,256]{1,0:T(8,128)S(1)}, u32[]{:S(2)}, u32[]{:S(2)}) collective-permute-start(f32[40,256]{1,0:T(8,128)S(1)} %get-tuple-element.33.refs_0_), channel_id=1, source_target_pairs={{0,1},{1,0},{2,3},{3,2},{4,5},{5,4},{6,7},{7,6},{8,9},{9,8},{10,11... | collective-permute-start | bytes 122888 | tf_op jit(solution)/shard_map/ppermute | solution.py:65
  16.8 3.3 %shard_map.142 = (bf16[64,640]{1,0:T(8,128)(2,1)S(1)}, f32[32,64]{1,0:T(8,128)S(1)}, f32[32,64]{1,0:T(8,128)S(1)}, f32[32,1]{1,0:T(8,128)S(1)}, f32[1,512]{1,0:T(1,128)S(1)}, /*index=5*/f32[1,2048]{1,0:T(1,128)S(1)}) custom-call(bf16[32,2048]{1,0:T(8,128)(2,1)S(1)} %get-tuple-element.34.normed_ref, bf16[2048,1152]{1,0:T(8,128)(2,1)} %weight_ref.1, ...), custom_call_target="tpu_custom_call" | custom-call | flops 150994944 | bytes 4718592 | tf_op jit(solution)/shard_map/pallas_call | solution.py:40
  21.0 2.4 %collective-permute-start.8 = (bf16[96,640]{1,0:T(8,128)(2,1)S(1)}, bf16[96,640]{1,0:T(8,128)(2,1)S(1)}, u32[]{:S(2)}, u32[]{:S(2)}) collective-permute-start(bf16[96,640]{1,0:T(8,128)(2,1)S(1)} %get-tuple-element.40), channel_id=1, source_target_pairs={{0,24},{4,28},{8,16},{12,20},{16,8},{20,12},{24,0},{28,4},{1,25},{... | collective-permute-start | bytes 368648 | tf_op jit(solution)/shard_map/ppermute | solution.py:65
  24.5 2.7 %collective-permute-done.8 = bf16[96,640]{1,0:T(8,128)(2,1)S(1)} collective-permute-done((bf16[96,640]{1,0:T(8,128)(2,1)S(1)}, bf16[96,640]{1,0:T(8,128)(2,1)S(1)}, u32[]{:S(2)}, u32[]{:S(2)}) %collective-permute-start.8) | collective-permute-done | bytes 122912 | tf_op jit(solution)/shard_map/ppermute | solution.py:65
  27.2 1.3 %collective-permute-done.7 = bf16[96,640]{1,0:T(8,128)(2,1)S(1)} collective-permute-done((bf16[96,640]{1,0:T(8,128)(2,1)S(1)}, bf16[96,640]{1,0:T(8,128)(2,1)S(1)}, u32[]{:S(2)}, u32[]{:S(2)}) %collective-permute-start.7) | collective-permute-done | bytes 122912 | tf_op jit(solution)/shard_map/ppermute | solution.py:65
  29.0 1.9 %collective-permute-done.9.theirs_ref.theirs_tail_ref = bf16[4,96,640]{2,1,0:T(8,128)(2,1)S(1)} collective-permute-done((bf16[4,96,640]{2,1,0:T(8,128)(2,1)S(1)}, bf16[4,96,640]{2,1,0:T(8,128)(2,1)S(1)}, u32[]{:S(2)}, u32[]{:S(2)}) %collective-permute-start.9) | collective-permute-done | bytes 491552 | tf_op jit(solution)/shard_map/ppermute | solution.py:65
  30.9 2.0 %shard_map.144.refs_0_ = bf16[256,256]{1,0:T(8,128)(2,1)S(1)} custom-call(bf16[4,96,640]{2,1,0:T(8,128)(2,1)S(1)} %pad_maximum_fusion.2.mine_ref.mine_tail_ref, bf16[4,96,640]{2,1,0:T(8,128)(2,1)S(1)} %collective-permute-done.9.theirs_ref.theirs_tail_ref, bf16[1024,256]{1,0:T(8,128)(2,1)} %weight_hbm.1), custom_call_target="tpu_custom_call" | custom-call | flops 134217728 | bytes 524288 | tf_op jit(solution)/shard_map/pallas_call | solution.py:40
  32.9 1.5 %collective-permute-start.12 = (bf16[256,256]{1,0:T(8,128)(2,1)S(1)}, bf16[256,256]{1,0:T(8,128)(2,1)S(1)}, u32[]{:S(2)}, u32[]{:S(2)}) collective-permute-start(bf16[256,256]{1,0:T(8,128)(2,1)S(1)} %shard_map.144.refs_0_), channel_id=1, source_target_pairs={{0,3},{1,2},{2,1},{3,0},{4,7},{5,6},{6,5},{7,4},{8,11},{9,10},{10,... | collective-permute-start | bytes 393224 | tf_op jit(solution)/shard_map/ppermute | solution.py:65
  35.0 2.3 %collective-permute-start.10 = (bf16[256,256]{1,0:T(8,128)(2,1)S(1)}, bf16[256,256]{1,0:T(8,128)(2,1)S(1)}, u32[]{:S(2)}, u32[]{:S(2)}) collective-permute-start(bf16[256,256]{1,0:T(8,128)(2,1)S(1)} %shard_map.144.refs_0_), channel_id=1, source_target_pairs={{0,1},{1,0},{2,3},{3,2},{4,5},{5,4},{6,7},{7,6},{8,9},{9,8},{10,11... | collective-permute-start | bytes 393224 | tf_op jit(solution)/shard_map/ppermute | solution.py:65
  37.3 1.5 %collective-permute-start.19 = (bf16[32,2048]{1,0:T(8,128)(2,1)S(1)}, bf16[32,2048]{1,0:T(8,128)(2,1)S(1)}, u32[]{:S(2)}, u32[]{:S(2)}) collective-permute-start(bf16[32,2048]{1,0:T(8,128)(2,1)S(1)} %get-tuple-element.41), channel_id=1, source_target_pairs={{0,24},{4,28},{8,16},{12,20},{16,8},{20,12},{24,0},{28,4},{1,25},{... | collective-permute-start | bytes 393224 | tf_op jit(solution)/shard_map/ppermute | solution.py:65
  39.6 1.6 %collective-permute-done.12.refs_3_ = bf16[256,256]{1,0:T(8,128)(2,1)S(1)} collective-permute-done((bf16[256,256]{1,0:T(8,128)(2,1)S(1)}, bf16[256,256]{1,0:T(8,128)(2,1)S(1)}, u32[]{:S(2)}, u32[]{:S(2)}) %collective-permute-start.12) | collective-permute-done | bytes 131104 | tf_op jit(solution)/shard_map/ppermute | solution.py:65
  41.2 0.9 %collective-permute-start.17 = (bf16[32,2048]{1,0:T(8,128)(2,1)S(1)}, bf16[32,2048]{1,0:T(8,128)(2,1)S(1)}, u32[]{:S(2)}, u32[]{:S(2)}) collective-permute-start(bf16[32,2048]{1,0:T(8,128)(2,1)S(1)} %get-tuple-element.41), channel_id=1, source_target_pairs={{0,8},{4,12},{8,0},{12,4},{16,24},{20,28},{24,16},{28,20},{1,9},{5... | collective-permute-start | bytes 393224 | tf_op jit(solution)/shard_map/ppermute | solution.py:65
  42.1 4.9 %collective-permute-done.11.refs_2_ = bf16[256,256]{1,0:T(8,128)(2,1)S(1)} collective-permute-done((bf16[256,256]{1,0:T(8,128)(2,1)S(1)}, bf16[256,256]{1,0:T(8,128)(2,1)S(1)}, u32[]{:S(2)}, u32[]{:S(2)}) %collective-permute-start.11) | collective-permute-done | bytes 131104 | tf_op jit(solution)/shard_map/ppermute | solution.py:65
  47.0 1.6 %collective-permute-start.15 = (bf16[256,256]{1,0:T(8,128)(2,1)S(1)}, bf16[256,256]{1,0:T(8,128)(2,1)S(1)}, u32[]{:S(2)}, u32[]{:S(2)}) collective-permute-start(bf16[256,256]{1,0:T(8,128)(2,1)S(1)} %shard_map.145), channel_id=1, source_target_pairs={{0,24},{4,28},{8,16},{12,20},{16,8},{20,12},{24,0},{28,4},{1,25},{... | collective-permute-start | bytes 393224 | tf_op jit(solution)/shard_map/ppermute | solution.py:65
  49.4 1.2 %collective-permute-start.13 = (bf16[256,256]{1,0:T(8,128)(2,1)S(1)}, bf16[256,256]{1,0:T(8,128)(2,1)S(1)}, u32[]{:S(2)}, u32[]{:S(2)}) collective-permute-start(bf16[256,256]{1,0:T(8,128)(2,1)S(1)} %shard_map.145), channel_id=1, source_target_pairs={{0,8},{4,12},{8,0},{12,4},{16,24},{20,28},{24,16},{28,20},{1,9},{5... | collective-permute-start | bytes 393224 | tf_op jit(solution)/shard_map/ppermute | solution.py:65
  50.8 3.4 %collective-permute-done.15 = bf16[256,256]{1,0:T(8,128)(2,1)S(1)} collective-permute-done((bf16[256,256]{1,0:T(8,128)(2,1)S(1)}, bf16[256,256]{1,0:T(8,128)(2,1)S(1)}, u32[]{:S(2)}, u32[]{:S(2)}) %collective-permute-start.15) | collective-permute-done | bytes 131104 | tf_op jit(solution)/shard_map/ppermute | solution.py:65
  54.2 1.3 %collective-permute-done.14 = bf16[256,256]{1,0:T(8,128)(2,1)S(1)} collective-permute-done((bf16[256,256]{1,0:T(8,128)(2,1)S(1)}, bf16[256,256]{1,0:T(8,128)(2,1)S(1)}, u32[]{:S(2)}, u32[]{:S(2)}) %collective-permute-start.14) | collective-permute-done | bytes 131104 | tf_op jit(solution)/shard_map/ppermute | solution.py:65
  55.8 1.9 %collective-permute-done.16.refs_1_ = bf16[4,256,256]{2,1,0:T(8,128)(2,1)S(1)} collective-permute-done((bf16[4,256,256]{2,1,0:T(8,128)(2,1)S(1)}, bf16[4,256,256]{2,1,0:T(8,128)(2,1)S(1)}, u32[]{:S(2)}, u32[]{:S(2)}) %collective-permute-start.16) | collective-permute-done | bytes 524320 | tf_op jit(solution)/shard_map/ppermute | solution.py:65
  58.4 2.7 %shard_map.147 = (bf16[128,2048]{1,0:T(8,128)(2,1)S(1)}, bf16[128,2048]{1,0:T(8,128)(2,1)S(1)}) custom-call(bf16[256,2048]{1,0:T(8,128)(2,1)S(1)} %get-tuple-element.43.rows_ref, bf16[4,96,640]{2,1,0:T(8,128)(2,1)S(1)} %pad_maximum_fusion.2.mine_ref.mine_tail_ref, bf16[4,96,640]{2,1,0:T(8,128)(2,1)S(1)} %collective-permute-done.9.theirs_ref.theirs_tail_ref, ...), custom_call_target="tpu_custom_call" | custom-call | flops 2214592512 | bytes 8650752 | tf_op jit(solution)/shard_map/pallas_call | solution.py:40
  61.2 1.8 %collective-permute-done.21.back_ref = bf16[128,2048]{1,0:T(8,128)(2,1)S(1)} collective-permute-done((bf16[128,2048]{1,0:T(8,128)(2,1)S(1)}, bf16[128,2048]{1,0:T(8,128)(2,1)S(1)}, u32[]{:S(2)}, u32[]{:S(2)}) %collective-permute-start.21) | collective-permute-done | bytes 524320 | tf_op jit(solution)/shard_map/ppermute | solution.py:65
  64.0 1.2 %collective-permute-start.23 = (bf16[32,2048]{1,0:T(8,128)(2,1)S(1)}, bf16[32,2048]{1,0:T(8,128)(2,1)S(1)}, u32[]{:S(2)}, u32[]{:S(2)}) collective-permute-start(bf16[32,2048]{1,0:T(8,128)(2,1)S(1)} %get-tuple-element.48), channel_id=1, source_target_pairs={{0,16},{4,20},{8,24},{12,28},{16,0},{20,4},{24,8},{28,12},{1,17},{... | collective-permute-start | bytes 393224 | tf_op jit(solution)/shard_map/ppermute | solution.py:65
  65.2 1.5 %collective-permute-start.24 = (bf16[32,2048]{1,0:T(8,128)(2,1)S(1)}, bf16[32,2048]{1,0:T(8,128)(2,1)S(1)}, u32[]{:S(2)}, u32[]{:S(2)}) collective-permute-start(bf16[32,2048]{1,0:T(8,128)(2,1)S(1)} %get-tuple-element.49), channel_id=1, source_target_pairs={{0,24},{4,28},{8,16},{12,20},{16,8},{20,12},{24,0},{28,4},{1,25},{... | collective-permute-start | bytes 393224 | tf_op jit(solution)/shard_map/ppermute | solution.py:65
  66.7 2.9 %collective-permute-done.22.refs_1_ = bf16[32,2048]{1,0:T(8,128)(2,1)S(1)} collective-permute-done((bf16[32,2048]{1,0:T(8,128)(2,1)S(1)}, bf16[32,2048]{1,0:T(8,128)(2,1)S(1)}, u32[]{:S(2)}, u32[]{:S(2)}) %collective-permute-start.22) | collective-permute-done | bytes 131104 | tf_op jit(solution)/shard_map/ppermute | solution.py:65
  70.1 2.0 %collective-permute-done.24.refs_3_ = bf16[32,2048]{1,0:T(8,128)(2,1)S(1)} collective-permute-done((bf16[32,2048]{1,0:T(8,128)(2,1)S(1)}, bf16[32,2048]{1,0:T(8,128)(2,1)S(1)}, u32[]{:S(2)}, u32[]{:S(2)}) %collective-permute-start.24) | collective-permute-done | bytes 131104 | tf_op jit(solution)/shard_map/ppermute | solution.py:65
  72.5 2.2 %collective-permute-start.26 = (bf16[8,2048]{1,0:T(8,128)(2,1)S(1)}, bf16[8,2048]{1,0:T(8,128)(2,1)S(1)}, u32[]{:S(2)}, u32[]{:S(2)}) collective-permute-start(bf16[8,2048]{1,0:T(8,128)(2,1)S(1)} %get-tuple-element.52), channel_id=1, source_target_pairs={{0,2},{1,3},{2,0},{3,1},{4,6},{5,7},{6,4},{7,5},{8,10},{9,11},{10,... | collective-permute-start | bytes 98312 | tf_op jit(solution)/shard_map/ppermute | solution.py:65
  74.7 1.9 %collective-permute-start.27 = (bf16[8,2048]{1,0:T(8,128)(2,1)S(1)}, bf16[8,2048]{1,0:T(8,128)(2,1)S(1)}, u32[]{:S(2)}, u32[]{:S(2)}) collective-permute-start(bf16[8,2048]{1,0:T(8,128)(2,1)S(1)} %get-tuple-element.53), channel_id=1, source_target_pairs={{0,3},{1,2},{2,1},{3,0},{4,7},{5,6},{6,5},{7,4},{8,11},{9,10},{10,... | collective-permute-start | bytes 98312 | tf_op jit(solution)/shard_map/ppermute | solution.py:65
  77.3 3.1 %collective-permute-done.27.refs_3_ = bf16[8,2048]{1,0:T(8,128)(2,1)S(1)} collective-permute-done((bf16[8,2048]{1,0:T(8,128)(2,1)S(1)}, bf16[8,2048]{1,0:T(8,128)(2,1)S(1)}, u32[]{:S(2)}, u32[]{:S(2)}) %collective-permute-start.27) | collective-permute-done | bytes 32800 | tf_op jit(solution)/shard_map/ppermute | solution.py:65
  (42 shorter events, 11.0 us)
Async XLA Ops:
  2.0 7.0 %collective-permute-start.2 = (bf16[32,512]{1,0:T(8,128)(2,1)S(1)}, bf16[32,512]{1,0:T(8,128)(2,1)S(1)}, u32[]{:S(2)}, u32[]{:S(2)}) collective-permute-start(bf16[32,512]{1,0:T(8,128)(2,1)S(1)} %get-tuple-element.29.refs_0_), channel_id=1, source_target_pairs={{0,3},{1,2},{2,1},{3,0},{4,7},{5,6},{6,5},{7,4},{8,11},{9,10},{10,... | collective-permute-start | bytes 98312 | tf_op jit(solution)/shard_map/ppermute | solution.py:65
  7.2 4.8 %collective-permute-start.1 = (bf16[32,512]{1,0:T(8,128)(2,1)S(1)}, bf16[32,512]{1,0:T(8,128)(2,1)S(1)}, u32[]{:S(2)}, u32[]{:S(2)}) collective-permute-start(bf16[32,512]{1,0:T(8,128)(2,1)S(1)} %get-tuple-element.29.refs_0_), channel_id=1, source_target_pairs={{0,2},{1,3},{2,0},{3,1},{4,6},{5,7},{6,4},{7,5},{8,10},{9,11},{10,... | collective-permute-start | bytes 98312 | tf_op jit(solution)/shard_map/ppermute | solution.py:65
  7.2 4.8 %collective-permute-start = (bf16[32,512]{1,0:T(8,128)(2,1)S(1)}, bf16[32,512]{1,0:T(8,128)(2,1)S(1)}, u32[]{:S(2)}, u32[]{:S(2)}) collective-permute-start(bf16[32,512]{1,0:T(8,128)(2,1)S(1)} %get-tuple-element.29.refs_0_), channel_id=1, source_target_pairs={{0,1},{1,0},{2,3},{3,2},{4,5},{5,4},{6,7},{7,6},{8,9},{9,8},{10,11... | collective-permute-start | bytes 98312 | tf_op jit(solution)/shard_map/ppermute | solution.py:65
  12.4 7.8 %collective-permute-start.5 = (f32[40,256]{1,0:T(8,128)S(1)}, f32[40,256]{1,0:T(8,128)S(1)}, u32[]{:S(2)}, u32[]{:S(2)}) collective-permute-start(f32[40,256]{1,0:T(8,128)S(1)} %get-tuple-element.33.refs_0_), channel_id=1, source_target_pairs={{0,3},{1,2},{2,1},{3,0},{4,7},{5,6},{6,5},{7,4},{8,11},{9,10},{10,... | collective-permute-start | bytes 122888 | tf_op jit(solution)/shard_map/ppermute | solution.py:65
  13.9 6.3 %collective-permute-start.4 = (f32[40,256]{1,0:T(8,128)S(1)}, f32[40,256]{1,0:T(8,128)S(1)}, u32[]{:S(2)}, u32[]{:S(2)}) collective-permute-start(f32[40,256]{1,0:T(8,128)S(1)} %get-tuple-element.33.refs_0_), channel_id=1, source_target_pairs={{0,2},{1,3},{2,0},{3,1},{4,6},{5,7},{6,4},{7,5},{8,10},{9,11},{10,... | collective-permute-start | bytes 122888 | tf_op jit(solution)/shard_map/ppermute | solution.py:65
  14.5 5.6 %collective-permute-start.3 = (f32[40,256]{1,0:T(8,128)S(1)}, f32[40,256]{1,0:T(8,128)S(1)}, u32[]{:S(2)}, u32[]{:S(2)}) collective-permute-start(f32[40,256]{1,0:T(8,128)S(1)} %get-tuple-element.33.refs_0_), channel_id=1, source_target_pairs={{0,1},{1,0},{2,3},{3,2},{4,5},{5,4},{6,7},{7,6},{8,9},{9,8},{10,11... | collective-permute-start | bytes 122888 | tf_op jit(solution)/shard_map/ppermute | solution.py:65
  16.8 41.6 %copy-start.1 = (bf16[1,704,2048]{2,1,0:T(8,128)(2,1)S(1)}, bf16[1,704,2048]{2,1,0:T(8,128)(2,1)}, u32[]{:S(2)}) copy-start(bf16[1,704,2048]{2,1,0:T(8,128)(2,1)} %param.25) | copy-start | bytes 8650756
  20.1 38.2 %copy-start = (bf16[1,2,2048,704]{2,3,1,0:T(8,128)(2,1)S(1)}, bf16[1,2,2048,704]{2,3,1,0:T(8,128)(2,1)}, u32[]{:S(2)}) copy-start(bf16[1,2,2048,704]{2,3,1,0:T(8,128)(2,1)} %param.24) | copy-start | bytes 17301508
  21.0 6.2 %collective-permute-start.8 = (bf16[96,640]{1,0:T(8,128)(2,1)S(1)}, bf16[96,640]{1,0:T(8,128)(2,1)S(1)}, u32[]{:S(2)}, u32[]{:S(2)}) collective-permute-start(bf16[96,640]{1,0:T(8,128)(2,1)S(1)} %get-tuple-element.40), channel_id=1, source_target_pairs={{0,24},{4,28},{8,16},{12,20},{16,8},{20,12},{24,0},{28,4},{1,25},{... | collective-permute-start | bytes 368648 | tf_op jit(solution)/shard_map/ppermute | solution.py:65
  23.5 5.0 %collective-permute-start.7 = (bf16[96,640]{1,0:T(8,128)(2,1)S(1)}, bf16[96,640]{1,0:T(8,128)(2,1)S(1)}, u32[]{:S(2)}, u32[]{:S(2)}) collective-permute-start(bf16[96,640]{1,0:T(8,128)(2,1)S(1)} %get-tuple-element.40), channel_id=1, source_target_pairs={{0,16},{4,20},{8,24},{12,28},{16,0},{20,4},{24,8},{28,12},{1,17},{... | collective-permute-start | bytes 368648 | tf_op jit(solution)/shard_map/ppermute | solution.py:65
  24.0 4.9 %collective-permute-start.6 = (bf16[96,640]{1,0:T(8,128)(2,1)S(1)}, bf16[96,640]{1,0:T(8,128)(2,1)S(1)}, u32[]{:S(2)}, u32[]{:S(2)}) collective-permute-start(bf16[96,640]{1,0:T(8,128)(2,1)S(1)} %get-tuple-element.40), channel_id=1, source_target_pairs={{0,8},{4,12},{8,0},{12,4},{16,24},{20,28},{24,16},{28,20},{1,9},{5... | collective-permute-start | bytes 368648 | tf_op jit(solution)/shard_map/ppermute | solution.py:65
  28.9 1.9 %collective-permute-start.9 = (bf16[4,96,640]{2,1,0:T(8,128)(2,1)S(1)}, bf16[4,96,640]{2,1,0:T(8,128)(2,1)S(1)}, u32[]{:S(2)}, u32[]{:S(2)}) collective-permute-start(bf16[4,96,640]{2,1,0:T(8,128)(2,1)S(1)} %pad_maximum_fusion.2.mine_ref.mine_tail_ref), channel_id=1, source_target_pairs={{0,4},{4,0},{8,12},{12,8},{16,20},{20,16},{24,28},{28,24},{1,5},{5... | collective-permute-start | bytes 1474568 | tf_op jit(solution)/shard_map/ppermute | solution.py:65
  32.9 8.4 %collective-permute-start.12 = (bf16[256,256]{1,0:T(8,128)(2,1)S(1)}, bf16[256,256]{1,0:T(8,128)(2,1)S(1)}, u32[]{:S(2)}, u32[]{:S(2)}) collective-permute-start(bf16[256,256]{1,0:T(8,128)(2,1)S(1)} %shard_map.144.refs_0_), channel_id=1, source_target_pairs={{0,3},{1,2},{2,1},{3,0},{4,7},{5,6},{6,5},{7,4},{8,11},{9,10},{10,... | collective-permute-start | bytes 393224 | tf_op jit(solution)/shard_map/ppermute | solution.py:65
  34.4 12.6 %collective-permute-start.11 = (bf16[256,256]{1,0:T(8,128)(2,1)S(1)}, bf16[256,256]{1,0:T(8,128)(2,1)S(1)}, u32[]{:S(2)}, u32[]{:S(2)}) collective-permute-start(bf16[256,256]{1,0:T(8,128)(2,1)S(1)} %shard_map.144.refs_0_), channel_id=1, source_target_pairs={{0,2},{1,3},{2,0},{3,1},{4,6},{5,7},{6,4},{7,5},{8,10},{9,11},{10,... | collective-permute-start | bytes 393224 | tf_op jit(solution)/shard_map/ppermute | solution.py:65
  35.0 11.9 %collective-permute-start.10 = (bf16[256,256]{1,0:T(8,128)(2,1)S(1)}, bf16[256,256]{1,0:T(8,128)(2,1)S(1)}, u32[]{:S(2)}, u32[]{:S(2)}) collective-permute-start(bf16[256,256]{1,0:T(8,128)(2,1)S(1)} %shard_map.144.refs_0_), channel_id=1, source_target_pairs={{0,1},{1,0},{2,3},{3,2},{4,5},{5,4},{6,7},{7,6},{8,9},{9,8},{10,11... | collective-permute-start | bytes 393224 | tf_op jit(solution)/shard_map/ppermute | solution.py:65
  37.3 12.1 %collective-permute-start.19 = (bf16[32,2048]{1,0:T(8,128)(2,1)S(1)}, bf16[32,2048]{1,0:T(8,128)(2,1)S(1)}, u32[]{:S(2)}, u32[]{:S(2)}) collective-permute-start(bf16[32,2048]{1,0:T(8,128)(2,1)S(1)} %get-tuple-element.41), channel_id=1, source_target_pairs={{0,24},{4,28},{8,16},{12,20},{16,8},{20,12},{24,0},{28,4},{1,25},{... | collective-permute-start | bytes 393224 | tf_op jit(solution)/shard_map/ppermute | solution.py:65
  38.8 11.8 %collective-permute-start.18 = (bf16[32,2048]{1,0:T(8,128)(2,1)S(1)}, bf16[32,2048]{1,0:T(8,128)(2,1)S(1)}, u32[]{:S(2)}, u32[]{:S(2)}) collective-permute-start(bf16[32,2048]{1,0:T(8,128)(2,1)S(1)} %get-tuple-element.41), channel_id=1, source_target_pairs={{0,16},{4,20},{8,24},{12,28},{16,0},{20,4},{24,8},{28,12},{1,17},{... | collective-permute-start | bytes 393224 | tf_op jit(solution)/shard_map/ppermute | solution.py:65
  41.2 9.4 %collective-permute-start.17 = (bf16[32,2048]{1,0:T(8,128)(2,1)S(1)}, bf16[32,2048]{1,0:T(8,128)(2,1)S(1)}, u32[]{:S(2)}, u32[]{:S(2)}) collective-permute-start(bf16[32,2048]{1,0:T(8,128)(2,1)S(1)} %get-tuple-element.41), channel_id=1, source_target_pairs={{0,8},{4,12},{8,0},{12,4},{16,24},{20,28},{24,16},{28,20},{1,9},{5... | collective-permute-start | bytes 393224 | tf_op jit(solution)/shard_map/ppermute | solution.py:65
  47.0 7.2 %collective-permute-start.15 = (bf16[256,256]{1,0:T(8,128)(2,1)S(1)}, bf16[256,256]{1,0:T(8,128)(2,1)S(1)}, u32[]{:S(2)}, u32[]{:S(2)}) collective-permute-start(bf16[256,256]{1,0:T(8,128)(2,1)S(1)} %shard_map.145), channel_id=1, source_target_pairs={{0,24},{4,28},{8,16},{12,20},{16,8},{20,12},{24,0},{28,4},{1,25},{... | collective-permute-start | bytes 393224 | tf_op jit(solution)/shard_map/ppermute | solution.py:65
  48.6 6.9 %collective-permute-start.14 = (bf16[256,256]{1,0:T(8,128)(2,1)S(1)}, bf16[256,256]{1,0:T(8,128)(2,1)S(1)}, u32[]{:S(2)}, u32[]{:S(2)}) collective-permute-start(bf16[256,256]{1,0:T(8,128)(2,1)S(1)} %shard_map.145), channel_id=1, source_target_pairs={{0,16},{4,20},{8,24},{12,28},{16,0},{20,4},{24,8},{28,12},{1,17},{... | collective-permute-start | bytes 393224 | tf_op jit(solution)/shard_map/ppermute | solution.py:65
  49.4 6.2 %collective-permute-start.13 = (bf16[256,256]{1,0:T(8,128)(2,1)S(1)}, bf16[256,256]{1,0:T(8,128)(2,1)S(1)}, u32[]{:S(2)}, u32[]{:S(2)}) collective-permute-start(bf16[256,256]{1,0:T(8,128)(2,1)S(1)} %shard_map.145), channel_id=1, source_target_pairs={{0,8},{4,12},{8,0},{12,4},{16,24},{20,28},{24,16},{28,20},{1,9},{5... | collective-permute-start | bytes 393224 | tf_op jit(solution)/shard_map/ppermute | solution.py:65
  50.7 5.1 %collective-permute-start.20 = (bf16[4,32,2048]{2,1,0:T(8,128)(2,1)S(1)}, bf16[4,32,2048]{2,1,0:T(8,128)(2,1)S(1)}, u32[]{:S(2)}, u32[]{:S(2)}) collective-permute-start(bf16[4,32,2048]{2,1,0:T(8,128)(2,1)S(1)} %pad_maximum_fusion.1.refs_2_), channel_id=1, source_target_pairs={{0,4},{4,0},{8,12},{12,8},{16,20},{20,16},{24,28},{28,24},{1,5},{5... | collective-permute-start | bytes 1572872 | tf_op jit(solution)/shard_map/ppermute | solution.py:65
  55.7 2.0 %collective-permute-start.16 = (bf16[4,256,256]{2,1,0:T(8,128)(2,1)S(1)}, bf16[4,256,256]{2,1,0:T(8,128)(2,1)S(1)}, u32[]{:S(2)}, u32[]{:S(2)}) collective-permute-start(bf16[4,256,256]{2,1,0:T(8,128)(2,1)S(1)} %pad_maximum_fusion.refs_0_), channel_id=1, source_target_pairs={{0,4},{4,0},{8,12},{12,8},{16,20},{20,16},{24,28},{28,24},{1,5},{5... | collective-permute-start | bytes 1572872 | tf_op jit(solution)/shard_map/ppermute | solution.py:65
  61.0 2.0 %collective-permute-start.21 = (bf16[128,2048]{1,0:T(8,128)(2,1)S(1)}, bf16[128,2048]{1,0:T(8,128)(2,1)S(1)}, u32[]{:S(2)}, u32[]{:S(2)}) collective-permute-start(bf16[128,2048]{1,0:T(8,128)(2,1)S(1)} %get-tuple-element.45), channel_id=1, source_target_pairs={{0,4},{4,0},{8,12},{12,8},{16,20},{20,16},{24,28},{28,24},{1,5},{5... | collective-permute-start | bytes 1572872 | tf_op jit(solution)/shard_map/ppermute | solution.py:65
  63.1 6.4 %collective-permute-start.22 = (bf16[32,2048]{1,0:T(8,128)(2,1)S(1)}, bf16[32,2048]{1,0:T(8,128)(2,1)S(1)}, u32[]{:S(2)}, u32[]{:S(2)}) collective-permute-start(bf16[32,2048]{1,0:T(8,128)(2,1)S(1)} %get-tuple-element.47), channel_id=1, source_target_pairs={{0,8},{4,12},{8,0},{12,4},{16,24},{20,28},{24,16},{28,20},{1,9},{5... | collective-permute-start | bytes 393224 | tf_op jit(solution)/shard_map/ppermute | solution.py:65
  64.0 6.1 %collective-permute-start.23 = (bf16[32,2048]{1,0:T(8,128)(2,1)S(1)}, bf16[32,2048]{1,0:T(8,128)(2,1)S(1)}, u32[]{:S(2)}, u32[]{:S(2)}) collective-permute-start(bf16[32,2048]{1,0:T(8,128)(2,1)S(1)} %get-tuple-element.48), channel_id=1, source_target_pairs={{0,16},{4,20},{8,24},{12,28},{16,0},{20,4},{24,8},{28,12},{1,17},{... | collective-permute-start | bytes 393224 | tf_op jit(solution)/shard_map/ppermute | solution.py:65
  65.2 6.9 %collective-permute-start.24 = (bf16[32,2048]{1,0:T(8,128)(2,1)S(1)}, bf16[32,2048]{1,0:T(8,128)(2,1)S(1)}, u32[]{:S(2)}, u32[]{:S(2)}) collective-permute-start(bf16[32,2048]{1,0:T(8,128)(2,1)S(1)} %get-tuple-element.49), channel_id=1, source_target_pairs={{0,24},{4,28},{8,16},{12,20},{16,8},{20,12},{24,0},{28,4},{1,25},{... | collective-permute-start | bytes 393224 | tf_op jit(solution)/shard_map/ppermute | solution.py:65
  72.1 4.5 %collective-permute-start.25 = (bf16[8,2048]{1,0:T(8,128)(2,1)S(1)}, bf16[8,2048]{1,0:T(8,128)(2,1)S(1)}, u32[]{:S(2)}, u32[]{:S(2)}) collective-permute-start(bf16[8,2048]{1,0:T(8,128)(2,1)S(1)} %get-tuple-element.51), channel_id=1, source_target_pairs={{0,1},{1,0},{2,3},{3,2},{4,5},{5,4},{6,7},{7,6},{8,9},{9,8},{10,11... | collective-permute-start | bytes 98312 | tf_op jit(solution)/shard_map/ppermute | solution.py:65
  72.5 4.8 %collective-permute-start.26 = (bf16[8,2048]{1,0:T(8,128)(2,1)S(1)}, bf16[8,2048]{1,0:T(8,128)(2,1)S(1)}, u32[]{:S(2)}, u32[]{:S(2)}) collective-permute-start(bf16[8,2048]{1,0:T(8,128)(2,1)S(1)} %get-tuple-element.52), channel_id=1, source_target_pairs={{0,2},{1,3},{2,0},{3,1},{4,6},{5,7},{6,4},{7,5},{8,10},{9,11},{10,... | collective-permute-start | bytes 98312 | tf_op jit(solution)/shard_map/ppermute | solution.py:65
  74.7 5.7 %collective-permute-start.27 = (bf16[8,2048]{1,0:T(8,128)(2,1)S(1)}, bf16[8,2048]{1,0:T(8,128)(2,1)S(1)}, u32[]{:S(2)}, u32[]{:S(2)}) collective-permute-start(bf16[8,2048]{1,0:T(8,128)(2,1)S(1)} %get-tuple-element.53), channel_id=1, source_target_pairs={{0,3},{1,2},{2,1},{3,0},{4,7},{5,6},{6,5},{7,4},{8,11},{9,10},{10,... | collective-permute-start | bytes 98312 | tf_op jit(solution)/shard_map/ppermute | solution.py:65

commit v2 on v1

--- a/solution.py
+++ b/solution.py
@@ -81,45 +81,32 @@
     return parts
 
 
-def pick_kernel(
-    keep_hbm,
-    raw_hbm,
-    weight_hbm,
-    gain_hbm,
-    ids_hbm,
-    gates_hbm,
-    slot_hbm,
-    out_ref,
-    weight_ref,
-    gain_ref,
-    dense_ref,
-    keep_ref,
-    raw_ref,
-    ids_ref,
-    gates_ref,
-    slot_ref,
-    sem,
-):
-    pairs = [
-        (keep_hbm, keep_ref),
-        (raw_hbm, raw_ref),
-        (ids_hbm, ids_ref),
-        (gates_hbm, gates_ref),
-        (slot_hbm, slot_ref),
-        (gain_hbm, gain_ref),
-        (weight_hbm, weight_ref),
-    ]
+def fetch(pairs, sem):
     copies = [pltpu.make_async_copy(a, b, sem.at[n]) for n, (a, b) in enumerate(pairs)]
     for copy in copies:
         copy.start()
-    copies[0].wait()
-    copies[1].wait()
+    return copies
+
+
+def pick_kernel(keep_hbm, raw_hbm, out_ref, keep_ref, raw_ref, sem):
+    for copy in fetch([(keep_hbm, keep_ref), (raw_hbm, raw_ref)], sem):
+        copy.wait()
     rows = lax.broadcasted_iota(jnp.int32, (raw_ref.shape[0], keep_ref.shape[1]), 0)
     hits = jnp.where(rows == keep_ref[...], 1.0, 0.0).astype(BF16)
     out_ref[...] = lax.dot_general(
         hits, raw_ref[...], (((0,), (0,)), ((), ())), preferred_element_type=F32
     ).astype(BF16)
-    for copy in copies[2:]:
+
+
+def prepare_kernel(raw_rows, *refs):
+    keep_hbm, ids_hbm, gates_hbm, slot_hbm = refs[:4]
+    sources = refs[4:9]
+    targets = refs[9:14]
+    dense_ref, cos_ref, sin_ref, live_ref = refs[14:18]
+    keep_ref, ids_ref, gates_ref, slot_ref, sem = refs[18:]
+    small = [(keep_hbm, keep_ref), (ids_hbm, ids_ref), (gates_hbm, gates_ref), (slot_hbm, slot_ref)]
+    copies = fetch(small + list(zip(sources, targets)), sem)
+    for copy in copies[:4]:
         copy.wait()
     ids = ids_ref[...]
     slots = jnp.zeros_like(ids)
@@ -130,6 +117,25 @@
     for t in range(ids.shape[1]):
         gates = gates + jnp.where(lane == slots[:, t : t + 1], gates_ref[:, t : t + 1], 0.0)
     dense_ref[...] = gates
+    rows, rope = cos_ref.shape
+    diagonal = lax.broadcasted_iota(jnp.int32, (rows, rows), 0) == lax.broadcasted_iota(
+        jnp.int32, (rows, rows), 1
+    )
+    listing = jnp.sum(
+        jnp.where(diagonal, keep_ref[...].astype(F32), 0.0), axis=1, keepdims=True
+    )
+    live_ref[...] = jnp.where(listing >= 0, 1.0, 0.0)
+    positions = (here()[0] * raw_rows).astype(F32) + jnp.maximum(listing, 0.0)
+    half = rope // 2
+    lane = lax.broadcasted_iota(jnp.int32, (rows, rope), 1)
+    first = lane < half
+    place = jnp.where(first, lane, lane - half).astype(F32)
+    angles = positions * jnp.exp(place * (-2.0 / rope * math.log(THETA)))
+    cos_ref[...] = jnp.cos(angles)
+    sine = jnp.sin(angles)
+    sin_ref[...] = jnp.where(first, -sine, sine)
+    for copy in copies[4:]:
+        copy.wait()
 
 
 def latent_kernel(spans, *refs):
@@ -155,59 +161,11 @@
     return values * cosine + swapped * sine
 
 
-def query_kernel(
-    heads,
-    raw_rows,
-    normed_ref,
-    weight_ref,
-    keep_hbm,
-    kv_hbm,
-    moe_hbm,
-    out_ref,
-    cos_ref,
-    sin_ref,
-    live_ref,
-    kv_ref,
-    moe_ref,
-    buf,
-    keep_ref,
-    sem,
-):
+def query_kernel(heads, normed_ref, weight_ref, cos_ref, sin_ref, out_ref):
     rows = normed_ref.shape[0]
     latent = weight_ref.shape[1] // heads
-    steps = buf.shape[0]
-    deep = buf.shape[1]
-    small = [(keep_hbm, keep_ref), (kv_hbm, kv_ref), (moe_hbm, moe_ref)]
-    small = [pltpu.make_async_copy(a, b, sem.at[steps + n]) for n, (a, b) in enumerate(small)]
-    copies = [
-        pltpu.make_async_copy(weight_ref.at[pl.ds(n * deep, deep), :], buf.at[n], sem.at[n])
-        for n in range(steps)
-    ]
-    for copy in small + copies:
-        copy.start()
-    small[0].wait()
-    diagonal = lax.broadcasted_iota(jnp.int32, (rows, rows), 0) == lax.broadcasted_iota(
-        jnp.int32, (rows, rows), 1
-    )
-    listing = jnp.sum(
-        jnp.where(diagonal, keep_ref[...].astype(F32), 0.0), axis=1, keepdims=True
-    )
-    live_ref[...] = jnp.where(listing >= 0, 1.0, 0.0)
-    positions = (here()[0] * raw_rows).astype(F32) + jnp.maximum(listing, 0.0)
-    rope = cos_ref.shape[1]
-    half = rope // 2
-    lane = lax.broadcasted_iota(jnp.int32, (rows, rope), 1)
-    first = lane < half
-    place = jnp.where(first, lane, lane - half).astype(F32)
-    angles = positions * jnp.exp(place * (-2.0 / rope * math.log(THETA)))
-    cos_ref[...] = jnp.cos(angles)
-    sine = jnp.sin(angles)
-    sin_ref[...] = jnp.where(first, -sine, sine)
-    total = jnp.zeros((rows, weight_ref.shape[1]), F32)
-    for n in range(steps):
-        copies[n].wait()
-        total = total + nn(normed_ref[:, n * deep : (n + 1) * deep], buf[n])
-    kv_rank = latent - rope
+    total = nn(normed_ref[...], weight_ref[...])
+    kv_rank = latent - cos_ref.shape[1]
     out_ref[...] = jnp.zeros(out_ref.shape, BF16)
     for h in range(heads):
         one = total[:, h * latent : (h + 1) * latent]
@@ -215,8 +173,6 @@
         out_ref[h * rows : (h + 1) * rows, kv_rank:latent] = rotated(
             one[:, kv_rank:], cos_ref[...], sin_ref[...]
         ).astype(BF16)
-    for copy in small[1:]:
-        copy.wait()
 
 
 def cache_kernel(spans, width, experts, *refs):
@@ -294,69 +250,130 @@
     refs[-1][...] = sum(ref[...].astype(F32) for ref in refs[:-1]).astype(BF16)
 
 
-def resid_kernel(blocks, *refs):
-    mine_ref, theirs_ref, mine_rows, their_rows, gain_ref, own_ref, out_ref, buf = refs
+def scaled_rows(blocks, odd, pieces_ref, mine_rows, their_rows, gain_ref, part_ref, rows_ref):
     order = places(blocks)
     half = blocks // 2
-    index = here()
-    count, width = mine_rows.shape[1], mine_ref.shape[2]
-    for n, i in enumerate(order):
-        ref, p = (mine_ref, n) if n < half else (theirs_ref, n - half)
-        lanes = pl.ds(pl.multiple_of((index[0] ^ i) * width, width), width)
+    index = here()[0]
+    count, width = mine_rows.shape[1], pieces_ref.shape[2]
+    squares = [jnp.zeros((count, 1), F32)] * blocks
+    for p in range(half):
+        i = 2 * p + odd
+        lanes = pl.ds(pl.multiple_of((index ^ i) * width, width), width)
+        gain = gain_ref[:, lanes]
         for at, j in enumerate(order):
             to = order.index(i ^ j)
-            buf[to * count : (to + 1) * count, lanes] = ref[
+            rows = mine_rows if to < half else their_rows
+            resid = rows[to % half, :, lanes].astype(F32) + pieces_ref[
                 p, at * count : (at + 1) * count, :
             ].astype(F32)
-    for n in range(blocks):
-        rows, p = (mine_rows, n) if n < half else (their_rows, n - half)
-        at = slice(n * count, (n + 1) * count)
-        resid = rows[p].astype(F32) + buf[at, :]
-        factor = lax.rsqrt(jnp.mean(resid * resid, axis=1, keepdims=True) + EPS)
-        out_ref[at, :] = (resid * factor * gain_ref[...]).astype(BF16)
-        if n == 0:
-            buf[at, :] = resid
-    size = own_ref.shape[0]
-    own_ref[...] = buf[pl.ds(pl.multiple_of(index[1] * size, size), size), :]
+            squares[to] = squares[to] + jnp.sum(resid * resid, axis=1, keepdims=True)
+            rows_ref[to * count : (to + 1) * count, p * width : (p + 1) * width] = (
+                resid * gain
+            ).astype(BF16)
+            if to == 0:
+                part_ref[:, p * width : (p + 1) * width] = resid
+    return jnp.concatenate(squares, axis=0)
+
+
+def products(blocks, odd, width, rows_ref, in_ref, half, start, size):
+    index = here()[0]
+    total = jnp.zeros((rows_ref.shape[0], size), F32)
+    for p in range(blocks // 2):
+        lanes = pl.ds(pl.multiple_of((index ^ (2 * p + odd)) * width, width), width)
+        total = total + nt(
+            rows_ref[:, p * width : (p + 1) * width], in_ref[half, start : start + size, lanes]
+        )
+    return total
+
+
+def begin_kernel(
+    blocks,
+    cuts,
+    mine_ref,
+    mine_rows,
+    their_rows,
+    gain_ref,
+    in_ref,
+    part_ref,
+    square_ref,
+    gate_ref,
+    upper_ref,
+    rows_ref,
+):
+    square_ref[...] = scaled_rows(
+        blocks, 0, mine_ref, mine_rows, their_rows, gain_ref, part_ref, rows_ref
+    )
+    width = mine_ref.shape[2]
+    for start, size in cuts:
+        at = slice(start, start + size)
+        gate_ref[:, at] = products(blocks, 0, width, rows_ref, in_ref, 0, start, size)
+        upper_ref[:, at] = products(blocks, 0, width, rows_ref, in_ref, 1, start, size)
 
 
 def expert_kernel(
+    blocks,
     first_lane,
     tail_at,
     experts,
     cuts,
     columns,
-    rows_ref,
+    theirs_ref,
+    mine_rows,
+    their_rows,
+    gain_ref,
+    in_ref,
+    part_ref,
+    square_ref,
+    gate_ref,
+    upper_ref,
     mine_tail_ref,
     theirs_tail_ref,
-    in_ref,
     out_weight_ref,
     near_ref,
     far_ref,
+    own_ref,
+    rows_ref,
     act_ref,
+    rest_ref,
+    whole_ref,
 ):
-    rows = rows_ref[...]
+    square = square_ref[...] + scaled_rows(
+        blocks, 1, theirs_ref, mine_rows, their_rows, gain_ref, rest_ref, rows_ref
+    )
+    index = here()
+    width = theirs_ref.shape[2]
+    for p in range(blocks // 2):
+        for odd, ref in enumerate((part_ref, rest_ref)):
+            lanes = pl.ds(pl.multiple_of((index[0] ^ (2 * p + odd)) * width, width), width)
+            whole_ref[:, lanes] = ref[:, p * width : (p + 1) * width]
+    size = own_ref.shape[0]
+    own_ref[...] = whole_ref[pl.ds(pl.multiple_of(index[1] * size, size), size), :]
+    factor = lax.rsqrt(square / (blocks * width) + EPS)
+    for start, size in cuts:
+        at = slice(start, start + size)
+        gate = factor * (
+            gate_ref[:, at] + products(blocks, 1, width, rows_ref, in_ref, 0, start, size)
+        )
+        upper = factor * (
+            upper_ref[:, at] + products(blocks, 1, width, rows_ref, in_ref, 1, start, size)
+        )
+        act_ref[:, at] = (gate / (1.0 + jnp.exp(-gate)) * upper).astype(BF16)
+    half = near_ref.shape[0]
     pieces = mine_tail_ref.shape[0]
-    count = rows.shape[0] // (2 * pieces)
+    count = half // pieces
     tail = jnp.concatenate(
         [ref[p, :count, tail_at:] for ref in (mine_tail_ref, theirs_tail_ref) for p in range(pieces)],
         axis=0,
     )
     tail = tail.astype(F32)
     lane = lax.broadcasted_iota(jnp.int32, tail.shape, 1) - first_lane
-    index = here()
     slot = lax.div(index[0] * lax.axis_size("span") + index[1], 2)
     scale = jnp.sum(
         jnp.where((lane == slot) | (lane == slot + experts), tail, 0.0), axis=1, keepdims=True
     )
-    for start, size in cuts:
-        gate = nt(rows, in_ref[0, start : start + size, :])
-        upper = nt(rows, in_ref[1, start : start + size, :])
-        act_ref[:, start : start + size] = (gate / (1.0 + jnp.exp(-gate)) * upper).astype(BF16)
-    half = near_ref.shape[0]
-    width = out_weight_ref.shape[1] // columns
+    wide = out_weight_ref.shape[1] // columns
     for n in range(columns):
-        span = slice(n * width, (n + 1) * width)
+        span = slice(n * wide, (n + 1) * wide)
         done = nn(act_ref[...], out_weight_ref[:, span])
         done = jnp.where(scale > 0, done * scale, 0.0).astype(BF16)
         near_ref[:, span] = done[:half]
@@ -423,28 +440,44 @@
     hidden = expert_in.shape[3]
     evens = list(range(0, contexts, 2))
 
-    sent_width = up(max(part_width, experts))
-    picked, near_weight, gain, dense = call(
+    picked = call(
         pick_kernel,
-        [
-            shape((kept, raw_tokens.shape[1]), BF16),
-            shape((part_width, model), BF16),
-            shape((1, model), F32),
-            shape((rows_dev, sent_width), F32),
-        ],
-        [HBM] * 7,
-        (keep, raw_tokens, latent_weight.T, attn_gain[None], expert_ids, gate_values, expert_slot),
+        shape((kept, raw_tokens.shape[1]), BF16),
+        [HBM] * 2,
+        (keep, raw_tokens),
         scratch=[
             pltpu.VMEM(keep.shape, jnp.int32),
             pltpu.VMEM(raw_tokens.shape, BF16),
+            pltpu.SemaphoreType.DMA((2,)),
+        ],
+        limit=4,
+    )
+    parts = gathered(picked, "span", range(1, spans))
+
+    sent_width = up(max(part_width, experts))
+    moved = (latent_weight.T, attn_gain[None], kv_gain[None], moe_gain[None], query_weight)
+    near_weight, gain, near_kv, near_moe, near_query, dense, cosine, sine, live = call(
+        functools.partial(prepare_kernel, raw_rows),
+        [shape(value.shape, value.dtype) for value in moved]
+        + [
+            shape((rows_dev, sent_width), F32),
+            shape((kept, rope), F32),
+            shape((kept, rope), F32),
+            shape((kept, 1), F32),
+        ],
+        [HBM] * 9,
+        (keep, expert_ids, gate_values, expert_slot, *moved),
+        scratch=[
+            pltpu.VMEM(keep.shape, jnp.int32),
             pltpu.VMEM(expert_ids.shape, jnp.int32),
             pltpu.VMEM(gate_values.shape, F32),
             pltpu.SMEM(expert_slot.shape, jnp.int32),
-            pltpu.SemaphoreType.DMA((7,)),
+            pltpu.SemaphoreType.DMA((9,)),
         ],
-        limit=4,
-    )
-    parts = gathered(picked, "span", range(1, spans))
+        moved=2 * query_weight.size,
+        limit=12,
+    )
+
     compact, normed, sent = call(
         functools.partial(latent_kernel, spans),
         [
@@ -459,25 +492,12 @@
         limit=4,
     )
     parts = gathered(sent, "span", range(1, spans))
-    steps = 8
     row_width = up(latent_width + 2 * experts + 1)
-    query, cosine, sine, live, near_kv, near_moe = call(
-        functools.partial(query_kernel, heads, raw_rows),
-        [
-            shape((heads * kept, row_width), BF16),
-            shape((kept, rope), F32),
-            shape((kept, rope), F32),
-            shape((kept, 1), F32),
-            shape((1, kv_rank), F32),
-            shape((1, model), F32),
-        ],
-        [VM] + [HBM] * 4,
-        (normed, query_weight, keep, kv_gain[None], moe_gain[None]),
-        scratch=[
-            pltpu.VMEM((steps, model // steps, query_weight.shape[1]), BF16),
-            pltpu.VMEM(keep.shape, jnp.int32),
-            pltpu.SemaphoreType.DMA((steps + 3,)),
-        ],
+    query = call(
+        functools.partial(query_kernel, heads),
+        shape((heads * kept, row_width), BF16),
+        [VM] * 4,
+        (normed, near_query, cosine, sine),
         flops=2 * kept * query_weight.size,
         moved=2 * query_weight.size,
         limit=10,
@@ -516,28 +536,53 @@
     mine = jnp.stack(gathered(column, "context", evens[1:]))
     theirs = partner(mine, "context", 1)
     half = mine.shape[0] * kept
-    own, moe_in = call(
-        functools.partial(resid_kernel, contexts),
-        [shape((rows_dev, model), F32), shape((2 * half, model), BF16)],
-        [VM] * 5,
-        (mine, theirs, mine_rows, their_rows, near_moe),
-        scratch=[pltpu.VMEM((2 * half, model), F32)],
-        limit=16,
-    )
     cuts, start = [], 0
     while start < hidden:
         size = min(2 * LANES, hidden - start)
         cuts.append((start, size))
         start += size
-    near, far = call(
-        functools.partial(expert_kernel, latent_width - kv_rank, kv_rank, experts, cuts, 4),
-        [shape((half, model), BF16), shape((half, model), BF16)],
+    weights_in = jnp.swapaxes(expert_in[0], 1, 2)
+    begun = call(
+        functools.partial(begin_kernel, contexts, cuts),
+        [
+            shape((kept, model // 2), F32),
+            shape((2 * half, 1), F32),
+            shape((2 * half, hidden), F32),
+            shape((2 * half, hidden), F32),
+        ],
         [VM] * 5,
-        (moe_in, mine_keys, their_keys, jnp.swapaxes(expert_in[0], 1, 2), expert_out[0]),
-        scratch=[pltpu.VMEM((2 * half, hidden), BF16)],
-        flops=6 * 2 * half * hidden * model,
-        moved=6 * hidden * model,
-        limit=24,
+        (mine, mine_rows, their_rows, near_moe, weights_in),
+        scratch=[pltpu.VMEM((2 * half, model // 2), BF16)],
+        flops=2 * 2 * half * hidden * model,
+        moved=4 * hidden * model,
+        limit=20,
+    )
+    near, far, own = call(
+        functools.partial(
+            expert_kernel, contexts, latent_width - kv_rank, kv_rank, experts, cuts, 4
+        ),
+        [shape((half, model), BF16), shape((half, model), BF16), shape((rows_dev, model), F32)],
+        [VM] * 12,
+        (
+            theirs,
+            mine_rows,
+            their_rows,
+            near_moe,
+            weights_in,
+            *begun,
+            mine_keys,
+            their_keys,
+            expert_out[0],
+        ),
+        scratch=[
+            pltpu.VMEM((2 * half, model // 2), BF16),
+            pltpu.VMEM((2 * half, hidden), BF16),
+            pltpu.VMEM((kept, model // 2), F32),
+            pltpu.VMEM((kept, model), F32),
+        ],
+        flops=4 * 2 * half * hidden * model,
+        moved=4 * hidden * model,
+        limit=20,
     )
 
     levels = call(

time: 81.3 us -> 80.2 us (0.986)
  waiting for transfers between devices: 34.5 us -> 33.4 us
    ppermute x28, waiting for transfers between devices: 34.5 us -> 33.4 us  [partner(): return lax.ppermute(values, axis, [(i, i ^ mask) for i in range(count)])]
    pallas_call x11 -> x12, Pallas kernels: 12.3 us -> 12.3 us  [call(): pl.pallas_call(kernel, out_shape=outs, in_specs=in_specs, out_specs=VM if...]
  transfers between devices with their start and end apart: 28 -> 28, of which waited for: 18 -> 19; matrix products, arithmetic and copies ran while one was open for 0% -> 0% of each run, Pallas kernels for 4% -> 6%
where the time goes in v2:
time: 80.2 us; the launch traced here: 80 us
  waiting for transfers between devices  33.4 us (42%)
  starting transfers between devices  33.3 us (42%)
  Pallas kernels  12.3 us (15%)
    ppermute x28, waiting for transfers between devices, partner(): return lax.ppermute(values, axis, [(i, i ^ mask) for i in range(count)])  33.4 us
    ppermute x28, starting transfers between devices, partner(): return lax.ppermute(values, axis, [(i, i ^ mask) for i in range(count)])  33.3 us
    pallas_call x12, Pallas kernels, call(): pl.pallas_call(kernel, out_shape=outs, in_specs=in_specs, out_specs=VM if...  12.3 us
  transfers between devices with their start and end apart: 28, of which 19 were waited for; matrix products, arithmetic and copies ran while one was open for 0% of the time, Pallas kernels for 6%

profile of v2, /device:TPU:0, one launch (start us, length us, event | category | flops | bytes accessed | tf_op | source)
XLA Modules:
  0.0 80.0 jit_solution(11670099912331265481)
XLA Ops:
  0.6 1.1 %shard_map.140.refs_0_ = bf16[32,512]{1,0:T(8,128)(2,1)S(1)} custom-call(s32[1,32]{1,0:T(1,128)} %refs_0_.1, bf16[192,512]{1,0:T(8,128)(2,1)} %raw_hbm.1), custom_call_target="tpu_custom_call" | custom-call | tf_op jit(solution)/shard_map/pallas_call | solution.py:40
  1.8 5.1 %collective-permute-start.2 = (bf16[32,512]{1,0:T(8,128)(2,1)S(1)}, bf16[32,512]{1,0:T(8,128)(2,1)S(1)}, u32[]{:S(2)}, u32[]{:S(2)}) collective-permute-start(bf16[32,512]{1,0:T(8,128)(2,1)S(1)} %shard_map.140.refs_0_), channel_id=1, source_target_pairs={{0,3},{1,2},{2,1},{3,0},{4,7},{5,6},{6,5},{7,4},{8,11},{9,10},{10,... | collective-permute-start | bytes 98312 | tf_op jit(solution)/shard_map/ppermute | solution.py:65
  7.6 2.7 %shard_map.141 = (bf16[144,2048]{1,0:T(8,128)(2,1)S(1)}, f32[1,2048]{1,0:T(1,128)S(1)}, f32[1,512]{1,0:T(1,128)S(1)}, f32[1,2048]{1,0:T(1,128)S(1)}, bf16[2048,1...) custom-call(s32[1,32]{1,0:T(1,128)} %refs_0_.1, ...), custom_call_target="tpu_custom_call" | custom-call | bytes 4718592 | tf_op jit(solution)/shard_map/pallas_call | solution.py:40
  10.3 1.5 %collective-permute-done.1.refs_2_ = bf16[32,512]{1,0:T(8,128)(2,1)S(1)} collective-permute-done((bf16[32,512]{1,0:T(8,128)(2,1)S(1)}, bf16[32,512]{1,0:T(8,128)(2,1)S(1)}, u32[]{:S(2)}, u32[]{:S(2)}) %collective-permute-start.1) | collective-permute-done | bytes 32800 | tf_op jit(solution)/shard_map/ppermute | solution.py:65
  12.1 2.4 %collective-permute-start.5 = (f32[40,256]{1,0:T(8,128)S(1)}, f32[40,256]{1,0:T(8,128)S(1)}, u32[]{:S(2)}, u32[]{:S(2)}) collective-permute-start(f32[40,256]{1,0:T(8,128)S(1)} %get-tuple-element.34.refs_0_), channel_id=1, source_target_pairs={{0,3},{1,2},{2,1},{3,0},{4,7},{5,6},{6,5},{7,4},{8,11},{9,10},{10,... | collective-permute-start | bytes 122888 | tf_op jit(solution)/shard_map/ppermute | solution.py:65
  14.5 2.1 %collective-permute-start.3 = (f32[40,256]{1,0:T(8,128)S(1)}, f32[40,256]{1,0:T(8,128)S(1)}, u32[]{:S(2)}, u32[]{:S(2)}) collective-permute-start(f32[40,256]{1,0:T(8,128)S(1)} %get-tuple-element.34.refs_0_), channel_id=1, source_target_pairs={{0,1},{1,0},{2,3},{3,2},{4,5},{5,4},{6,7},{7,6},{8,9},{9,8},{10,11... | collective-permute-start | bytes 122888 | tf_op jit(solution)/shard_map/ppermute | solution.py:65
  16.6 1.1 %shard_map.143.refs_8_ = bf16[64,640]{1,0:T(8,128)(2,1)S(1)} custom-call(bf16[32,2048]{1,0:T(8,128)(2,1)S(1)} %get-tuple-element.39.normed_ref, bf16[2048,1152]{1,0:T(8,128)(2,1)S(1)} %get-tuple-element.40.weight_ref, f32[32,64]{1,0:T(8,128)S(1)} %get-tuple-element.37.cos_ref.refs_6_, f32[32,64]{1,0:T(8,128)S(1)} %get-tuple-element.38.sin_ref.refs_7_), custom_call_target="tpu_custom_call" | custom-call | flops 150994944 | bytes 4718592 | tf_op jit(solution)/shard_map/pallas_call | solution.py:40
  18.1 1.5 %collective-permute-done.4.refs_2_ = f32[40,256]{1,0:T(8,128)S(1)} collective-permute-done((f32[40,256]{1,0:T(8,128)S(1)}, f32[40,256]{1,0:T(8,128)S(1)}, u32[]{:S(2)}, u32[]{:S(2)}) %collective-permute-start.4) | collective-permute-done | bytes 40992 | tf_op jit(solution)/shard_map/ppermute | solution.py:65
  20.4 2.4 %collective-permute-start.8 = (bf16[96,640]{1,0:T(8,128)(2,1)S(1)}, bf16[96,640]{1,0:T(8,128)(2,1)S(1)}, u32[]{:S(2)}, u32[]{:S(2)}) collective-permute-start(bf16[96,640]{1,0:T(8,128)(2,1)S(1)} %get-tuple-element.41), channel_id=1, source_target_pairs={{0,24},{4,28},{8,16},{12,20},{16,8},{20,12},{24,0},{28,4},{1,25},{... | collective-permute-start | bytes 368648 | tf_op jit(solution)/shard_map/ppermute | solution.py:65
  23.9 2.5 %collective-permute-done.8 = bf16[96,640]{1,0:T(8,128)(2,1)S(1)} collective-permute-done((bf16[96,640]{1,0:T(8,128)(2,1)S(1)}, bf16[96,640]{1,0:T(8,128)(2,1)S(1)}, u32[]{:S(2)}, u32[]{:S(2)}) %collective-permute-start.8) | collective-permute-done | bytes 122912 | tf_op jit(solution)/shard_map/ppermute | solution.py:65
  26.4 1.3 %collective-permute-done.7 = bf16[96,640]{1,0:T(8,128)(2,1)S(1)} collective-permute-done((bf16[96,640]{1,0:T(8,128)(2,1)S(1)}, bf16[96,640]{1,0:T(8,128)(2,1)S(1)}, u32[]{:S(2)}, u32[]{:S(2)}) %collective-permute-start.7) | collective-permute-done | bytes 122912 | tf_op jit(solution)/shard_map/ppermute | solution.py:65
  28.4 1.9 %collective-permute-done.9.theirs_ref.theirs_tail_ref = bf16[4,96,640]{2,1,0:T(8,128)(2,1)S(1)} collective-permute-done((bf16[4,96,640]{2,1,0:T(8,128)(2,1)S(1)}, bf16[4,96,640]{2,1,0:T(8,128)(2,1)S(1)}, u32[]{:S(2)}, u32[]{:S(2)}) %collective-permute-start.9) | collective-permute-done | bytes 491552 | tf_op jit(solution)/shard_map/ppermute | solution.py:65
  30.2 2.0 %shard_map.145.refs_0_ = bf16[256,256]{1,0:T(8,128)(2,1)S(1)} custom-call(bf16[4,96,640]{2,1,0:T(8,128)(2,1)S(1)} %pad_maximum_fusion.2.mine_ref.mine_tail_ref, bf16[4,96,640]{2,1,0:T(8,128)(2,1)S(1)} %collective-permute-done.9.theirs_ref.theirs_tail_ref, bf16[1024,256]{1,0:T(8,128)(2,1)} %weight_hbm.1), custom_call_target="tpu_custom_call" | custom-call | flops 134217728 | bytes 524288 | tf_op jit(solution)/shard_map/pallas_call | solution.py:40
  32.2 2.1 %collective-permute-start.12 = (bf16[256,256]{1,0:T(8,128)(2,1)S(1)}, bf16[256,256]{1,0:T(8,128)(2,1)S(1)}, u32[]{:S(2)}, u32[]{:S(2)}) collective-permute-start(bf16[256,256]{1,0:T(8,128)(2,1)S(1)} %shard_map.145.refs_0_), channel_id=1, source_target_pairs={{0,3},{1,2},{2,1},{3,0},{4,7},{5,6},{6,5},{7,4},{8,11},{9,10},{10,... | collective-permute-start | bytes 393224 | tf_op jit(solution)/shard_map/ppermute | solution.py:65
  34.8 1.9 %collective-permute-start.10 = (bf16[256,256]{1,0:T(8,128)(2,1)S(1)}, bf16[256,256]{1,0:T(8,128)(2,1)S(1)}, u32[]{:S(2)}, u32[]{:S(2)}) collective-permute-start(bf16[256,256]{1,0:T(8,128)(2,1)S(1)} %shard_map.145.refs_0_), channel_id=1, source_target_pairs={{0,1},{1,0},{2,3},{3,2},{4,5},{5,4},{6,7},{7,6},{8,9},{9,8},{10,11... | collective-permute-start | bytes 393224 | tf_op jit(solution)/shard_map/ppermute | solution.py:65
  36.7 1.5 %collective-permute-start.19 = (bf16[32,2048]{1,0:T(8,128)(2,1)S(1)}, bf16[32,2048]{1,0:T(8,128)(2,1)S(1)}, u32[]{:S(2)}, u32[]{:S(2)}) collective-permute-start(bf16[32,2048]{1,0:T(8,128)(2,1)S(1)} %get-tuple-element.42), channel_id=1, source_target_pairs={{0,24},{4,28},{8,16},{12,20},{16,8},{20,12},{24,0},{28,4},{1,25},{... | collective-permute-start | bytes 393224 | tf_op jit(solution)/shard_map/ppermute | solution.py:65
  39.0 1.6 %collective-permute-done.12.refs_3_ = bf16[256,256]{1,0:T(8,128)(2,1)S(1)} collective-permute-done((bf16[256,256]{1,0:T(8,128)(2,1)S(1)}, bf16[256,256]{1,0:T(8,128)(2,1)S(1)}, u32[]{:S(2)}, u32[]{:S(2)}) %collective-permute-start.12) | collective-permute-done | bytes 131104 | tf_op jit(solution)/shard_map/ppermute | solution.py:65
  41.4 5.3 %collective-permute-done.11.refs_2_ = bf16[256,256]{1,0:T(8,128)(2,1)S(1)} collective-permute-done((bf16[256,256]{1,0:T(8,128)(2,1)S(1)}, bf16[256,256]{1,0:T(8,128)(2,1)S(1)}, u32[]{:S(2)}, u32[]{:S(2)}) %collective-permute-start.11) | collective-permute-done | bytes 131104 | tf_op jit(solution)/shard_map/ppermute | solution.py:65
  46.8 1.6 %collective-permute-start.15 = (bf16[256,256]{1,0:T(8,128)(2,1)S(1)}, bf16[256,256]{1,0:T(8,128)(2,1)S(1)}, u32[]{:S(2)}, u32[]{:S(2)}) collective-permute-start(bf16[256,256]{1,0:T(8,128)(2,1)S(1)} %shard_map.146), channel_id=1, source_target_pairs={{0,24},{4,28},{8,16},{12,20},{16,8},{20,12},{24,0},{28,4},{1,25},{... | collective-permute-start | bytes 393224 | tf_op jit(solution)/shard_map/ppermute | solution.py:65
  49.2 1.2 %collective-permute-start.13 = (bf16[256,256]{1,0:T(8,128)(2,1)S(1)}, bf16[256,256]{1,0:T(8,128)(2,1)S(1)}, u32[]{:S(2)}, u32[]{:S(2)}) collective-permute-start(bf16[256,256]{1,0:T(8,128)(2,1)S(1)} %shard_map.146), channel_id=1, source_target_pairs={{0,8},{4,12},{8,0},{12,4},{16,24},{20,28},{24,16},{28,20},{1,9},{5... | collective-permute-start | bytes 393224 | tf_op jit(solution)/shard_map/ppermute | solution.py:65
  50.5 3.4 %collective-permute-done.15 = bf16[256,256]{1,0:T(8,128)(2,1)S(1)} collective-permute-done((bf16[256,256]{1,0:T(8,128)(2,1)S(1)}, bf16[256,256]{1,0:T(8,128)(2,1)S(1)}, u32[]{:S(2)}, u32[]{:S(2)}) %collective-permute-start.15) | collective-permute-done | bytes 131104 | tf_op jit(solution)/shard_map/ppermute | solution.py:65
  53.9 1.3 %collective-permute-done.14 = bf16[256,256]{1,0:T(8,128)(2,1)S(1)} collective-permute-done((bf16[256,256]{1,0:T(8,128)(2,1)S(1)}, bf16[256,256]{1,0:T(8,128)(2,1)S(1)}, u32[]{:S(2)}, u32[]{:S(2)}) %collective-permute-start.14) | collective-permute-done | bytes 131104 | tf_op jit(solution)/shard_map/ppermute | solution.py:65
  57.4 2.2 %shard_map.148 = (bf16[128,2048]{1,0:T(8,128)(2,1)S(1)}, bf16[128,2048]{1,0:T(8,128)(2,1)S(1)}, f32[8,2048]{1,0:T(8,128)S(1)}) custom-call(bf16[4,256,256]{2,1,0:T(8,128)(2,1)S(1)} %collective-permute-done.16.theirs_ref, bf16[4,32,2048]{2,1,0:T(8,128)(2,1)S(1)} %pad_maximum_fusion.1.mine_rows, bf16[4,32,2048]{2,1,0:T(8,128)(2,1)S(1)} %collective-permute-done.20.their_rows, ...), custom_call_target="tpu_custom_call" | custom-call | flops 1476395008 | bytes 5767168 | tf_op jit(solution)/shard_map/pallas_call | solution.py:40
  59.7 1.8 %collective-permute-done.21.back_ref = bf16[128,2048]{1,0:T(8,128)(2,1)S(1)} collective-permute-done((bf16[128,2048]{1,0:T(8,128)(2,1)S(1)}, bf16[128,2048]{1,0:T(8,128)(2,1)S(1)}, u32[]{:S(2)}, u32[]{:S(2)}) %collective-permute-start.21) | collective-permute-done | bytes 524320 | tf_op jit(solution)/shard_map/ppermute | solution.py:65
  62.5 1.2 %collective-permute-start.23 = (bf16[32,2048]{1,0:T(8,128)(2,1)S(1)}, bf16[32,2048]{1,0:T(8,128)(2,1)S(1)}, u32[]{:S(2)}, u32[]{:S(2)}) collective-permute-start(bf16[32,2048]{1,0:T(8,128)(2,1)S(1)} %get-tuple-element.52), channel_id=1, source_target_pairs={{0,16},{4,20},{8,24},{12,28},{16,0},{20,4},{24,8},{28,12},{1,17},{... | collective-permute-start | bytes 393224 | tf_op jit(solution)/shard_map/ppermute | solution.py:65
  63.7 1.5 %collective-permute-start.24 = (bf16[32,2048]{1,0:T(8,128)(2,1)S(1)}, bf16[32,2048]{1,0:T(8,128)(2,1)S(1)}, u32[]{:S(2)}, u32[]{:S(2)}) collective-permute-start(bf16[32,2048]{1,0:T(8,128)(2,1)S(1)} %get-tuple-element.53), channel_id=1, source_target_pairs={{0,24},{4,28},{8,16},{12,20},{16,8},{20,12},{24,0},{28,4},{1,25},{... | collective-permute-start | bytes 393224 | tf_op jit(solution)/shard_map/ppermute | solution.py:65
  65.2 2.9 %collective-permute-done.22.refs_1_ = bf16[32,2048]{1,0:T(8,128)(2,1)S(1)} collective-permute-done((bf16[32,2048]{1,0:T(8,128)(2,1)S(1)}, bf16[32,2048]{1,0:T(8,128)(2,1)S(1)}, u32[]{:S(2)}, u32[]{:S(2)}) %collective-permute-start.22) | collective-permute-done | bytes 131104 | tf_op jit(solution)/shard_map/ppermute | solution.py:65
  68.6 2.0 %collective-permute-done.24.refs_3_ = bf16[32,2048]{1,0:T(8,128)(2,1)S(1)} collective-permute-done((bf16[32,2048]{1,0:T(8,128)(2,1)S(1)}, bf16[32,2048]{1,0:T(8,128)(2,1)S(1)}, u32[]{:S(2)}, u32[]{:S(2)}) %collective-permute-start.24) | collective-permute-done | bytes 131104 | tf_op jit(solution)/shard_map/ppermute | solution.py:65
  71.3 2.2 %collective-permute-start.26 = (bf16[8,2048]{1,0:T(8,128)(2,1)S(1)}, bf16[8,2048]{1,0:T(8,128)(2,1)S(1)}, u32[]{:S(2)}, u32[]{:S(2)}) collective-permute-start(bf16[8,2048]{1,0:T(8,128)(2,1)S(1)} %get-tuple-element.56), channel_id=1, source_target_pairs={{0,2},{1,3},{2,0},{3,1},{4,6},{5,7},{6,4},{7,5},{8,10},{9,11},{10,... | collective-permute-start | bytes 98312 | tf_op jit(solution)/shard_map/ppermute | solution.py:65
  73.6 1.5 %collective-permute-start.27 = (bf16[8,2048]{1,0:T(8,128)(2,1)S(1)}, bf16[8,2048]{1,0:T(8,128)(2,1)S(1)}, u32[]{:S(2)}, u32[]{:S(2)}) collective-permute-start(bf16[8,2048]{1,0:T(8,128)(2,1)S(1)} %get-tuple-element.57), channel_id=1, source_target_pairs={{0,3},{1,2},{2,1},{3,0},{4,7},{5,6},{6,5},{7,4},{8,11},{9,10},{10,... | collective-permute-start | bytes 98312 | tf_op jit(solution)/shard_map/ppermute | solution.py:65
  75.1 1.1 %collective-permute-done.26.refs_2_ = bf16[8,2048]{1,0:T(8,128)(2,1)S(1)} collective-permute-done((bf16[8,2048]{1,0:T(8,128)(2,1)S(1)}, bf16[8,2048]{1,0:T(8,128)(2,1)S(1)}, u32[]{:S(2)}, u32[]{:S(2)}) %collective-permute-start.26) | collective-permute-done | bytes 32800 | tf_op jit(solution)/shard_map/ppermute | solution.py:65
  76.2 3.1 %collective-permute-done.27.refs_3_ = bf16[8,2048]{1,0:T(8,128)(2,1)S(1)} collective-permute-done((bf16[8,2048]{1,0:T(8,128)(2,1)S(1)}, bf16[8,2048]{1,0:T(8,128)(2,1)S(1)}, u32[]{:S(2)}, u32[]{:S(2)}) %collective-permute-start.27) | collective-permute-done | bytes 32800 | tf_op jit(solution)/shard_map/ppermute | solution.py:65
  (46 shorter events, 12.3 us)
Async XLA Ops:
  1.8 8.5 %collective-permute-start.2 = (bf16[32,512]{1,0:T(8,128)(2,1)S(1)}, bf16[32,512]{1,0:T(8,128)(2,1)S(1)}, u32[]{:S(2)}, u32[]{:S(2)}) collective-permute-start(bf16[32,512]{1,0:T(8,128)(2,1)S(1)} %shard_map.140.refs_0_), channel_id=1, source_target_pairs={{0,3},{1,2},{2,1},{3,0},{4,7},{5,6},{6,5},{7,4},{8,11},{9,10},{10,... | collective-permute-start | bytes 98312 | tf_op jit(solution)/shard_map/ppermute | solution.py:65
  6.9 4.8 %collective-permute-start.1 = (bf16[32,512]{1,0:T(8,128)(2,1)S(1)}, bf16[32,512]{1,0:T(8,128)(2,1)S(1)}, u32[]{:S(2)}, u32[]{:S(2)}) collective-permute-start(bf16[32,512]{1,0:T(8,128)(2,1)S(1)} %shard_map.140.refs_0_), channel_id=1, source_target_pairs={{0,2},{1,3},{2,0},{3,1},{4,6},{5,7},{6,4},{7,5},{8,10},{9,11},{10,... | collective-permute-start | bytes 98312 | tf_op jit(solution)/shard_map/ppermute | solution.py:65
  6.9 4.8 %collective-permute-start = (bf16[32,512]{1,0:T(8,128)(2,1)S(1)}, bf16[32,512]{1,0:T(8,128)(2,1)S(1)}, u32[]{:S(2)}, u32[]{:S(2)}) collective-permute-start(bf16[32,512]{1,0:T(8,128)(2,1)S(1)} %shard_map.140.refs_0_), channel_id=1, source_target_pairs={{0,1},{1,0},{2,3},{3,2},{4,5},{5,4},{6,7},{7,6},{8,9},{9,8},{10,11... | collective-permute-start | bytes 98312 | tf_op jit(solution)/shard_map/ppermute | solution.py:65
  11.7 43.8 %slice-start = ((s8[5767168]{0:T(1024)(128)(4,1)}), s8[4194304]{0:T(1024)(128)(4,1)S(1)}, s32[]{:S(2)}) async-start(s8[5767168]{0:T(1024)(128)(4,1)} %bitcast.20), calls=%async_computation | async-start | bytes 8388608
  12.1 5.9 %collective-permute-start.5 = (f32[40,256]{1,0:T(8,128)S(1)}, f32[40,256]{1,0:T(8,128)S(1)}, u32[]{:S(2)}, u32[]{:S(2)}) collective-permute-start(f32[40,256]{1,0:T(8,128)S(1)} %get-tuple-element.34.refs_0_), channel_id=1, source_target_pairs={{0,3},{1,2},{2,1},{3,0},{4,7},{5,6},{6,5},{7,4},{8,11},{9,10},{10,... | collective-permute-start | bytes 122888 | tf_op jit(solution)/shard_map/ppermute | solution.py:65
  14.5 5.0 %collective-permute-start.4 = (f32[40,256]{1,0:T(8,128)S(1)}, f32[40,256]{1,0:T(8,128)S(1)}, u32[]{:S(2)}, u32[]{:S(2)}) collective-permute-start(f32[40,256]{1,0:T(8,128)S(1)} %get-tuple-element.34.refs_0_), channel_id=1, source_target_pairs={{0,2},{1,3},{2,0},{3,1},{4,6},{5,7},{6,4},{7,5},{8,10},{9,11},{10,... | collective-permute-start | bytes 122888 | tf_op jit(solution)/shard_map/ppermute | solution.py:65
  14.5 5.0 %collective-permute-start.3 = (f32[40,256]{1,0:T(8,128)S(1)}, f32[40,256]{1,0:T(8,128)S(1)}, u32[]{:S(2)}, u32[]{:S(2)}) collective-permute-start(f32[40,256]{1,0:T(8,128)S(1)} %get-tuple-element.34.refs_0_), channel_id=1, source_target_pairs={{0,1},{1,0},{2,3},{3,2},{4,5},{5,4},{6,7},{7,6},{8,9},{9,8},{10,11... | collective-permute-start | bytes 122888 | tf_op jit(solution)/shard_map/ppermute | solution.py:65
  16.6 39.0 %slice-start.1 = ((s8[5767168]{0:T(1024)(128)(4,1)}), s8[1572864]{0:T(1024)(128)(4,1)S(1)}, s32[]{:S(2)}) async-start(s8[5767168]{0:T(1024)(128)(4,1)} %bitcast.20), calls=%async_computation.1 | async-start | bytes 3145728
  20.4 6.0 %collective-permute-start.8 = (bf16[96,640]{1,0:T(8,128)(2,1)S(1)}, bf16[96,640]{1,0:T(8,128)(2,1)S(1)}, u32[]{:S(2)}, u32[]{:S(2)}) collective-permute-start(bf16[96,640]{1,0:T(8,128)(2,1)S(1)} %get-tuple-element.41), channel_id=1, source_target_pairs={{0,24},{4,28},{8,16},{12,20},{16,8},{20,12},{24,0},{28,4},{1,25},{... | collective-permute-start | bytes 368648 | tf_op jit(solution)/shard_map/ppermute | solution.py:65
  22.8 4.9 %collective-permute-start.7 = (bf16[96,640]{1,0:T(8,128)(2,1)S(1)}, bf16[96,640]{1,0:T(8,128)(2,1)S(1)}, u32[]{:S(2)}, u32[]{:S(2)}) collective-permute-start(bf16[96,640]{1,0:T(8,128)(2,1)S(1)} %get-tuple-element.41), channel_id=1, source_target_pairs={{0,16},{4,20},{8,24},{12,28},{16,0},{20,4},{24,8},{28,12},{1,17},{... | collective-permute-start | bytes 368648 | tf_op jit(solution)/shard_map/ppermute | solution.py:65
  23.3 4.9 %collective-permute-start.6 = (bf16[96,640]{1,0:T(8,128)(2,1)S(1)}, bf16[96,640]{1,0:T(8,128)(2,1)S(1)}, u32[]{:S(2)}, u32[]{:S(2)}) collective-permute-start(bf16[96,640]{1,0:T(8,128)(2,1)S(1)} %get-tuple-element.41), channel_id=1, source_target_pairs={{0,8},{4,12},{8,0},{12,4},{16,24},{20,28},{24,16},{28,20},{1,9},{5... | collective-permute-start | bytes 368648 | tf_op jit(solution)/shard_map/ppermute | solution.py:65
  28.3 1.9 %collective-permute-start.9 = (bf16[4,96,640]{2,1,0:T(8,128)(2,1)S(1)}, bf16[4,96,640]{2,1,0:T(8,128)(2,1)S(1)}, u32[]{:S(2)}, u32[]{:S(2)}) collective-permute-start(bf16[4,96,640]{2,1,0:T(8,128)(2,1)S(1)} %pad_maximum_fusion.2.mine_ref.mine_tail_ref), channel_id=1, source_target_pairs={{0,4},{4,0},{8,12},{12,8},{16,20},{20,16},{24,28},{28,24},{1,5},{5... | collective-permute-start | bytes 1474568 | tf_op jit(solution)/shard_map/ppermute | solution.py:65
  32.2 8.4 %collective-permute-start.12 = (bf16[256,256]{1,0:T(8,128)(2,1)S(1)}, bf16[256,256]{1,0:T(8,128)(2,1)S(1)}, u32[]{:S(2)}, u32[]{:S(2)}) collective-permute-start(bf16[256,256]{1,0:T(8,128)(2,1)S(1)} %shard_map.145.refs_0_), channel_id=1, source_target_pairs={{0,3},{1,2},{2,1},{3,0},{4,7},{5,6},{6,5},{7,4},{8,11},{9,10},{10,... | collective-permute-start | bytes 393224 | tf_op jit(solution)/shard_map/ppermute | solution.py:65
  34.3 12.4 %collective-permute-start.11 = (bf16[256,256]{1,0:T(8,128)(2,1)S(1)}, bf16[256,256]{1,0:T(8,128)(2,1)S(1)}, u32[]{:S(2)}, u32[]{:S(2)}) collective-permute-start(bf16[256,256]{1,0:T(8,128)(2,1)S(1)} %shard_map.145.refs_0_), channel_id=1, source_target_pairs={{0,2},{1,3},{2,0},{3,1},{4,6},{5,7},{6,4},{7,5},{8,10},{9,11},{10,... | collective-permute-start | bytes 393224 | tf_op jit(solution)/shard_map/ppermute | solution.py:65
  34.8 11.9 %collective-permute-start.10 = (bf16[256,256]{1,0:T(8,128)(2,1)S(1)}, bf16[256,256]{1,0:T(8,128)(2,1)S(1)}, u32[]{:S(2)}, u32[]{:S(2)}) collective-permute-start(bf16[256,256]{1,0:T(8,128)(2,1)S(1)} %shard_map.145.refs_0_), channel_id=1, source_target_pairs={{0,1},{1,0},{2,3},{3,2},{4,5},{5,4},{6,7},{7,6},{8,9},{9,8},{10,11... | collective-permute-start | bytes 393224 | tf_op jit(solution)/shard_map/ppermute | solution.py:65
  36.7 12.5 %collective-permute-start.19 = (bf16[32,2048]{1,0:T(8,128)(2,1)S(1)}, bf16[32,2048]{1,0:T(8,128)(2,1)S(1)}, u32[]{:S(2)}, u32[]{:S(2)}) collective-permute-start(bf16[32,2048]{1,0:T(8,128)(2,1)S(1)} %get-tuple-element.42), channel_id=1, source_target_pairs={{0,24},{4,28},{8,16},{12,20},{16,8},{20,12},{24,0},{28,4},{1,25},{... | collective-permute-start | bytes 393224 | tf_op jit(solution)/shard_map/ppermute | solution.py:65
  38.2 12.2 %collective-permute-start.18 = (bf16[32,2048]{1,0:T(8,128)(2,1)S(1)}, bf16[32,2048]{1,0:T(8,128)(2,1)S(1)}, u32[]{:S(2)}, u32[]{:S(2)}) collective-permute-start(bf16[32,2048]{1,0:T(8,128)(2,1)S(1)} %get-tuple-element.42), channel_id=1, source_target_pairs={{0,16},{4,20},{8,24},{12,28},{16,0},{20,4},{24,8},{28,12},{1,17},{... | collective-permute-start | bytes 393224 | tf_op jit(solution)/shard_map/ppermute | solution.py:65
  40.6 9.8 %collective-permute-start.17 = (bf16[32,2048]{1,0:T(8,128)(2,1)S(1)}, bf16[32,2048]{1,0:T(8,128)(2,1)S(1)}, u32[]{:S(2)}, u32[]{:S(2)}) collective-permute-start(bf16[32,2048]{1,0:T(8,128)(2,1)S(1)} %get-tuple-element.42), channel_id=1, source_target_pairs={{0,8},{4,12},{8,0},{12,4},{16,24},{20,28},{24,16},{28,20},{1,9},{5... | collective-permute-start | bytes 393224 | tf_op jit(solution)/shard_map/ppermute | solution.py:65
  46.8 7.2 %collective-permute-start.15 = (bf16[256,256]{1,0:T(8,128)(2,1)S(1)}, bf16[256,256]{1,0:T(8,128)(2,1)S(1)}, u32[]{:S(2)}, u32[]{:S(2)}) collective-permute-start(bf16[256,256]{1,0:T(8,128)(2,1)S(1)} %shard_map.146), channel_id=1, source_target_pairs={{0,24},{4,28},{8,16},{12,20},{16,8},{20,12},{24,0},{28,4},{1,25},{... | collective-permute-start | bytes 393224 | tf_op jit(solution)/shard_map/ppermute | solution.py:65
  48.4 6.9 %collective-permute-start.14 = (bf16[256,256]{1,0:T(8,128)(2,1)S(1)}, bf16[256,256]{1,0:T(8,128)(2,1)S(1)}, u32[]{:S(2)}, u32[]{:S(2)}) collective-permute-start(bf16[256,256]{1,0:T(8,128)(2,1)S(1)} %shard_map.146), channel_id=1, source_target_pairs={{0,16},{4,20},{8,24},{12,28},{16,0},{20,4},{24,8},{28,12},{1,17},{... | collective-permute-start | bytes 393224 | tf_op jit(solution)/shard_map/ppermute | solution.py:65
  49.2 6.2 %collective-permute-start.13 = (bf16[256,256]{1,0:T(8,128)(2,1)S(1)}, bf16[256,256]{1,0:T(8,128)(2,1)S(1)}, u32[]{:S(2)}, u32[]{:S(2)}) collective-permute-start(bf16[256,256]{1,0:T(8,128)(2,1)S(1)} %shard_map.146), channel_id=1, source_target_pairs={{0,8},{4,12},{8,0},{12,4},{16,24},{20,28},{24,16},{28,20},{1,9},{5... | collective-permute-start | bytes 393224 | tf_op jit(solution)/shard_map/ppermute | solution.py:65
  50.4 7.0 %copy-start = (bf16[1,704,2048]{2,1,0:T(8,128)(2,1)S(1)}, bf16[1,704,2048]{2,1,0:T(8,128)(2,1)}, u32[]{:S(2)}) copy-start(bf16[1,704,2048]{2,1,0:T(8,128)(2,1)} %param.25) | copy-start | bytes 8650756
  50.4 5.1 %collective-permute-start.20 = (bf16[4,32,2048]{2,1,0:T(8,128)(2,1)S(1)}, bf16[4,32,2048]{2,1,0:T(8,128)(2,1)S(1)}, u32[]{:S(2)}, u32[]{:S(2)}) collective-permute-start(bf16[4,32,2048]{2,1,0:T(8,128)(2,1)S(1)} %pad_maximum_fusion.1.mine_rows), channel_id=1, source_target_pairs={{0,4},{4,0},{8,12},{12,8},{16,20},{20,16},{24,28},{28,24},{1,5},{5... | collective-permute-start | bytes 1572872 | tf_op jit(solution)/shard_map/ppermute | solution.py:65
  55.4 2.0 %collective-permute-start.16 = (bf16[4,256,256]{2,1,0:T(8,128)(2,1)S(1)}, bf16[4,256,256]{2,1,0:T(8,128)(2,1)S(1)}, u32[]{:S(2)}, u32[]{:S(2)}) collective-permute-start(bf16[4,256,256]{2,1,0:T(8,128)(2,1)S(1)} %pad_maximum_fusion.mine_ref), channel_id=1, source_target_pairs={{0,4},{4,0},{8,12},{12,8},{16,20},{20,16},{24,28},{28,24},{1,5},{5... | collective-permute-start | bytes 1572872 | tf_op jit(solution)/shard_map/ppermute | solution.py:65
  59.6 2.0 %collective-permute-start.21 = (bf16[128,2048]{1,0:T(8,128)(2,1)S(1)}, bf16[128,2048]{1,0:T(8,128)(2,1)S(1)}, u32[]{:S(2)}, u32[]{:S(2)}) collective-permute-start(bf16[128,2048]{1,0:T(8,128)(2,1)S(1)} %get-tuple-element.49), channel_id=1, source_target_pairs={{0,4},{4,0},{8,12},{12,8},{16,20},{20,16},{24,28},{28,24},{1,5},{5... | collective-permute-start | bytes 1572872 | tf_op jit(solution)/shard_map/ppermute | solution.py:65
  61.7 6.4 %collective-permute-start.22 = (bf16[32,2048]{1,0:T(8,128)(2,1)S(1)}, bf16[32,2048]{1,0:T(8,128)(2,1)S(1)}, u32[]{:S(2)}, u32[]{:S(2)}) collective-permute-start(bf16[32,2048]{1,0:T(8,128)(2,1)S(1)} %get-tuple-element.51), channel_id=1, source_target_pairs={{0,8},{4,12},{8,0},{12,4},{16,24},{20,28},{24,16},{28,20},{1,9},{5... | collective-permute-start | bytes 393224 | tf_op jit(solution)/shard_map/ppermute | solution.py:65
  62.5 6.1 %collective-permute-start.23 = (bf16[32,2048]{1,0:T(8,128)(2,1)S(1)}, bf16[32,2048]{1,0:T(8,128)(2,1)S(1)}, u32[]{:S(2)}, u32[]{:S(2)}) collective-permute-start(bf16[32,2048]{1,0:T(8,128)(2,1)S(1)} %get-tuple-element.52), channel_id=1, source_target_pairs={{0,16},{4,20},{8,24},{12,28},{16,0},{20,4},{24,8},{28,12},{1,17},{... | collective-permute-start | bytes 393224 | tf_op jit(solution)/shard_map/ppermute | solution.py:65
  63.7 6.9 %collective-permute-start.24 = (bf16[32,2048]{1,0:T(8,128)(2,1)S(1)}, bf16[32,2048]{1,0:T(8,128)(2,1)S(1)}, u32[]{:S(2)}, u32[]{:S(2)}) collective-permute-start(bf16[32,2048]{1,0:T(8,128)(2,1)S(1)} %get-tuple-element.53), channel_id=1, source_target_pairs={{0,24},{4,28},{8,16},{12,20},{16,8},{20,12},{24,0},{28,4},{1,25},{... | collective-permute-start | bytes 393224 | tf_op jit(solution)/shard_map/ppermute | solution.py:65
  70.6 4.5 %collective-permute-start.25 = (bf16[8,2048]{1,0:T(8,128)(2,1)S(1)}, bf16[8,2048]{1,0:T(8,128)(2,1)S(1)}, u32[]{:S(2)}, u32[]{:S(2)}) collective-permute-start(bf16[8,2048]{1,0:T(8,128)(2,1)S(1)} %get-tuple-element.55), channel_id=1, source_target_pairs={{0,1},{1,0},{2,3},{3,2},{4,5},{5,4},{6,7},{7,6},{8,9},{9,8},{10,11... | collective-permute-start | bytes 98312 | tf_op jit(solution)/shard_map/ppermute | solution.py:65
  71.3 4.8 %collective-permute-start.26 = (bf16[8,2048]{1,0:T(8,128)(2,1)S(1)}, bf16[8,2048]{1,0:T(8,128)(2,1)S(1)}, u32[]{:S(2)}, u32[]{:S(2)}) collective-permute-start(bf16[8,2048]{1,0:T(8,128)(2,1)S(1)} %get-tuple-element.56), channel_id=1, source_target_pairs={{0,2},{1,3},{2,0},{3,1},{4,6},{5,7},{6,4},{7,5},{8,10},{9,11},{10,... | collective-permute-start | bytes 98312 | tf_op jit(solution)/shard_map/ppermute | solution.py:65
  73.6 5.7 %collective-permute-start.27 = (bf16[8,2048]{1,0:T(8,128)(2,1)S(1)}, bf16[8,2048]{1,0:T(8,128)(2,1)S(1)}, u32[]{:S(2)}, u32[]{:S(2)}) collective-permute-start(bf16[8,2048]{1,0:T(8,128)(2,1)S(1)} %get-tuple-element.57), channel_id=1, source_target_pairs={{0,3},{1,2},{2,1},{3,0},{4,7},{5,6},{6,5},{7,4},{8,11},{9,10},{10,... | collective-permute-start | bytes 98312 | tf_op jit(solution)/shard_map/ppermute | solution.py:65

commit v3 on v2

--- a/solution.py
+++ b/solution.py
@@ -21,6 +21,7 @@
 
 VM = pl.BlockSpec(memory_space=pltpu.VMEM)
 HBM = pl.BlockSpec(memory_space=pltpu.HBM)
+ANY = pl.BlockSpec(memory_space=pl.ANY)
 
 
 def up(count, unit=LANES):
@@ -177,7 +178,7 @@
 
 def cache_kernel(spans, width, experts, *refs):
     parts = refs[:spans]
-    live_ref, gain_ref, cos_ref, sin_ref, query_ref, cached_ref, sent_ref = refs[spans:]
+    live_ref, gain_ref, cos_ref, sin_ref, query_ref, sent_ref = refs[spans:]
     rows = live_ref.shape[0]
     kv_rank = gain_ref.shape[1]
     values = natural([p[...] for p in parts], here()[1])
@@ -187,8 +188,6 @@
     factor = lax.rsqrt(jnp.mean(nope * nope, axis=1, keepdims=True) + EPS)
     nope = nope * factor * gain_ref[...]
     rope = rotated(latent[:, kv_rank:], cos_ref[...], sin_ref[...])
-    cached_ref[:, :kv_rank] = nope.astype(BF16)
-    cached_ref[:, kv_rank:] = rope.astype(BF16)
     high = gates.astype(BF16).astype(F32)
     used = rope.shape[1] + 2 * experts + 1
     tail = [rope, high, gates - high, live_ref[...]]
@@ -200,26 +199,22 @@
     sent_ref[rows:, :] = query_ref[...]
 
 
-def places(blocks):
-    return list(range(0, blocks, 2)) + list(range(1, blocks, 2))
+def emit_kernel(sent_ref, out_ref):
+    out_ref[...] = sent_ref[: out_ref.shape[0], : out_ref.shape[1]]
 
 
 def attend_kernel(
-    heads, kv_rank, flag_lane, blocks, mine_ref, theirs_ref, weight_hbm, out_ref, weight_ref, sem
+    heads, kv_rank, flag_lane, mine_ref, theirs_ref, weight_hbm, other_hbm, out_ref, buf, sem
 ):
-    copy = pltpu.make_async_copy(weight_hbm, weight_ref, sem)
-    copy.start()
-    count = mine_ref.shape[1] // (1 + heads)
+    copies = fetch([(weight_hbm, buf.at[0]), (other_hbm, buf.at[1])], sem)
+    pieces = mine_ref.shape[0]
+    count = theirs_ref.shape[1]
     index = here()[0]
-    half = blocks // 2
-    pieces = [(mine_ref, n) for n in range(half)] + [(theirs_ref, n) for n in range(half)]
-
-    def gather(n):
-        return jnp.concatenate(
-            [ref[p, n * count : (n + 1) * count, :] for ref, p in pieces], axis=0
-        )
-
-    keys = gather(0)
+
+    def gather(ref, n):
+        return [ref[p, n * count : (n + 1) * count, :] for p in range(pieces)]
+
+    keys = jnp.concatenate(gather(mine_ref, 0) + gather(theirs_ref, 0), axis=0)
     total, width = keys.shape
     lane = lax.broadcasted_iota(jnp.int32, (8, width), 1)
     flags = nt(jnp.where(lane == flag_lane, 1.0, 0.0).astype(BF16), keys)[0:1, :]
@@ -227,157 +222,87 @@
     def slot(dims, axis):
         line = lax.broadcasted_iota(jnp.int32, dims, axis)
         at = line // count
-        which = jnp.where(at < half, 2 * at, 2 * (at - half) + 1)
+        which = jnp.where(at < pieces, 2 * at, 2 * (at - pieces) + 1)
         return (which ^ index) * count + line % count
 
-    allowed = (slot((1, total), 1) <= slot((total, 1), 0)) & (flags > 0)
-    result = jnp.zeros(out_ref.shape, F32)
+    allowed = (slot((1, total), 1) <= slot((pieces * count, 1), 0)) & (flags > 0)
+    results = [0.0, 0.0]
     for h in range(heads):
-        scores = nt(gather(1 + h), keys) * SCALE
+        scores = nt(jnp.concatenate(gather(mine_ref, 1 + h), axis=0), keys) * SCALE
         scores = jnp.where(allowed, scores, NEGATIVE)
         highest = jnp.max(scores, axis=1, keepdims=True)
         weight = jnp.where(allowed, jnp.exp(scores - highest), 0.0)
         denominator = jnp.sum(weight, axis=1, keepdims=True)
         summed = nn(weight.astype(BF16), keys[:, :kv_rank])
         mixed = (summed / denominator).astype(BF16)
-        if h == 0:
-            copy.wait()
-        result = result + nn(mixed, weight_ref[h * kv_rank : (h + 1) * kv_rank, :])
-    out_ref[...] = result.astype(BF16)
+        for n in range(2):
+            if h == 0:
+                copies[n].wait()
+            results[n] = results[n] + nn(mixed, buf[n, h * kv_rank : (h + 1) * kv_rank, :])
+    block = buf.shape[2]
+    for n in range(2):
+        lanes = pl.ds(pl.multiple_of(((index ^ n) & 1) * block, block), block)
+        out_ref[:, lanes] = results[n].astype(BF16)
 
 
 def sum_kernel(*refs):
     refs[-1][...] = sum(ref[...].astype(F32) for ref in refs[:-1]).astype(BF16)
 
 
-def scaled_rows(blocks, odd, pieces_ref, mine_rows, their_rows, gain_ref, part_ref, rows_ref):
-    order = places(blocks)
-    half = blocks // 2
-    index = here()[0]
-    count, width = mine_rows.shape[1], pieces_ref.shape[2]
-    squares = [jnp.zeros((count, 1), F32)] * blocks
-    for p in range(half):
-        i = 2 * p + odd
-        lanes = pl.ds(pl.multiple_of((index ^ i) * width, width), width)
-        gain = gain_ref[:, lanes]
-        for at, j in enumerate(order):
-            to = order.index(i ^ j)
-            rows = mine_rows if to < half else their_rows
-            resid = rows[to % half, :, lanes].astype(F32) + pieces_ref[
-                p, at * count : (at + 1) * count, :
-            ].astype(F32)
-            squares[to] = squares[to] + jnp.sum(resid * resid, axis=1, keepdims=True)
-            rows_ref[to * count : (to + 1) * count, p * width : (p + 1) * width] = (
-                resid * gain
-            ).astype(BF16)
-            if to == 0:
-                part_ref[:, p * width : (p + 1) * width] = resid
-    return jnp.concatenate(squares, axis=0)
-
-
-def products(blocks, odd, width, rows_ref, in_ref, half, start, size):
-    index = here()[0]
-    total = jnp.zeros((rows_ref.shape[0], size), F32)
-    for p in range(blocks // 2):
-        lanes = pl.ds(pl.multiple_of((index ^ (2 * p + odd)) * width, width), width)
-        total = total + nt(
-            rows_ref[:, p * width : (p + 1) * width], in_ref[half, start : start + size, lanes]
-        )
-    return total
-
-
-def begin_kernel(
-    blocks,
-    cuts,
-    mine_ref,
-    mine_rows,
-    their_rows,
-    gain_ref,
-    in_ref,
-    part_ref,
-    square_ref,
-    gate_ref,
-    upper_ref,
-    rows_ref,
-):
-    square_ref[...] = scaled_rows(
-        blocks, 0, mine_ref, mine_rows, their_rows, gain_ref, part_ref, rows_ref
-    )
-    width = mine_ref.shape[2]
-    for start, size in cuts:
-        at = slice(start, start + size)
-        gate_ref[:, at] = products(blocks, 0, width, rows_ref, in_ref, 0, start, size)
-        upper_ref[:, at] = products(blocks, 0, width, rows_ref, in_ref, 1, start, size)
+def resid_kernel(pieces_ref, rows_ref, gain_ref, out_ref, own_ref, buf):
+    pieces, count = rows_ref.shape[:2]
+    width = pieces_ref.shape[2]
+    index = here()
+    for p in range(pieces):
+        place = lax.div(index[0] ^ (2 * p), 2)
+        lanes = pl.ds(pl.multiple_of(place * width, width), width)
+        for at in range(pieces):
+            to = p ^ at
+            buf[to * count : (to + 1) * count, lanes] = rows_ref[to, :, lanes].astype(
+                F32
+            ) + pieces_ref[p, at * count : (at + 1) * count, :].astype(F32)
+    for n in range(pieces):
+        at = slice(n * count, (n + 1) * count)
+        resid = buf[at, :]
+        factor = lax.rsqrt(jnp.mean(resid * resid, axis=1, keepdims=True) + EPS)
+        out_ref[at, :] = (resid * factor * gain_ref[...]).astype(BF16)
+    size = own_ref.shape[0]
+    own_ref[...] = buf[pl.ds(pl.multiple_of(index[1] * size, size), size), :]
 
 
 def expert_kernel(
-    blocks,
     first_lane,
     tail_at,
     experts,
     cuts,
     columns,
-    theirs_ref,
-    mine_rows,
-    their_rows,
-    gain_ref,
+    rows_ref,
+    tail_ref,
     in_ref,
-    part_ref,
-    square_ref,
-    gate_ref,
-    upper_ref,
-    mine_tail_ref,
-    theirs_tail_ref,
     out_weight_ref,
-    near_ref,
-    far_ref,
-    own_ref,
-    rows_ref,
+    out_ref,
     act_ref,
-    rest_ref,
-    whole_ref,
 ):
-    square = square_ref[...] + scaled_rows(
-        blocks, 1, theirs_ref, mine_rows, their_rows, gain_ref, rest_ref, rows_ref
-    )
-    index = here()
-    width = theirs_ref.shape[2]
-    for p in range(blocks // 2):
-        for odd, ref in enumerate((part_ref, rest_ref)):
-            lanes = pl.ds(pl.multiple_of((index[0] ^ (2 * p + odd)) * width, width), width)
-            whole_ref[:, lanes] = ref[:, p * width : (p + 1) * width]
-    size = own_ref.shape[0]
-    own_ref[...] = whole_ref[pl.ds(pl.multiple_of(index[1] * size, size), size), :]
-    factor = lax.rsqrt(square / (blocks * width) + EPS)
-    for start, size in cuts:
-        at = slice(start, start + size)
-        gate = factor * (
-            gate_ref[:, at] + products(blocks, 1, width, rows_ref, in_ref, 0, start, size)
-        )
-        upper = factor * (
-            upper_ref[:, at] + products(blocks, 1, width, rows_ref, in_ref, 1, start, size)
-        )
-        act_ref[:, at] = (gate / (1.0 + jnp.exp(-gate)) * upper).astype(BF16)
-    half = near_ref.shape[0]
-    pieces = mine_tail_ref.shape[0]
-    count = half // pieces
-    tail = jnp.concatenate(
-        [ref[p, :count, tail_at:] for ref in (mine_tail_ref, theirs_tail_ref) for p in range(pieces)],
-        axis=0,
-    )
+    rows = rows_ref[...]
+    pieces = tail_ref.shape[0]
+    count = rows.shape[0] // pieces
+    tail = jnp.concatenate([tail_ref[p, :count, tail_at:] for p in range(pieces)], axis=0)
     tail = tail.astype(F32)
     lane = lax.broadcasted_iota(jnp.int32, tail.shape, 1) - first_lane
+    index = here()
     slot = lax.div(index[0] * lax.axis_size("span") + index[1], 2)
     scale = jnp.sum(
         jnp.where((lane == slot) | (lane == slot + experts), tail, 0.0), axis=1, keepdims=True
     )
+    for start, size in cuts:
+        gate = nt(rows, in_ref[0, start : start + size, :])
+        upper = nt(rows, in_ref[1, start : start + size, :])
+        act_ref[:, start : start + size] = (gate / (1.0 + jnp.exp(-gate)) * upper).astype(BF16)
     wide = out_weight_ref.shape[1] // columns
     for n in range(columns):
         span = slice(n * wide, (n + 1) * wide)
         done = nn(act_ref[...], out_weight_ref[:, span])
-        done = jnp.where(scale > 0, done * scale, 0.0).astype(BF16)
-        near_ref[:, span] = done[:half]
-        far_ref[:, span] = done[half:]
+        out_ref[:, span] = jnp.where(scale > 0, done * scale, 0.0).astype(BF16)
 
 
 def level_kernel(near_ref, back_ref, *outs):
@@ -453,6 +378,7 @@
         limit=4,
     )
     parts = gathered(picked, "span", range(1, spans))
+    other_weight = partner(out_weight, "context", 1)
 
     sent_width = up(max(part_width, experts))
     moved = (latent_weight.T, attn_gain[None], kv_gain[None], moe_gain[None], query_weight)
@@ -502,24 +428,27 @@
         moved=2 * query_weight.size,
         limit=10,
     )
-    cached, sent = call(
+    sent = call(
         functools.partial(cache_kernel, spans, part_width, experts),
-        [shape((kept, latent_width), BF16), shape(((1 + heads) * kept, row_width), BF16)],
+        shape(((1 + heads) * kept, row_width), BF16),
         [VM] * (spans + 5),
         (*parts, live, near_kv, cosine, sine, query),
         limit=4,
     )
-
-    mine_keys = jnp.stack(gathered(sent, "context", evens[1:]))
-    their_keys = partner(mine_keys, "context", 1)
+    cached = call(emit_kernel, shape((kept, latent_width), BF16), [VM], (sent,), limit=4)
+
+    mine_keys = gathered(sent, "context", evens[1:])
+    their_keys = partner(jnp.stack([part[:kept] for part in mine_keys]), "context", 1)
+    mine_keys = jnp.stack(mine_keys)
+    half = mine_keys.shape[0] * kept
     partial = call(
-        functools.partial(attend_kernel, heads, kv_rank, latent_width + 2 * experts, contexts),
-        shape((contexts * kept, out_weight.shape[1]), BF16),
-        [VM, VM, HBM],
-        (mine_keys, their_keys, out_weight),
-        scratch=[pltpu.VMEM(out_weight.shape, BF16), pltpu.SemaphoreType.DMA],
+        functools.partial(attend_kernel, heads, kv_rank, latent_width + 2 * experts),
+        shape((half, 2 * out_weight.shape[1]), BF16),
+        [VM, VM, HBM, ANY],
+        (mine_keys, their_keys, out_weight, other_weight),
+        scratch=[pltpu.VMEM((2, *out_weight.shape), BF16), pltpu.SemaphoreType.DMA((2,))],
         flops=2 * kept * contexts * out_weight.size,
-        moved=2 * out_weight.size,
+        moved=4 * out_weight.size,
         limit=12,
     )
 
@@ -531,59 +460,38 @@
         limit=4,
     )
     mine_rows = jnp.stack(gathered(compact, "context", evens[1:]))
-    their_rows = partner(mine_rows, "context", 1)
-
-    mine = jnp.stack(gathered(column, "context", evens[1:]))
-    theirs = partner(mine, "context", 1)
-    half = mine.shape[0] * kept
+
+    pieces = jnp.stack(gathered(column, "context", evens[1:]))
+    moe_in, own = call(
+        resid_kernel,
+        [shape((half, model), BF16), shape((rows_dev, model), F32)],
+        [VM] * 3,
+        (pieces, mine_rows, near_moe),
+        scratch=[pltpu.VMEM((half, model), F32)],
+        limit=8,
+    )
+    theirs = partner(moe_in, "context", 1)
     cuts, start = [], 0
     while start < hidden:
         size = min(2 * LANES, hidden - start)
         cuts.append((start, size))
         start += size
     weights_in = jnp.swapaxes(expert_in[0], 1, 2)
-    begun = call(
-        functools.partial(begin_kernel, contexts, cuts),
-        [
-            shape((kept, model // 2), F32),
-            shape((2 * half, 1), F32),
-            shape((2 * half, hidden), F32),
-            shape((2 * half, hidden), F32),
-        ],
-        [VM] * 5,
-        (mine, mine_rows, their_rows, near_moe, weights_in),
-        scratch=[pltpu.VMEM((2 * half, model // 2), BF16)],
-        flops=2 * 2 * half * hidden * model,
-        moved=4 * hidden * model,
-        limit=20,
-    )
-    near, far, own = call(
-        functools.partial(
-            expert_kernel, contexts, latent_width - kv_rank, kv_rank, experts, cuts, 4
-        ),
-        [shape((half, model), BF16), shape((half, model), BF16), shape((rows_dev, model), F32)],
-        [VM] * 12,
-        (
-            theirs,
-            mine_rows,
-            their_rows,
-            near_moe,
-            weights_in,
-            *begun,
-            mine_keys,
-            their_keys,
-            expert_out[0],
-        ),
-        scratch=[
-            pltpu.VMEM((2 * half, model // 2), BF16),
-            pltpu.VMEM((2 * half, hidden), BF16),
-            pltpu.VMEM((kept, model // 2), F32),
-            pltpu.VMEM((kept, model), F32),
-        ],
-        flops=4 * 2 * half * hidden * model,
-        moved=4 * hidden * model,
-        limit=20,
-    )
+    near, far = [
+        call(
+            functools.partial(
+                expert_kernel, latent_width - kv_rank, kv_rank, experts, cuts, 4
+            ),
+            shape((half, model), BF16),
+            [VM] * 4,
+            (rows, tails, weights_in, expert_out[0]),
+            scratch=[pltpu.VMEM((half, hidden), BF16)],
+            flops=6 * half * hidden * model,
+            moved=6 * hidden * model,
+            limit=12,
+        )
+        for rows, tails in ((moe_in, mine_keys), (theirs, their_keys))
+    ]
 
     levels = call(
         level_kernel,

time: 80.2 us -> 81.9 us (1.021)
  waiting for transfers between devices: 33.4 us -> 31 us
  Pallas kernels: 12.3 us -> 14.5 us
  starting transfers between devices: 33.3 us -> 35 us
    ppermute x28, waiting for transfers between devices: 33.4 us -> 31 us  [partner(): return lax.ppermute(values, axis, [(i, i ^ mask) for i in range(count)])]
    pallas_call x12 -> x14, Pallas kernels: 12.3 us -> 14.5 us  [call(): pl.pallas_call(kernel, out_shape=outs, in_specs=in_specs, out_specs=VM if...]
    ppermute x28, starting transfers between devices: 33.3 us -> 35 us  [partner(): return lax.ppermute(values, axis, [(i, i ^ mask) for i in range(count)])]
  transfers between devices with their start and end apart: 28 -> 28, of which waited for: 19 -> 15; matrix products, arithmetic and copies ran while one was open for 0% -> 0% of each run, Pallas kernels for 6% -> 9%
where the time goes in v3:
time: 81.9 us; the launch traced here: 81.7 us
  starting transfers between devices  35 us (43%)
  waiting for transfers between devices  31 us (38%)
  Pallas kernels  14.5 us (18%)
  between operations  0.82 us (1%)
    ppermute x28, starting transfers between devices, partner(): return lax.ppermute(values, axis, [(i, i ^ mask) for i in range(count)])  35 us
    ppermute x28, waiting for transfers between devices, partner(): return lax.ppermute(values, axis, [(i, i ^ mask) for i in range(count)])  31 us
    pallas_call x14, Pallas kernels, call(): pl.pallas_call(kernel, out_shape=outs, in_specs=in_specs, out_specs=VM if...  14.5 us
  transfers between devices with their start and end apart: 28, of which 15 were waited for; matrix products, arithmetic and copies ran while one was open for 0% of the time, Pallas kernels for 9%

profile of v3, /device:TPU:0, one launch (start us, length us, event | category | flops | bytes accessed | tf_op | source)
XLA Modules:
  0.0 81.7 jit_solution(13825698736318279035)
XLA Ops:
  0.6 1.2 %shard_map.140.refs_0_ = bf16[32,512]{1,0:T(8,128)(2,1)S(1)} custom-call(s32[1,32]{1,0:T(1,128)} %refs_0_.1, bf16[192,512]{1,0:T(8,128)(2,1)} %raw_hbm.1), custom_call_target="tpu_custom_call" | custom-call | tf_op jit(solution)/shard_map/pallas_call | solution.py:41
  1.8 3.1 %collective-permute-start = (bf16[32,512]{1,0:T(8,128)(2,1)S(1)}, bf16[32,512]{1,0:T(8,128)(2,1)S(1)}, u32[]{:S(2)}, u32[]{:S(2)}) collective-permute-start(bf16[32,512]{1,0:T(8,128)(2,1)S(1)} %shard_map.140.refs_0_), channel_id=1, source_target_pairs={{0,1},{1,0},{2,3},{3,2},{4,5},{5,4},{6,7},{7,6},{8,9},{9,8},{10,11... | collective-permute-start | bytes 98312 | tf_op jit(solution)/shard_map/ppermute | solution.py:66
  5.0 2.6 %collective-permute-start.1 = (bf16[32,512]{1,0:T(8,128)(2,1)S(1)}, bf16[32,512]{1,0:T(8,128)(2,1)S(1)}, u32[]{:S(2)}, u32[]{:S(2)}) collective-permute-start(bf16[32,512]{1,0:T(8,128)(2,1)S(1)} %shard_map.140.refs_0_), channel_id=1, source_target_pairs={{0,2},{1,3},{2,0},{3,1},{4,6},{5,7},{6,4},{7,5},{8,10},{9,11},{10,... | collective-permute-start | bytes 98312 | tf_op jit(solution)/shard_map/ppermute | solution.py:66
  7.6 2.8 %shard_map.141 = (bf16[144,2048]{1,0:T(8,128)(2,1)S(1)}, f32[1,2048]{1,0:T(1,128)S(1)}, f32[1,512]{1,0:T(1,128)S(1)}, f32[1,2048]{1,0:T(1,128)S(1)}, bf16[2048,1...) custom-call(s32[1,32]{1,0:T(1,128)} %refs_0_.1, ...), custom_call_target="tpu_custom_call" | custom-call | bytes 4718592 | tf_op jit(solution)/shard_map/pallas_call | solution.py:41
  10.4 2.8 %collective-permute-done.2.refs_3_ = bf16[32,512]{1,0:T(8,128)(2,1)S(1)} collective-permute-done((bf16[32,512]{1,0:T(8,128)(2,1)S(1)}, bf16[32,512]{1,0:T(8,128)(2,1)S(1)}, u32[]{:S(2)}, u32[]{:S(2)}) %collective-permute-start.2) | collective-permute-done | bytes 32800 | tf_op jit(solution)/shard_map/ppermute | solution.py:66
  13.7 1.5 %collective-permute-start.4 = (f32[40,256]{1,0:T(8,128)S(1)}, f32[40,256]{1,0:T(8,128)S(1)}, u32[]{:S(2)}, u32[]{:S(2)}) collective-permute-start(f32[40,256]{1,0:T(8,128)S(1)} %get-tuple-element.27.refs_0_), channel_id=1, source_target_pairs={{0,2},{1,3},{2,0},{3,1},{4,6},{5,7},{6,4},{7,5},{8,10},{9,11},{10,... | collective-permute-start | bytes 122888 | tf_op jit(solution)/shard_map/ppermute | solution.py:66
  15.3 2.8 %collective-permute-start.5 = (f32[40,256]{1,0:T(8,128)S(1)}, f32[40,256]{1,0:T(8,128)S(1)}, u32[]{:S(2)}, u32[]{:S(2)}) collective-permute-start(f32[40,256]{1,0:T(8,128)S(1)} %get-tuple-element.27.refs_0_), channel_id=1, source_target_pairs={{0,3},{1,2},{2,1},{3,0},{4,7},{5,6},{6,5},{7,4},{8,11},{9,10},{10,... | collective-permute-start | bytes 122888 | tf_op jit(solution)/shard_map/ppermute | solution.py:66
  19.2 1.8 %collective-permute-done.5.refs_3_ = f32[40,256]{1,0:T(8,128)S(1)} collective-permute-done((f32[40,256]{1,0:T(8,128)S(1)}, f32[40,256]{1,0:T(8,128)S(1)}, u32[]{:S(2)}, u32[]{:S(2)}) %collective-permute-start.5) | collective-permute-done | bytes 40992 | tf_op jit(solution)/shard_map/ppermute | solution.py:66
  21.3 2.5 %collective-permute-start.8 = (bf16[96,640]{1,0:T(8,128)(2,1)S(1)}, bf16[96,640]{1,0:T(8,128)(2,1)S(1)}, u32[]{:S(2)}, u32[]{:S(2)}) collective-permute-start(bf16[96,640]{1,0:T(8,128)(2,1)S(1)} %shard_map.144.sent_ref), channel_id=1, source_target_pairs={{0,24},{4,28},{8,16},{12,20},{16,8},{20,12},{24,0},{28,4},{1,25},{... | collective-permute-start | bytes 368648 | tf_op jit(solution)/shard_map/ppermute | solution.py:66
  24.8 3.4 %collective-permute-done.8 = bf16[96,640]{1,0:T(8,128)(2,1)S(1)} collective-permute-done((bf16[96,640]{1,0:T(8,128)(2,1)S(1)}, bf16[96,640]{1,0:T(8,128)(2,1)S(1)}, u32[]{:S(2)}, u32[]{:S(2)}) %collective-permute-start.8) | collective-permute-done | bytes 122912 | tf_op jit(solution)/shard_map/ppermute | solution.py:66
  29.4 1.3 %collective-permute-done.9.theirs_ref.tail_ref = bf16[4,32,640]{2,1,0:T(8,128)(2,1)S(1)} collective-permute-done((bf16[4,32,640]{2,1,0:T(8,128)(2,1)S(1)}, bf16[4,32,640]{2,1,0:T(8,128)(2,1)S(1)}, u32[]{:S(2)}, u32[]{:S(2)}) %collective-permute-start.9) | collective-permute-done | bytes 163872 | tf_op jit(solution)/shard_map/ppermute | solution.py:66
  30.7 1.9 %shard_map.145.refs_0_ = bf16[128,512]{1,0:T(8,128)(2,1)S(1)} custom-call(bf16[4,96,640]{2,1,0:T(8,128)(2,1)S(1)} %pad_maximum_fusion.2.mine_ref.tail_ref, bf16[4,32,640]{2,1,0:T(8,128)(2,1)S(1)} %collective-permute-done.9.theirs_ref.tail_ref, bf16[1024,256]{1,0:T(8,128)(2,1)} %weight_hbm.1, bf16[1024,256]{1,0:T(8,128)(2,1)S(1)} %collective-permute-done.10.other_hbm), custom_call_target="tpu_custom_call" | custom-call | flops 134217728 | bytes 1048576 | tf_op jit(solution)/shard_map/pallas_call | solution.py:41
  32.6 3.4 %collective-permute-start.12 = (bf16[128,512]{1,0:T(8,128)(2,1)S(1)}, bf16[128,512]{1,0:T(8,128)(2,1)S(1)}, u32[]{:S(2)}, u32[]{:S(2)}) collective-permute-start(bf16[128,512]{1,0:T(8,128)(2,1)S(1)} %shard_map.145.refs_0_), channel_id=1, source_target_pairs={{0,2},{1,3},{2,0},{3,1},{4,6},{5,7},{6,4},{7,5},{8,10},{9,11},{10,... | collective-permute-start | bytes 393224 | tf_op jit(solution)/shard_map/ppermute | solution.py:66
  37.0 1.5 %collective-permute-start.19 = (bf16[32,2048]{1,0:T(8,128)(2,1)S(1)}, bf16[32,2048]{1,0:T(8,128)(2,1)S(1)}, u32[]{:S(2)}, u32[]{:S(2)}) collective-permute-start(bf16[32,2048]{1,0:T(8,128)(2,1)S(1)} %get-tuple-element.34), channel_id=1, source_target_pairs={{0,24},{4,28},{8,16},{12,20},{16,8},{20,12},{24,0},{28,4},{1,25},{... | collective-permute-start | bytes 393224 | tf_op jit(solution)/shard_map/ppermute | solution.py:66
  38.5 1.2 %collective-permute-start.18 = (bf16[32,2048]{1,0:T(8,128)(2,1)S(1)}, bf16[32,2048]{1,0:T(8,128)(2,1)S(1)}, u32[]{:S(2)}, u32[]{:S(2)}) collective-permute-start(bf16[32,2048]{1,0:T(8,128)(2,1)S(1)} %get-tuple-element.34), channel_id=1, source_target_pairs={{0,16},{4,20},{8,24},{12,28},{16,0},{20,4},{24,8},{28,12},{1,17},{... | collective-permute-start | bytes 393224 | tf_op jit(solution)/shard_map/ppermute | solution.py:66
  40.4 1.2 %collective-permute-start.17 = (bf16[32,2048]{1,0:T(8,128)(2,1)S(1)}, bf16[32,2048]{1,0:T(8,128)(2,1)S(1)}, u32[]{:S(2)}, u32[]{:S(2)}) collective-permute-start(bf16[32,2048]{1,0:T(8,128)(2,1)S(1)} %get-tuple-element.34), channel_id=1, source_target_pairs={{0,8},{4,12},{8,0},{12,4},{16,24},{20,28},{24,16},{28,20},{1,9},{5... | collective-permute-start | bytes 393224 | tf_op jit(solution)/shard_map/ppermute | solution.py:66
  41.7 4.4 %collective-permute-done.12.refs_2_ = bf16[128,512]{1,0:T(8,128)(2,1)S(1)} collective-permute-done((bf16[128,512]{1,0:T(8,128)(2,1)S(1)}, bf16[128,512]{1,0:T(8,128)(2,1)S(1)}, u32[]{:S(2)}, u32[]{:S(2)}) %collective-permute-start.12) | collective-permute-done | bytes 131104 | tf_op jit(solution)/shard_map/ppermute | solution.py:66
  46.1 1.6 %collective-permute-start.16 = (bf16[128,512]{1,0:T(8,128)(2,1)S(1)}, bf16[128,512]{1,0:T(8,128)(2,1)S(1)}, u32[]{:S(2)}, u32[]{:S(2)}) collective-permute-start(bf16[128,512]{1,0:T(8,128)(2,1)S(1)} %shard_map.146), channel_id=1, source_target_pairs={{0,24},{4,28},{8,16},{12,20},{16,8},{20,12},{24,0},{28,4},{1,25},{... | collective-permute-start | bytes 393224 | tf_op jit(solution)/shard_map/ppermute | solution.py:66
  48.5 1.2 %collective-permute-start.14 = (bf16[128,512]{1,0:T(8,128)(2,1)S(1)}, bf16[128,512]{1,0:T(8,128)(2,1)S(1)}, u32[]{:S(2)}, u32[]{:S(2)}) collective-permute-start(bf16[128,512]{1,0:T(8,128)(2,1)S(1)} %shard_map.146), channel_id=1, source_target_pairs={{0,8},{4,12},{8,0},{12,4},{16,24},{20,28},{24,16},{28,20},{1,9},{5... | collective-permute-start | bytes 393224 | tf_op jit(solution)/shard_map/ppermute | solution.py:66
  49.7 2.8 %collective-permute-done.16 = bf16[128,512]{1,0:T(8,128)(2,1)S(1)} collective-permute-done((bf16[128,512]{1,0:T(8,128)(2,1)S(1)}, bf16[128,512]{1,0:T(8,128)(2,1)S(1)}, u32[]{:S(2)}, u32[]{:S(2)}) %collective-permute-start.16) | collective-permute-done | bytes 131104 | tf_op jit(solution)/shard_map/ppermute | solution.py:66
  52.5 1.2 %collective-permute-done.15 = bf16[128,512]{1,0:T(8,128)(2,1)S(1)} collective-permute-done((bf16[128,512]{1,0:T(8,128)(2,1)S(1)}, bf16[128,512]{1,0:T(8,128)(2,1)S(1)}, u32[]{:S(2)}, u32[]{:S(2)}) %collective-permute-start.15) | collective-permute-done | bytes 131104 | tf_op jit(solution)/shard_map/ppermute | solution.py:66
  54.4 1.9 %collective-permute-done.20.rows_ref = bf16[128,2048]{1,0:T(8,128)(2,1)S(1)} collective-permute-done((bf16[128,2048]{1,0:T(8,128)(2,1)S(1)}, bf16[128,2048]{1,0:T(8,128)(2,1)S(1)}, u32[]{:S(2)}, u32[]{:S(2)}) %collective-permute-start.20) | collective-permute-done | bytes 524320 | tf_op jit(solution)/shard_map/ppermute | solution.py:66
  56.3 2.5 %shard_map.149 = bf16[128,2048]{1,0:T(8,128)(2,1)S(1)} custom-call(bf16[128,2048]{1,0:T(8,128)(2,1)S(1)} %collective-permute-done.20.rows_ref, bf16[4,32,640]{2,1,0:T(8,128)(2,1)S(1)} %collective-permute-done.9.theirs_ref.tail_ref, bf16[2,704,2048]{2,1,0:T(8,128)(2,1)S(1)} %bitcast.30, bf16[704,2048]{1,0:T(8,128)(2,1)S(1)} %bitcast.32), custom_call_target="tpu_custom_call" | custom-call | flops 1107296256 | bytes 8650752 | tf_op jit(solution)/shard_map/pallas_call | solution.py:41
  59.0 2.5 %shard_map.148.near_ref = bf16[128,2048]{1,0:T(8,128)(2,1)S(1)} custom-call(bf16[128,2048]{1,0:T(8,128)(2,1)S(1)} %get-tuple-element.36.rows_ref, bf16[4,96,640]{2,1,0:T(8,128)(2,1)S(1)} %pad_maximum_fusion.2.mine_ref.tail_ref, bf16[2,704,2048]{2,1,0:T(8,128)(2,1)S(1)} %bitcast.31, bf16[704,2048]{1,0:T(8,128)(2,1)S(1)} %bitcast.33), custom_call_target="tpu_custom_call" | custom-call | flops 1107296256 | bytes 8650752 | tf_op jit(solution)/shard_map/pallas_call | solution.py:41
  62.7 1.2 %collective-permute-start.23 = (bf16[32,2048]{1,0:T(8,128)(2,1)S(1)}, bf16[32,2048]{1,0:T(8,128)(2,1)S(1)}, u32[]{:S(2)}, u32[]{:S(2)}) collective-permute-start(bf16[32,2048]{1,0:T(8,128)(2,1)S(1)} %get-tuple-element.39), channel_id=1, source_target_pairs={{0,16},{4,20},{8,24},{12,28},{16,0},{20,4},{24,8},{28,12},{1,17},{... | collective-permute-start | bytes 393224 | tf_op jit(solution)/shard_map/ppermute | solution.py:66
  63.9 1.2 %collective-permute-start.24 = (bf16[32,2048]{1,0:T(8,128)(2,1)S(1)}, bf16[32,2048]{1,0:T(8,128)(2,1)S(1)}, u32[]{:S(2)}, u32[]{:S(2)}) collective-permute-start(bf16[32,2048]{1,0:T(8,128)(2,1)S(1)} %get-tuple-element.40), channel_id=1, source_target_pairs={{0,24},{4,28},{8,16},{12,20},{16,8},{20,12},{24,0},{28,4},{1,25},{... | collective-permute-start | bytes 393224 | tf_op jit(solution)/shard_map/ppermute | solution.py:66
  65.2 2.9 %collective-permute-done.22.refs_1_ = bf16[32,2048]{1,0:T(8,128)(2,1)S(1)} collective-permute-done((bf16[32,2048]{1,0:T(8,128)(2,1)S(1)}, bf16[32,2048]{1,0:T(8,128)(2,1)S(1)}, u32[]{:S(2)}, u32[]{:S(2)}) %collective-permute-start.22) | collective-permute-done | bytes 131104 | tf_op jit(solution)/shard_map/ppermute | solution.py:66
  68.0 3.0 %collective-permute-done.23.refs_2_ = bf16[32,2048]{1,0:T(8,128)(2,1)S(1)} collective-permute-done((bf16[32,2048]{1,0:T(8,128)(2,1)S(1)}, bf16[32,2048]{1,0:T(8,128)(2,1)S(1)}, u32[]{:S(2)}, u32[]{:S(2)}) %collective-permute-start.23) | collective-permute-done | bytes 131104 | tf_op jit(solution)/shard_map/ppermute | solution.py:66
  71.1 3.1 %collective-permute-start.25 = (bf16[8,2048]{1,0:T(8,128)(2,1)S(1)}, bf16[8,2048]{1,0:T(8,128)(2,1)S(1)}, u32[]{:S(2)}, u32[]{:S(2)}) collective-permute-start(bf16[8,2048]{1,0:T(8,128)(2,1)S(1)} %get-tuple-element.42), channel_id=1, source_target_pairs={{0,1},{1,0},{2,3},{3,2},{4,5},{5,4},{6,7},{7,6},{8,9},{9,8},{10,11... | collective-permute-start | bytes 98312 | tf_op jit(solution)/shard_map/ppermute | solution.py:66
  75.3 1.4 %collective-permute-start.27 = (bf16[8,2048]{1,0:T(8,128)(2,1)S(1)}, bf16[8,2048]{1,0:T(8,128)(2,1)S(1)}, u32[]{:S(2)}, u32[]{:S(2)}) collective-permute-start(bf16[8,2048]{1,0:T(8,128)(2,1)S(1)} %get-tuple-element.44), channel_id=1, source_target_pairs={{0,3},{1,2},{2,1},{3,0},{4,7},{5,6},{6,5},{7,4},{8,11},{9,10},{10,... | collective-permute-start | bytes 98312 | tf_op jit(solution)/shard_map/ppermute | solution.py:66
  77.3 2.3 %collective-permute-done.26.refs_2_ = bf16[8,2048]{1,0:T(8,128)(2,1)S(1)} collective-permute-done((bf16[8,2048]{1,0:T(8,128)(2,1)S(1)}, bf16[8,2048]{1,0:T(8,128)(2,1)S(1)}, u32[]{:S(2)}, u32[]{:S(2)}) %collective-permute-start.26) | collective-permute-done | bytes 32800 | tf_op jit(solution)/shard_map/ppermute | solution.py:66
  79.6 1.4 %collective-permute-done.27.refs_3_ = bf16[8,2048]{1,0:T(8,128)(2,1)S(1)} collective-permute-done((bf16[8,2048]{1,0:T(8,128)(2,1)S(1)}, bf16[8,2048]{1,0:T(8,128)(2,1)S(1)}, u32[]{:S(2)}, u32[]{:S(2)}) %collective-permute-start.27) | collective-permute-done | bytes 32800 | tf_op jit(solution)/shard_map/ppermute | solution.py:66
  (55 shorter events, 11.3 us)
Async XLA Ops:
  0.6 17.5 %copy-start.1 = (bf16[1024,256]{1,0:T(8,128)(2,1)S(1)}, bf16[1024,256]{1,0:T(8,128)(2,1)}, u32[]{:S(2)}) copy-start(bf16[1024,256]{1,0:T(8,128)(2,1)} %weight_hbm.1) | copy-start | bytes 1572868
  1.8 8.6 %collective-permute-start = (bf16[32,512]{1,0:T(8,128)(2,1)S(1)}, bf16[32,512]{1,0:T(8,128)(2,1)S(1)}, u32[]{:S(2)}, u32[]{:S(2)}) collective-permute-start(bf16[32,512]{1,0:T(8,128)(2,1)S(1)} %shard_map.140.refs_0_), channel_id=1, source_target_pairs={{0,1},{1,0},{2,3},{3,2},{4,5},{5,4},{6,7},{7,6},{8,9},{9,8},{10,11... | collective-permute-start | bytes 98312 | tf_op jit(solution)/shard_map/ppermute | solution.py:66
  5.0 5.5 %collective-permute-start.1 = (bf16[32,512]{1,0:T(8,128)(2,1)S(1)}, bf16[32,512]{1,0:T(8,128)(2,1)S(1)}, u32[]{:S(2)}, u32[]{:S(2)}) collective-permute-start(bf16[32,512]{1,0:T(8,128)(2,1)S(1)} %shard_map.140.refs_0_), channel_id=1, source_target_pairs={{0,2},{1,3},{2,0},{3,1},{4,6},{5,7},{6,4},{7,5},{8,10},{9,11},{10,... | collective-permute-start | bytes 98312 | tf_op jit(solution)/shard_map/ppermute | solution.py:66
  7.6 5.7 %collective-permute-start.2 = (bf16[32,512]{1,0:T(8,128)(2,1)S(1)}, bf16[32,512]{1,0:T(8,128)(2,1)S(1)}, u32[]{:S(2)}, u32[]{:S(2)}) collective-permute-start(bf16[32,512]{1,0:T(8,128)(2,1)S(1)} %shard_map.140.refs_0_), channel_id=1, source_target_pairs={{0,3},{1,2},{2,1},{3,0},{4,7},{5,6},{6,5},{7,4},{8,11},{9,10},{10,... | collective-permute-start | bytes 98312 | tf_op jit(solution)/shard_map/ppermute | solution.py:66
  7.6 48.7 %slice-start = ((s8[5767168]{0:T(1024)(128)(4,1)}), s8[4194304]{0:T(1024)(128)(4,1)S(1)}, s32[]{:S(2)}) async-start(s8[5767168]{0:T(1024)(128)(4,1)} %bitcast.28), calls=%async_computation | async-start | bytes 8388608
  13.7 5.6 %collective-permute-start.3 = (f32[40,256]{1,0:T(8,128)S(1)}, f32[40,256]{1,0:T(8,128)S(1)}, u32[]{:S(2)}, u32[]{:S(2)}) collective-permute-start(f32[40,256]{1,0:T(8,128)S(1)} %get-tuple-element.27.refs_0_), channel_id=1, source_target_pairs={{0,1},{1,0},{2,3},{3,2},{4,5},{5,4},{6,7},{7,6},{8,9},{9,8},{10,11... | collective-permute-start | bytes 122888 | tf_op jit(solution)/shard_map/ppermute | solution.py:66
  13.7 5.5 %collective-permute-start.4 = (f32[40,256]{1,0:T(8,128)S(1)}, f32[40,256]{1,0:T(8,128)S(1)}, u32[]{:S(2)}, u32[]{:S(2)}) collective-permute-start(f32[40,256]{1,0:T(8,128)S(1)} %get-tuple-element.27.refs_0_), channel_id=1, source_target_pairs={{0,2},{1,3},{2,0},{3,1},{4,6},{5,7},{6,4},{7,5},{8,10},{9,11},{10,... | collective-permute-start | bytes 122888 | tf_op jit(solution)/shard_map/ppermute | solution.py:66
  15.3 5.8 %collective-permute-start.5 = (f32[40,256]{1,0:T(8,128)S(1)}, f32[40,256]{1,0:T(8,128)S(1)}, u32[]{:S(2)}, u32[]{:S(2)}) collective-permute-start(f32[40,256]{1,0:T(8,128)S(1)} %get-tuple-element.27.refs_0_), channel_id=1, source_target_pairs={{0,3},{1,2},{2,1},{3,0},{4,7},{5,6},{6,5},{7,4},{8,11},{9,10},{10,... | collective-permute-start | bytes 122888 | tf_op jit(solution)/shard_map/ppermute | solution.py:66
  18.1 12.6 %collective-permute-start.10 = (bf16[1024,256]{1,0:T(8,128)(2,1)S(1)}, bf16[1024,256]{1,0:T(8,128)(2,1)S(1)}, u32[]{:S(2)}, u32[]{:S(2)}) collective-permute-start(bf16[1024,256]{1,0:T(8,128)(2,1)S(1)} %copy-done.1), channel_id=1, source_target_pairs={{0,4},{4,0},{8,12},{12,8},{16,20},{20,16},{24,28},{28,24},{1,5},{5... | collective-permute-start | bytes 1572872 | tf_op jit(solution)/shard_map/ppermute | solution.py:66
  18.1 38.2 %slice-start.1 = ((s8[5767168]{0:T(1024)(128)(4,1)}), s8[1572864]{0:T(1024)(128)(4,1)S(1)}, s32[]{:S(2)}) async-start(s8[5767168]{0:T(1024)(128)(4,1)} %bitcast.28), calls=%async_computation.1 | async-start | bytes 3145728
  19.2 37.0 %copy-start = (bf16[1,704,2048]{2,1,0:T(8,128)(2,1)S(1)}, bf16[1,704,2048]{2,1,0:T(8,128)(2,1)}, u32[]{:S(2)}) copy-start(bf16[1,704,2048]{2,1,0:T(8,128)(2,1)} %param.25) | copy-start | bytes 8650756
  21.3 7.0 %collective-permute-start.8 = (bf16[96,640]{1,0:T(8,128)(2,1)S(1)}, bf16[96,640]{1,0:T(8,128)(2,1)S(1)}, u32[]{:S(2)}, u32[]{:S(2)}) collective-permute-start(bf16[96,640]{1,0:T(8,128)(2,1)S(1)} %shard_map.144.sent_ref), channel_id=1, source_target_pairs={{0,24},{4,28},{8,16},{12,20},{16,8},{20,12},{24,0},{28,4},{1,25},{... | collective-permute-start | bytes 368648 | tf_op jit(solution)/shard_map/ppermute | solution.py:66
  23.8 5.3 %collective-permute-start.7 = (bf16[96,640]{1,0:T(8,128)(2,1)S(1)}, bf16[96,640]{1,0:T(8,128)(2,1)S(1)}, u32[]{:S(2)}, u32[]{:S(2)}) collective-permute-start(bf16[96,640]{1,0:T(8,128)(2,1)S(1)} %shard_map.144.sent_ref), channel_id=1, source_target_pairs={{0,16},{4,20},{8,24},{12,28},{16,0},{20,4},{24,8},{28,12},{1,17},{... | collective-permute-start | bytes 368648 | tf_op jit(solution)/shard_map/ppermute | solution.py:66
  24.3 4.9 %collective-permute-start.6 = (bf16[96,640]{1,0:T(8,128)(2,1)S(1)}, bf16[96,640]{1,0:T(8,128)(2,1)S(1)}, u32[]{:S(2)}, u32[]{:S(2)}) collective-permute-start(bf16[96,640]{1,0:T(8,128)(2,1)S(1)} %shard_map.144.sent_ref), channel_id=1, source_target_pairs={{0,8},{4,12},{8,0},{12,4},{16,24},{20,28},{24,16},{28,20},{1,9},{5... | collective-permute-start | bytes 368648 | tf_op jit(solution)/shard_map/ppermute | solution.py:66
  29.2 1.5 %collective-permute-start.9 = (bf16[4,32,640]{2,1,0:T(8,128)(2,1)S(1)}, bf16[4,32,640]{2,1,0:T(8,128)(2,1)S(1)}, u32[]{:S(2)}, u32[]{:S(2)}) collective-permute-start(bf16[4,32,640]{2,1,0:T(8,128)(2,1)S(1)} %pad_maximum_fusion.3), channel_id=1, source_target_pairs={{0,4},{4,0},{8,12},{12,8},{16,20},{20,16},{24,28},{28,24},{1,5},{5... | collective-permute-start | bytes 491528 | tf_op jit(solution)/shard_map/ppermute | solution.py:66
  32.5 7.9 %collective-permute-start.11 = (bf16[128,512]{1,0:T(8,128)(2,1)S(1)}, bf16[128,512]{1,0:T(8,128)(2,1)S(1)}, u32[]{:S(2)}, u32[]{:S(2)}) collective-permute-start(bf16[128,512]{1,0:T(8,128)(2,1)S(1)} %shard_map.145.refs_0_), channel_id=1, source_target_pairs={{0,1},{1,0},{2,3},{3,2},{4,5},{5,4},{6,7},{7,6},{8,9},{9,8},{10,11... | collective-permute-start | bytes 393224 | tf_op jit(solution)/shard_map/ppermute | solution.py:66
  32.6 13.4 %collective-permute-start.12 = (bf16[128,512]{1,0:T(8,128)(2,1)S(1)}, bf16[128,512]{1,0:T(8,128)(2,1)S(1)}, u32[]{:S(2)}, u32[]{:S(2)}) collective-permute-start(bf16[128,512]{1,0:T(8,128)(2,1)S(1)} %shard_map.145.refs_0_), channel_id=1, source_target_pairs={{0,2},{1,3},{2,0},{3,1},{4,6},{5,7},{6,4},{7,5},{8,10},{9,11},{10,... | collective-permute-start | bytes 393224 | tf_op jit(solution)/shard_map/ppermute | solution.py:66
  36.0 10.0 %collective-permute-start.13 = (bf16[128,512]{1,0:T(8,128)(2,1)S(1)}, bf16[128,512]{1,0:T(8,128)(2,1)S(1)}, u32[]{:S(2)}, u32[]{:S(2)}) collective-permute-start(bf16[128,512]{1,0:T(8,128)(2,1)S(1)} %shard_map.145.refs_0_), channel_id=1, source_target_pairs={{0,3},{1,2},{2,1},{3,0},{4,7},{5,6},{6,5},{7,4},{8,11},{9,10},{10,... | collective-permute-start | bytes 393224 | tf_op jit(solution)/shard_map/ppermute | solution.py:66
  37.0 11.5 %collective-permute-start.19 = (bf16[32,2048]{1,0:T(8,128)(2,1)S(1)}, bf16[32,2048]{1,0:T(8,128)(2,1)S(1)}, u32[]{:S(2)}, u32[]{:S(2)}) collective-permute-start(bf16[32,2048]{1,0:T(8,128)(2,1)S(1)} %get-tuple-element.34), channel_id=1, source_target_pairs={{0,24},{4,28},{8,16},{12,20},{16,8},{20,12},{24,0},{28,4},{1,25},{... | collective-permute-start | bytes 393224 | tf_op jit(solution)/shard_map/ppermute | solution.py:66
  38.5 11.2 %collective-permute-start.18 = (bf16[32,2048]{1,0:T(8,128)(2,1)S(1)}, bf16[32,2048]{1,0:T(8,128)(2,1)S(1)}, u32[]{:S(2)}, u32[]{:S(2)}) collective-permute-start(bf16[32,2048]{1,0:T(8,128)(2,1)S(1)} %get-tuple-element.34), channel_id=1, source_target_pairs={{0,16},{4,20},{8,24},{12,28},{16,0},{20,4},{24,8},{28,12},{1,17},{... | collective-permute-start | bytes 393224 | tf_op jit(solution)/shard_map/ppermute | solution.py:66
  40.4 9.2 %collective-permute-start.17 = (bf16[32,2048]{1,0:T(8,128)(2,1)S(1)}, bf16[32,2048]{1,0:T(8,128)(2,1)S(1)}, u32[]{:S(2)}, u32[]{:S(2)}) collective-permute-start(bf16[32,2048]{1,0:T(8,128)(2,1)S(1)} %get-tuple-element.34), channel_id=1, source_target_pairs={{0,8},{4,12},{8,0},{12,4},{16,24},{20,28},{24,16},{28,20},{1,9},{5... | collective-permute-start | bytes 393224 | tf_op jit(solution)/shard_map/ppermute | solution.py:66
  46.1 6.4 %collective-permute-start.16 = (bf16[128,512]{1,0:T(8,128)(2,1)S(1)}, bf16[128,512]{1,0:T(8,128)(2,1)S(1)}, u32[]{:S(2)}, u32[]{:S(2)}) collective-permute-start(bf16[128,512]{1,0:T(8,128)(2,1)S(1)} %shard_map.146), channel_id=1, source_target_pairs={{0,24},{4,28},{8,16},{12,20},{16,8},{20,12},{24,0},{28,4},{1,25},{... | collective-permute-start | bytes 393224 | tf_op jit(solution)/shard_map/ppermute | solution.py:66
  47.6 6.1 %collective-permute-start.15 = (bf16[128,512]{1,0:T(8,128)(2,1)S(1)}, bf16[128,512]{1,0:T(8,128)(2,1)S(1)}, u32[]{:S(2)}, u32[]{:S(2)}) collective-permute-start(bf16[128,512]{1,0:T(8,128)(2,1)S(1)} %shard_map.146), channel_id=1, source_target_pairs={{0,16},{4,20},{8,24},{12,28},{16,0},{20,4},{24,8},{28,12},{1,17},{... | collective-permute-start | bytes 393224 | tf_op jit(solution)/shard_map/ppermute | solution.py:66
  48.5 5.4 %collective-permute-start.14 = (bf16[128,512]{1,0:T(8,128)(2,1)S(1)}, bf16[128,512]{1,0:T(8,128)(2,1)S(1)}, u32[]{:S(2)}, u32[]{:S(2)}) collective-permute-start(bf16[128,512]{1,0:T(8,128)(2,1)S(1)} %shard_map.146), channel_id=1, source_target_pairs={{0,8},{4,12},{8,0},{12,4},{16,24},{20,28},{24,16},{28,20},{1,9},{5... | collective-permute-start | bytes 393224 | tf_op jit(solution)/shard_map/ppermute | solution.py:66
  54.3 2.0 %collective-permute-start.20 = (bf16[128,2048]{1,0:T(8,128)(2,1)S(1)}, bf16[128,2048]{1,0:T(8,128)(2,1)S(1)}, u32[]{:S(2)}, u32[]{:S(2)}) collective-permute-start(bf16[128,2048]{1,0:T(8,128)(2,1)S(1)} %get-tuple-element.36.rows_ref), channel_id=1, source_target_pairs={{0,4},{4,0},{8,12},{12,8},{16,20},{20,16},{24,28},{28,24},{1,5},{5... | collective-permute-start | bytes 1572872 | tf_op jit(solution)/shard_map/ppermute | solution.py:66
  58.8 2.7 %collective-permute-start.21 = (bf16[128,2048]{1,0:T(8,128)(2,1)S(1)}, bf16[128,2048]{1,0:T(8,128)(2,1)S(1)}, u32[]{:S(2)}, u32[]{:S(2)}) collective-permute-start(bf16[128,2048]{1,0:T(8,128)(2,1)S(1)} %shard_map.149), channel_id=1, source_target_pairs={{0,4},{4,0},{8,12},{12,8},{16,20},{20,16},{24,28},{28,24},{1,5},{5... | collective-permute-start | bytes 1572872 | tf_op jit(solution)/shard_map/ppermute | solution.py:66
  61.6 6.4 %collective-permute-start.22 = (bf16[32,2048]{1,0:T(8,128)(2,1)S(1)}, bf16[32,2048]{1,0:T(8,128)(2,1)S(1)}, u32[]{:S(2)}, u32[]{:S(2)}) collective-permute-start(bf16[32,2048]{1,0:T(8,128)(2,1)S(1)} %get-tuple-element.38), channel_id=1, source_target_pairs={{0,8},{4,12},{8,0},{12,4},{16,24},{20,28},{24,16},{28,20},{1,9},{5... | collective-permute-start | bytes 393224 | tf_op jit(solution)/shard_map/ppermute | solution.py:66
  62.7 8.3 %collective-permute-start.23 = (bf16[32,2048]{1,0:T(8,128)(2,1)S(1)}, bf16[32,2048]{1,0:T(8,128)(2,1)S(1)}, u32[]{:S(2)}, u32[]{:S(2)}) collective-permute-start(bf16[32,2048]{1,0:T(8,128)(2,1)S(1)} %get-tuple-element.39), channel_id=1, source_target_pairs={{0,16},{4,20},{8,24},{12,28},{16,0},{20,4},{24,8},{28,12},{1,17},{... | collective-permute-start | bytes 393224 | tf_op jit(solution)/shard_map/ppermute | solution.py:66
  63.9 7.1 %collective-permute-start.24 = (bf16[32,2048]{1,0:T(8,128)(2,1)S(1)}, bf16[32,2048]{1,0:T(8,128)(2,1)S(1)}, u32[]{:S(2)}, u32[]{:S(2)}) collective-permute-start(bf16[32,2048]{1,0:T(8,128)(2,1)S(1)} %get-tuple-element.40), channel_id=1, source_target_pairs={{0,24},{4,28},{8,16},{12,20},{16,8},{20,12},{24,0},{28,4},{1,25},{... | collective-permute-start | bytes 393224 | tf_op jit(solution)/shard_map/ppermute | solution.py:66
  71.1 6.2 %collective-permute-start.25 = (bf16[8,2048]{1,0:T(8,128)(2,1)S(1)}, bf16[8,2048]{1,0:T(8,128)(2,1)S(1)}, u32[]{:S(2)}, u32[]{:S(2)}) collective-permute-start(bf16[8,2048]{1,0:T(8,128)(2,1)S(1)} %get-tuple-element.42), channel_id=1, source_target_pairs={{0,1},{1,0},{2,3},{3,2},{4,5},{5,4},{6,7},{7,6},{8,9},{9,8},{10,11... | collective-permute-start | bytes 98312 | tf_op jit(solution)/shard_map/ppermute | solution.py:66
  74.2 5.4 %collective-permute-start.26 = (bf16[8,2048]{1,0:T(8,128)(2,1)S(1)}, bf16[8,2048]{1,0:T(8,128)(2,1)S(1)}, u32[]{:S(2)}, u32[]{:S(2)}) collective-permute-start(bf16[8,2048]{1,0:T(8,128)(2,1)S(1)} %get-tuple-element.43), channel_id=1, source_target_pairs={{0,2},{1,3},{2,0},{3,1},{4,6},{5,7},{6,4},{7,5},{8,10},{9,11},{10,... | collective-permute-start | bytes 98312 | tf_op jit(solution)/shard_map/ppermute | solution.py:66
  75.3 5.7 %collective-permute-start.27 = (bf16[8,2048]{1,0:T(8,128)(2,1)S(1)}, bf16[8,2048]{1,0:T(8,128)(2,1)S(1)}, u32[]{:S(2)}, u32[]{:S(2)}) collective-permute-start(bf16[8,2048]{1,0:T(8,128)(2,1)S(1)} %get-tuple-element.44), channel_id=1, source_target_pairs={{0,3},{1,2},{2,1},{3,0},{4,7},{5,6},{6,5},{7,4},{8,11},{9,10},{10,... | collective-permute-start | bytes 98312 | tf_op jit(solution)/shard_map/ppermute | solution.py:66

commit v4 on v2

--- a/solution.py
+++ b/solution.py
@@ -14,6 +14,7 @@
 SCALE = 192.0 ** (-0.5)
 NEGATIVE = -1e30
 LANES = 128
+EARLY = 4
 F32 = jnp.float32
 BF16 = jnp.bfloat16
 MIB = 1 << 20
@@ -98,15 +99,27 @@
     ).astype(BF16)
 
 
-def prepare_kernel(raw_rows, *refs):
-    keep_hbm, ids_hbm, gates_hbm, slot_hbm = refs[:4]
-    sources = refs[4:9]
-    targets = refs[9:14]
-    dense_ref, cos_ref, sin_ref, live_ref = refs[14:18]
-    keep_ref, ids_ref, gates_ref, slot_ref, sem = refs[18:]
-    small = [(keep_hbm, keep_ref), (ids_hbm, ids_ref), (gates_hbm, gates_ref), (slot_hbm, slot_ref)]
-    copies = fetch(small + list(zip(sources, targets)), sem)
-    for copy in copies[:4]:
+def prepare_kernel(
+    ids_hbm,
+    gates_hbm,
+    slot_hbm,
+    weight_hbm,
+    gain_hbm,
+    query_hbm,
+    weight_ref,
+    gain_ref,
+    query_ref,
+    dense_ref,
+    ids_ref,
+    gates_ref,
+    slot_ref,
+    sem,
+):
+    early = query_hbm.at[pl.ds(0, query_ref.shape[0]), :]
+    small = [(ids_hbm, ids_ref), (gates_hbm, gates_ref), (slot_hbm, slot_ref)]
+    large = [(weight_hbm, weight_ref), (gain_hbm, gain_ref), (early, query_ref)]
+    copies = fetch(small + large, sem)
+    for copy in copies[:3]:
         copy.wait()
     ids = ids_ref[...]
     slots = jnp.zeros_like(ids)
@@ -117,24 +130,7 @@
     for t in range(ids.shape[1]):
         gates = gates + jnp.where(lane == slots[:, t : t + 1], gates_ref[:, t : t + 1], 0.0)
     dense_ref[...] = gates
-    rows, rope = cos_ref.shape
-    diagonal = lax.broadcasted_iota(jnp.int32, (rows, rows), 0) == lax.broadcasted_iota(
-        jnp.int32, (rows, rows), 1
-    )
-    listing = jnp.sum(
-        jnp.where(diagonal, keep_ref[...].astype(F32), 0.0), axis=1, keepdims=True
-    )
-    live_ref[...] = jnp.where(listing >= 0, 1.0, 0.0)
-    positions = (here()[0] * raw_rows).astype(F32) + jnp.maximum(listing, 0.0)
-    half = rope // 2
-    lane = lax.broadcasted_iota(jnp.int32, (rows, rope), 1)
-    first = lane < half
-    place = jnp.where(first, lane, lane - half).astype(F32)
-    angles = positions * jnp.exp(place * (-2.0 / rope * math.log(THETA)))
-    cos_ref[...] = jnp.cos(angles)
-    sine = jnp.sin(angles)
-    sin_ref[...] = jnp.where(first, -sine, sine)
-    for copy in copies[4:]:
+    for copy in copies[3:]:
         copy.wait()
 
 
@@ -161,11 +157,55 @@
     return values * cosine + swapped * sine
 
 
-def query_kernel(heads, normed_ref, weight_ref, cos_ref, sin_ref, out_ref):
-    rows = normed_ref.shape[0]
-    latent = weight_ref.shape[1] // heads
-    total = nn(normed_ref[...], weight_ref[...])
-    kv_rank = latent - cos_ref.shape[1]
+def query_kernel(
+    heads,
+    raw_rows,
+    normed_ref,
+    early_ref,
+    weight_hbm,
+    keep_hbm,
+    kv_hbm,
+    moe_hbm,
+    out_ref,
+    cos_ref,
+    sin_ref,
+    live_ref,
+    kv_ref,
+    moe_ref,
+    buf,
+    keep_ref,
+    sem,
+):
+    begun = early_ref.shape[0]
+    steps, deep = buf.shape[:2]
+    small = [(keep_hbm, keep_ref), (kv_hbm, kv_ref), (moe_hbm, moe_ref)]
+    late = [(weight_hbm.at[pl.ds(begun + n * deep, deep), :], buf.at[n]) for n in range(steps)]
+    copies = fetch(small + late, sem)
+    copies[0].wait()
+    rows, rope = cos_ref.shape
+    diagonal = lax.broadcasted_iota(jnp.int32, (rows, rows), 0) == lax.broadcasted_iota(
+        jnp.int32, (rows, rows), 1
+    )
+    listing = jnp.sum(
+        jnp.where(diagonal, keep_ref[...].astype(F32), 0.0), axis=1, keepdims=True
+    )
+    live_ref[...] = jnp.where(listing >= 0, 1.0, 0.0)
+    positions = (here()[0] * raw_rows).astype(F32) + jnp.maximum(listing, 0.0)
+    half = rope // 2
+    lane = lax.broadcasted_iota(jnp.int32, (rows, rope), 1)
+    first = lane < half
+    place = jnp.where(first, lane, lane - half).astype(F32)
+    angles = positions * jnp.exp(place * (-2.0 / rope * math.log(THETA)))
+    cos_ref[...] = jnp.cos(angles)
+    sine = jnp.sin(angles)
+    sin_ref[...] = jnp.where(first, -sine, sine)
+    latent = early_ref.shape[1] // heads
+    total = nn(normed_ref[:, :begun], early_ref[...])
+    for n in range(steps):
+        copies[3 + n].wait()
+        at = begun + n * deep
+        total = total + nn(normed_ref[:, at : at + deep], buf[n])
+    kv_rank = latent - rope
     out_ref[...] = jnp.zeros(out_ref.shape, BF16)
     for h in range(heads):
         one = total[:, h * latent : (h + 1) * latent]
@@ -173,11 +213,13 @@
         out_ref[h * rows : (h + 1) * rows, kv_rank:latent] = rotated(
             one[:, kv_rank:], cos_ref[...], sin_ref[...]
         ).astype(BF16)
+    for copy in copies[1:3]:
+        copy.wait()
 
 
 def cache_kernel(spans, width, experts, *refs):
     parts = refs[:spans]
-    live_ref, gain_ref, cos_ref, sin_ref, query_ref, cached_ref, sent_ref = refs[spans:]
+    live_ref, gain_ref, cos_ref, sin_ref, query_ref, sent_ref = refs[spans:]
     rows = live_ref.shape[0]
     kv_rank = gain_ref.shape[1]
     values = natural([p[...] for p in parts], here()[1])
@@ -187,8 +229,6 @@
     factor = lax.rsqrt(jnp.mean(nope * nope, axis=1, keepdims=True) + EPS)
     nope = nope * factor * gain_ref[...]
     rope = rotated(latent[:, kv_rank:], cos_ref[...], sin_ref[...])
-    cached_ref[:, :kv_rank] = nope.astype(BF16)
-    cached_ref[:, kv_rank:] = rope.astype(BF16)
     high = gates.astype(BF16).astype(F32)
     used = rope.shape[1] + 2 * experts + 1
     tail = [rope, high, gates - high, live_ref[...]]
@@ -198,6 +238,10 @@
     sent_ref[:rows, :kv_rank] = nope.astype(BF16)
     sent_ref[:rows, kv_rank:] = jnp.concatenate(tail, axis=1).astype(BF16)
     sent_ref[rows:, :] = query_ref[...]
+
+
+def emit_kernel(sent_ref, out_ref):
+    out_ref[...] = sent_ref[: out_ref.shape[0], : out_ref.shape[1]]
 
 
 def places(blocks):
@@ -455,27 +499,25 @@
     parts = gathered(picked, "span", range(1, spans))
 
     sent_width = up(max(part_width, experts))
-    moved = (latent_weight.T, attn_gain[None], kv_gain[None], moe_gain[None], query_weight)
-    near_weight, gain, near_kv, near_moe, near_query, dense, cosine, sine, live = call(
-        functools.partial(prepare_kernel, raw_rows),
-        [shape(value.shape, value.dtype) for value in moved]
-        + [
+    begun = model // EARLY
+    near_weight, gain, early_query, dense = call(
+        prepare_kernel,
+        [
+            shape((part_width, model), BF16),
+            shape((1, model), F32),
+            shape((begun, query_weight.shape[1]), BF16),
             shape((rows_dev, sent_width), F32),
-            shape((kept, rope), F32),
-            shape((kept, rope), F32),
-            shape((kept, 1), F32),
-        ],
-        [HBM] * 9,
-        (keep, expert_ids, gate_values, expert_slot, *moved),
+        ],
+        [HBM] * 6,
+        (expert_ids, gate_values, expert_slot, latent_weight.T, attn_gain[None], query_weight),
         scratch=[
-            pltpu.VMEM(keep.shape, jnp.int32),
             pltpu.VMEM(expert_ids.shape, jnp.int32),
             pltpu.VMEM(gate_values.shape, F32),
             pltpu.SMEM(expert_slot.shape, jnp.int32),
-            pltpu.SemaphoreType.DMA((9,)),
-        ],
-        moved=2 * query_weight.size,
-        limit=12,
+            pltpu.SemaphoreType.DMA((6,)),
+        ],
+        moved=query_weight.size,
+        limit=8,
     )
 
     compact, normed, sent = call(
@@ -493,22 +535,37 @@
     )
     parts = gathered(sent, "span", range(1, spans))
     row_width = up(latent_width + 2 * experts + 1)
-    query = call(
-        functools.partial(query_kernel, heads),
-        shape((heads * kept, row_width), BF16),
-        [VM] * 4,
-        (normed, near_query, cosine, sine),
+    steps = 3
+    query, cosine, sine, live, near_kv, near_moe = call(
+        functools.partial(query_kernel, heads, raw_rows),
+        [
+            shape((heads * kept, row_width), BF16),
+            shape((kept, rope), F32),
+            shape((kept, rope), F32),
+            shape((kept, 1), F32),
+            shape((1, kv_rank), F32),
+            shape((1, model), F32),
+        ],
+        [VM, VM] + [HBM] * 4,
+        (normed, early_query, query_weight, keep, kv_gain[None], moe_gain[None]),
+        scratch=[
+            pltpu.VMEM((steps, (model - begun) // steps, query_weight.shape[1]), BF16),
+            pltpu.VMEM(keep.shape, jnp.int32),
+            pltpu.SemaphoreType.DMA((steps + 3,)),
+        ],
         flops=2 * kept * query_weight.size,
-        moved=2 * query_weight.size,
+        moved=query_weight.size,
         limit=10,
     )
-    cached, sent = call(
+    sent = call(
         functools.partial(cache_kernel, spans, part_width, experts),
-        [shape((kept, latent_width), BF16), shape(((1 + heads) * kept, row_width), BF16)],
+        shape(((1 + heads) * kept, row_width), BF16),
         [VM] * (spans + 5),
         (*parts, live, near_kv, cosine, sine, query),
         limit=4,
     )
+
+    cached = call(emit_kernel, shape((kept, latent_width), BF16), [VM], (sent,), limit=4)
 
     mine_keys = jnp.stack(gathered(sent, "context", evens[1:]))
     their_keys = partner(mine_keys, "context", 1)

time: 80.2 us -> 78.9 us (0.984)
  waiting for transfers between devices: 33.4 us -> 31.3 us
    ppermute x28, waiting for transfers between devices: 33.4 us -> 31.3 us  [partner(): return lax.ppermute(values, axis, [(i, i ^ mask) for i in range(count)])]
    pallas_call x12 -> x13, Pallas kernels: 12.3 us -> 13 us  [call(): pl.pallas_call(kernel, out_shape=outs, in_specs=in_specs, out_specs=VM if...]
  transfers between devices with their start and end apart: 28 -> 28, of which waited for: 19 -> 16; matrix products, arithmetic and copies ran while one was open for 0% -> 0% of each run, Pallas kernels for 6% -> 8%
where the time goes in v4:
time: 78.9 us; the launch traced here: 78.6 us
  starting transfers between devices  33.3 us (42%)
  waiting for transfers between devices  31.3 us (40%)
  Pallas kernels  13 us (16%)
  between operations  0.83 us (1%)
    ppermute x28, starting transfers between devices, partner(): return lax.ppermute(values, axis, [(i, i ^ mask) for i in range(count)])  33.3 us
    ppermute x28, waiting for transfers between devices, partner(): return lax.ppermute(values, axis, [(i, i ^ mask) for i in range(count)])  31.3 us
    pallas_call x13, Pallas kernels, call(): pl.pallas_call(kernel, out_shape=outs, in_specs=in_specs, out_specs=VM if...  13 us
  transfers between devices with their start and end apart: 28, of which 16 were waited for; matrix products, arithmetic and copies ran while one was open for 0% of the time, Pallas kernels for 8%

profile of v4, /device:TPU:0, one launch (start us, length us, event | category | flops | bytes accessed | tf_op | source)
XLA Modules:
  0.0 78.6 jit_solution(6644540174478567808)
XLA Ops:
  0.6 1.1 %shard_map.140.refs_0_ = bf16[32,512]{1,0:T(8,128)(2,1)S(1)} custom-call(s32[1,32]{1,0:T(1,128)} %keep_hbm.3, bf16[192,512]{1,0:T(8,128)(2,1)} %raw_hbm.1), custom_call_target="tpu_custom_call" | custom-call | tf_op jit(solution)/shard_map/pallas_call | solution.py:41
  1.8 5.1 %collective-permute-start.2 = (bf16[32,512]{1,0:T(8,128)(2,1)S(1)}, bf16[32,512]{1,0:T(8,128)(2,1)S(1)}, u32[]{:S(2)}, u32[]{:S(2)}) collective-permute-start(bf16[32,512]{1,0:T(8,128)(2,1)S(1)} %shard_map.140.refs_0_), channel_id=1, source_target_pairs={{0,3},{1,2},{2,1},{3,0},{4,7},{5,6},{6,5},{7,4},{8,11},{9,10},{10,... | collective-permute-start | bytes 98312 | tf_op jit(solution)/shard_map/ppermute | solution.py:66
  7.6 1.5 %shard_map.141 = (bf16[144,2048]{1,0:T(8,128)(2,1)S(1)}, f32[1,2048]{1,0:T(1,128)S(1)}, bf16[512,1152]{1,0:T(8,128)(2,1)S(1)}, f32[8,256]{1,0:T(8,128)S(1)}) custom-call(s32[8,6]{1,0:T(8,128)} %ids_hbm.1, f32[8,6]{1,0:T(8,128)} %gates_hbm.1, s32[16]{0:T(128)} %slot_hbm.1, bf16[144,2048]{1,0:T(8,128)(2,1)} %bitcast.28, f32[1,2048]{1,0:T(1,128)} %bitcast.38, ...), custom_call_target="tpu_custom_call" | custom-call | bytes 2359296 | tf_op jit(solution)/shard_map/pallas_call | solution.py:41
  9.1 2.6 %collective-permute-done.1.refs_2_ = bf16[32,512]{1,0:T(8,128)(2,1)S(1)} collective-permute-done((bf16[32,512]{1,0:T(8,128)(2,1)S(1)}, bf16[32,512]{1,0:T(8,128)(2,1)S(1)}, u32[]{:S(2)}, u32[]{:S(2)}) %collective-permute-start.1) | collective-permute-done | bytes 32800 | tf_op jit(solution)/shard_map/ppermute | solution.py:66
  12.1 1.5 %collective-permute-start.5 = (f32[40,256]{1,0:T(8,128)S(1)}, f32[40,256]{1,0:T(8,128)S(1)}, u32[]{:S(2)}, u32[]{:S(2)}) collective-permute-start(f32[40,256]{1,0:T(8,128)S(1)} %get-tuple-element.33.refs_0_), channel_id=1, source_target_pairs={{0,3},{1,2},{2,1},{3,0},{4,7},{5,6},{6,5},{7,4},{8,11},{9,10},{10,... | collective-permute-start | bytes 122888 | tf_op jit(solution)/shard_map/ppermute | solution.py:66
  14.3 2.3 %collective-permute-start.3 = (f32[40,256]{1,0:T(8,128)S(1)}, f32[40,256]{1,0:T(8,128)S(1)}, u32[]{:S(2)}, u32[]{:S(2)}) collective-permute-start(f32[40,256]{1,0:T(8,128)S(1)} %get-tuple-element.33.refs_0_), channel_id=1, source_target_pairs={{0,1},{1,0},{2,3},{3,2},{4,5},{5,4},{6,7},{7,6},{8,9},{9,8},{10,11... | collective-permute-start | bytes 122888 | tf_op jit(solution)/shard_map/ppermute | solution.py:66
  16.6 2.9 %shard_map.143 = (bf16[64,640]{1,0:T(8,128)(2,1)S(1)}, f32[32,64]{1,0:T(8,128)S(1)}, f32[32,64]{1,0:T(8,128)S(1)}, f32[32,1]{1,0:T(8,128)S(1)}, f32[1,512]{1,0:T(1,128)S(1)}, /*index=5*/f32[1,2048]{1,0:T(1,128)S(1)}) custom-call(bf16[32,2048]{1,0:T(8,128)(2,1)S(1)} %get-tuple-element.34.normed_ref, bf16[512,1152]{1,0:T(8,128)(2,1)S(1)} %get-tuple-element.35.early_ref, ...), custom_call_target="tpu_custom_call" | custom-call | flops 150994944 | bytes 2359296 | tf_op jit(solution)/shard_map/pallas_call | solution.py:41
  19.7 2.5 %collective-permute-start.8 = (bf16[96,640]{1,0:T(8,128)(2,1)S(1)}, bf16[96,640]{1,0:T(8,128)(2,1)S(1)}, u32[]{:S(2)}, u32[]{:S(2)}) collective-permute-start(bf16[96,640]{1,0:T(8,128)(2,1)S(1)} %shard_map.144.sent_ref), channel_id=1, source_target_pairs={{0,24},{4,28},{8,16},{12,20},{16,8},{20,12},{24,0},{28,4},{1,25},{... | collective-permute-start | bytes 368648 | tf_op jit(solution)/shard_map/ppermute | solution.py:66
  23.3 2.7 %collective-permute-done.8 = bf16[96,640]{1,0:T(8,128)(2,1)S(1)} collective-permute-done((bf16[96,640]{1,0:T(8,128)(2,1)S(1)}, bf16[96,640]{1,0:T(8,128)(2,1)S(1)}, u32[]{:S(2)}, u32[]{:S(2)}) %collective-permute-start.8) | collective-permute-done | bytes 122912 | tf_op jit(solution)/shard_map/ppermute | solution.py:66
  25.9 1.3 %collective-permute-done.7 = bf16[96,640]{1,0:T(8,128)(2,1)S(1)} collective-permute-done((bf16[96,640]{1,0:T(8,128)(2,1)S(1)}, bf16[96,640]{1,0:T(8,128)(2,1)S(1)}, u32[]{:S(2)}, u32[]{:S(2)}) %collective-permute-start.7) | collective-permute-done | bytes 122912 | tf_op jit(solution)/shard_map/ppermute | solution.py:66
  27.8 1.9 %collective-permute-done.9.theirs_ref.theirs_tail_ref = bf16[4,96,640]{2,1,0:T(8,128)(2,1)S(1)} collective-permute-done((bf16[4,96,640]{2,1,0:T(8,128)(2,1)S(1)}, bf16[4,96,640]{2,1,0:T(8,128)(2,1)S(1)}, u32[]{:S(2)}, u32[]{:S(2)}) %collective-permute-start.9) | collective-permute-done | bytes 491552 | tf_op jit(solution)/shard_map/ppermute | solution.py:66
  29.6 2.0 %shard_map.145.refs_0_ = bf16[256,256]{1,0:T(8,128)(2,1)S(1)} custom-call(bf16[4,96,640]{2,1,0:T(8,128)(2,1)S(1)} %pad_maximum_fusion.2.mine_ref.mine_tail_ref, bf16[4,96,640]{2,1,0:T(8,128)(2,1)S(1)} %collective-permute-done.9.theirs_ref.theirs_tail_ref, bf16[1024,256]{1,0:T(8,128)(2,1)} %weight_hbm.3), custom_call_target="tpu_custom_call" | custom-call | flops 134217728 | bytes 524288 | tf_op jit(solution)/shard_map/pallas_call | solution.py:41
  31.6 1.9 %collective-permute-start.12 = (bf16[256,256]{1,0:T(8,128)(2,1)S(1)}, bf16[256,256]{1,0:T(8,128)(2,1)S(1)}, u32[]{:S(2)}, u32[]{:S(2)}) collective-permute-start(bf16[256,256]{1,0:T(8,128)(2,1)S(1)} %shard_map.145.refs_0_), channel_id=1, source_target_pairs={{0,3},{1,2},{2,1},{3,0},{4,7},{5,6},{6,5},{7,4},{8,11},{9,10},{10,... | collective-permute-start | bytes 393224 | tf_op jit(solution)/shard_map/ppermute | solution.py:66
  34.2 1.9 %collective-permute-start.10 = (bf16[256,256]{1,0:T(8,128)(2,1)S(1)}, bf16[256,256]{1,0:T(8,128)(2,1)S(1)}, u32[]{:S(2)}, u32[]{:S(2)}) collective-permute-start(bf16[256,256]{1,0:T(8,128)(2,1)S(1)} %shard_map.145.refs_0_), channel_id=1, source_target_pairs={{0,1},{1,0},{2,3},{3,2},{4,5},{5,4},{6,7},{7,6},{8,9},{9,8},{10,11... | collective-permute-start | bytes 393224 | tf_op jit(solution)/shard_map/ppermute | solution.py:66
  36.1 1.5 %collective-permute-start.19 = (bf16[32,2048]{1,0:T(8,128)(2,1)S(1)}, bf16[32,2048]{1,0:T(8,128)(2,1)S(1)}, u32[]{:S(2)}, u32[]{:S(2)}) collective-permute-start(bf16[32,2048]{1,0:T(8,128)(2,1)S(1)} %get-tuple-element.41), channel_id=1, source_target_pairs={{0,24},{4,28},{8,16},{12,20},{16,8},{20,12},{24,0},{28,4},{1,25},{... | collective-permute-start | bytes 393224 | tf_op jit(solution)/shard_map/ppermute | solution.py:66
  38.4 1.6 %collective-permute-done.12.refs_3_ = bf16[256,256]{1,0:T(8,128)(2,1)S(1)} collective-permute-done((bf16[256,256]{1,0:T(8,128)(2,1)S(1)}, bf16[256,256]{1,0:T(8,128)(2,1)S(1)}, u32[]{:S(2)}, u32[]{:S(2)}) %collective-permute-start.12) | collective-permute-done | bytes 131104 | tf_op jit(solution)/shard_map/ppermute | solution.py:66
  40.0 0.8 %collective-permute-start.17 = (bf16[32,2048]{1,0:T(8,128)(2,1)S(1)}, bf16[32,2048]{1,0:T(8,128)(2,1)S(1)}, u32[]{:S(2)}, u32[]{:S(2)}) collective-permute-start(bf16[32,2048]{1,0:T(8,128)(2,1)S(1)} %get-tuple-element.41), channel_id=1, source_target_pairs={{0,8},{4,12},{8,0},{12,4},{16,24},{20,28},{24,16},{28,20},{1,9},{5... | collective-permute-start | bytes 393224 | tf_op jit(solution)/shard_map/ppermute | solution.py:66
  40.9 5.3 %collective-permute-done.11.refs_2_ = bf16[256,256]{1,0:T(8,128)(2,1)S(1)} collective-permute-done((bf16[256,256]{1,0:T(8,128)(2,1)S(1)}, bf16[256,256]{1,0:T(8,128)(2,1)S(1)}, u32[]{:S(2)}, u32[]{:S(2)}) %collective-permute-start.11) | collective-permute-done | bytes 131104 | tf_op jit(solution)/shard_map/ppermute | solution.py:66
  46.2 1.6 %collective-permute-start.15 = (bf16[256,256]{1,0:T(8,128)(2,1)S(1)}, bf16[256,256]{1,0:T(8,128)(2,1)S(1)}, u32[]{:S(2)}, u32[]{:S(2)}) collective-permute-start(bf16[256,256]{1,0:T(8,128)(2,1)S(1)} %shard_map.146), channel_id=1, source_target_pairs={{0,24},{4,28},{8,16},{12,20},{16,8},{20,12},{24,0},{28,4},{1,25},{... | collective-permute-start | bytes 393224 | tf_op jit(solution)/shard_map/ppermute | solution.py:66
  48.6 1.2 %collective-permute-start.13 = (bf16[256,256]{1,0:T(8,128)(2,1)S(1)}, bf16[256,256]{1,0:T(8,128)(2,1)S(1)}, u32[]{:S(2)}, u32[]{:S(2)}) collective-permute-start(bf16[256,256]{1,0:T(8,128)(2,1)S(1)} %shard_map.146), channel_id=1, source_target_pairs={{0,8},{4,12},{8,0},{12,4},{16,24},{20,28},{24,16},{28,20},{1,9},{5... | collective-permute-start | bytes 393224 | tf_op jit(solution)/shard_map/ppermute | solution.py:66
  50.0 3.4 %collective-permute-done.15 = bf16[256,256]{1,0:T(8,128)(2,1)S(1)} collective-permute-done((bf16[256,256]{1,0:T(8,128)(2,1)S(1)}, bf16[256,256]{1,0:T(8,128)(2,1)S(1)}, u32[]{:S(2)}, u32[]{:S(2)}) %collective-permute-start.15) | collective-permute-done | bytes 131104 | tf_op jit(solution)/shard_map/ppermute | solution.py:66
  53.4 1.3 %collective-permute-done.14 = bf16[256,256]{1,0:T(8,128)(2,1)S(1)} collective-permute-done((bf16[256,256]{1,0:T(8,128)(2,1)S(1)}, bf16[256,256]{1,0:T(8,128)(2,1)S(1)}, u32[]{:S(2)}, u32[]{:S(2)}) %collective-permute-start.14) | collective-permute-done | bytes 131104 | tf_op jit(solution)/shard_map/ppermute | solution.py:66
  55.0 1.0 %shard_map.147 = (f32[32,1024]{1,0:T(8,128)S(1)}, f32[256,1]{1,0:T(8,128)S(1)}, f32[256,704]{1,0:T(8,128)S(1)}, f32[256,704]{1,0:T(8,128)S(1)}) custom-call(bf16[4,256,256]{2,1,0:T(8,128)(2,1)S(1)} %pad_maximum_fusion.mine_ref, bf16[4,32,2048]{2,1,0:T(8,128)(2,1)S(1)} %pad_maximum_fusion.1.mine_rows, ...), custom_call_target="tpu_custom_call" | custom-call | flops 738197504 | bytes 5767168 | tf_op jit(solution)/shard_map/pallas_call | solution.py:41
  56.9 2.1 %shard_map.148 = (bf16[128,2048]{1,0:T(8,128)(2,1)S(1)}, bf16[128,2048]{1,0:T(8,128)(2,1)S(1)}, f32[8,2048]{1,0:T(8,128)S(1)}) custom-call(bf16[4,256,256]{2,1,0:T(8,128)(2,1)S(1)} %collective-permute-done.16.theirs_ref, bf16[4,32,2048]{2,1,0:T(8,128)(2,1)S(1)} %pad_maximum_fusion.1.mine_rows, bf16[4,32,2048]{2,1,0:T(8,128)(2,1)S(1)} %collective-permute-done.20.their_rows, ...), custom_call_target="tpu_custom_call" | custom-call | flops 1476395008 | bytes 5767168 | tf_op jit(solution)/shard_map/pallas_call | solution.py:41
  59.2 1.8 %collective-permute-done.21.back_ref = bf16[128,2048]{1,0:T(8,128)(2,1)S(1)} collective-permute-done((bf16[128,2048]{1,0:T(8,128)(2,1)S(1)}, bf16[128,2048]{1,0:T(8,128)(2,1)S(1)}, u32[]{:S(2)}, u32[]{:S(2)}) %collective-permute-start.21) | collective-permute-done | bytes 524320 | tf_op jit(solution)/shard_map/ppermute | solution.py:66
  61.9 1.2 %collective-permute-start.23 = (bf16[32,2048]{1,0:T(8,128)(2,1)S(1)}, bf16[32,2048]{1,0:T(8,128)(2,1)S(1)}, u32[]{:S(2)}, u32[]{:S(2)}) collective-permute-start(bf16[32,2048]{1,0:T(8,128)(2,1)S(1)} %get-tuple-element.51), channel_id=1, source_target_pairs={{0,16},{4,20},{8,24},{12,28},{16,0},{20,4},{24,8},{28,12},{1,17},{... | collective-permute-start | bytes 393224 | tf_op jit(solution)/shard_map/ppermute | solution.py:66
  63.1 1.5 %collective-permute-start.24 = (bf16[32,2048]{1,0:T(8,128)(2,1)S(1)}, bf16[32,2048]{1,0:T(8,128)(2,1)S(1)}, u32[]{:S(2)}, u32[]{:S(2)}) collective-permute-start(bf16[32,2048]{1,0:T(8,128)(2,1)S(1)} %get-tuple-element.52), channel_id=1, source_target_pairs={{0,24},{4,28},{8,16},{12,20},{16,8},{20,12},{24,0},{28,4},{1,25},{... | collective-permute-start | bytes 393224 | tf_op jit(solution)/shard_map/ppermute | solution.py:66
  64.7 2.9 %collective-permute-done.22.refs_1_ = bf16[32,2048]{1,0:T(8,128)(2,1)S(1)} collective-permute-done((bf16[32,2048]{1,0:T(8,128)(2,1)S(1)}, bf16[32,2048]{1,0:T(8,128)(2,1)S(1)}, u32[]{:S(2)}, u32[]{:S(2)}) %collective-permute-start.22) | collective-permute-done | bytes 131104 | tf_op jit(solution)/shard_map/ppermute | solution.py:66
  68.0 2.0 %collective-permute-done.24.refs_3_ = bf16[32,2048]{1,0:T(8,128)(2,1)S(1)} collective-permute-done((bf16[32,2048]{1,0:T(8,128)(2,1)S(1)}, bf16[32,2048]{1,0:T(8,128)(2,1)S(1)}, u32[]{:S(2)}, u32[]{:S(2)}) %collective-permute-start.24) | collective-permute-done | bytes 131104 | tf_op jit(solution)/shard_map/ppermute | solution.py:66
  70.2 2.1 %collective-permute-start.26 = (bf16[8,2048]{1,0:T(8,128)(2,1)S(1)}, bf16[8,2048]{1,0:T(8,128)(2,1)S(1)}, u32[]{:S(2)}, u32[]{:S(2)}) collective-permute-start(bf16[8,2048]{1,0:T(8,128)(2,1)S(1)} %get-tuple-element.55), channel_id=1, source_target_pairs={{0,2},{1,3},{2,0},{3,1},{4,6},{5,7},{6,4},{7,5},{8,10},{9,11},{10,... | collective-permute-start | bytes 98312 | tf_op jit(solution)/shard_map/ppermute | solution.py:66
  72.2 2.3 %collective-permute-start.27 = (bf16[8,2048]{1,0:T(8,128)(2,1)S(1)}, bf16[8,2048]{1,0:T(8,128)(2,1)S(1)}, u32[]{:S(2)}, u32[]{:S(2)}) collective-permute-start(bf16[8,2048]{1,0:T(8,128)(2,1)S(1)} %get-tuple-element.56), channel_id=1, source_target_pairs={{0,3},{1,2},{2,1},{3,0},{4,7},{5,6},{6,5},{7,4},{8,11},{9,10},{10,... | collective-permute-start | bytes 98312 | tf_op jit(solution)/shard_map/ppermute | solution.py:66
  75.2 2.8 %collective-permute-done.27.refs_3_ = bf16[8,2048]{1,0:T(8,128)(2,1)S(1)} collective-permute-done((bf16[8,2048]{1,0:T(8,128)(2,1)S(1)}, bf16[8,2048]{1,0:T(8,128)(2,1)S(1)}, u32[]{:S(2)}, u32[]{:S(2)}) %collective-permute-start.27) | collective-permute-done | bytes 32800 | tf_op jit(solution)/shard_map/ppermute | solution.py:66
  (47 shorter events, 10.1 us)
Async XLA Ops:
  1.8 7.3 %collective-permute-start.2 = (bf16[32,512]{1,0:T(8,128)(2,1)S(1)}, bf16[32,512]{1,0:T(8,128)(2,1)S(1)}, u32[]{:S(2)}, u32[]{:S(2)}) collective-permute-start(bf16[32,512]{1,0:T(8,128)(2,1)S(1)} %shard_map.140.refs_0_), channel_id=1, source_target_pairs={{0,3},{1,2},{2,1},{3,0},{4,7},{5,6},{6,5},{7,4},{8,11},{9,10},{10,... | collective-permute-start | bytes 98312 | tf_op jit(solution)/shard_map/ppermute | solution.py:66
  6.9 4.8 %collective-permute-start.1 = (bf16[32,512]{1,0:T(8,128)(2,1)S(1)}, bf16[32,512]{1,0:T(8,128)(2,1)S(1)}, u32[]{:S(2)}, u32[]{:S(2)}) collective-permute-start(bf16[32,512]{1,0:T(8,128)(2,1)S(1)} %shard_map.140.refs_0_), channel_id=1, source_target_pairs={{0,2},{1,3},{2,0},{3,1},{4,6},{5,7},{6,4},{7,5},{8,10},{9,11},{10,... | collective-permute-start | bytes 98312 | tf_op jit(solution)/shard_map/ppermute | solution.py:66
  6.9 4.8 %collective-permute-start = (bf16[32,512]{1,0:T(8,128)(2,1)S(1)}, bf16[32,512]{1,0:T(8,128)(2,1)S(1)}, u32[]{:S(2)}, u32[]{:S(2)}) collective-permute-start(bf16[32,512]{1,0:T(8,128)(2,1)S(1)} %shard_map.140.refs_0_), channel_id=1, source_target_pairs={{0,1},{1,0},{2,3},{3,2},{4,5},{5,4},{6,7},{7,6},{8,9},{9,8},{10,11... | collective-permute-start | bytes 98312 | tf_op jit(solution)/shard_map/ppermute | solution.py:66
  12.1 7.3 %collective-permute-start.5 = (f32[40,256]{1,0:T(8,128)S(1)}, f32[40,256]{1,0:T(8,128)S(1)}, u32[]{:S(2)}, u32[]{:S(2)}) collective-permute-start(f32[40,256]{1,0:T(8,128)S(1)} %get-tuple-element.33.refs_0_), channel_id=1, source_target_pairs={{0,3},{1,2},{2,1},{3,0},{4,7},{5,6},{6,5},{7,4},{8,11},{9,10},{10,... | collective-permute-start | bytes 122888 | tf_op jit(solution)/shard_map/ppermute | solution.py:66
  13.6 5.8 %collective-permute-start.4 = (f32[40,256]{1,0:T(8,128)S(1)}, f32[40,256]{1,0:T(8,128)S(1)}, u32[]{:S(2)}, u32[]{:S(2)}) collective-permute-start(f32[40,256]{1,0:T(8,128)S(1)} %get-tuple-element.33.refs_0_), channel_id=1, source_target_pairs={{0,2},{1,3},{2,0},{3,1},{4,6},{5,7},{6,4},{7,5},{8,10},{9,11},{10,... | collective-permute-start | bytes 122888 | tf_op jit(solution)/shard_map/ppermute | solution.py:66
  14.3 5.2 %collective-permute-start.3 = (f32[40,256]{1,0:T(8,128)S(1)}, f32[40,256]{1,0:T(8,128)S(1)}, u32[]{:S(2)}, u32[]{:S(2)}) collective-permute-start(f32[40,256]{1,0:T(8,128)S(1)} %get-tuple-element.33.refs_0_), channel_id=1, source_target_pairs={{0,1},{1,0},{2,3},{3,2},{4,5},{5,4},{6,7},{7,6},{8,9},{9,8},{10,11... | collective-permute-start | bytes 122888 | tf_op jit(solution)/shard_map/ppermute | solution.py:66
  16.6 38.4 %slice-start = ((s8[5767168]{0:T(1024)(128)(4,1)}), s8[4194304]{0:T(1024)(128)(4,1)S(1)}, s32[]{:S(2)}) async-start(s8[5767168]{0:T(1024)(128)(4,1)} %bitcast.20), calls=%async_computation | async-start | bytes 8388608
  16.6 38.4 %slice-start.1 = ((s8[5767168]{0:T(1024)(128)(4,1)}), s8[1572864]{0:T(1024)(128)(4,1)S(1)}, s32[]{:S(2)}) async-start(s8[5767168]{0:T(1024)(128)(4,1)} %bitcast.20), calls=%async_computation.1 | async-start | bytes 3145728
  19.7 6.2 %collective-permute-start.8 = (bf16[96,640]{1,0:T(8,128)(2,1)S(1)}, bf16[96,640]{1,0:T(8,128)(2,1)S(1)}, u32[]{:S(2)}, u32[]{:S(2)}) collective-permute-start(bf16[96,640]{1,0:T(8,128)(2,1)S(1)} %shard_map.144.sent_ref), channel_id=1, source_target_pairs={{0,24},{4,28},{8,16},{12,20},{16,8},{20,12},{24,0},{28,4},{1,25},{... | collective-permute-start | bytes 368648 | tf_op jit(solution)/shard_map/ppermute | solution.py:66
  22.2 5.0 %collective-permute-start.7 = (bf16[96,640]{1,0:T(8,128)(2,1)S(1)}, bf16[96,640]{1,0:T(8,128)(2,1)S(1)}, u32[]{:S(2)}, u32[]{:S(2)}) collective-permute-start(bf16[96,640]{1,0:T(8,128)(2,1)S(1)} %shard_map.144.sent_ref), channel_id=1, source_target_pairs={{0,16},{4,20},{8,24},{12,28},{16,0},{20,4},{24,8},{28,12},{1,17},{... | collective-permute-start | bytes 368648 | tf_op jit(solution)/shard_map/ppermute | solution.py:66
  22.7 4.9 %collective-permute-start.6 = (bf16[96,640]{1,0:T(8,128)(2,1)S(1)}, bf16[96,640]{1,0:T(8,128)(2,1)S(1)}, u32[]{:S(2)}, u32[]{:S(2)}) collective-permute-start(bf16[96,640]{1,0:T(8,128)(2,1)S(1)} %shard_map.144.sent_ref), channel_id=1, source_target_pairs={{0,8},{4,12},{8,0},{12,4},{16,24},{20,28},{24,16},{28,20},{1,9},{5... | collective-permute-start | bytes 368648 | tf_op jit(solution)/shard_map/ppermute | solution.py:66
  27.7 1.9 %collective-permute-start.9 = (bf16[4,96,640]{2,1,0:T(8,128)(2,1)S(1)}, bf16[4,96,640]{2,1,0:T(8,128)(2,1)S(1)}, u32[]{:S(2)}, u32[]{:S(2)}) collective-permute-start(bf16[4,96,640]{2,1,0:T(8,128)(2,1)S(1)} %pad_maximum_fusion.2.mine_ref.mine_tail_ref), channel_id=1, source_target_pairs={{0,4},{4,0},{8,12},{12,8},{16,20},{20,16},{24,28},{28,24},{1,5},{5... | collective-permute-start | bytes 1474568 | tf_op jit(solution)/shard_map/ppermute | solution.py:66
  31.6 8.4 %collective-permute-start.12 = (bf16[256,256]{1,0:T(8,128)(2,1)S(1)}, bf16[256,256]{1,0:T(8,128)(2,1)S(1)}, u32[]{:S(2)}, u32[]{:S(2)}) collective-permute-start(bf16[256,256]{1,0:T(8,128)(2,1)S(1)} %shard_map.145.refs_0_), channel_id=1, source_target_pairs={{0,3},{1,2},{2,1},{3,0},{4,7},{5,6},{6,5},{7,4},{8,11},{9,10},{10,... | collective-permute-start | bytes 393224 | tf_op jit(solution)/shard_map/ppermute | solution.py:66
  33.5 12.6 %collective-permute-start.11 = (bf16[256,256]{1,0:T(8,128)(2,1)S(1)}, bf16[256,256]{1,0:T(8,128)(2,1)S(1)}, u32[]{:S(2)}, u32[]{:S(2)}) collective-permute-start(bf16[256,256]{1,0:T(8,128)(2,1)S(1)} %shard_map.145.refs_0_), channel_id=1, source_target_pairs={{0,2},{1,3},{2,0},{3,1},{4,6},{5,7},{6,4},{7,5},{8,10},{9,11},{10,... | collective-permute-start | bytes 393224 | tf_op jit(solution)/shard_map/ppermute | solution.py:66
  34.2 11.9 %collective-permute-start.10 = (bf16[256,256]{1,0:T(8,128)(2,1)S(1)}, bf16[256,256]{1,0:T(8,128)(2,1)S(1)}, u32[]{:S(2)}, u32[]{:S(2)}) collective-permute-start(bf16[256,256]{1,0:T(8,128)(2,1)S(1)} %shard_map.145.refs_0_), channel_id=1, source_target_pairs={{0,1},{1,0},{2,3},{3,2},{4,5},{5,4},{6,7},{7,6},{8,9},{9,8},{10,11... | collective-permute-start | bytes 393224 | tf_op jit(solution)/shard_map/ppermute | solution.py:66
  36.1 12.5 %collective-permute-start.19 = (bf16[32,2048]{1,0:T(8,128)(2,1)S(1)}, bf16[32,2048]{1,0:T(8,128)(2,1)S(1)}, u32[]{:S(2)}, u32[]{:S(2)}) collective-permute-start(bf16[32,2048]{1,0:T(8,128)(2,1)S(1)} %get-tuple-element.41), channel_id=1, source_target_pairs={{0,24},{4,28},{8,16},{12,20},{16,8},{20,12},{24,0},{28,4},{1,25},{... | collective-permute-start | bytes 393224 | tf_op jit(solution)/shard_map/ppermute | solution.py:66
  37.6 12.2 %collective-permute-start.18 = (bf16[32,2048]{1,0:T(8,128)(2,1)S(1)}, bf16[32,2048]{1,0:T(8,128)(2,1)S(1)}, u32[]{:S(2)}, u32[]{:S(2)}) collective-permute-start(bf16[32,2048]{1,0:T(8,128)(2,1)S(1)} %get-tuple-element.41), channel_id=1, source_target_pairs={{0,16},{4,20},{8,24},{12,28},{16,0},{20,4},{24,8},{28,12},{1,17},{... | collective-permute-start | bytes 393224 | tf_op jit(solution)/shard_map/ppermute | solution.py:66
  40.0 9.8 %collective-permute-start.17 = (bf16[32,2048]{1,0:T(8,128)(2,1)S(1)}, bf16[32,2048]{1,0:T(8,128)(2,1)S(1)}, u32[]{:S(2)}, u32[]{:S(2)}) collective-permute-start(bf16[32,2048]{1,0:T(8,128)(2,1)S(1)} %get-tuple-element.41), channel_id=1, source_target_pairs={{0,8},{4,12},{8,0},{12,4},{16,24},{20,28},{24,16},{28,20},{1,9},{5... | collective-permute-start | bytes 393224 | tf_op jit(solution)/shard_map/ppermute | solution.py:66
  46.2 7.2 %collective-permute-start.15 = (bf16[256,256]{1,0:T(8,128)(2,1)S(1)}, bf16[256,256]{1,0:T(8,128)(2,1)S(1)}, u32[]{:S(2)}, u32[]{:S(2)}) collective-permute-start(bf16[256,256]{1,0:T(8,128)(2,1)S(1)} %shard_map.146), channel_id=1, source_target_pairs={{0,24},{4,28},{8,16},{12,20},{16,8},{20,12},{24,0},{28,4},{1,25},{... | collective-permute-start | bytes 393224 | tf_op jit(solution)/shard_map/ppermute | solution.py:66
  47.8 6.9 %collective-permute-start.14 = (bf16[256,256]{1,0:T(8,128)(2,1)S(1)}, bf16[256,256]{1,0:T(8,128)(2,1)S(1)}, u32[]{:S(2)}, u32[]{:S(2)}) collective-permute-start(bf16[256,256]{1,0:T(8,128)(2,1)S(1)} %shard_map.146), channel_id=1, source_target_pairs={{0,16},{4,20},{8,24},{12,28},{16,0},{20,4},{24,8},{28,12},{1,17},{... | collective-permute-start | bytes 393224 | tf_op jit(solution)/shard_map/ppermute | solution.py:66
  48.6 6.2 %collective-permute-start.13 = (bf16[256,256]{1,0:T(8,128)(2,1)S(1)}, bf16[256,256]{1,0:T(8,128)(2,1)S(1)}, u32[]{:S(2)}, u32[]{:S(2)}) collective-permute-start(bf16[256,256]{1,0:T(8,128)(2,1)S(1)} %shard_map.146), channel_id=1, source_target_pairs={{0,8},{4,12},{8,0},{12,4},{16,24},{20,28},{24,16},{28,20},{1,9},{5... | collective-permute-start | bytes 393224 | tf_op jit(solution)/shard_map/ppermute | solution.py:66
  49.8 7.0 %copy-start = (bf16[1,704,2048]{2,1,0:T(8,128)(2,1)S(1)}, bf16[1,704,2048]{2,1,0:T(8,128)(2,1)}, u32[]{:S(2)}) copy-start(bf16[1,704,2048]{2,1,0:T(8,128)(2,1)} %param.25) | copy-start | bytes 8650756
  49.9 5.1 %collective-permute-start.20 = (bf16[4,32,2048]{2,1,0:T(8,128)(2,1)S(1)}, bf16[4,32,2048]{2,1,0:T(8,128)(2,1)S(1)}, u32[]{:S(2)}, u32[]{:S(2)}) collective-permute-start(bf16[4,32,2048]{2,1,0:T(8,128)(2,1)S(1)} %pad_maximum_fusion.1.mine_rows), channel_id=1, source_target_pairs={{0,4},{4,0},{8,12},{12,8},{16,20},{20,16},{24,28},{28,24},{1,5},{5... | collective-permute-start | bytes 1572872 | tf_op jit(solution)/shard_map/ppermute | solution.py:66
  54.9 2.0 %collective-permute-start.16 = (bf16[4,256,256]{2,1,0:T(8,128)(2,1)S(1)}, bf16[4,256,256]{2,1,0:T(8,128)(2,1)S(1)}, u32[]{:S(2)}, u32[]{:S(2)}) collective-permute-start(bf16[4,256,256]{2,1,0:T(8,128)(2,1)S(1)} %pad_maximum_fusion.mine_ref), channel_id=1, source_target_pairs={{0,4},{4,0},{8,12},{12,8},{16,20},{20,16},{24,28},{28,24},{1,5},{5... | collective-permute-start | bytes 1572872 | tf_op jit(solution)/shard_map/ppermute | solution.py:66
  59.0 2.0 %collective-permute-start.21 = (bf16[128,2048]{1,0:T(8,128)(2,1)S(1)}, bf16[128,2048]{1,0:T(8,128)(2,1)S(1)}, u32[]{:S(2)}, u32[]{:S(2)}) collective-permute-start(bf16[128,2048]{1,0:T(8,128)(2,1)S(1)} %get-tuple-element.48), channel_id=1, source_target_pairs={{0,4},{4,0},{8,12},{12,8},{16,20},{20,16},{24,28},{28,24},{1,5},{5... | collective-permute-start | bytes 1572872 | tf_op jit(solution)/shard_map/ppermute | solution.py:66
  61.1 6.4 %collective-permute-start.22 = (bf16[32,2048]{1,0:T(8,128)(2,1)S(1)}, bf16[32,2048]{1,0:T(8,128)(2,1)S(1)}, u32[]{:S(2)}, u32[]{:S(2)}) collective-permute-start(bf16[32,2048]{1,0:T(8,128)(2,1)S(1)} %get-tuple-element.50), channel_id=1, source_target_pairs={{0,8},{4,12},{8,0},{12,4},{16,24},{20,28},{24,16},{28,20},{1,9},{5... | collective-permute-start | bytes 393224 | tf_op jit(solution)/shard_map/ppermute | solution.py:66
  61.9 6.1 %collective-permute-start.23 = (bf16[32,2048]{1,0:T(8,128)(2,1)S(1)}, bf16[32,2048]{1,0:T(8,128)(2,1)S(1)}, u32[]{:S(2)}, u32[]{:S(2)}) collective-permute-start(bf16[32,2048]{1,0:T(8,128)(2,1)S(1)} %get-tuple-element.51), channel_id=1, source_target_pairs={{0,16},{4,20},{8,24},{12,28},{16,0},{20,4},{24,8},{28,12},{1,17},{... | collective-permute-start | bytes 393224 | tf_op jit(solution)/shard_map/ppermute | solution.py:66
  63.1 6.9 %collective-permute-start.24 = (bf16[32,2048]{1,0:T(8,128)(2,1)S(1)}, bf16[32,2048]{1,0:T(8,128)(2,1)S(1)}, u32[]{:S(2)}, u32[]{:S(2)}) collective-permute-start(bf16[32,2048]{1,0:T(8,128)(2,1)S(1)} %get-tuple-element.52), channel_id=1, source_target_pairs={{0,24},{4,28},{8,16},{12,20},{16,8},{20,12},{24,0},{28,4},{1,25},{... | collective-permute-start | bytes 393224 | tf_op jit(solution)/shard_map/ppermute | solution.py:66
  70.1 5.1 %collective-permute-start.25 = (bf16[8,2048]{1,0:T(8,128)(2,1)S(1)}, bf16[8,2048]{1,0:T(8,128)(2,1)S(1)}, u32[]{:S(2)}, u32[]{:S(2)}) collective-permute-start(bf16[8,2048]{1,0:T(8,128)(2,1)S(1)} %get-tuple-element.54), channel_id=1, source_target_pairs={{0,1},{1,0},{2,3},{3,2},{4,5},{5,4},{6,7},{7,6},{8,9},{9,8},{10,11... | collective-permute-start | bytes 98312 | tf_op jit(solution)/shard_map/ppermute | solution.py:66
  70.2 5.0 %collective-permute-start.26 = (bf16[8,2048]{1,0:T(8,128)(2,1)S(1)}, bf16[8,2048]{1,0:T(8,128)(2,1)S(1)}, u32[]{:S(2)}, u32[]{:S(2)}) collective-permute-start(bf16[8,2048]{1,0:T(8,128)(2,1)S(1)} %get-tuple-element.55), channel_id=1, source_target_pairs={{0,2},{1,3},{2,0},{3,1},{4,6},{5,7},{6,4},{7,5},{8,10},{9,11},{10,... | collective-permute-start | bytes 98312 | tf_op jit(solution)/shard_map/ppermute | solution.py:66
  72.2 5.7 %collective-permute-start.27 = (bf16[8,2048]{1,0:T(8,128)(2,1)S(1)}, bf16[8,2048]{1,0:T(8,128)(2,1)S(1)}, u32[]{:S(2)}, u32[]{:S(2)}) collective-permute-start(bf16[8,2048]{1,0:T(8,128)(2,1)S(1)} %get-tuple-element.56), channel_id=1, source_target_pairs={{0,3},{1,2},{2,1},{3,0},{4,7},{5,6},{6,5},{7,4},{8,11},{9,10},{10,... | collective-permute-start | bytes 98312 | tf_op jit(solution)/shard_map/ppermute | solution.py:66

commit v5 on v4

--- a/solution.py
+++ b/solution.py
@@ -259,33 +259,40 @@
     pieces = [(mine_ref, n) for n in range(half)] + [(theirs_ref, n) for n in range(half)]
 
     def gather(n):
-        return jnp.concatenate(
-            [ref[p, n * count : (n + 1) * count, :] for ref, p in pieces], axis=0
-        )
-
-    keys = gather(0)
+        return [ref[p, n * count : (n + 1) * count, :] for ref, p in pieces]
+
+    keys = jnp.concatenate(gather(0), axis=0)
     total, width = keys.shape
-    lane = lax.broadcasted_iota(jnp.int32, (8, width), 1)
-    flags = nt(jnp.where(lane == flag_lane, 1.0, 0.0).astype(BF16), keys)[0:1, :]
+    lane = lax.broadcasted_iota(jnp.int32, (16, width), 1)
+    flag_rows = jnp.where(lane == flag_lane, 1.0, 0.0).astype(BF16)
+    queries = sum([gather(1 + h) for h in range(heads)], [])
+    both = nt(jnp.concatenate(queries + [flag_rows], axis=0), keys)
+    flags = both[heads * total : heads * total + 1, :]
+    shift = count.bit_length() - 1
 
     def slot(dims, axis):
         line = lax.broadcasted_iota(jnp.int32, dims, axis)
-        at = line // count
+        if count == 1 << shift:
+            at, rest = line >> shift, line & (count - 1)
+        else:
+            at, rest = line // count, line % count
         which = jnp.where(at < half, 2 * at, 2 * (at - half) + 1)
-        return (which ^ index) * count + line % count
+        return (which ^ index) * count + rest
 
     allowed = (slot((1, total), 1) <= slot((total, 1), 0)) & (flags > 0)
-    result = jnp.zeros(out_ref.shape, F32)
+    weights, shares = [], []
     for h in range(heads):
-        scores = nt(gather(1 + h), keys) * SCALE
+        scores = both[h * total : (h + 1) * total, :] * SCALE
         scores = jnp.where(allowed, scores, NEGATIVE)
         highest = jnp.max(scores, axis=1, keepdims=True)
         weight = jnp.where(allowed, jnp.exp(scores - highest), 0.0)
-        denominator = jnp.sum(weight, axis=1, keepdims=True)
-        summed = nn(weight.astype(BF16), keys[:, :kv_rank])
-        mixed = (summed / denominator).astype(BF16)
-        if h == 0:
-            copy.wait()
+        shares.append(1.0 / jnp.sum(weight, axis=1, keepdims=True))
+        weights.append(weight.astype(BF16))
+    summed = nn(jnp.concatenate(weights, axis=0), keys[:, :kv_rank])
+    copy.wait()
+    result = jnp.zeros(out_ref.shape, F32)
+    for h in range(heads):
+        mixed = (summed[h * total : (h + 1) * total] * shares[h]).astype(BF16)
         result = result + nn(mixed, weight_ref[h * kv_rank : (h + 1) * kv_rank, :])
     out_ref[...] = result.astype(BF16)
 
@@ -580,13 +587,16 @@
         limit=12,
     )
 
-    column = call(
-        sum_kernel,
-        shape(partial.shape, BF16),
-        [VM] * spans,
-        gathered(partial, "span", range(1, spans)),
-        limit=4,
-    )
+    column, bit = partial, 1
+    while bit < spans:
+        column = call(
+            sum_kernel,
+            shape(partial.shape, BF16),
+            [VM] * 2,
+            gathered(column, "span", [bit]),
+            limit=4,
+        )
+        bit *= 2
     mine_rows = jnp.stack(gathered(compact, "context", evens[1:]))
     their_rows = partner(mine_rows, "context", 1)
 
@@ -649,7 +659,9 @@
         (near, partner(far, "context", 1)),
         limit=6,
     )
-    got = [partner(level, "context", i) for level, i in zip(levels[1:], evens[1:])]
+    got = []
+    for level, i in zip(levels[1:], evens[1:]):
+        got.append(partner(level, "context", i))
     rows = call(
         functools.partial(rows_kernel, spans),
         [shape((rows_dev, model), F32)] + [shape((rows_dev, model), BF16)] * (spans - 1),

time: 78.9 us -> 79.5 us (level)
  waiting for transfers between devices: 31.3 us -> 33.5 us
  starting transfers between devices: 33.3 us -> 31.5 us
    ppermute x28 -> x27, waiting for transfers between devices: 31.3 us -> 33.5 us  [partner(): return lax.ppermute(values, axis, [(i, i ^ mask) for i in range(count)])]
    ppermute x28 -> x27, starting transfers between devices: 33.3 us -> 31.5 us  [partner(): return lax.ppermute(values, axis, [(i, i ^ mask) for i in range(count)])]
    pallas_call x13 -> x14, Pallas kernels: 13 us -> 13.2 us  [call(): pl.pallas_call(kernel, out_shape=outs, in_specs=in_specs, out_specs=VM if...]
  transfers between devices with their start and end apart: 28 -> 27, of which waited for: 16 -> 16; matrix products, arithmetic and copies ran while one was open for 0% -> 0% of each run, Pallas kernels for 8% -> 8%
where the time goes in v5:
time: 79.5 us; the launch traced here: 79.3 us
  waiting for transfers between devices  33.5 us (42%)
  starting transfers between devices  31.5 us (40%)
  Pallas kernels  13.2 us (17%)
  between operations  0.83 us (1%)
    ppermute x27, waiting for transfers between devices, partner(): return lax.ppermute(values, axis, [(i, i ^ mask) for i in range(count)])  33.5 us
    ppermute x27, starting transfers between devices, partner(): return lax.ppermute(values, axis, [(i, i ^ mask) for i in range(count)])  31.5 us
    pallas_call x14, Pallas kernels, call(): pl.pallas_call(kernel, out_shape=outs, in_specs=in_specs, out_specs=VM if...  13.2 us
  transfers between devices with their start and end apart: 27, of which 16 were waited for; matrix products, arithmetic and copies ran while one was open for 0% of the time, Pallas kernels for 8%

profile of v5, /device:TPU:0, one launch (start us, length us, event | category | flops | bytes accessed | tf_op | source)
XLA Modules:
  0.0 79.3 jit_solution(18167068015950758186)
XLA Ops:
  0.6 1.1 %shard_map.140.refs_0_ = bf16[32,512]{1,0:T(8,128)(2,1)S(1)} custom-call(s32[1,32]{1,0:T(1,128)} %keep_hbm.3, bf16[192,512]{1,0:T(8,128)(2,1)} %raw_hbm.1), custom_call_target="tpu_custom_call" | custom-call | tf_op jit(solution)/shard_map/pallas_call | solution.py:41
  1.8 5.1 %collective-permute-start.2 = (bf16[32,512]{1,0:T(8,128)(2,1)S(1)}, bf16[32,512]{1,0:T(8,128)(2,1)S(1)}, u32[]{:S(2)}, u32[]{:S(2)}) collective-permute-start(bf16[32,512]{1,0:T(8,128)(2,1)S(1)} %shard_map.140.refs_0_), channel_id=1, source_target_pairs={{0,3},{1,2},{2,1},{3,0},{4,7},{5,6},{6,5},{7,4},{8,11},{9,10},{10,... | collective-permute-start | bytes 98312 | tf_op jit(solution)/shard_map/ppermute | solution.py:66
  7.6 1.5 %shard_map.141 = (bf16[144,2048]{1,0:T(8,128)(2,1)S(1)}, f32[1,2048]{1,0:T(1,128)S(1)}, bf16[512,1152]{1,0:T(8,128)(2,1)S(1)}, f32[8,256]{1,0:T(8,128)S(1)}) custom-call(s32[8,6]{1,0:T(8,128)} %ids_hbm.1, f32[8,6]{1,0:T(8,128)} %gates_hbm.1, s32[16]{0:T(128)} %slot_hbm.1, bf16[144,2048]{1,0:T(8,128)(2,1)} %bitcast.28, f32[1,2048]{1,0:T(1,128)} %bitcast.38, ...), custom_call_target="tpu_custom_call" | custom-call | bytes 2359296 | tf_op jit(solution)/shard_map/pallas_call | solution.py:41
  9.1 2.6 %collective-permute-done.1.refs_2_ = bf16[32,512]{1,0:T(8,128)(2,1)S(1)} collective-permute-done((bf16[32,512]{1,0:T(8,128)(2,1)S(1)}, bf16[32,512]{1,0:T(8,128)(2,1)S(1)}, u32[]{:S(2)}, u32[]{:S(2)}) %collective-permute-start.1) | collective-permute-done | bytes 32800 | tf_op jit(solution)/shard_map/ppermute | solution.py:66
  12.1 1.5 %collective-permute-start.5 = (f32[40,256]{1,0:T(8,128)S(1)}, f32[40,256]{1,0:T(8,128)S(1)}, u32[]{:S(2)}, u32[]{:S(2)}) collective-permute-start(f32[40,256]{1,0:T(8,128)S(1)} %get-tuple-element.33.refs_0_), channel_id=1, source_target_pairs={{0,3},{1,2},{2,1},{3,0},{4,7},{5,6},{6,5},{7,4},{8,11},{9,10},{10,... | collective-permute-start | bytes 122888 | tf_op jit(solution)/shard_map/ppermute | solution.py:66
  14.3 2.3 %collective-permute-start.3 = (f32[40,256]{1,0:T(8,128)S(1)}, f32[40,256]{1,0:T(8,128)S(1)}, u32[]{:S(2)}, u32[]{:S(2)}) collective-permute-start(f32[40,256]{1,0:T(8,128)S(1)} %get-tuple-element.33.refs_0_), channel_id=1, source_target_pairs={{0,1},{1,0},{2,3},{3,2},{4,5},{5,4},{6,7},{7,6},{8,9},{9,8},{10,11... | collective-permute-start | bytes 122888 | tf_op jit(solution)/shard_map/ppermute | solution.py:66
  16.6 2.9 %shard_map.143 = (bf16[64,640]{1,0:T(8,128)(2,1)S(1)}, f32[32,64]{1,0:T(8,128)S(1)}, f32[32,64]{1,0:T(8,128)S(1)}, f32[32,1]{1,0:T(8,128)S(1)}, f32[1,512]{1,0:T(1,128)S(1)}, /*index=5*/f32[1,2048]{1,0:T(1,128)S(1)}) custom-call(bf16[32,2048]{1,0:T(8,128)(2,1)S(1)} %get-tuple-element.34.normed_ref, bf16[512,1152]{1,0:T(8,128)(2,1)S(1)} %get-tuple-element.35.early_ref, ...), custom_call_target="tpu_custom_call" | custom-call | flops 150994944 | bytes 2359296 | tf_op jit(solution)/shard_map/pallas_call | solution.py:41
  19.7 2.5 %collective-permute-start.8 = (bf16[96,640]{1,0:T(8,128)(2,1)S(1)}, bf16[96,640]{1,0:T(8,128)(2,1)S(1)}, u32[]{:S(2)}, u32[]{:S(2)}) collective-permute-start(bf16[96,640]{1,0:T(8,128)(2,1)S(1)} %shard_map.144.sent_ref), channel_id=1, source_target_pairs={{0,24},{4,28},{8,16},{12,20},{16,8},{20,12},{24,0},{28,4},{1,25},{... | collective-permute-start | bytes 368648 | tf_op jit(solution)/shard_map/ppermute | solution.py:66
  23.3 2.7 %collective-permute-done.8 = bf16[96,640]{1,0:T(8,128)(2,1)S(1)} collective-permute-done((bf16[96,640]{1,0:T(8,128)(2,1)S(1)}, bf16[96,640]{1,0:T(8,128)(2,1)S(1)}, u32[]{:S(2)}, u32[]{:S(2)}) %collective-permute-start.8) | collective-permute-done | bytes 122912 | tf_op jit(solution)/shard_map/ppermute | solution.py:66
  25.9 1.3 %collective-permute-done.7 = bf16[96,640]{1,0:T(8,128)(2,1)S(1)} collective-permute-done((bf16[96,640]{1,0:T(8,128)(2,1)S(1)}, bf16[96,640]{1,0:T(8,128)(2,1)S(1)}, u32[]{:S(2)}, u32[]{:S(2)}) %collective-permute-start.7) | collective-permute-done | bytes 122912 | tf_op jit(solution)/shard_map/ppermute | solution.py:66
  27.8 1.9 %collective-permute-done.9.theirs_ref.theirs_tail_ref = bf16[4,96,640]{2,1,0:T(8,128)(2,1)S(1)} collective-permute-done((bf16[4,96,640]{2,1,0:T(8,128)(2,1)S(1)}, bf16[4,96,640]{2,1,0:T(8,128)(2,1)S(1)}, u32[]{:S(2)}, u32[]{:S(2)}) %collective-permute-start.9) | collective-permute-done | bytes 491552 | tf_op jit(solution)/shard_map/ppermute | solution.py:66
  29.6 2.2 %shard_map.145.refs_0_ = bf16[256,256]{1,0:T(8,128)(2,1)S(1)} custom-call(bf16[4,96,640]{2,1,0:T(8,128)(2,1)S(1)} %pad_maximum_fusion.2.mine_ref.mine_tail_ref, bf16[4,96,640]{2,1,0:T(8,128)(2,1)S(1)} %collective-permute-done.9.theirs_ref.theirs_tail_ref, bf16[1024,256]{1,0:T(8,128)(2,1)} %weight_hbm.3), custom_call_target="tpu_custom_call" | custom-call | flops 134217728 | bytes 524288 | tf_op jit(solution)/shard_map/pallas_call | solution.py:41
  31.9 1.1 %collective-permute-start.10 = (bf16[256,256]{1,0:T(8,128)(2,1)S(1)}, bf16[256,256]{1,0:T(8,128)(2,1)S(1)}, u32[]{:S(2)}, u32[]{:S(2)}) collective-permute-start(bf16[256,256]{1,0:T(8,128)(2,1)S(1)} %shard_map.145.refs_0_), channel_id=1, source_target_pairs={{0,1},{1,0},{2,3},{3,2},{4,5},{5,4},{6,7},{7,6},{8,9},{9,8},{10,11... | collective-permute-start | bytes 393224 | tf_op jit(solution)/shard_map/ppermute | solution.py:66
  33.0 4.5 %collective-permute-done.10.refs_1_ = bf16[256,256]{1,0:T(8,128)(2,1)S(1)} collective-permute-done((bf16[256,256]{1,0:T(8,128)(2,1)S(1)}, bf16[256,256]{1,0:T(8,128)(2,1)S(1)}, u32[]{:S(2)}, u32[]{:S(2)}) %collective-permute-start.10) | collective-permute-done | bytes 131104 | tf_op jit(solution)/shard_map/ppermute | solution.py:66
  37.5 1.2 %collective-permute-start.11 = (bf16[256,256]{1,0:T(8,128)(2,1)S(1)}, bf16[256,256]{1,0:T(8,128)(2,1)S(1)}, u32[]{:S(2)}, u32[]{:S(2)}) collective-permute-start(bf16[256,256]{1,0:T(8,128)(2,1)S(1)} %shard_map.146.refs_0_), channel_id=1, source_target_pairs={{0,2},{1,3},{2,0},{3,1},{4,6},{5,7},{6,4},{7,5},{8,10},{9,11},{10,... | collective-permute-start | bytes 393224 | tf_op jit(solution)/shard_map/ppermute | solution.py:66
  38.7 1.5 %collective-permute-start.18 = (bf16[32,2048]{1,0:T(8,128)(2,1)S(1)}, bf16[32,2048]{1,0:T(8,128)(2,1)S(1)}, u32[]{:S(2)}, u32[]{:S(2)}) collective-permute-start(bf16[32,2048]{1,0:T(8,128)(2,1)S(1)} %get-tuple-element.41), channel_id=1, source_target_pairs={{0,24},{4,28},{8,16},{12,20},{16,8},{20,12},{24,0},{28,4},{1,25},{... | collective-permute-start | bytes 393224 | tf_op jit(solution)/shard_map/ppermute | solution.py:66
  41.0 1.2 %collective-permute-start.16 = (bf16[32,2048]{1,0:T(8,128)(2,1)S(1)}, bf16[32,2048]{1,0:T(8,128)(2,1)S(1)}, u32[]{:S(2)}, u32[]{:S(2)}) collective-permute-start(bf16[32,2048]{1,0:T(8,128)(2,1)S(1)} %get-tuple-element.41), channel_id=1, source_target_pairs={{0,8},{4,12},{8,0},{12,4},{16,24},{20,28},{24,16},{28,20},{1,9},{5... | collective-permute-start | bytes 393224 | tf_op jit(solution)/shard_map/ppermute | solution.py:66
  42.2 3.8 %collective-permute-done.11.refs_1_ = bf16[256,256]{1,0:T(8,128)(2,1)S(1)} collective-permute-done((bf16[256,256]{1,0:T(8,128)(2,1)S(1)}, bf16[256,256]{1,0:T(8,128)(2,1)S(1)}, u32[]{:S(2)}, u32[]{:S(2)}) %collective-permute-start.11) | collective-permute-done | bytes 131104 | tf_op jit(solution)/shard_map/ppermute | solution.py:66
  46.0 1.6 %collective-permute-start.14 = (bf16[256,256]{1,0:T(8,128)(2,1)S(1)}, bf16[256,256]{1,0:T(8,128)(2,1)S(1)}, u32[]{:S(2)}, u32[]{:S(2)}) collective-permute-start(bf16[256,256]{1,0:T(8,128)(2,1)S(1)} %shard_map.147), channel_id=1, source_target_pairs={{0,24},{4,28},{8,16},{12,20},{16,8},{20,12},{24,0},{28,4},{1,25},{... | collective-permute-start | bytes 393224 | tf_op jit(solution)/shard_map/ppermute | solution.py:66
  48.4 1.2 %collective-permute-start.12 = (bf16[256,256]{1,0:T(8,128)(2,1)S(1)}, bf16[256,256]{1,0:T(8,128)(2,1)S(1)}, u32[]{:S(2)}, u32[]{:S(2)}) collective-permute-start(bf16[256,256]{1,0:T(8,128)(2,1)S(1)} %shard_map.147), channel_id=1, source_target_pairs={{0,8},{4,12},{8,0},{12,4},{16,24},{20,28},{24,16},{28,20},{1,9},{5... | collective-permute-start | bytes 393224 | tf_op jit(solution)/shard_map/ppermute | solution.py:66
  49.7 3.6 %collective-permute-done.14 = bf16[256,256]{1,0:T(8,128)(2,1)S(1)} collective-permute-done((bf16[256,256]{1,0:T(8,128)(2,1)S(1)}, bf16[256,256]{1,0:T(8,128)(2,1)S(1)}, u32[]{:S(2)}, u32[]{:S(2)}) %collective-permute-start.14) | collective-permute-done | bytes 131104 | tf_op jit(solution)/shard_map/ppermute | solution.py:66
  53.3 1.4 %collective-permute-done.13 = bf16[256,256]{1,0:T(8,128)(2,1)S(1)} collective-permute-done((bf16[256,256]{1,0:T(8,128)(2,1)S(1)}, bf16[256,256]{1,0:T(8,128)(2,1)S(1)}, u32[]{:S(2)}, u32[]{:S(2)}) %collective-permute-start.13) | collective-permute-done | bytes 131104 | tf_op jit(solution)/shard_map/ppermute | solution.py:66
  55.0 1.0 %shard_map.148 = (f32[32,1024]{1,0:T(8,128)S(1)}, f32[256,1]{1,0:T(8,128)S(1)}, f32[256,704]{1,0:T(8,128)S(1)}, f32[256,704]{1,0:T(8,128)S(1)}) custom-call(bf16[4,256,256]{2,1,0:T(8,128)(2,1)S(1)} %pad_maximum_fusion.mine_ref, bf16[4,32,2048]{2,1,0:T(8,128)(2,1)S(1)} %pad_maximum_fusion.1.mine_rows, ...), custom_call_target="tpu_custom_call" | custom-call | flops 738197504 | bytes 5767168 | tf_op jit(solution)/shard_map/pallas_call | solution.py:41
  56.8 2.1 %shard_map.149 = (bf16[128,2048]{1,0:T(8,128)(2,1)S(1)}, bf16[128,2048]{1,0:T(8,128)(2,1)S(1)}, f32[8,2048]{1,0:T(8,128)S(1)}) custom-call(bf16[4,256,256]{2,1,0:T(8,128)(2,1)S(1)} %collective-permute-done.15.theirs_ref, bf16[4,32,2048]{2,1,0:T(8,128)(2,1)S(1)} %pad_maximum_fusion.1.mine_rows, bf16[4,32,2048]{2,1,0:T(8,128)(2,1)S(1)} %collective-permute-done.19.their_rows, ...), custom_call_target="tpu_custom_call" | custom-call | flops 1476395008 | bytes 5767168 | tf_op jit(solution)/shard_map/pallas_call | solution.py:41
  59.2 1.8 %collective-permute-done.20.back_ref = bf16[128,2048]{1,0:T(8,128)(2,1)S(1)} collective-permute-done((bf16[128,2048]{1,0:T(8,128)(2,1)S(1)}, bf16[128,2048]{1,0:T(8,128)(2,1)S(1)}, u32[]{:S(2)}, u32[]{:S(2)}) %collective-permute-start.20) | collective-permute-done | bytes 524320 | tf_op jit(solution)/shard_map/ppermute | solution.py:66
  61.9 1.2 %collective-permute-start.22 = (bf16[32,2048]{1,0:T(8,128)(2,1)S(1)}, bf16[32,2048]{1,0:T(8,128)(2,1)S(1)}, u32[]{:S(2)}, u32[]{:S(2)}) collective-permute-start(bf16[32,2048]{1,0:T(8,128)(2,1)S(1)} %get-tuple-element.51), channel_id=1, source_target_pairs={{0,16},{4,20},{8,24},{12,28},{16,0},{20,4},{24,8},{28,12},{1,17},{... | collective-permute-start | bytes 393224 | tf_op jit(solution)/shard_map/ppermute | solution.py:66
  63.1 1.5 %collective-permute-start.23 = (bf16[32,2048]{1,0:T(8,128)(2,1)S(1)}, bf16[32,2048]{1,0:T(8,128)(2,1)S(1)}, u32[]{:S(2)}, u32[]{:S(2)}) collective-permute-start(bf16[32,2048]{1,0:T(8,128)(2,1)S(1)} %get-tuple-element.52), channel_id=1, source_target_pairs={{0,24},{4,28},{8,16},{12,20},{16,8},{20,12},{24,0},{28,4},{1,25},{... | collective-permute-start | bytes 393224 | tf_op jit(solution)/shard_map/ppermute | solution.py:66
  64.6 2.9 %collective-permute-done.21.refs_1_ = bf16[32,2048]{1,0:T(8,128)(2,1)S(1)} collective-permute-done((bf16[32,2048]{1,0:T(8,128)(2,1)S(1)}, bf16[32,2048]{1,0:T(8,128)(2,1)S(1)}, u32[]{:S(2)}, u32[]{:S(2)}) %collective-permute-start.21) | collective-permute-done | bytes 131104 | tf_op jit(solution)/shard_map/ppermute | solution.py:66
  68.0 2.0 %collective-permute-done.23.refs_3_ = bf16[32,2048]{1,0:T(8,128)(2,1)S(1)} collective-permute-done((bf16[32,2048]{1,0:T(8,128)(2,1)S(1)}, bf16[32,2048]{1,0:T(8,128)(2,1)S(1)}, u32[]{:S(2)}, u32[]{:S(2)}) %collective-permute-start.23) | collective-permute-done | bytes 131104 | tf_op jit(solution)/shard_map/ppermute | solution.py:66
  70.1 2.7 %collective-permute-start.25 = (bf16[8,2048]{1,0:T(8,128)(2,1)S(1)}, bf16[8,2048]{1,0:T(8,128)(2,1)S(1)}, u32[]{:S(2)}, u32[]{:S(2)}) collective-permute-start(bf16[8,2048]{1,0:T(8,128)(2,1)S(1)} %get-tuple-element.55), channel_id=1, source_target_pairs={{0,2},{1,3},{2,0},{3,1},{4,6},{5,7},{6,4},{7,5},{8,10},{9,11},{10,... | collective-permute-start | bytes 98312 | tf_op jit(solution)/shard_map/ppermute | solution.py:66
  72.9 1.7 %collective-permute-start.26 = (bf16[8,2048]{1,0:T(8,128)(2,1)S(1)}, bf16[8,2048]{1,0:T(8,128)(2,1)S(1)}, u32[]{:S(2)}, u32[]{:S(2)}) collective-permute-start(bf16[8,2048]{1,0:T(8,128)(2,1)S(1)} %get-tuple-element.56), channel_id=1, source_target_pairs={{0,3},{1,2},{2,1},{3,0},{4,7},{5,6},{6,5},{7,4},{8,11},{9,10},{10,... | collective-permute-start | bytes 98312 | tf_op jit(solution)/shard_map/ppermute | solution.py:66
  75.2 3.4 %collective-permute-done.26.refs_3_ = bf16[8,2048]{1,0:T(8,128)(2,1)S(1)} collective-permute-done((bf16[8,2048]{1,0:T(8,128)(2,1)S(1)}, bf16[8,2048]{1,0:T(8,128)(2,1)S(1)}, u32[]{:S(2)}, u32[]{:S(2)}) %collective-permute-start.26) | collective-permute-done | bytes 32800 | tf_op jit(solution)/shard_map/ppermute | solution.py:66
  (46 shorter events, 9.4 us)
Async XLA Ops:
  1.8 7.3 %collective-permute-start.2 = (bf16[32,512]{1,0:T(8,128)(2,1)S(1)}, bf16[32,512]{1,0:T(8,128)(2,1)S(1)}, u32[]{:S(2)}, u32[]{:S(2)}) collective-permute-start(bf16[32,512]{1,0:T(8,128)(2,1)S(1)} %shard_map.140.refs_0_), channel_id=1, source_target_pairs={{0,3},{1,2},{2,1},{3,0},{4,7},{5,6},{6,5},{7,4},{8,11},{9,10},{10,... | collective-permute-start | bytes 98312 | tf_op jit(solution)/shard_map/ppermute | solution.py:66
  6.9 4.8 %collective-permute-start.1 = (bf16[32,512]{1,0:T(8,128)(2,1)S(1)}, bf16[32,512]{1,0:T(8,128)(2,1)S(1)}, u32[]{:S(2)}, u32[]{:S(2)}) collective-permute-start(bf16[32,512]{1,0:T(8,128)(2,1)S(1)} %shard_map.140.refs_0_), channel_id=1, source_target_pairs={{0,2},{1,3},{2,0},{3,1},{4,6},{5,7},{6,4},{7,5},{8,10},{9,11},{10,... | collective-permute-start | bytes 98312 | tf_op jit(solution)/shard_map/ppermute | solution.py:66
  6.9 4.8 %collective-permute-start = (bf16[32,512]{1,0:T(8,128)(2,1)S(1)}, bf16[32,512]{1,0:T(8,128)(2,1)S(1)}, u32[]{:S(2)}, u32[]{:S(2)}) collective-permute-start(bf16[32,512]{1,0:T(8,128)(2,1)S(1)} %shard_map.140.refs_0_), channel_id=1, source_target_pairs={{0,1},{1,0},{2,3},{3,2},{4,5},{5,4},{6,7},{7,6},{8,9},{9,8},{10,11... | collective-permute-start | bytes 98312 | tf_op jit(solution)/shard_map/ppermute | solution.py:66
  12.1 7.3 %collective-permute-start.5 = (f32[40,256]{1,0:T(8,128)S(1)}, f32[40,256]{1,0:T(8,128)S(1)}, u32[]{:S(2)}, u32[]{:S(2)}) collective-permute-start(f32[40,256]{1,0:T(8,128)S(1)} %get-tuple-element.33.refs_0_), channel_id=1, source_target_pairs={{0,3},{1,2},{2,1},{3,0},{4,7},{5,6},{6,5},{7,4},{8,11},{9,10},{10,... | collective-permute-start | bytes 122888 | tf_op jit(solution)/shard_map/ppermute | solution.py:66
  13.6 5.8 %collective-permute-start.4 = (f32[40,256]{1,0:T(8,128)S(1)}, f32[40,256]{1,0:T(8,128)S(1)}, u32[]{:S(2)}, u32[]{:S(2)}) collective-permute-start(f32[40,256]{1,0:T(8,128)S(1)} %get-tuple-element.33.refs_0_), channel_id=1, source_target_pairs={{0,2},{1,3},{2,0},{3,1},{4,6},{5,7},{6,4},{7,5},{8,10},{9,11},{10,... | collective-permute-start | bytes 122888 | tf_op jit(solution)/shard_map/ppermute | solution.py:66
  14.3 5.2 %collective-permute-start.3 = (f32[40,256]{1,0:T(8,128)S(1)}, f32[40,256]{1,0:T(8,128)S(1)}, u32[]{:S(2)}, u32[]{:S(2)}) collective-permute-start(f32[40,256]{1,0:T(8,128)S(1)} %get-tuple-element.33.refs_0_), channel_id=1, source_target_pairs={{0,1},{1,0},{2,3},{3,2},{4,5},{5,4},{6,7},{7,6},{8,9},{9,8},{10,11... | collective-permute-start | bytes 122888 | tf_op jit(solution)/shard_map/ppermute | solution.py:66
  16.6 38.4 %slice-start = ((s8[5767168]{0:T(1024)(128)(4,1)}), s8[4194304]{0:T(1024)(128)(4,1)S(1)}, s32[]{:S(2)}) async-start(s8[5767168]{0:T(1024)(128)(4,1)} %bitcast.20), calls=%async_computation | async-start | bytes 8388608
  16.6 38.4 %slice-start.1 = ((s8[5767168]{0:T(1024)(128)(4,1)}), s8[1572864]{0:T(1024)(128)(4,1)S(1)}, s32[]{:S(2)}) async-start(s8[5767168]{0:T(1024)(128)(4,1)} %bitcast.20), calls=%async_computation.1 | async-start | bytes 3145728
  19.7 6.2 %collective-permute-start.8 = (bf16[96,640]{1,0:T(8,128)(2,1)S(1)}, bf16[96,640]{1,0:T(8,128)(2,1)S(1)}, u32[]{:S(2)}, u32[]{:S(2)}) collective-permute-start(bf16[96,640]{1,0:T(8,128)(2,1)S(1)} %shard_map.144.sent_ref), channel_id=1, source_target_pairs={{0,24},{4,28},{8,16},{12,20},{16,8},{20,12},{24,0},{28,4},{1,25},{... | collective-permute-start | bytes 368648 | tf_op jit(solution)/shard_map/ppermute | solution.py:66
  22.2 5.0 %collective-permute-start.7 = (bf16[96,640]{1,0:T(8,128)(2,1)S(1)}, bf16[96,640]{1,0:T(8,128)(2,1)S(1)}, u32[]{:S(2)}, u32[]{:S(2)}) collective-permute-start(bf16[96,640]{1,0:T(8,128)(2,1)S(1)} %shard_map.144.sent_ref), channel_id=1, source_target_pairs={{0,16},{4,20},{8,24},{12,28},{16,0},{20,4},{24,8},{28,12},{1,17},{... | collective-permute-start | bytes 368648 | tf_op jit(solution)/shard_map/ppermute | solution.py:66
  22.7 4.9 %collective-permute-start.6 = (bf16[96,640]{1,0:T(8,128)(2,1)S(1)}, bf16[96,640]{1,0:T(8,128)(2,1)S(1)}, u32[]{:S(2)}, u32[]{:S(2)}) collective-permute-start(bf16[96,640]{1,0:T(8,128)(2,1)S(1)} %shard_map.144.sent_ref), channel_id=1, source_target_pairs={{0,8},{4,12},{8,0},{12,4},{16,24},{20,28},{24,16},{28,20},{1,9},{5... | collective-permute-start | bytes 368648 | tf_op jit(solution)/shard_map/ppermute | solution.py:66
  27.7 1.9 %collective-permute-start.9 = (bf16[4,96,640]{2,1,0:T(8,128)(2,1)S(1)}, bf16[4,96,640]{2,1,0:T(8,128)(2,1)S(1)}, u32[]{:S(2)}, u32[]{:S(2)}) collective-permute-start(bf16[4,96,640]{2,1,0:T(8,128)(2,1)S(1)} %pad_maximum_fusion.2.mine_ref.mine_tail_ref), channel_id=1, source_target_pairs={{0,4},{4,0},{8,12},{12,8},{16,20},{20,16},{24,28},{28,24},{1,5},{5... | collective-permute-start | bytes 1474568 | tf_op jit(solution)/shard_map/ppermute | solution.py:66
  31.9 5.6 %collective-permute-start.10 = (bf16[256,256]{1,0:T(8,128)(2,1)S(1)}, bf16[256,256]{1,0:T(8,128)(2,1)S(1)}, u32[]{:S(2)}, u32[]{:S(2)}) collective-permute-start(bf16[256,256]{1,0:T(8,128)(2,1)S(1)} %shard_map.145.refs_0_), channel_id=1, source_target_pairs={{0,1},{1,0},{2,3},{3,2},{4,5},{5,4},{6,7},{7,6},{8,9},{9,8},{10,11... | collective-permute-start | bytes 393224 | tf_op jit(solution)/shard_map/ppermute | solution.py:66
  37.5 8.5 %collective-permute-start.11 = (bf16[256,256]{1,0:T(8,128)(2,1)S(1)}, bf16[256,256]{1,0:T(8,128)(2,1)S(1)}, u32[]{:S(2)}, u32[]{:S(2)}) collective-permute-start(bf16[256,256]{1,0:T(8,128)(2,1)S(1)} %shard_map.146.refs_0_), channel_id=1, source_target_pairs={{0,2},{1,3},{2,0},{3,1},{4,6},{5,7},{6,4},{7,5},{8,10},{9,11},{10,... | collective-permute-start | bytes 393224 | tf_op jit(solution)/shard_map/ppermute | solution.py:66
  38.7 9.7 %collective-permute-start.18 = (bf16[32,2048]{1,0:T(8,128)(2,1)S(1)}, bf16[32,2048]{1,0:T(8,128)(2,1)S(1)}, u32[]{:S(2)}, u32[]{:S(2)}) collective-permute-start(bf16[32,2048]{1,0:T(8,128)(2,1)S(1)} %get-tuple-element.41), channel_id=1, source_target_pairs={{0,24},{4,28},{8,16},{12,20},{16,8},{20,12},{24,0},{28,4},{1,25},{... | collective-permute-start | bytes 393224 | tf_op jit(solution)/shard_map/ppermute | solution.py:66
  40.2 9.4 %collective-permute-start.17 = (bf16[32,2048]{1,0:T(8,128)(2,1)S(1)}, bf16[32,2048]{1,0:T(8,128)(2,1)S(1)}, u32[]{:S(2)}, u32[]{:S(2)}) collective-permute-start(bf16[32,2048]{1,0:T(8,128)(2,1)S(1)} %get-tuple-element.41), channel_id=1, source_target_pairs={{0,16},{4,20},{8,24},{12,28},{16,0},{20,4},{24,8},{28,12},{1,17},{... | collective-permute-start | bytes 393224 | tf_op jit(solution)/shard_map/ppermute | solution.py:66
  41.0 8.6 %collective-permute-start.16 = (bf16[32,2048]{1,0:T(8,128)(2,1)S(1)}, bf16[32,2048]{1,0:T(8,128)(2,1)S(1)}, u32[]{:S(2)}, u32[]{:S(2)}) collective-permute-start(bf16[32,2048]{1,0:T(8,128)(2,1)S(1)} %get-tuple-element.41), channel_id=1, source_target_pairs={{0,8},{4,12},{8,0},{12,4},{16,24},{20,28},{24,16},{28,20},{1,9},{5... | collective-permute-start | bytes 393224 | tf_op jit(solution)/shard_map/ppermute | solution.py:66
  46.0 7.3 %collective-permute-start.14 = (bf16[256,256]{1,0:T(8,128)(2,1)S(1)}, bf16[256,256]{1,0:T(8,128)(2,1)S(1)}, u32[]{:S(2)}, u32[]{:S(2)}) collective-permute-start(bf16[256,256]{1,0:T(8,128)(2,1)S(1)} %shard_map.147), channel_id=1, source_target_pairs={{0,24},{4,28},{8,16},{12,20},{16,8},{20,12},{24,0},{28,4},{1,25},{... | collective-permute-start | bytes 393224 | tf_op jit(solution)/shard_map/ppermute | solution.py:66
  47.6 7.1 %collective-permute-start.13 = (bf16[256,256]{1,0:T(8,128)(2,1)S(1)}, bf16[256,256]{1,0:T(8,128)(2,1)S(1)}, u32[]{:S(2)}, u32[]{:S(2)}) collective-permute-start(bf16[256,256]{1,0:T(8,128)(2,1)S(1)} %shard_map.147), channel_id=1, source_target_pairs={{0,16},{4,20},{8,24},{12,28},{16,0},{20,4},{24,8},{28,12},{1,17},{... | collective-permute-start | bytes 393224 | tf_op jit(solution)/shard_map/ppermute | solution.py:66
  48.4 6.4 %collective-permute-start.12 = (bf16[256,256]{1,0:T(8,128)(2,1)S(1)}, bf16[256,256]{1,0:T(8,128)(2,1)S(1)}, u32[]{:S(2)}, u32[]{:S(2)}) collective-permute-start(bf16[256,256]{1,0:T(8,128)(2,1)S(1)} %shard_map.147), channel_id=1, source_target_pairs={{0,8},{4,12},{8,0},{12,4},{16,24},{20,28},{24,16},{28,20},{1,9},{5... | collective-permute-start | bytes 393224 | tf_op jit(solution)/shard_map/ppermute | solution.py:66
  49.6 7.3 %copy-start = (bf16[1,704,2048]{2,1,0:T(8,128)(2,1)S(1)}, bf16[1,704,2048]{2,1,0:T(8,128)(2,1)}, u32[]{:S(2)}) copy-start(bf16[1,704,2048]{2,1,0:T(8,128)(2,1)} %param.25) | copy-start | bytes 8650756
  49.7 5.3 %collective-permute-start.19 = (bf16[4,32,2048]{2,1,0:T(8,128)(2,1)S(1)}, bf16[4,32,2048]{2,1,0:T(8,128)(2,1)S(1)}, u32[]{:S(2)}, u32[]{:S(2)}) collective-permute-start(bf16[4,32,2048]{2,1,0:T(8,128)(2,1)S(1)} %pad_maximum_fusion.1.mine_rows), channel_id=1, source_target_pairs={{0,4},{4,0},{8,12},{12,8},{16,20},{20,16},{24,28},{28,24},{1,5},{5... | collective-permute-start | bytes 1572872 | tf_op jit(solution)/shard_map/ppermute | solution.py:66
  54.9 2.0 %collective-permute-start.15 = (bf16[4,256,256]{2,1,0:T(8,128)(2,1)S(1)}, bf16[4,256,256]{2,1,0:T(8,128)(2,1)S(1)}, u32[]{:S(2)}, u32[]{:S(2)}) collective-permute-start(bf16[4,256,256]{2,1,0:T(8,128)(2,1)S(1)} %pad_maximum_fusion.mine_ref), channel_id=1, source_target_pairs={{0,4},{4,0},{8,12},{12,8},{16,20},{20,16},{24,28},{28,24},{1,5},{5... | collective-permute-start | bytes 1572872 | tf_op jit(solution)/shard_map/ppermute | solution.py:66
  59.0 2.0 %collective-permute-start.20 = (bf16[128,2048]{1,0:T(8,128)(2,1)S(1)}, bf16[128,2048]{1,0:T(8,128)(2,1)S(1)}, u32[]{:S(2)}, u32[]{:S(2)}) collective-permute-start(bf16[128,2048]{1,0:T(8,128)(2,1)S(1)} %get-tuple-element.48), channel_id=1, source_target_pairs={{0,4},{4,0},{8,12},{12,8},{16,20},{20,16},{24,28},{28,24},{1,5},{5... | collective-permute-start | bytes 1572872 | tf_op jit(solution)/shard_map/ppermute | solution.py:66
  61.1 6.4 %collective-permute-start.21 = (bf16[32,2048]{1,0:T(8,128)(2,1)S(1)}, bf16[32,2048]{1,0:T(8,128)(2,1)S(1)}, u32[]{:S(2)}, u32[]{:S(2)}) collective-permute-start(bf16[32,2048]{1,0:T(8,128)(2,1)S(1)} %get-tuple-element.50), channel_id=1, source_target_pairs={{0,8},{4,12},{8,0},{12,4},{16,24},{20,28},{24,16},{28,20},{1,9},{5... | collective-permute-start | bytes 393224 | tf_op jit(solution)/shard_map/ppermute | solution.py:66
  61.9 6.1 %collective-permute-start.22 = (bf16[32,2048]{1,0:T(8,128)(2,1)S(1)}, bf16[32,2048]{1,0:T(8,128)(2,1)S(1)}, u32[]{:S(2)}, u32[]{:S(2)}) collective-permute-start(bf16[32,2048]{1,0:T(8,128)(2,1)S(1)} %get-tuple-element.51), channel_id=1, source_target_pairs={{0,16},{4,20},{8,24},{12,28},{16,0},{20,4},{24,8},{28,12},{1,17},{... | collective-permute-start | bytes 393224 | tf_op jit(solution)/shard_map/ppermute | solution.py:66
  63.1 6.9 %collective-permute-start.23 = (bf16[32,2048]{1,0:T(8,128)(2,1)S(1)}, bf16[32,2048]{1,0:T(8,128)(2,1)S(1)}, u32[]{:S(2)}, u32[]{:S(2)}) collective-permute-start(bf16[32,2048]{1,0:T(8,128)(2,1)S(1)} %get-tuple-element.52), channel_id=1, source_target_pairs={{0,24},{4,28},{8,16},{12,20},{16,8},{20,12},{24,0},{28,4},{1,25},{... | collective-permute-start | bytes 393224 | tf_op jit(solution)/shard_map/ppermute | solution.py:66
  70.1 5.1 %collective-permute-start.24 = (bf16[8,2048]{1,0:T(8,128)(2,1)S(1)}, bf16[8,2048]{1,0:T(8,128)(2,1)S(1)}, u32[]{:S(2)}, u32[]{:S(2)}) collective-permute-start(bf16[8,2048]{1,0:T(8,128)(2,1)S(1)} %get-tuple-element.54), channel_id=1, source_target_pairs={{0,1},{1,0},{2,3},{3,2},{4,5},{5,4},{6,7},{7,6},{8,9},{9,8},{10,11... | collective-permute-start | bytes 98312 | tf_op jit(solution)/shard_map/ppermute | solution.py:66
  70.1 5.0 %collective-permute-start.25 = (bf16[8,2048]{1,0:T(8,128)(2,1)S(1)}, bf16[8,2048]{1,0:T(8,128)(2,1)S(1)}, u32[]{:S(2)}, u32[]{:S(2)}) collective-permute-start(bf16[8,2048]{1,0:T(8,128)(2,1)S(1)} %get-tuple-element.55), channel_id=1, source_target_pairs={{0,2},{1,3},{2,0},{3,1},{4,6},{5,7},{6,4},{7,5},{8,10},{9,11},{10,... | collective-permute-start | bytes 98312 | tf_op jit(solution)/shard_map/ppermute | solution.py:66
  72.9 5.7 %collective-permute-start.26 = (bf16[8,2048]{1,0:T(8,128)(2,1)S(1)}, bf16[8,2048]{1,0:T(8,128)(2,1)S(1)}, u32[]{:S(2)}, u32[]{:S(2)}) collective-permute-start(bf16[8,2048]{1,0:T(8,128)(2,1)S(1)} %get-tuple-element.56), channel_id=1, source_target_pairs={{0,3},{1,2},{2,1},{3,0},{4,7},{5,6},{6,5},{7,4},{8,11},{9,10},{10,... | collective-permute-start | bytes 98312 | tf_op jit(solution)/shard_map/ppermute | solution.py:66

commit v6 on v5

--- a/solution.py
+++ b/solution.py
@@ -259,15 +259,15 @@
     pieces = [(mine_ref, n) for n in range(half)] + [(theirs_ref, n) for n in range(half)]
 
     def gather(n):
-        return [ref[p, n * count : (n + 1) * count, :] for ref, p in pieces]
-
-    keys = jnp.concatenate(gather(0), axis=0)
+        return jnp.concatenate(
+            [ref[p, n * count : (n + 1) * count, :] for ref, p in pieces], axis=0
+        )
+
+    keys = gather(0)
     total, width = keys.shape
-    lane = lax.broadcasted_iota(jnp.int32, (16, width), 1)
-    flag_rows = jnp.where(lane == flag_lane, 1.0, 0.0).astype(BF16)
-    queries = sum([gather(1 + h) for h in range(heads)], [])
-    both = nt(jnp.concatenate(queries + [flag_rows], axis=0), keys)
-    flags = both[heads * total : heads * total + 1, :]
+    lane = lax.broadcasted_iota(jnp.int32, (8, width), 1)
+    flags = nt(jnp.where(lane == flag_lane, 1.0, 0.0).astype(BF16), keys)[0:1, :]
+
     shift = count.bit_length() - 1
 
     def slot(dims, axis):
@@ -280,19 +280,17 @@
         return (which ^ index) * count + rest
 
     allowed = (slot((1, total), 1) <= slot((total, 1), 0)) & (flags > 0)
-    weights, shares = [], []
+    result = jnp.zeros(out_ref.shape, F32)
     for h in range(heads):
-        scores = both[h * total : (h + 1) * total, :] * SCALE
+        scores = nt(gather(1 + h), keys) * SCALE
         scores = jnp.where(allowed, scores, NEGATIVE)
         highest = jnp.max(scores, axis=1, keepdims=True)
         weight = jnp.where(allowed, jnp.exp(scores - highest), 0.0)
-        shares.append(1.0 / jnp.sum(weight, axis=1, keepdims=True))
-        weights.append(weight.astype(BF16))
-    summed = nn(jnp.concatenate(weights, axis=0), keys[:, :kv_rank])
-    copy.wait()
-    result = jnp.zeros(out_ref.shape, F32)
-    for h in range(heads):
-        mixed = (summed[h * total : (h + 1) * total] * shares[h]).astype(BF16)
+        share = 1.0 / jnp.sum(weight, axis=1, keepdims=True)
+        summed = nn(weight.astype(BF16), keys[:, :kv_rank])
+        mixed = (summed * share).astype(BF16)
+        if h == 0:
+            copy.wait()
         result = result + nn(mixed, weight_ref[h * kv_rank : (h + 1) * kv_rank, :])
     out_ref[...] = result.astype(BF16)
 

time: 79.5 us -> 79.2 us (level)
  no operation moved by 1% of the time
where the time goes in v6:
time: 79.2 us; the launch traced here: 79 us
  waiting for transfers between devices  33.5 us (42%)
  starting transfers between devices  31.5 us (40%)
  Pallas kernels  13 us (16%)
  between operations  0.83 us (1%)
    ppermute x27, waiting for transfers between devices, partner(): return lax.ppermute(values, axis, [(i, i ^ mask) for i in range(count)])  33.5 us
    ppermute x27, starting transfers between devices, partner(): return lax.ppermute(values, axis, [(i, i ^ mask) for i in range(count)])  31.5 us
    pallas_call x14, Pallas kernels, call(): pl.pallas_call(kernel, out_shape=outs, in_specs=in_specs, out_specs=VM if...  13 us
  transfers between devices with their start and end apart: 27, of which 16 were waited for; matrix products, arithmetic and copies ran while one was open for 0% of the time, Pallas kernels for 8%

profile of v6, /device:TPU:0, one launch (start us, length us, event | category | flops | bytes accessed | tf_op | source)
XLA Modules:
  0.0 79.0 jit_solution(2422382613977880240)
XLA Ops:
  0.6 1.1 %shard_map.140.refs_0_ = bf16[32,512]{1,0:T(8,128)(2,1)S(1)} custom-call(s32[1,32]{1,0:T(1,128)} %keep_hbm.3, bf16[192,512]{1,0:T(8,128)(2,1)} %raw_hbm.1), custom_call_target="tpu_custom_call" | custom-call | tf_op jit(solution)/shard_map/pallas_call | solution.py:41
  1.8 5.1 %collective-permute-start.2 = (bf16[32,512]{1,0:T(8,128)(2,1)S(1)}, bf16[32,512]{1,0:T(8,128)(2,1)S(1)}, u32[]{:S(2)}, u32[]{:S(2)}) collective-permute-start(bf16[32,512]{1,0:T(8,128)(2,1)S(1)} %shard_map.140.refs_0_), channel_id=1, source_target_pairs={{0,3},{1,2},{2,1},{3,0},{4,7},{5,6},{6,5},{7,4},{8,11},{9,10},{10,... | collective-permute-start | bytes 98312 | tf_op jit(solution)/shard_map/ppermute | solution.py:66
  7.6 1.5 %shard_map.141 = (bf16[144,2048]{1,0:T(8,128)(2,1)S(1)}, f32[1,2048]{1,0:T(1,128)S(1)}, bf16[512,1152]{1,0:T(8,128)(2,1)S(1)}, f32[8,256]{1,0:T(8,128)S(1)}) custom-call(s32[8,6]{1,0:T(8,128)} %ids_hbm.1, f32[8,6]{1,0:T(8,128)} %gates_hbm.1, s32[16]{0:T(128)} %slot_hbm.1, bf16[144,2048]{1,0:T(8,128)(2,1)} %bitcast.28, f32[1,2048]{1,0:T(1,128)} %bitcast.38, ...), custom_call_target="tpu_custom_call" | custom-call | bytes 2359296 | tf_op jit(solution)/shard_map/pallas_call | solution.py:41
  9.1 2.6 %collective-permute-done.1.refs_2_ = bf16[32,512]{1,0:T(8,128)(2,1)S(1)} collective-permute-done((bf16[32,512]{1,0:T(8,128)(2,1)S(1)}, bf16[32,512]{1,0:T(8,128)(2,1)S(1)}, u32[]{:S(2)}, u32[]{:S(2)}) %collective-permute-start.1) | collective-permute-done | bytes 32800 | tf_op jit(solution)/shard_map/ppermute | solution.py:66
  12.1 1.5 %collective-permute-start.5 = (f32[40,256]{1,0:T(8,128)S(1)}, f32[40,256]{1,0:T(8,128)S(1)}, u32[]{:S(2)}, u32[]{:S(2)}) collective-permute-start(f32[40,256]{1,0:T(8,128)S(1)} %get-tuple-element.33.refs_0_), channel_id=1, source_target_pairs={{0,3},{1,2},{2,1},{3,0},{4,7},{5,6},{6,5},{7,4},{8,11},{9,10},{10,... | collective-permute-start | bytes 122888 | tf_op jit(solution)/shard_map/ppermute | solution.py:66
  14.3 2.3 %collective-permute-start.3 = (f32[40,256]{1,0:T(8,128)S(1)}, f32[40,256]{1,0:T(8,128)S(1)}, u32[]{:S(2)}, u32[]{:S(2)}) collective-permute-start(f32[40,256]{1,0:T(8,128)S(1)} %get-tuple-element.33.refs_0_), channel_id=1, source_target_pairs={{0,1},{1,0},{2,3},{3,2},{4,5},{5,4},{6,7},{7,6},{8,9},{9,8},{10,11... | collective-permute-start | bytes 122888 | tf_op jit(solution)/shard_map/ppermute | solution.py:66
  16.6 2.9 %shard_map.143 = (bf16[64,640]{1,0:T(8,128)(2,1)S(1)}, f32[32,64]{1,0:T(8,128)S(1)}, f32[32,64]{1,0:T(8,128)S(1)}, f32[32,1]{1,0:T(8,128)S(1)}, f32[1,512]{1,0:T(1,128)S(1)}, /*index=5*/f32[1,2048]{1,0:T(1,128)S(1)}) custom-call(bf16[32,2048]{1,0:T(8,128)(2,1)S(1)} %get-tuple-element.34.normed_ref, bf16[512,1152]{1,0:T(8,128)(2,1)S(1)} %get-tuple-element.35.early_ref, ...), custom_call_target="tpu_custom_call" | custom-call | flops 150994944 | bytes 2359296 | tf_op jit(solution)/shard_map/pallas_call | solution.py:41
  19.7 2.5 %collective-permute-start.8 = (bf16[96,640]{1,0:T(8,128)(2,1)S(1)}, bf16[96,640]{1,0:T(8,128)(2,1)S(1)}, u32[]{:S(2)}, u32[]{:S(2)}) collective-permute-start(bf16[96,640]{1,0:T(8,128)(2,1)S(1)} %shard_map.144.sent_ref), channel_id=1, source_target_pairs={{0,24},{4,28},{8,16},{12,20},{16,8},{20,12},{24,0},{28,4},{1,25},{... | collective-permute-start | bytes 368648 | tf_op jit(solution)/shard_map/ppermute | solution.py:66
  23.3 2.7 %collective-permute-done.8 = bf16[96,640]{1,0:T(8,128)(2,1)S(1)} collective-permute-done((bf16[96,640]{1,0:T(8,128)(2,1)S(1)}, bf16[96,640]{1,0:T(8,128)(2,1)S(1)}, u32[]{:S(2)}, u32[]{:S(2)}) %collective-permute-start.8) | collective-permute-done | bytes 122912 | tf_op jit(solution)/shard_map/ppermute | solution.py:66
  25.9 1.3 %collective-permute-done.7 = bf16[96,640]{1,0:T(8,128)(2,1)S(1)} collective-permute-done((bf16[96,640]{1,0:T(8,128)(2,1)S(1)}, bf16[96,640]{1,0:T(8,128)(2,1)S(1)}, u32[]{:S(2)}, u32[]{:S(2)}) %collective-permute-start.7) | collective-permute-done | bytes 122912 | tf_op jit(solution)/shard_map/ppermute | solution.py:66
  27.8 1.9 %collective-permute-done.9.theirs_ref.theirs_tail_ref = bf16[4,96,640]{2,1,0:T(8,128)(2,1)S(1)} collective-permute-done((bf16[4,96,640]{2,1,0:T(8,128)(2,1)S(1)}, bf16[4,96,640]{2,1,0:T(8,128)(2,1)S(1)}, u32[]{:S(2)}, u32[]{:S(2)}) %collective-permute-start.9) | collective-permute-done | bytes 491552 | tf_op jit(solution)/shard_map/ppermute | solution.py:66
  29.6 2.0 %shard_map.145.refs_0_ = bf16[256,256]{1,0:T(8,128)(2,1)S(1)} custom-call(bf16[4,96,640]{2,1,0:T(8,128)(2,1)S(1)} %pad_maximum_fusion.2.mine_ref.mine_tail_ref, bf16[4,96,640]{2,1,0:T(8,128)(2,1)S(1)} %collective-permute-done.9.theirs_ref.theirs_tail_ref, bf16[1024,256]{1,0:T(8,128)(2,1)} %weight_hbm.3), custom_call_target="tpu_custom_call" | custom-call | flops 134217728 | bytes 524288 | tf_op jit(solution)/shard_map/pallas_call | solution.py:41
  31.6 1.1 %collective-permute-start.10 = (bf16[256,256]{1,0:T(8,128)(2,1)S(1)}, bf16[256,256]{1,0:T(8,128)(2,1)S(1)}, u32[]{:S(2)}, u32[]{:S(2)}) collective-permute-start(bf16[256,256]{1,0:T(8,128)(2,1)S(1)} %shard_map.145.refs_0_), channel_id=1, source_target_pairs={{0,1},{1,0},{2,3},{3,2},{4,5},{5,4},{6,7},{7,6},{8,9},{9,8},{10,11... | collective-permute-start | bytes 393224 | tf_op jit(solution)/shard_map/ppermute | solution.py:66
  32.8 4.5 %collective-permute-done.10.refs_1_ = bf16[256,256]{1,0:T(8,128)(2,1)S(1)} collective-permute-done((bf16[256,256]{1,0:T(8,128)(2,1)S(1)}, bf16[256,256]{1,0:T(8,128)(2,1)S(1)}, u32[]{:S(2)}, u32[]{:S(2)}) %collective-permute-start.10) | collective-permute-done | bytes 131104 | tf_op jit(solution)/shard_map/ppermute | solution.py:66
  37.3 1.2 %collective-permute-start.11 = (bf16[256,256]{1,0:T(8,128)(2,1)S(1)}, bf16[256,256]{1,0:T(8,128)(2,1)S(1)}, u32[]{:S(2)}, u32[]{:S(2)}) collective-permute-start(bf16[256,256]{1,0:T(8,128)(2,1)S(1)} %shard_map.146.refs_0_), channel_id=1, source_target_pairs={{0,2},{1,3},{2,0},{3,1},{4,6},{5,7},{6,4},{7,5},{8,10},{9,11},{10,... | collective-permute-start | bytes 393224 | tf_op jit(solution)/shard_map/ppermute | solution.py:66
  38.5 1.5 %collective-permute-start.18 = (bf16[32,2048]{1,0:T(8,128)(2,1)S(1)}, bf16[32,2048]{1,0:T(8,128)(2,1)S(1)}, u32[]{:S(2)}, u32[]{:S(2)}) collective-permute-start(bf16[32,2048]{1,0:T(8,128)(2,1)S(1)} %get-tuple-element.41), channel_id=1, source_target_pairs={{0,24},{4,28},{8,16},{12,20},{16,8},{20,12},{24,0},{28,4},{1,25},{... | collective-permute-start | bytes 393224 | tf_op jit(solution)/shard_map/ppermute | solution.py:66
  40.8 1.2 %collective-permute-start.16 = (bf16[32,2048]{1,0:T(8,128)(2,1)S(1)}, bf16[32,2048]{1,0:T(8,128)(2,1)S(1)}, u32[]{:S(2)}, u32[]{:S(2)}) collective-permute-start(bf16[32,2048]{1,0:T(8,128)(2,1)S(1)} %get-tuple-element.41), channel_id=1, source_target_pairs={{0,8},{4,12},{8,0},{12,4},{16,24},{20,28},{24,16},{28,20},{1,9},{5... | collective-permute-start | bytes 393224 | tf_op jit(solution)/shard_map/ppermute | solution.py:66
  42.0 3.8 %collective-permute-done.11.refs_1_ = bf16[256,256]{1,0:T(8,128)(2,1)S(1)} collective-permute-done((bf16[256,256]{1,0:T(8,128)(2,1)S(1)}, bf16[256,256]{1,0:T(8,128)(2,1)S(1)}, u32[]{:S(2)}, u32[]{:S(2)}) %collective-permute-start.11) | collective-permute-done | bytes 131104 | tf_op jit(solution)/shard_map/ppermute | solution.py:66
  45.8 1.6 %collective-permute-start.14 = (bf16[256,256]{1,0:T(8,128)(2,1)S(1)}, bf16[256,256]{1,0:T(8,128)(2,1)S(1)}, u32[]{:S(2)}, u32[]{:S(2)}) collective-permute-start(bf16[256,256]{1,0:T(8,128)(2,1)S(1)} %shard_map.147), channel_id=1, source_target_pairs={{0,24},{4,28},{8,16},{12,20},{16,8},{20,12},{24,0},{28,4},{1,25},{... | collective-permute-start | bytes 393224 | tf_op jit(solution)/shard_map/ppermute | solution.py:66
  48.2 1.2 %collective-permute-start.12 = (bf16[256,256]{1,0:T(8,128)(2,1)S(1)}, bf16[256,256]{1,0:T(8,128)(2,1)S(1)}, u32[]{:S(2)}, u32[]{:S(2)}) collective-permute-start(bf16[256,256]{1,0:T(8,128)(2,1)S(1)} %shard_map.147), channel_id=1, source_target_pairs={{0,8},{4,12},{8,0},{12,4},{16,24},{20,28},{24,16},{28,20},{1,9},{5... | collective-permute-start | bytes 393224 | tf_op jit(solution)/shard_map/ppermute | solution.py:66
  49.5 3.6 %collective-permute-done.14 = bf16[256,256]{1,0:T(8,128)(2,1)S(1)} collective-permute-done((bf16[256,256]{1,0:T(8,128)(2,1)S(1)}, bf16[256,256]{1,0:T(8,128)(2,1)S(1)}, u32[]{:S(2)}, u32[]{:S(2)}) %collective-permute-start.14) | collective-permute-done | bytes 131104 | tf_op jit(solution)/shard_map/ppermute | solution.py:66
  53.1 1.4 %collective-permute-done.13 = bf16[256,256]{1,0:T(8,128)(2,1)S(1)} collective-permute-done((bf16[256,256]{1,0:T(8,128)(2,1)S(1)}, bf16[256,256]{1,0:T(8,128)(2,1)S(1)}, u32[]{:S(2)}, u32[]{:S(2)}) %collective-permute-start.13) | collective-permute-done | bytes 131104 | tf_op jit(solution)/shard_map/ppermute | solution.py:66
  54.7 1.0 %shard_map.148 = (f32[32,1024]{1,0:T(8,128)S(1)}, f32[256,1]{1,0:T(8,128)S(1)}, f32[256,704]{1,0:T(8,128)S(1)}, f32[256,704]{1,0:T(8,128)S(1)}) custom-call(bf16[4,256,256]{2,1,0:T(8,128)(2,1)S(1)} %pad_maximum_fusion.mine_ref, bf16[4,32,2048]{2,1,0:T(8,128)(2,1)S(1)} %pad_maximum_fusion.1.mine_rows, ...), custom_call_target="tpu_custom_call" | custom-call | flops 738197504 | bytes 5767168 | tf_op jit(solution)/shard_map/pallas_call | solution.py:41
  56.6 2.1 %shard_map.149 = (bf16[128,2048]{1,0:T(8,128)(2,1)S(1)}, bf16[128,2048]{1,0:T(8,128)(2,1)S(1)}, f32[8,2048]{1,0:T(8,128)S(1)}) custom-call(bf16[4,256,256]{2,1,0:T(8,128)(2,1)S(1)} %collective-permute-done.15.theirs_ref, bf16[4,32,2048]{2,1,0:T(8,128)(2,1)S(1)} %pad_maximum_fusion.1.mine_rows, bf16[4,32,2048]{2,1,0:T(8,128)(2,1)S(1)} %collective-permute-done.19.their_rows, ...), custom_call_target="tpu_custom_call" | custom-call | flops 1476395008 | bytes 5767168 | tf_op jit(solution)/shard_map/pallas_call | solution.py:41
  58.9 1.8 %collective-permute-done.20.back_ref = bf16[128,2048]{1,0:T(8,128)(2,1)S(1)} collective-permute-done((bf16[128,2048]{1,0:T(8,128)(2,1)S(1)}, bf16[128,2048]{1,0:T(8,128)(2,1)S(1)}, u32[]{:S(2)}, u32[]{:S(2)}) %collective-permute-start.20) | collective-permute-done | bytes 524320 | tf_op jit(solution)/shard_map/ppermute | solution.py:66
  61.7 1.2 %collective-permute-start.22 = (bf16[32,2048]{1,0:T(8,128)(2,1)S(1)}, bf16[32,2048]{1,0:T(8,128)(2,1)S(1)}, u32[]{:S(2)}, u32[]{:S(2)}) collective-permute-start(bf16[32,2048]{1,0:T(8,128)(2,1)S(1)} %get-tuple-element.51), channel_id=1, source_target_pairs={{0,16},{4,20},{8,24},{12,28},{16,0},{20,4},{24,8},{28,12},{1,17},{... | collective-permute-start | bytes 393224 | tf_op jit(solution)/shard_map/ppermute | solution.py:66
  62.9 1.5 %collective-permute-start.23 = (bf16[32,2048]{1,0:T(8,128)(2,1)S(1)}, bf16[32,2048]{1,0:T(8,128)(2,1)S(1)}, u32[]{:S(2)}, u32[]{:S(2)}) collective-permute-start(bf16[32,2048]{1,0:T(8,128)(2,1)S(1)} %get-tuple-element.52), channel_id=1, source_target_pairs={{0,24},{4,28},{8,16},{12,20},{16,8},{20,12},{24,0},{28,4},{1,25},{... | collective-permute-start | bytes 393224 | tf_op jit(solution)/shard_map/ppermute | solution.py:66
  64.4 2.9 %collective-permute-done.21.refs_1_ = bf16[32,2048]{1,0:T(8,128)(2,1)S(1)} collective-permute-done((bf16[32,2048]{1,0:T(8,128)(2,1)S(1)}, bf16[32,2048]{1,0:T(8,128)(2,1)S(1)}, u32[]{:S(2)}, u32[]{:S(2)}) %collective-permute-start.21) | collective-permute-done | bytes 131104 | tf_op jit(solution)/shard_map/ppermute | solution.py:66
  67.8 2.0 %collective-permute-done.23.refs_3_ = bf16[32,2048]{1,0:T(8,128)(2,1)S(1)} collective-permute-done((bf16[32,2048]{1,0:T(8,128)(2,1)S(1)}, bf16[32,2048]{1,0:T(8,128)(2,1)S(1)}, u32[]{:S(2)}, u32[]{:S(2)}) %collective-permute-start.23) | collective-permute-done | bytes 131104 | tf_op jit(solution)/shard_map/ppermute | solution.py:66
  69.9 2.7 %collective-permute-start.25 = (bf16[8,2048]{1,0:T(8,128)(2,1)S(1)}, bf16[8,2048]{1,0:T(8,128)(2,1)S(1)}, u32[]{:S(2)}, u32[]{:S(2)}) collective-permute-start(bf16[8,2048]{1,0:T(8,128)(2,1)S(1)} %get-tuple-element.55), channel_id=1, source_target_pairs={{0,2},{1,3},{2,0},{3,1},{4,6},{5,7},{6,4},{7,5},{8,10},{9,11},{10,... | collective-permute-start | bytes 98312 | tf_op jit(solution)/shard_map/ppermute | solution.py:66
  72.6 1.7 %collective-permute-start.26 = (bf16[8,2048]{1,0:T(8,128)(2,1)S(1)}, bf16[8,2048]{1,0:T(8,128)(2,1)S(1)}, u32[]{:S(2)}, u32[]{:S(2)}) collective-permute-start(bf16[8,2048]{1,0:T(8,128)(2,1)S(1)} %get-tuple-element.56), channel_id=1, source_target_pairs={{0,3},{1,2},{2,1},{3,0},{4,7},{5,6},{6,5},{7,4},{8,11},{9,10},{10,... | collective-permute-start | bytes 98312 | tf_op jit(solution)/shard_map/ppermute | solution.py:66
  74.9 3.4 %collective-permute-done.26.refs_3_ = bf16[8,2048]{1,0:T(8,128)(2,1)S(1)} collective-permute-done((bf16[8,2048]{1,0:T(8,128)(2,1)S(1)}, bf16[8,2048]{1,0:T(8,128)(2,1)S(1)}, u32[]{:S(2)}, u32[]{:S(2)}) %collective-permute-start.26) | collective-permute-done | bytes 32800 | tf_op jit(solution)/shard_map/ppermute | solution.py:66
  (46 shorter events, 9.4 us)
Async XLA Ops:
  1.8 7.3 %collective-permute-start.2 = (bf16[32,512]{1,0:T(8,128)(2,1)S(1)}, bf16[32,512]{1,0:T(8,128)(2,1)S(1)}, u32[]{:S(2)}, u32[]{:S(2)}) collective-permute-start(bf16[32,512]{1,0:T(8,128)(2,1)S(1)} %shard_map.140.refs_0_), channel_id=1, source_target_pairs={{0,3},{1,2},{2,1},{3,0},{4,7},{5,6},{6,5},{7,4},{8,11},{9,10},{10,... | collective-permute-start | bytes 98312 | tf_op jit(solution)/shard_map/ppermute | solution.py:66
  6.9 4.8 %collective-permute-start.1 = (bf16[32,512]{1,0:T(8,128)(2,1)S(1)}, bf16[32,512]{1,0:T(8,128)(2,1)S(1)}, u32[]{:S(2)}, u32[]{:S(2)}) collective-permute-start(bf16[32,512]{1,0:T(8,128)(2,1)S(1)} %shard_map.140.refs_0_), channel_id=1, source_target_pairs={{0,2},{1,3},{2,0},{3,1},{4,6},{5,7},{6,4},{7,5},{8,10},{9,11},{10,... | collective-permute-start | bytes 98312 | tf_op jit(solution)/shard_map/ppermute | solution.py:66
  6.9 4.8 %collective-permute-start = (bf16[32,512]{1,0:T(8,128)(2,1)S(1)}, bf16[32,512]{1,0:T(8,128)(2,1)S(1)}, u32[]{:S(2)}, u32[]{:S(2)}) collective-permute-start(bf16[32,512]{1,0:T(8,128)(2,1)S(1)} %shard_map.140.refs_0_), channel_id=1, source_target_pairs={{0,1},{1,0},{2,3},{3,2},{4,5},{5,4},{6,7},{7,6},{8,9},{9,8},{10,11... | collective-permute-start | bytes 98312 | tf_op jit(solution)/shard_map/ppermute | solution.py:66
  12.1 7.3 %collective-permute-start.5 = (f32[40,256]{1,0:T(8,128)S(1)}, f32[40,256]{1,0:T(8,128)S(1)}, u32[]{:S(2)}, u32[]{:S(2)}) collective-permute-start(f32[40,256]{1,0:T(8,128)S(1)} %get-tuple-element.33.refs_0_), channel_id=1, source_target_pairs={{0,3},{1,2},{2,1},{3,0},{4,7},{5,6},{6,5},{7,4},{8,11},{9,10},{10,... | collective-permute-start | bytes 122888 | tf_op jit(solution)/shard_map/ppermute | solution.py:66
  13.6 5.8 %collective-permute-start.4 = (f32[40,256]{1,0:T(8,128)S(1)}, f32[40,256]{1,0:T(8,128)S(1)}, u32[]{:S(2)}, u32[]{:S(2)}) collective-permute-start(f32[40,256]{1,0:T(8,128)S(1)} %get-tuple-element.33.refs_0_), channel_id=1, source_target_pairs={{0,2},{1,3},{2,0},{3,1},{4,6},{5,7},{6,4},{7,5},{8,10},{9,11},{10,... | collective-permute-start | bytes 122888 | tf_op jit(solution)/shard_map/ppermute | solution.py:66
  14.3 5.2 %collective-permute-start.3 = (f32[40,256]{1,0:T(8,128)S(1)}, f32[40,256]{1,0:T(8,128)S(1)}, u32[]{:S(2)}, u32[]{:S(2)}) collective-permute-start(f32[40,256]{1,0:T(8,128)S(1)} %get-tuple-element.33.refs_0_), channel_id=1, source_target_pairs={{0,1},{1,0},{2,3},{3,2},{4,5},{5,4},{6,7},{7,6},{8,9},{9,8},{10,11... | collective-permute-start | bytes 122888 | tf_op jit(solution)/shard_map/ppermute | solution.py:66
  16.6 38.2 %slice-start = ((s8[5767168]{0:T(1024)(128)(4,1)}), s8[4194304]{0:T(1024)(128)(4,1)S(1)}, s32[]{:S(2)}) async-start(s8[5767168]{0:T(1024)(128)(4,1)} %bitcast.20), calls=%async_computation | async-start | bytes 8388608
  16.6 38.2 %slice-start.1 = ((s8[5767168]{0:T(1024)(128)(4,1)}), s8[1572864]{0:T(1024)(128)(4,1)S(1)}, s32[]{:S(2)}) async-start(s8[5767168]{0:T(1024)(128)(4,1)} %bitcast.20), calls=%async_computation.1 | async-start | bytes 3145728
  19.7 6.2 %collective-permute-start.8 = (bf16[96,640]{1,0:T(8,128)(2,1)S(1)}, bf16[96,640]{1,0:T(8,128)(2,1)S(1)}, u32[]{:S(2)}, u32[]{:S(2)}) collective-permute-start(bf16[96,640]{1,0:T(8,128)(2,1)S(1)} %shard_map.144.sent_ref), channel_id=1, source_target_pairs={{0,24},{4,28},{8,16},{12,20},{16,8},{20,12},{24,0},{28,4},{1,25},{... | collective-permute-start | bytes 368648 | tf_op jit(solution)/shard_map/ppermute | solution.py:66
  22.2 5.0 %collective-permute-start.7 = (bf16[96,640]{1,0:T(8,128)(2,1)S(1)}, bf16[96,640]{1,0:T(8,128)(2,1)S(1)}, u32[]{:S(2)}, u32[]{:S(2)}) collective-permute-start(bf16[96,640]{1,0:T(8,128)(2,1)S(1)} %shard_map.144.sent_ref), channel_id=1, source_target_pairs={{0,16},{4,20},{8,24},{12,28},{16,0},{20,4},{24,8},{28,12},{1,17},{... | collective-permute-start | bytes 368648 | tf_op jit(solution)/shard_map/ppermute | solution.py:66
  22.7 4.9 %collective-permute-start.6 = (bf16[96,640]{1,0:T(8,128)(2,1)S(1)}, bf16[96,640]{1,0:T(8,128)(2,1)S(1)}, u32[]{:S(2)}, u32[]{:S(2)}) collective-permute-start(bf16[96,640]{1,0:T(8,128)(2,1)S(1)} %shard_map.144.sent_ref), channel_id=1, source_target_pairs={{0,8},{4,12},{8,0},{12,4},{16,24},{20,28},{24,16},{28,20},{1,9},{5... | collective-permute-start | bytes 368648 | tf_op jit(solution)/shard_map/ppermute | solution.py:66
  27.7 1.9 %collective-permute-start.9 = (bf16[4,96,640]{2,1,0:T(8,128)(2,1)S(1)}, bf16[4,96,640]{2,1,0:T(8,128)(2,1)S(1)}, u32[]{:S(2)}, u32[]{:S(2)}) collective-permute-start(bf16[4,96,640]{2,1,0:T(8,128)(2,1)S(1)} %pad_maximum_fusion.2.mine_ref.mine_tail_ref), channel_id=1, source_target_pairs={{0,4},{4,0},{8,12},{12,8},{16,20},{20,16},{24,28},{28,24},{1,5},{5... | collective-permute-start | bytes 1474568 | tf_op jit(solution)/shard_map/ppermute | solution.py:66
  31.6 5.6 %collective-permute-start.10 = (bf16[256,256]{1,0:T(8,128)(2,1)S(1)}, bf16[256,256]{1,0:T(8,128)(2,1)S(1)}, u32[]{:S(2)}, u32[]{:S(2)}) collective-permute-start(bf16[256,256]{1,0:T(8,128)(2,1)S(1)} %shard_map.145.refs_0_), channel_id=1, source_target_pairs={{0,1},{1,0},{2,3},{3,2},{4,5},{5,4},{6,7},{7,6},{8,9},{9,8},{10,11... | collective-permute-start | bytes 393224 | tf_op jit(solution)/shard_map/ppermute | solution.py:66
  37.3 8.5 %collective-permute-start.11 = (bf16[256,256]{1,0:T(8,128)(2,1)S(1)}, bf16[256,256]{1,0:T(8,128)(2,1)S(1)}, u32[]{:S(2)}, u32[]{:S(2)}) collective-permute-start(bf16[256,256]{1,0:T(8,128)(2,1)S(1)} %shard_map.146.refs_0_), channel_id=1, source_target_pairs={{0,2},{1,3},{2,0},{3,1},{4,6},{5,7},{6,4},{7,5},{8,10},{9,11},{10,... | collective-permute-start | bytes 393224 | tf_op jit(solution)/shard_map/ppermute | solution.py:66
  38.5 9.7 %collective-permute-start.18 = (bf16[32,2048]{1,0:T(8,128)(2,1)S(1)}, bf16[32,2048]{1,0:T(8,128)(2,1)S(1)}, u32[]{:S(2)}, u32[]{:S(2)}) collective-permute-start(bf16[32,2048]{1,0:T(8,128)(2,1)S(1)} %get-tuple-element.41), channel_id=1, source_target_pairs={{0,24},{4,28},{8,16},{12,20},{16,8},{20,12},{24,0},{28,4},{1,25},{... | collective-permute-start | bytes 393224 | tf_op jit(solution)/shard_map/ppermute | solution.py:66
  40.0 9.4 %collective-permute-start.17 = (bf16[32,2048]{1,0:T(8,128)(2,1)S(1)}, bf16[32,2048]{1,0:T(8,128)(2,1)S(1)}, u32[]{:S(2)}, u32[]{:S(2)}) collective-permute-start(bf16[32,2048]{1,0:T(8,128)(2,1)S(1)} %get-tuple-element.41), channel_id=1, source_target_pairs={{0,16},{4,20},{8,24},{12,28},{16,0},{20,4},{24,8},{28,12},{1,17},{... | collective-permute-start | bytes 393224 | tf_op jit(solution)/shard_map/ppermute | solution.py:66
  40.8 8.6 %collective-permute-start.16 = (bf16[32,2048]{1,0:T(8,128)(2,1)S(1)}, bf16[32,2048]{1,0:T(8,128)(2,1)S(1)}, u32[]{:S(2)}, u32[]{:S(2)}) collective-permute-start(bf16[32,2048]{1,0:T(8,128)(2,1)S(1)} %get-tuple-element.41), channel_id=1, source_target_pairs={{0,8},{4,12},{8,0},{12,4},{16,24},{20,28},{24,16},{28,20},{1,9},{5... | collective-permute-start | bytes 393224 | tf_op jit(solution)/shard_map/ppermute | solution.py:66
  45.8 7.3 %collective-permute-start.14 = (bf16[256,256]{1,0:T(8,128)(2,1)S(1)}, bf16[256,256]{1,0:T(8,128)(2,1)S(1)}, u32[]{:S(2)}, u32[]{:S(2)}) collective-permute-start(bf16[256,256]{1,0:T(8,128)(2,1)S(1)} %shard_map.147), channel_id=1, source_target_pairs={{0,24},{4,28},{8,16},{12,20},{16,8},{20,12},{24,0},{28,4},{1,25},{... | collective-permute-start | bytes 393224 | tf_op jit(solution)/shard_map/ppermute | solution.py:66
  47.3 7.1 %collective-permute-start.13 = (bf16[256,256]{1,0:T(8,128)(2,1)S(1)}, bf16[256,256]{1,0:T(8,128)(2,1)S(1)}, u32[]{:S(2)}, u32[]{:S(2)}) collective-permute-start(bf16[256,256]{1,0:T(8,128)(2,1)S(1)} %shard_map.147), channel_id=1, source_target_pairs={{0,16},{4,20},{8,24},{12,28},{16,0},{20,4},{24,8},{28,12},{1,17},{... | collective-permute-start | bytes 393224 | tf_op jit(solution)/shard_map/ppermute | solution.py:66
  48.2 6.4 %collective-permute-start.12 = (bf16[256,256]{1,0:T(8,128)(2,1)S(1)}, bf16[256,256]{1,0:T(8,128)(2,1)S(1)}, u32[]{:S(2)}, u32[]{:S(2)}) collective-permute-start(bf16[256,256]{1,0:T(8,128)(2,1)S(1)} %shard_map.147), channel_id=1, source_target_pairs={{0,8},{4,12},{8,0},{12,4},{16,24},{20,28},{24,16},{28,20},{1,9},{5... | collective-permute-start | bytes 393224 | tf_op jit(solution)/shard_map/ppermute | solution.py:66
  49.3 7.3 %copy-start = (bf16[1,704,2048]{2,1,0:T(8,128)(2,1)S(1)}, bf16[1,704,2048]{2,1,0:T(8,128)(2,1)}, u32[]{:S(2)}) copy-start(bf16[1,704,2048]{2,1,0:T(8,128)(2,1)} %param.25) | copy-start | bytes 8650756
  49.4 5.3 %collective-permute-start.19 = (bf16[4,32,2048]{2,1,0:T(8,128)(2,1)S(1)}, bf16[4,32,2048]{2,1,0:T(8,128)(2,1)S(1)}, u32[]{:S(2)}, u32[]{:S(2)}) collective-permute-start(bf16[4,32,2048]{2,1,0:T(8,128)(2,1)S(1)} %pad_maximum_fusion.1.mine_rows), channel_id=1, source_target_pairs={{0,4},{4,0},{8,12},{12,8},{16,20},{20,16},{24,28},{28,24},{1,5},{5... | collective-permute-start | bytes 1572872 | tf_op jit(solution)/shard_map/ppermute | solution.py:66
  54.6 2.0 %collective-permute-start.15 = (bf16[4,256,256]{2,1,0:T(8,128)(2,1)S(1)}, bf16[4,256,256]{2,1,0:T(8,128)(2,1)S(1)}, u32[]{:S(2)}, u32[]{:S(2)}) collective-permute-start(bf16[4,256,256]{2,1,0:T(8,128)(2,1)S(1)} %pad_maximum_fusion.mine_ref), channel_id=1, source_target_pairs={{0,4},{4,0},{8,12},{12,8},{16,20},{20,16},{24,28},{28,24},{1,5},{5... | collective-permute-start | bytes 1572872 | tf_op jit(solution)/shard_map/ppermute | solution.py:66
  58.8 2.0 %collective-permute-start.20 = (bf16[128,2048]{1,0:T(8,128)(2,1)S(1)}, bf16[128,2048]{1,0:T(8,128)(2,1)S(1)}, u32[]{:S(2)}, u32[]{:S(2)}) collective-permute-start(bf16[128,2048]{1,0:T(8,128)(2,1)S(1)} %get-tuple-element.48), channel_id=1, source_target_pairs={{0,4},{4,0},{8,12},{12,8},{16,20},{20,16},{24,28},{28,24},{1,5},{5... | collective-permute-start | bytes 1572872 | tf_op jit(solution)/shard_map/ppermute | solution.py:66
  60.9 6.4 %collective-permute-start.21 = (bf16[32,2048]{1,0:T(8,128)(2,1)S(1)}, bf16[32,2048]{1,0:T(8,128)(2,1)S(1)}, u32[]{:S(2)}, u32[]{:S(2)}) collective-permute-start(bf16[32,2048]{1,0:T(8,128)(2,1)S(1)} %get-tuple-element.50), channel_id=1, source_target_pairs={{0,8},{4,12},{8,0},{12,4},{16,24},{20,28},{24,16},{28,20},{1,9},{5... | collective-permute-start | bytes 393224 | tf_op jit(solution)/shard_map/ppermute | solution.py:66
  61.7 6.1 %collective-permute-start.22 = (bf16[32,2048]{1,0:T(8,128)(2,1)S(1)}, bf16[32,2048]{1,0:T(8,128)(2,1)S(1)}, u32[]{:S(2)}, u32[]{:S(2)}) collective-permute-start(bf16[32,2048]{1,0:T(8,128)(2,1)S(1)} %get-tuple-element.51), channel_id=1, source_target_pairs={{0,16},{4,20},{8,24},{12,28},{16,0},{20,4},{24,8},{28,12},{1,17},{... | collective-permute-start | bytes 393224 | tf_op jit(solution)/shard_map/ppermute | solution.py:66
  62.9 6.9 %collective-permute-start.23 = (bf16[32,2048]{1,0:T(8,128)(2,1)S(1)}, bf16[32,2048]{1,0:T(8,128)(2,1)S(1)}, u32[]{:S(2)}, u32[]{:S(2)}) collective-permute-start(bf16[32,2048]{1,0:T(8,128)(2,1)S(1)} %get-tuple-element.52), channel_id=1, source_target_pairs={{0,24},{4,28},{8,16},{12,20},{16,8},{20,12},{24,0},{28,4},{1,25},{... | collective-permute-start | bytes 393224 | tf_op jit(solution)/shard_map/ppermute | solution.py:66
  69.8 5.1 %collective-permute-start.24 = (bf16[8,2048]{1,0:T(8,128)(2,1)S(1)}, bf16[8,2048]{1,0:T(8,128)(2,1)S(1)}, u32[]{:S(2)}, u32[]{:S(2)}) collective-permute-start(bf16[8,2048]{1,0:T(8,128)(2,1)S(1)} %get-tuple-element.54), channel_id=1, source_target_pairs={{0,1},{1,0},{2,3},{3,2},{4,5},{5,4},{6,7},{7,6},{8,9},{9,8},{10,11... | collective-permute-start | bytes 98312 | tf_op jit(solution)/shard_map/ppermute | solution.py:66
  69.9 5.0 %collective-permute-start.25 = (bf16[8,2048]{1,0:T(8,128)(2,1)S(1)}, bf16[8,2048]{1,0:T(8,128)(2,1)S(1)}, u32[]{:S(2)}, u32[]{:S(2)}) collective-permute-start(bf16[8,2048]{1,0:T(8,128)(2,1)S(1)} %get-tuple-element.55), channel_id=1, source_target_pairs={{0,2},{1,3},{2,0},{3,1},{4,6},{5,7},{6,4},{7,5},{8,10},{9,11},{10,... | collective-permute-start | bytes 98312 | tf_op jit(solution)/shard_map/ppermute | solution.py:66
  72.6 5.7 %collective-permute-start.26 = (bf16[8,2048]{1,0:T(8,128)(2,1)S(1)}, bf16[8,2048]{1,0:T(8,128)(2,1)S(1)}, u32[]{:S(2)}, u32[]{:S(2)}) collective-permute-start(bf16[8,2048]{1,0:T(8,128)(2,1)S(1)} %get-tuple-element.56), channel_id=1, source_target_pairs={{0,3},{1,2},{2,1},{3,0},{4,7},{5,6},{6,5},{7,4},{8,11},{9,10},{10,... | collective-permute-start | bytes 98312 | tf_op jit(solution)/shard_map/ppermute | solution.py:66

commit v7 on v6

--- a/solution.py
+++ b/solution.py
@@ -381,8 +381,9 @@
     near_ref,
     far_ref,
     own_ref,
+    act_ref,
+    scale_ref,
     rows_ref,
-    act_ref,
     rest_ref,
     whole_ref,
 ):
@@ -420,20 +421,36 @@
     scale = jnp.sum(
         jnp.where((lane == slot) | (lane == slot + experts), tail, 0.0), axis=1, keepdims=True
     )
-    wide = out_weight_ref.shape[1] // columns
+    scale_ref[...] = scale
+    project(0, columns, scale, act_ref, out_weight_ref, near_ref, far_ref)
+
+
+def project(first, columns, scale, act_ref, weight_ref, near_ref, far_ref):
+    half, width = near_ref.shape
+    wide = width // columns
     for n in range(columns):
         span = slice(n * wide, (n + 1) * wide)
-        done = nn(act_ref[...], out_weight_ref[:, span])
+        done = nn(act_ref[...], weight_ref[:, first + n * wide : first + (n + 1) * wide])
         done = jnp.where(scale > 0, done * scale, 0.0).astype(BF16)
         near_ref[:, span] = done[:half]
         far_ref[:, span] = done[half:]
 
 
-def level_kernel(near_ref, back_ref, *outs):
+def finish_kernel(columns, act_ref, scale_ref, weight_ref, near_ref, far_ref):
+    project(near_ref.shape[1], columns, scale_ref[...], act_ref, weight_ref, near_ref, far_ref)
+
+
+def level_kernel(*refs):
+    parts, outs = refs[:4], refs[4:]
     rows = outs[0].shape[0]
+    width = parts[0].shape[1]
     for n, out in enumerate(outs):
         at = slice(n * rows, (n + 1) * rows)
-        out[...] = (near_ref[at, :].astype(F32) + back_ref[at, :].astype(F32)).astype(out.dtype)
+        for side in range(2):
+            near_ref, back_ref = parts[2 * side : 2 * side + 2]
+            out[:, side * width : (side + 1) * width] = (
+                near_ref[at, :].astype(F32) + back_ref[at, :].astype(F32)
+            ).astype(out.dtype)
 
 
 def rows_kernel(spans, *refs):
@@ -622,11 +639,18 @@
         moved=4 * hidden * model,
         limit=20,
     )
-    near, far, own = call(
+    side = model // 2
+    near, far, own, act, scale = call(
         functools.partial(
-            expert_kernel, contexts, latent_width - kv_rank, kv_rank, experts, cuts, 4
+            expert_kernel, contexts, latent_width - kv_rank, kv_rank, experts, cuts, 2
         ),
-        [shape((half, model), BF16), shape((half, model), BF16), shape((rows_dev, model), F32)],
+        [
+            shape((half, side), BF16),
+            shape((half, side), BF16),
+            shape((rows_dev, model), F32),
+            shape((2 * half, hidden), BF16),
+            shape((2 * half, 1), F32),
+        ],
         [VM] * 12,
         (
             theirs,
@@ -641,7 +665,6 @@
         ),
         scratch=[
             pltpu.VMEM((2 * half, model // 2), BF16),
-            pltpu.VMEM((2 * half, hidden), BF16),
             pltpu.VMEM((kept, model // 2), F32),
             pltpu.VMEM((kept, model), F32),
         ],
@@ -650,11 +673,23 @@
         limit=20,
     )
 
+    back = partner(far, "context", 1)
+    later, far = call(
+        functools.partial(finish_kernel, 2),
+        [shape((half, side), BF16), shape((half, side), BF16)],
+        [VM] * 3,
+        (act, scale, expert_out[0]),
+        flops=2 * half * hidden * model,
+        moved=hidden * model,
+        limit=12,
+    )
+    later_back = partner(far, "context", 1)
+
     levels = call(
         level_kernel,
         [shape((kept, model), F32)] + [shape((kept, model), BF16)] * (len(evens) - 1),
-        [VM, VM],
-        (near, partner(far, "context", 1)),
+        [VM] * 4,
+        (near, back, later, later_back),
         limit=6,
     )
     got = []

time: 79.2 us -> 79.5 us (level)
    ppermute x27 -> x28, starting transfers between devices: 31.5 us -> 32 us  [partner(): return lax.ppermute(values, axis, [(i, i ^ mask) for i in range(count)])]
    ppermute x27 -> x28, waiting for transfers between devices: 33.5 us -> 33.1 us  [partner(): return lax.ppermute(values, axis, [(i, i ^ mask) for i in range(count)])]
    pallas_call x14 -> x15, Pallas kernels: 13 us -> 13.1 us  [call(): pl.pallas_call(kernel, out_shape=outs, in_specs=in_specs, out_specs=VM if...]
  transfers between devices with their start and end apart: 27 -> 28, of which waited for: 16 -> 18; matrix products, arithmetic and copies ran while one was open for 0% -> 0% of each run, Pallas kernels for 8% -> 8%
where the time goes in v7:
time: 79.5 us; the launch traced here: 79.3 us
  waiting for transfers between devices  33.1 us (42%)
  starting transfers between devices  32 us (40%)
  Pallas kernels  13.1 us (16%)
  between operations  0.84 us (1%)
    ppermute x28, waiting for transfers between devices, partner(): return lax.ppermute(values, axis, [(i, i ^ mask) for i in range(count)])  33.1 us
    ppermute x28, starting transfers between devices, partner(): return lax.ppermute(values, axis, [(i, i ^ mask) for i in range(count)])  32 us
    pallas_call x15, Pallas kernels, call(): pl.pallas_call(kernel, out_shape=outs, in_specs=in_specs, out_specs=VM if...  13.1 us
  transfers between devices with their start and end apart: 28, of which 18 were waited for; matrix products, arithmetic and copies ran while one was open for 0% of the time, Pallas kernels for 8%

profile of v7, /device:TPU:0, one launch (start us, length us, event | category | flops | bytes accessed | tf_op | source)
XLA Modules:
  0.0 79.3 jit_solution(15436296463110360985)
XLA Ops:
  0.6 1.1 %shard_map.140.refs_0_ = bf16[32,512]{1,0:T(8,128)(2,1)S(1)} custom-call(s32[1,32]{1,0:T(1,128)} %keep_hbm.3, bf16[192,512]{1,0:T(8,128)(2,1)} %raw_hbm.1), custom_call_target="tpu_custom_call" | custom-call | tf_op jit(solution)/shard_map/pallas_call | solution.py:41
  1.8 5.1 %collective-permute-start.2 = (bf16[32,512]{1,0:T(8,128)(2,1)S(1)}, bf16[32,512]{1,0:T(8,128)(2,1)S(1)}, u32[]{:S(2)}, u32[]{:S(2)}) collective-permute-start(bf16[32,512]{1,0:T(8,128)(2,1)S(1)} %shard_map.140.refs_0_), channel_id=1, source_target_pairs={{0,3},{1,2},{2,1},{3,0},{4,7},{5,6},{6,5},{7,4},{8,11},{9,10},{10,... | collective-permute-start | bytes 98312 | tf_op jit(solution)/shard_map/ppermute | solution.py:66
  7.6 1.5 %shard_map.141 = (bf16[144,2048]{1,0:T(8,128)(2,1)S(1)}, f32[1,2048]{1,0:T(1,128)S(1)}, bf16[512,1152]{1,0:T(8,128)(2,1)S(1)}, f32[8,256]{1,0:T(8,128)S(1)}) custom-call(s32[8,6]{1,0:T(8,128)} %ids_hbm.1, f32[8,6]{1,0:T(8,128)} %gates_hbm.1, s32[16]{0:T(128)} %slot_hbm.1, bf16[144,2048]{1,0:T(8,128)(2,1)} %bitcast.29, f32[1,2048]{1,0:T(1,128)} %bitcast.39, ...), custom_call_target="tpu_custom_call" | custom-call | bytes 2359296 | tf_op jit(solution)/shard_map/pallas_call | solution.py:41
  9.1 2.6 %collective-permute-done.1.refs_2_ = bf16[32,512]{1,0:T(8,128)(2,1)S(1)} collective-permute-done((bf16[32,512]{1,0:T(8,128)(2,1)S(1)}, bf16[32,512]{1,0:T(8,128)(2,1)S(1)}, u32[]{:S(2)}, u32[]{:S(2)}) %collective-permute-start.1) | collective-permute-done | bytes 32800 | tf_op jit(solution)/shard_map/ppermute | solution.py:66
  12.1 1.5 %collective-permute-start.5 = (f32[40,256]{1,0:T(8,128)S(1)}, f32[40,256]{1,0:T(8,128)S(1)}, u32[]{:S(2)}, u32[]{:S(2)}) collective-permute-start(f32[40,256]{1,0:T(8,128)S(1)} %get-tuple-element.37.refs_0_), channel_id=1, source_target_pairs={{0,3},{1,2},{2,1},{3,0},{4,7},{5,6},{6,5},{7,4},{8,11},{9,10},{10,... | collective-permute-start | bytes 122888 | tf_op jit(solution)/shard_map/ppermute | solution.py:66
  14.3 2.3 %collective-permute-start.3 = (f32[40,256]{1,0:T(8,128)S(1)}, f32[40,256]{1,0:T(8,128)S(1)}, u32[]{:S(2)}, u32[]{:S(2)}) collective-permute-start(f32[40,256]{1,0:T(8,128)S(1)} %get-tuple-element.37.refs_0_), channel_id=1, source_target_pairs={{0,1},{1,0},{2,3},{3,2},{4,5},{5,4},{6,7},{7,6},{8,9},{9,8},{10,11... | collective-permute-start | bytes 122888 | tf_op jit(solution)/shard_map/ppermute | solution.py:66
  16.6 2.9 %shard_map.143 = (bf16[64,640]{1,0:T(8,128)(2,1)S(1)}, f32[32,64]{1,0:T(8,128)S(1)}, f32[32,64]{1,0:T(8,128)S(1)}, f32[32,1]{1,0:T(8,128)S(1)}, f32[1,512]{1,0:T(1,128)S(1)}, /*index=5*/f32[1,2048]{1,0:T(1,128)S(1)}) custom-call(bf16[32,2048]{1,0:T(8,128)(2,1)S(1)} %get-tuple-element.38.normed_ref, bf16[512,1152]{1,0:T(8,128)(2,1)S(1)} %get-tuple-element.39.early_ref, ...), custom_call_target="tpu_custom_call" | custom-call | flops 150994944 | bytes 2359296 | tf_op jit(solution)/shard_map/pallas_call | solution.py:41
  19.7 2.5 %collective-permute-start.8 = (bf16[96,640]{1,0:T(8,128)(2,1)S(1)}, bf16[96,640]{1,0:T(8,128)(2,1)S(1)}, u32[]{:S(2)}, u32[]{:S(2)}) collective-permute-start(bf16[96,640]{1,0:T(8,128)(2,1)S(1)} %shard_map.144.sent_ref), channel_id=1, source_target_pairs={{0,24},{4,28},{8,16},{12,20},{16,8},{20,12},{24,0},{28,4},{1,25},{... | collective-permute-start | bytes 368648 | tf_op jit(solution)/shard_map/ppermute | solution.py:66
  23.3 2.7 %collective-permute-done.8 = bf16[96,640]{1,0:T(8,128)(2,1)S(1)} collective-permute-done((bf16[96,640]{1,0:T(8,128)(2,1)S(1)}, bf16[96,640]{1,0:T(8,128)(2,1)S(1)}, u32[]{:S(2)}, u32[]{:S(2)}) %collective-permute-start.8) | collective-permute-done | bytes 122912 | tf_op jit(solution)/shard_map/ppermute | solution.py:66
  25.9 1.3 %collective-permute-done.7 = bf16[96,640]{1,0:T(8,128)(2,1)S(1)} collective-permute-done((bf16[96,640]{1,0:T(8,128)(2,1)S(1)}, bf16[96,640]{1,0:T(8,128)(2,1)S(1)}, u32[]{:S(2)}, u32[]{:S(2)}) %collective-permute-start.7) | collective-permute-done | bytes 122912 | tf_op jit(solution)/shard_map/ppermute | solution.py:66
  27.8 1.9 %collective-permute-done.9.theirs_ref.theirs_tail_ref = bf16[4,96,640]{2,1,0:T(8,128)(2,1)S(1)} collective-permute-done((bf16[4,96,640]{2,1,0:T(8,128)(2,1)S(1)}, bf16[4,96,640]{2,1,0:T(8,128)(2,1)S(1)}, u32[]{:S(2)}, u32[]{:S(2)}) %collective-permute-start.9) | collective-permute-done | bytes 491552 | tf_op jit(solution)/shard_map/ppermute | solution.py:66
  29.6 2.0 %shard_map.145.refs_0_ = bf16[256,256]{1,0:T(8,128)(2,1)S(1)} custom-call(bf16[4,96,640]{2,1,0:T(8,128)(2,1)S(1)} %pad_maximum_fusion.2.mine_ref.mine_tail_ref, bf16[4,96,640]{2,1,0:T(8,128)(2,1)S(1)} %collective-permute-done.9.theirs_ref.theirs_tail_ref, bf16[1024,256]{1,0:T(8,128)(2,1)} %weight_hbm.3), custom_call_target="tpu_custom_call" | custom-call | flops 134217728 | bytes 524288 | tf_op jit(solution)/shard_map/pallas_call | solution.py:41
  31.6 1.1 %collective-permute-start.10 = (bf16[256,256]{1,0:T(8,128)(2,1)S(1)}, bf16[256,256]{1,0:T(8,128)(2,1)S(1)}, u32[]{:S(2)}, u32[]{:S(2)}) collective-permute-start(bf16[256,256]{1,0:T(8,128)(2,1)S(1)} %shard_map.145.refs_0_), channel_id=1, source_target_pairs={{0,1},{1,0},{2,3},{3,2},{4,5},{5,4},{6,7},{7,6},{8,9},{9,8},{10,11... | collective-permute-start | bytes 393224 | tf_op jit(solution)/shard_map/ppermute | solution.py:66
  32.8 4.5 %collective-permute-done.10.refs_1_ = bf16[256,256]{1,0:T(8,128)(2,1)S(1)} collective-permute-done((bf16[256,256]{1,0:T(8,128)(2,1)S(1)}, bf16[256,256]{1,0:T(8,128)(2,1)S(1)}, u32[]{:S(2)}, u32[]{:S(2)}) %collective-permute-start.10) | collective-permute-done | bytes 131104 | tf_op jit(solution)/shard_map/ppermute | solution.py:66
  37.3 1.2 %collective-permute-start.11 = (bf16[256,256]{1,0:T(8,128)(2,1)S(1)}, bf16[256,256]{1,0:T(8,128)(2,1)S(1)}, u32[]{:S(2)}, u32[]{:S(2)}) collective-permute-start(bf16[256,256]{1,0:T(8,128)(2,1)S(1)} %shard_map.146.refs_0_), channel_id=1, source_target_pairs={{0,2},{1,3},{2,0},{3,1},{4,6},{5,7},{6,4},{7,5},{8,10},{9,11},{10,... | collective-permute-start | bytes 393224 | tf_op jit(solution)/shard_map/ppermute | solution.py:66
  38.5 1.5 %collective-permute-start.18 = (bf16[32,2048]{1,0:T(8,128)(2,1)S(1)}, bf16[32,2048]{1,0:T(8,128)(2,1)S(1)}, u32[]{:S(2)}, u32[]{:S(2)}) collective-permute-start(bf16[32,2048]{1,0:T(8,128)(2,1)S(1)} %get-tuple-element.45), channel_id=1, source_target_pairs={{0,24},{4,28},{8,16},{12,20},{16,8},{20,12},{24,0},{28,4},{1,25},{... | collective-permute-start | bytes 393224 | tf_op jit(solution)/shard_map/ppermute | solution.py:66
  40.8 1.2 %collective-permute-start.16 = (bf16[32,2048]{1,0:T(8,128)(2,1)S(1)}, bf16[32,2048]{1,0:T(8,128)(2,1)S(1)}, u32[]{:S(2)}, u32[]{:S(2)}) collective-permute-start(bf16[32,2048]{1,0:T(8,128)(2,1)S(1)} %get-tuple-element.45), channel_id=1, source_target_pairs={{0,8},{4,12},{8,0},{12,4},{16,24},{20,28},{24,16},{28,20},{1,9},{5... | collective-permute-start | bytes 393224 | tf_op jit(solution)/shard_map/ppermute | solution.py:66
  42.0 3.8 %collective-permute-done.11.refs_1_ = bf16[256,256]{1,0:T(8,128)(2,1)S(1)} collective-permute-done((bf16[256,256]{1,0:T(8,128)(2,1)S(1)}, bf16[256,256]{1,0:T(8,128)(2,1)S(1)}, u32[]{:S(2)}, u32[]{:S(2)}) %collective-permute-start.11) | collective-permute-done | bytes 131104 | tf_op jit(solution)/shard_map/ppermute | solution.py:66
  45.8 1.6 %collective-permute-start.14 = (bf16[256,256]{1,0:T(8,128)(2,1)S(1)}, bf16[256,256]{1,0:T(8,128)(2,1)S(1)}, u32[]{:S(2)}, u32[]{:S(2)}) collective-permute-start(bf16[256,256]{1,0:T(8,128)(2,1)S(1)} %shard_map.147), channel_id=1, source_target_pairs={{0,24},{4,28},{8,16},{12,20},{16,8},{20,12},{24,0},{28,4},{1,25},{... | collective-permute-start | bytes 393224 | tf_op jit(solution)/shard_map/ppermute | solution.py:66
  48.2 1.2 %collective-permute-start.12 = (bf16[256,256]{1,0:T(8,128)(2,1)S(1)}, bf16[256,256]{1,0:T(8,128)(2,1)S(1)}, u32[]{:S(2)}, u32[]{:S(2)}) collective-permute-start(bf16[256,256]{1,0:T(8,128)(2,1)S(1)} %shard_map.147), channel_id=1, source_target_pairs={{0,8},{4,12},{8,0},{12,4},{16,24},{20,28},{24,16},{28,20},{1,9},{5... | collective-permute-start | bytes 393224 | tf_op jit(solution)/shard_map/ppermute | solution.py:66
  49.5 3.6 %collective-permute-done.14 = bf16[256,256]{1,0:T(8,128)(2,1)S(1)} collective-permute-done((bf16[256,256]{1,0:T(8,128)(2,1)S(1)}, bf16[256,256]{1,0:T(8,128)(2,1)S(1)}, u32[]{:S(2)}, u32[]{:S(2)}) %collective-permute-start.14) | collective-permute-done | bytes 131104 | tf_op jit(solution)/shard_map/ppermute | solution.py:66
  53.1 1.4 %collective-permute-done.13 = bf16[256,256]{1,0:T(8,128)(2,1)S(1)} collective-permute-done((bf16[256,256]{1,0:T(8,128)(2,1)S(1)}, bf16[256,256]{1,0:T(8,128)(2,1)S(1)}, u32[]{:S(2)}, u32[]{:S(2)}) %collective-permute-start.13) | collective-permute-done | bytes 131104 | tf_op jit(solution)/shard_map/ppermute | solution.py:66
  54.7 1.0 %shard_map.148 = (f32[32,1024]{1,0:T(8,128)S(1)}, f32[256,1]{1,0:T(8,128)S(1)}, f32[256,704]{1,0:T(8,128)S(1)}, f32[256,704]{1,0:T(8,128)S(1)}) custom-call(bf16[4,256,256]{2,1,0:T(8,128)(2,1)S(1)} %pad_maximum_fusion.mine_ref, bf16[4,32,2048]{2,1,0:T(8,128)(2,1)S(1)} %pad_maximum_fusion.1.mine_rows, ...), custom_call_target="tpu_custom_call" | custom-call | flops 738197504 | bytes 5767168 | tf_op jit(solution)/shard_map/pallas_call | solution.py:41
  56.6 1.7 %shard_map.149 = (bf16[128,1024]{1,0:T(8,128)(2,1)S(1)}, bf16[128,1024]{1,0:T(8,128)(2,1)S(1)}, f32[8,2048]{1,0:T(8,128)S(1)}, bf16[256,704]{1,0:T(8,128)(2,1)S(1)}, f32[256,1]{1,0:T(8,128)S(1)}) custom-call(bf16[4,256,256]{2,1,0:T(8,128)(2,1)S(1)} %collective-permute-done.15.theirs_ref, bf16[4,32,2048]{2,1,0:T(8,128)(2,1)S(1)} %pad_maximum_fusion.1.mine_rows, ...), custom_call_target="tpu_custom_call" | custom-call | flops 1476395008 | bytes 5767168 | tf_op jit(solution)/shard_map/pallas_call | solution.py:41
  60.9 0.8 %collective-permute-start.22 = (bf16[32,2048]{1,0:T(8,128)(2,1)S(1)}, bf16[32,2048]{1,0:T(8,128)(2,1)S(1)}, u32[]{:S(2)}, u32[]{:S(2)}) collective-permute-start(bf16[32,2048]{1,0:T(8,128)(2,1)S(1)} %get-tuple-element.58), channel_id=1, source_target_pairs={{0,8},{4,12},{8,0},{12,4},{16,24},{20,28},{24,16},{28,20},{1,9},{5... | collective-permute-start | bytes 393224 | tf_op jit(solution)/shard_map/ppermute | solution.py:66
  61.7 1.2 %collective-permute-start.23 = (bf16[32,2048]{1,0:T(8,128)(2,1)S(1)}, bf16[32,2048]{1,0:T(8,128)(2,1)S(1)}, u32[]{:S(2)}, u32[]{:S(2)}) collective-permute-start(bf16[32,2048]{1,0:T(8,128)(2,1)S(1)} %get-tuple-element.59), channel_id=1, source_target_pairs={{0,16},{4,20},{8,24},{12,28},{16,0},{20,4},{24,8},{28,12},{1,17},{... | collective-permute-start | bytes 393224 | tf_op jit(solution)/shard_map/ppermute | solution.py:66
  62.9 1.5 %collective-permute-start.24 = (bf16[32,2048]{1,0:T(8,128)(2,1)S(1)}, bf16[32,2048]{1,0:T(8,128)(2,1)S(1)}, u32[]{:S(2)}, u32[]{:S(2)}) collective-permute-start(bf16[32,2048]{1,0:T(8,128)(2,1)S(1)} %get-tuple-element.60), channel_id=1, source_target_pairs={{0,24},{4,28},{8,16},{12,20},{16,8},{20,12},{24,0},{28,4},{1,25},{... | collective-permute-start | bytes 393224 | tf_op jit(solution)/shard_map/ppermute | solution.py:66
  64.4 2.9 %collective-permute-done.22.refs_1_ = bf16[32,2048]{1,0:T(8,128)(2,1)S(1)} collective-permute-done((bf16[32,2048]{1,0:T(8,128)(2,1)S(1)}, bf16[32,2048]{1,0:T(8,128)(2,1)S(1)}, u32[]{:S(2)}, u32[]{:S(2)}) %collective-permute-start.22) | collective-permute-done | bytes 131104 | tf_op jit(solution)/shard_map/ppermute | solution.py:66
  67.8 2.2 %collective-permute-done.24.refs_3_ = bf16[32,2048]{1,0:T(8,128)(2,1)S(1)} collective-permute-done((bf16[32,2048]{1,0:T(8,128)(2,1)S(1)}, bf16[32,2048]{1,0:T(8,128)(2,1)S(1)}, u32[]{:S(2)}, u32[]{:S(2)}) %collective-permute-start.24) | collective-permute-done | bytes 131104 | tf_op jit(solution)/shard_map/ppermute | solution.py:66
  70.2 2.7 %collective-permute-start.26 = (bf16[8,2048]{1,0:T(8,128)(2,1)S(1)}, bf16[8,2048]{1,0:T(8,128)(2,1)S(1)}, u32[]{:S(2)}, u32[]{:S(2)}) collective-permute-start(bf16[8,2048]{1,0:T(8,128)(2,1)S(1)} %get-tuple-element.63), channel_id=1, source_target_pairs={{0,2},{1,3},{2,0},{3,1},{4,6},{5,7},{6,4},{7,5},{8,10},{9,11},{10,... | collective-permute-start | bytes 98312 | tf_op jit(solution)/shard_map/ppermute | solution.py:66
  72.9 1.7 %collective-permute-start.27 = (bf16[8,2048]{1,0:T(8,128)(2,1)S(1)}, bf16[8,2048]{1,0:T(8,128)(2,1)S(1)}, u32[]{:S(2)}, u32[]{:S(2)}) collective-permute-start(bf16[8,2048]{1,0:T(8,128)(2,1)S(1)} %get-tuple-element.64), channel_id=1, source_target_pairs={{0,3},{1,2},{2,1},{3,0},{4,7},{5,6},{6,5},{7,4},{8,11},{9,10},{10,... | collective-permute-start | bytes 98312 | tf_op jit(solution)/shard_map/ppermute | solution.py:66
  75.3 3.3 %collective-permute-done.27.refs_3_ = bf16[8,2048]{1,0:T(8,128)(2,1)S(1)} collective-permute-done((bf16[8,2048]{1,0:T(8,128)(2,1)S(1)}, bf16[8,2048]{1,0:T(8,128)(2,1)S(1)}, u32[]{:S(2)}, u32[]{:S(2)}) %collective-permute-start.27) | collective-permute-done | bytes 32800 | tf_op jit(solution)/shard_map/ppermute | solution.py:66
  (49 shorter events, 10.9 us)
Async XLA Ops:
  1.8 7.3 %collective-permute-start.2 = (bf16[32,512]{1,0:T(8,128)(2,1)S(1)}, bf16[32,512]{1,0:T(8,128)(2,1)S(1)}, u32[]{:S(2)}, u32[]{:S(2)}) collective-permute-start(bf16[32,512]{1,0:T(8,128)(2,1)S(1)} %shard_map.140.refs_0_), channel_id=1, source_target_pairs={{0,3},{1,2},{2,1},{3,0},{4,7},{5,6},{6,5},{7,4},{8,11},{9,10},{10,... | collective-permute-start | bytes 98312 | tf_op jit(solution)/shard_map/ppermute | solution.py:66
  6.9 4.8 %collective-permute-start.1 = (bf16[32,512]{1,0:T(8,128)(2,1)S(1)}, bf16[32,512]{1,0:T(8,128)(2,1)S(1)}, u32[]{:S(2)}, u32[]{:S(2)}) collective-permute-start(bf16[32,512]{1,0:T(8,128)(2,1)S(1)} %shard_map.140.refs_0_), channel_id=1, source_target_pairs={{0,2},{1,3},{2,0},{3,1},{4,6},{5,7},{6,4},{7,5},{8,10},{9,11},{10,... | collective-permute-start | bytes 98312 | tf_op jit(solution)/shard_map/ppermute | solution.py:66
  6.9 4.8 %collective-permute-start = (bf16[32,512]{1,0:T(8,128)(2,1)S(1)}, bf16[32,512]{1,0:T(8,128)(2,1)S(1)}, u32[]{:S(2)}, u32[]{:S(2)}) collective-permute-start(bf16[32,512]{1,0:T(8,128)(2,1)S(1)} %shard_map.140.refs_0_), channel_id=1, source_target_pairs={{0,1},{1,0},{2,3},{3,2},{4,5},{5,4},{6,7},{7,6},{8,9},{9,8},{10,11... | collective-permute-start | bytes 98312 | tf_op jit(solution)/shard_map/ppermute | solution.py:66
  12.1 7.3 %collective-permute-start.5 = (f32[40,256]{1,0:T(8,128)S(1)}, f32[40,256]{1,0:T(8,128)S(1)}, u32[]{:S(2)}, u32[]{:S(2)}) collective-permute-start(f32[40,256]{1,0:T(8,128)S(1)} %get-tuple-element.37.refs_0_), channel_id=1, source_target_pairs={{0,3},{1,2},{2,1},{3,0},{4,7},{5,6},{6,5},{7,4},{8,11},{9,10},{10,... | collective-permute-start | bytes 122888 | tf_op jit(solution)/shard_map/ppermute | solution.py:66
  13.6 5.8 %collective-permute-start.4 = (f32[40,256]{1,0:T(8,128)S(1)}, f32[40,256]{1,0:T(8,128)S(1)}, u32[]{:S(2)}, u32[]{:S(2)}) collective-permute-start(f32[40,256]{1,0:T(8,128)S(1)} %get-tuple-element.37.refs_0_), channel_id=1, source_target_pairs={{0,2},{1,3},{2,0},{3,1},{4,6},{5,7},{6,4},{7,5},{8,10},{9,11},{10,... | collective-permute-start | bytes 122888 | tf_op jit(solution)/shard_map/ppermute | solution.py:66
  14.3 5.2 %collective-permute-start.3 = (f32[40,256]{1,0:T(8,128)S(1)}, f32[40,256]{1,0:T(8,128)S(1)}, u32[]{:S(2)}, u32[]{:S(2)}) collective-permute-start(f32[40,256]{1,0:T(8,128)S(1)} %get-tuple-element.37.refs_0_), channel_id=1, source_target_pairs={{0,1},{1,0},{2,3},{3,2},{4,5},{5,4},{6,7},{7,6},{8,9},{9,8},{10,11... | collective-permute-start | bytes 122888 | tf_op jit(solution)/shard_map/ppermute | solution.py:66
  16.6 38.2 %slice-start = ((s8[5767168]{0:T(1024)(128)(4,1)}), s8[4194304]{0:T(1024)(128)(4,1)S(1)}, s32[]{:S(2)}) async-start(s8[5767168]{0:T(1024)(128)(4,1)} %bitcast.20), calls=%async_computation | async-start | bytes 8388608
  16.6 38.2 %slice-start.1 = ((s8[5767168]{0:T(1024)(128)(4,1)}), s8[1572864]{0:T(1024)(128)(4,1)S(1)}, s32[]{:S(2)}) async-start(s8[5767168]{0:T(1024)(128)(4,1)} %bitcast.20), calls=%async_computation.1 | async-start | bytes 3145728
  19.7 6.2 %collective-permute-start.8 = (bf16[96,640]{1,0:T(8,128)(2,1)S(1)}, bf16[96,640]{1,0:T(8,128)(2,1)S(1)}, u32[]{:S(2)}, u32[]{:S(2)}) collective-permute-start(bf16[96,640]{1,0:T(8,128)(2,1)S(1)} %shard_map.144.sent_ref), channel_id=1, source_target_pairs={{0,24},{4,28},{8,16},{12,20},{16,8},{20,12},{24,0},{28,4},{1,25},{... | collective-permute-start | bytes 368648 | tf_op jit(solution)/shard_map/ppermute | solution.py:66
  22.2 5.0 %collective-permute-start.7 = (bf16[96,640]{1,0:T(8,128)(2,1)S(1)}, bf16[96,640]{1,0:T(8,128)(2,1)S(1)}, u32[]{:S(2)}, u32[]{:S(2)}) collective-permute-start(bf16[96,640]{1,0:T(8,128)(2,1)S(1)} %shard_map.144.sent_ref), channel_id=1, source_target_pairs={{0,16},{4,20},{8,24},{12,28},{16,0},{20,4},{24,8},{28,12},{1,17},{... | collective-permute-start | bytes 368648 | tf_op jit(solution)/shard_map/ppermute | solution.py:66
  22.7 4.9 %collective-permute-start.6 = (bf16[96,640]{1,0:T(8,128)(2,1)S(1)}, bf16[96,640]{1,0:T(8,128)(2,1)S(1)}, u32[]{:S(2)}, u32[]{:S(2)}) collective-permute-start(bf16[96,640]{1,0:T(8,128)(2,1)S(1)} %shard_map.144.sent_ref), channel_id=1, source_target_pairs={{0,8},{4,12},{8,0},{12,4},{16,24},{20,28},{24,16},{28,20},{1,9},{5... | collective-permute-start | bytes 368648 | tf_op jit(solution)/shard_map/ppermute | solution.py:66
  27.7 1.9 %collective-permute-start.9 = (bf16[4,96,640]{2,1,0:T(8,128)(2,1)S(1)}, bf16[4,96,640]{2,1,0:T(8,128)(2,1)S(1)}, u32[]{:S(2)}, u32[]{:S(2)}) collective-permute-start(bf16[4,96,640]{2,1,0:T(8,128)(2,1)S(1)} %pad_maximum_fusion.2.mine_ref.mine_tail_ref), channel_id=1, source_target_pairs={{0,4},{4,0},{8,12},{12,8},{16,20},{20,16},{24,28},{28,24},{1,5},{5... | collective-permute-start | bytes 1474568 | tf_op jit(solution)/shard_map/ppermute | solution.py:66
  31.6 5.6 %collective-permute-start.10 = (bf16[256,256]{1,0:T(8,128)(2,1)S(1)}, bf16[256,256]{1,0:T(8,128)(2,1)S(1)}, u32[]{:S(2)}, u32[]{:S(2)}) collective-permute-start(bf16[256,256]{1,0:T(8,128)(2,1)S(1)} %shard_map.145.refs_0_), channel_id=1, source_target_pairs={{0,1},{1,0},{2,3},{3,2},{4,5},{5,4},{6,7},{7,6},{8,9},{9,8},{10,11... | collective-permute-start | bytes 393224 | tf_op jit(solution)/shard_map/ppermute | solution.py:66
  37.3 8.5 %collective-permute-start.11 = (bf16[256,256]{1,0:T(8,128)(2,1)S(1)}, bf16[256,256]{1,0:T(8,128)(2,1)S(1)}, u32[]{:S(2)}, u32[]{:S(2)}) collective-permute-start(bf16[256,256]{1,0:T(8,128)(2,1)S(1)} %shard_map.146.refs_0_), channel_id=1, source_target_pairs={{0,2},{1,3},{2,0},{3,1},{4,6},{5,7},{6,4},{7,5},{8,10},{9,11},{10,... | collective-permute-start | bytes 393224 | tf_op jit(solution)/shard_map/ppermute | solution.py:66
  38.5 9.7 %collective-permute-start.18 = (bf16[32,2048]{1,0:T(8,128)(2,1)S(1)}, bf16[32,2048]{1,0:T(8,128)(2,1)S(1)}, u32[]{:S(2)}, u32[]{:S(2)}) collective-permute-start(bf16[32,2048]{1,0:T(8,128)(2,1)S(1)} %get-tuple-element.45), channel_id=1, source_target_pairs={{0,24},{4,28},{8,16},{12,20},{16,8},{20,12},{24,0},{28,4},{1,25},{... | collective-permute-start | bytes 393224 | tf_op jit(solution)/shard_map/ppermute | solution.py:66
  40.0 9.4 %collective-permute-start.17 = (bf16[32,2048]{1,0:T(8,128)(2,1)S(1)}, bf16[32,2048]{1,0:T(8,128)(2,1)S(1)}, u32[]{:S(2)}, u32[]{:S(2)}) collective-permute-start(bf16[32,2048]{1,0:T(8,128)(2,1)S(1)} %get-tuple-element.45), channel_id=1, source_target_pairs={{0,16},{4,20},{8,24},{12,28},{16,0},{20,4},{24,8},{28,12},{1,17},{... | collective-permute-start | bytes 393224 | tf_op jit(solution)/shard_map/ppermute | solution.py:66
  40.8 8.6 %collective-permute-start.16 = (bf16[32,2048]{1,0:T(8,128)(2,1)S(1)}, bf16[32,2048]{1,0:T(8,128)(2,1)S(1)}, u32[]{:S(2)}, u32[]{:S(2)}) collective-permute-start(bf16[32,2048]{1,0:T(8,128)(2,1)S(1)} %get-tuple-element.45), channel_id=1, source_target_pairs={{0,8},{4,12},{8,0},{12,4},{16,24},{20,28},{24,16},{28,20},{1,9},{5... | collective-permute-start | bytes 393224 | tf_op jit(solution)/shard_map/ppermute | solution.py:66
  45.8 7.3 %collective-permute-start.14 = (bf16[256,256]{1,0:T(8,128)(2,1)S(1)}, bf16[256,256]{1,0:T(8,128)(2,1)S(1)}, u32[]{:S(2)}, u32[]{:S(2)}) collective-permute-start(bf16[256,256]{1,0:T(8,128)(2,1)S(1)} %shard_map.147), channel_id=1, source_target_pairs={{0,24},{4,28},{8,16},{12,20},{16,8},{20,12},{24,0},{28,4},{1,25},{... | collective-permute-start | bytes 393224 | tf_op jit(solution)/shard_map/ppermute | solution.py:66
  47.3 7.1 %collective-permute-start.13 = (bf16[256,256]{1,0:T(8,128)(2,1)S(1)}, bf16[256,256]{1,0:T(8,128)(2,1)S(1)}, u32[]{:S(2)}, u32[]{:S(2)}) collective-permute-start(bf16[256,256]{1,0:T(8,128)(2,1)S(1)} %shard_map.147), channel_id=1, source_target_pairs={{0,16},{4,20},{8,24},{12,28},{16,0},{20,4},{24,8},{28,12},{1,17},{... | collective-permute-start | bytes 393224 | tf_op jit(solution)/shard_map/ppermute | solution.py:66
  48.2 6.4 %collective-permute-start.12 = (bf16[256,256]{1,0:T(8,128)(2,1)S(1)}, bf16[256,256]{1,0:T(8,128)(2,1)S(1)}, u32[]{:S(2)}, u32[]{:S(2)}) collective-permute-start(bf16[256,256]{1,0:T(8,128)(2,1)S(1)} %shard_map.147), channel_id=1, source_target_pairs={{0,8},{4,12},{8,0},{12,4},{16,24},{20,28},{24,16},{28,20},{1,9},{5... | collective-permute-start | bytes 393224 | tf_op jit(solution)/shard_map/ppermute | solution.py:66
  49.3 7.3 %copy-start = (bf16[1,704,2048]{2,1,0:T(8,128)(2,1)S(1)}, bf16[1,704,2048]{2,1,0:T(8,128)(2,1)}, u32[]{:S(2)}) copy-start(bf16[1,704,2048]{2,1,0:T(8,128)(2,1)} %param.25) | copy-start | bytes 8650756
  49.4 5.3 %collective-permute-start.19 = (bf16[4,32,2048]{2,1,0:T(8,128)(2,1)S(1)}, bf16[4,32,2048]{2,1,0:T(8,128)(2,1)S(1)}, u32[]{:S(2)}, u32[]{:S(2)}) collective-permute-start(bf16[4,32,2048]{2,1,0:T(8,128)(2,1)S(1)} %pad_maximum_fusion.1.mine_rows), channel_id=1, source_target_pairs={{0,4},{4,0},{8,12},{12,8},{16,20},{20,16},{24,28},{28,24},{1,5},{5... | collective-permute-start | bytes 1572872 | tf_op jit(solution)/shard_map/ppermute | solution.py:66
  54.6 2.0 %collective-permute-start.15 = (bf16[4,256,256]{2,1,0:T(8,128)(2,1)S(1)}, bf16[4,256,256]{2,1,0:T(8,128)(2,1)S(1)}, u32[]{:S(2)}, u32[]{:S(2)}) collective-permute-start(bf16[4,256,256]{2,1,0:T(8,128)(2,1)S(1)} %pad_maximum_fusion.mine_ref), channel_id=1, source_target_pairs={{0,4},{4,0},{8,12},{12,8},{16,20},{20,16},{24,28},{28,24},{1,5},{5... | collective-permute-start | bytes 1572872 | tf_op jit(solution)/shard_map/ppermute | solution.py:66
  58.4 1.6 %collective-permute-start.20 = (bf16[128,1024]{1,0:T(8,128)(2,1)S(1)}, bf16[128,1024]{1,0:T(8,128)(2,1)S(1)}, u32[]{:S(2)}, u32[]{:S(2)}) collective-permute-start(bf16[128,1024]{1,0:T(8,128)(2,1)S(1)} %get-tuple-element.52), channel_id=1, source_target_pairs={{0,4},{4,0},{8,12},{12,8},{16,20},{20,16},{24,28},{28,24},{1,5},{5... | collective-permute-start | bytes 786440 | tf_op jit(solution)/shard_map/ppermute | solution.py:66
  59.1 1.6 %collective-permute-start.21 = (bf16[128,1024]{1,0:T(8,128)(2,1)S(1)}, bf16[128,1024]{1,0:T(8,128)(2,1)S(1)}, u32[]{:S(2)}, u32[]{:S(2)}) collective-permute-start(bf16[128,1024]{1,0:T(8,128)(2,1)S(1)} %get-tuple-element.56), channel_id=1, source_target_pairs={{0,4},{4,0},{8,12},{12,8},{16,20},{20,16},{24,28},{28,24},{1,5},{5... | collective-permute-start | bytes 786440 | tf_op jit(solution)/shard_map/ppermute | solution.py:66
  60.9 6.4 %collective-permute-start.22 = (bf16[32,2048]{1,0:T(8,128)(2,1)S(1)}, bf16[32,2048]{1,0:T(8,128)(2,1)S(1)}, u32[]{:S(2)}, u32[]{:S(2)}) collective-permute-start(bf16[32,2048]{1,0:T(8,128)(2,1)S(1)} %get-tuple-element.58), channel_id=1, source_target_pairs={{0,8},{4,12},{8,0},{12,4},{16,24},{20,28},{24,16},{28,20},{1,9},{5... | collective-permute-start | bytes 393224 | tf_op jit(solution)/shard_map/ppermute | solution.py:66
  61.7 6.1 %collective-permute-start.23 = (bf16[32,2048]{1,0:T(8,128)(2,1)S(1)}, bf16[32,2048]{1,0:T(8,128)(2,1)S(1)}, u32[]{:S(2)}, u32[]{:S(2)}) collective-permute-start(bf16[32,2048]{1,0:T(8,128)(2,1)S(1)} %get-tuple-element.59), channel_id=1, source_target_pairs={{0,16},{4,20},{8,24},{12,28},{16,0},{20,4},{24,8},{28,12},{1,17},{... | collective-permute-start | bytes 393224 | tf_op jit(solution)/shard_map/ppermute | solution.py:66
  62.9 7.1 %collective-permute-start.24 = (bf16[32,2048]{1,0:T(8,128)(2,1)S(1)}, bf16[32,2048]{1,0:T(8,128)(2,1)S(1)}, u32[]{:S(2)}, u32[]{:S(2)}) collective-permute-start(bf16[32,2048]{1,0:T(8,128)(2,1)S(1)} %get-tuple-element.60), channel_id=1, source_target_pairs={{0,24},{4,28},{8,16},{12,20},{16,8},{20,12},{24,0},{28,4},{1,25},{... | collective-permute-start | bytes 393224 | tf_op jit(solution)/shard_map/ppermute | solution.py:66
  70.1 5.1 %collective-permute-start.25 = (bf16[8,2048]{1,0:T(8,128)(2,1)S(1)}, bf16[8,2048]{1,0:T(8,128)(2,1)S(1)}, u32[]{:S(2)}, u32[]{:S(2)}) collective-permute-start(bf16[8,2048]{1,0:T(8,128)(2,1)S(1)} %get-tuple-element.62), channel_id=1, source_target_pairs={{0,1},{1,0},{2,3},{3,2},{4,5},{5,4},{6,7},{7,6},{8,9},{9,8},{10,11... | collective-permute-start | bytes 98312 | tf_op jit(solution)/shard_map/ppermute | solution.py:66
  70.2 5.1 %collective-permute-start.26 = (bf16[8,2048]{1,0:T(8,128)(2,1)S(1)}, bf16[8,2048]{1,0:T(8,128)(2,1)S(1)}, u32[]{:S(2)}, u32[]{:S(2)}) collective-permute-start(bf16[8,2048]{1,0:T(8,128)(2,1)S(1)} %get-tuple-element.63), channel_id=1, source_target_pairs={{0,2},{1,3},{2,0},{3,1},{4,6},{5,7},{6,4},{7,5},{8,10},{9,11},{10,... | collective-permute-start | bytes 98312 | tf_op jit(solution)/shard_map/ppermute | solution.py:66
  72.9 5.7 %collective-permute-start.27 = (bf16[8,2048]{1,0:T(8,128)(2,1)S(1)}, bf16[8,2048]{1,0:T(8,128)(2,1)S(1)}, u32[]{:S(2)}, u32[]{:S(2)}) collective-permute-start(bf16[8,2048]{1,0:T(8,128)(2,1)S(1)} %get-tuple-element.64), channel_id=1, source_target_pairs={{0,3},{1,2},{2,1},{3,0},{4,7},{5,6},{6,5},{7,4},{8,11},{9,10},{10,... | collective-permute-start | bytes 98312 | tf_op jit(solution)/shard_map/ppermute | solution.py:66
